TPU v7x, 32 devices: a whole 2x2x4 slice. The times are simulated.
32 devices in a mesh: range: 8 (over z, y), alt: 4 (over x, core), freq: 1.
Axes of the slice: x: 2, y: 2, z: 4, core: 2. Of those that a mesh axis runs over, the one named last changes fastest.
Arguments:
- freq_scale: float32 [2], P('freq'), may hold values from 1 to 2
- base_profile: float32 [1024], P('alt'), may hold values from 1.5 to 3
- perturb: float32 [32, 1024], P('range', 'alt'), may hold values from -1 to 1
- start_block: float32 [96, 1024], P(None, 'alt'), may hold values from -6 to 6
- source: float32 [2, 2, 96], P('freq'), may hold values from -6 to 6
Outputs:
- field: float32 [2, 32, 2, 1024], P('freq', 'range', None, 'alt')
All inputs are finite; a program needn't handle non-finite values.
Results may differ from a plain program's by a relative error of at most 0.0003.
Values sent between devices are 32-bit elements; how exact they have to be, the bound alone decides.
No kernel may reach another device: no remote copies, remote signals or barrier semaphores. Data moves between devices by JAX's collectives and lax.ppermute only.
A program may use at most 128 MiB of HBM per device.

v0:
```python
import jax
import jax.numpy as jnp
from jax import lax
from jax.sharding import PartitionSpec as P

ITERS = 8


phase_step = 0.15
relief = 0.1


def with_halo(block, sides, width):
    for axis, dim in sides:
        count = lax.axis_size(axis)
        forward = [(i, i + 1) for i in range(count - 1)]
        backward = [(target, source) for source, target in forward]
        low = lax.ppermute(
            lax.slice_in_dim(block, block.shape[dim] - width, None, axis=dim), axis, forward
        )
        high = lax.ppermute(lax.slice_in_dim(block, 0, width, axis=dim), axis, backward)
        block = jnp.concatenate([low, block, high], axis=dim)
    return block


def shifted(value, axis, steps):
    count = lax.axis_size(axis)
    first, last = (max(0, -steps), min(count, count - steps))
    return lax.ppermute(value, axis, [(source, source + steps) for source in range(first, last)])


def mult(left, right):
    return jnp.einsum("...ij,...jk->...ik", left, right, precision=lax.Precision.HIGHEST)


def inner(left, right):
    return jnp.einsum("...mz,...nz->...mn", left, right, precision=lax.Precision.HIGHEST)


def solve_lower(lower, values):
    return lax.linalg.triangular_solve(lower, values, left_side=True, lower=True)


def build_transfer(ritz, correlation):
    count = ritz.shape[-1]
    unit = jnp.eye(count, dtype=ritz.dtype)
    phase = phase_step * ritz
    square = mult(phase, phase)
    cosine = unit - 0.5 * square + mult(square, square) / 24.0
    sine = phase - mult(phase, square) / 6.0
    turned = mult(correlation, cosine)
    skewed = mult(correlation, sine)
    upper = jnp.concatenate([turned, -skewed], axis=-1)
    below = jnp.concatenate([skewed, turned], axis=-1)
    return jnp.concatenate([upper, below], axis=-2)


def local(freq_scale, base_profile, perturb, start_block, source):
    freqs = freq_scale.shape[0]
    seg_count = perturb.shape[0]
    modes = start_block.shape[0]
    alt_local = start_block.shape[1]
    alt_total = alt_local * lax.axis_size("alt")
    coef = (
        freq_scale[:, None, None, None]
        * (base_profile[None, :] * (1.0 + relief * perturb))[None, :, None, :]
    )

    def apply_operator(block):
        padded = with_halo(block, (("alt", 3),), 1)
        return coef * block + 0.5 * (padded[..., 2:] + padded[..., :-2])

    iter_count = ITERS
    basis = jnp.broadcast_to(
        start_block / jnp.sqrt(float(alt_total)), (freqs, seg_count) + start_block.shape
    )
    for step in range(iter_count):
        image = apply_operator(basis)
        gram = lax.psum(inner(image, image), "alt")
        basis = solve_lower(jnp.linalg.cholesky(gram), image)
    himage = apply_operator(basis)
    upcoming = shifted(basis[:, 0], "range", -1)
    ahead = jnp.concatenate([basis[:, 1:], upcoming[:, None]], axis=1)
    ritz, correlation = lax.psum((inner(basis, himage), inner(ahead, basis)), "alt")
    transfer = build_transfer(ritz, correlation)
    width = 2 * modes
    product = jnp.broadcast_to(jnp.eye(width, dtype=jnp.float32), (freqs, width, width))
    for seg in range(seg_count):
        product = mult(transfer[:, seg], product)
    start = jnp.concatenate([source[:, 0], source[:, 1]], axis=-1)
    position = lax.axis_index("range")
    carry = jnp.where(position == 0, start, jnp.zeros_like(start))

    def relay_step(turn, state):
        leaving = jnp.einsum("fij,fj->fi", product, state, precision=lax.Precision.HIGHEST)
        arrived = shifted(leaving, "range", 1)
        return jnp.where(position == turn + 1, arrived, state)

    carry = lax.fori_loop(0, lax.axis_size("range") - 1, relay_step, carry)
    amp_list = []
    state = carry
    for seg in range(seg_count):
        amp_list.append(state)
        if seg + 1 < seg_count:
            state = jnp.einsum(
                "fij,fj->fi", transfer[:, seg], state, precision=lax.Precision.HIGHEST
            )
    amps = jnp.stack(amp_list, axis=1).reshape(freqs, seg_count, 2, modes)
    scale = jnp.sqrt(float(alt_total) / float(modes))
    return scale * jnp.einsum("fspm,fsmz->fspz", amps, basis, precision=lax.Precision.HIGHEST)


def solution(mesh):
    in_specs = (P("freq"), P("alt"), P("range", "alt"), P(None, "alt"), P("freq", None, None))
    out_specs = P("freq", "range", None, "alt")
    return jax.shard_map(local, mesh=mesh, in_specs=in_specs, out_specs=out_specs, check_vma=False)
```

profile of v0, /device:TPU:0, one launch (start us, length us, event | category | flops | bytes accessed | tf_op | source)
XLA Modules:
  0.0 1562.0 jit_solution(673033635187756319)
XLA Ops:
  16.3 40.6 %all-reduce.11.cloned.1.call-done = f32[2,4,96,96]{2,3,1,0:T(8,128)} async-done(((f32[2,4,96,96]{2,3,1,0:T(8,128)}), f32[2,4,96,96]{2,3,1,0:T(8,128)}) %all-reduce.11.cloned.1.call-update) | async-done | bytes 294928 | tf_op jit(solution)/shard_map/psum | solution.py:79
  59.1 70.3 %custom-call.20 = f32[2,4,96,96]{3,2,1,0:T(8,128)S(1)} custom-call(f32[2,4,96,96]{3,2,1,0:T(8,128)S(1)} %fusion.64), custom_call_target="Cholesky" | custom-call | tf_op jit(solution)/shard_map/jit(cholesky)/cholesky | solution.py:80
  129.8 59.0 %custom-call.21 = f32[2,4,1,96,96]{3,4,2,1,0:T(8,128)S(1)} custom-call(f32[2,4,1,96,96]{4,3,2,1,0:T(8,128)S(1)} %select_bitcast_fusion.7), custom_call_target="InvertDiagBlocksLowerTriangular" | custom-call | tf_op jit(solution)/shard_map/triangular_solve/custom-call.0 | solution.py:41
  198.9 37.7 %all-reduce.13.cloned.1.call-done = f32[2,4,96,96]{2,3,1,0:T(8,128)} async-done(((f32[2,4,96,96]{2,3,1,0:T(8,128)}), f32[2,4,96,96]{2,3,1,0:T(8,128)}) %all-reduce.13.cloned.1.call-update) | async-done | bytes 294928 | tf_op jit(solution)/shard_map/psum | solution.py:79
  238.8 70.3 %custom-call.22 = f32[2,4,96,96]{3,2,1,0:T(8,128)S(1)} custom-call(f32[2,4,96,96]{3,2,1,0:T(8,128)S(1)} %fusion.61), custom_call_target="Cholesky" | custom-call | tf_op jit(solution)/shard_map/jit(cholesky)/cholesky | solution.py:80
  309.5 59.0 %custom-call.23 = f32[2,4,1,96,96]{3,4,2,1,0:T(8,128)S(1)} custom-call(f32[2,4,1,96,96]{4,3,2,1,0:T(8,128)S(1)} %select_bitcast_fusion.6), custom_call_target="InvertDiagBlocksLowerTriangular" | custom-call | tf_op jit(solution)/shard_map/triangular_solve/custom-call.0 | solution.py:41
  378.9 37.5 %all-reduce.15.cloned.1.call-done = f32[2,4,96,96]{2,3,1,0:T(8,128)} async-done(((f32[2,4,96,96]{2,3,1,0:T(8,128)}), f32[2,4,96,96]{2,3,1,0:T(8,128)}) %all-reduce.15.cloned.1.call-update) | async-done | bytes 294928 | tf_op jit(solution)/shard_map/psum | solution.py:79
  418.6 70.3 %custom-call.24 = f32[2,4,96,96]{3,2,1,0:T(8,128)S(1)} custom-call(f32[2,4,96,96]{3,2,1,0:T(8,128)S(1)} %fusion.58), custom_call_target="Cholesky" | custom-call | tf_op jit(solution)/shard_map/jit(cholesky)/cholesky | solution.py:80
  489.3 59.0 %custom-call.25 = f32[2,4,1,96,96]{3,4,2,1,0:T(8,128)S(1)} custom-call(f32[2,4,1,96,96]{4,3,2,1,0:T(8,128)S(1)} %select_bitcast_fusion.5), custom_call_target="InvertDiagBlocksLowerTriangular" | custom-call | tf_op jit(solution)/shard_map/triangular_solve/custom-call.0 | solution.py:41
  558.3 37.8 %all-reduce.17.cloned.1.call-done = f32[2,4,96,96]{2,3,1,0:T(8,128)} async-done(((f32[2,4,96,96]{2,3,1,0:T(8,128)}), f32[2,4,96,96]{2,3,1,0:T(8,128)}) %all-reduce.17.cloned.1.call-update) | async-done | bytes 294928 | tf_op jit(solution)/shard_map/psum | solution.py:79
  598.3 70.3 %custom-call.26 = f32[2,4,96,96]{3,2,1,0:T(8,128)S(1)} custom-call(f32[2,4,96,96]{3,2,1,0:T(8,128)S(1)} %fusion.55), custom_call_target="Cholesky" | custom-call | tf_op jit(solution)/shard_map/jit(cholesky)/cholesky | solution.py:80
  669.0 59.0 %custom-call.27 = f32[2,4,1,96,96]{3,4,2,1,0:T(8,128)S(1)} custom-call(f32[2,4,1,96,96]{4,3,2,1,0:T(8,128)S(1)} %select_bitcast_fusion.4), custom_call_target="InvertDiagBlocksLowerTriangular" | custom-call | tf_op jit(solution)/shard_map/triangular_solve/custom-call.0 | solution.py:41
  737.5 38.6 %all-reduce.19.cloned.1.call-done = f32[2,4,96,96]{2,3,1,0:T(8,128)} async-done(((f32[2,4,96,96]{2,3,1,0:T(8,128)}), f32[2,4,96,96]{2,3,1,0:T(8,128)}) %all-reduce.19.cloned.1.call-update) | async-done | bytes 294928 | tf_op jit(solution)/shard_map/psum | solution.py:79
  778.3 70.3 %custom-call.28 = f32[2,4,96,96]{3,2,1,0:T(8,128)S(1)} custom-call(f32[2,4,96,96]{3,2,1,0:T(8,128)S(1)} %fusion.52), custom_call_target="Cholesky" | custom-call | tf_op jit(solution)/shard_map/jit(cholesky)/cholesky | solution.py:80
  849.0 59.0 %custom-call.29 = f32[2,4,1,96,96]{3,4,2,1,0:T(8,128)S(1)} custom-call(f32[2,4,1,96,96]{4,3,2,1,0:T(8,128)S(1)} %select_bitcast_fusion.3), custom_call_target="InvertDiagBlocksLowerTriangular" | custom-call | tf_op jit(solution)/shard_map/triangular_solve/custom-call.0 | solution.py:41
  918.1 37.8 %all-reduce.21.cloned.1.call-done = f32[2,4,96,96]{2,3,1,0:T(8,128)} async-done(((f32[2,4,96,96]{2,3,1,0:T(8,128)}), f32[2,4,96,96]{2,3,1,0:T(8,128)}) %all-reduce.21.cloned.1.call-update) | async-done | bytes 294928 | tf_op jit(solution)/shard_map/psum | solution.py:79
  958.1 70.3 %custom-call.30 = f32[2,4,96,96]{3,2,1,0:T(8,128)S(1)} custom-call(f32[2,4,96,96]{3,2,1,0:T(8,128)S(1)} %fusion.49), custom_call_target="Cholesky" | custom-call | tf_op jit(solution)/shard_map/jit(cholesky)/cholesky | solution.py:80
  1028.8 59.0 %custom-call.31 = f32[2,4,1,96,96]{3,4,2,1,0:T(8,128)S(1)} custom-call(f32[2,4,1,96,96]{4,3,2,1,0:T(8,128)S(1)} %select_bitcast_fusion.2), custom_call_target="InvertDiagBlocksLowerTriangular" | custom-call | tf_op jit(solution)/shard_map/triangular_solve/custom-call.0 | solution.py:41
  1097.9 37.7 %all-reduce.23.cloned.1.call-done = f32[2,4,96,96]{2,3,1,0:T(8,128)} async-done(((f32[2,4,96,96]{2,3,1,0:T(8,128)}), f32[2,4,96,96]{2,3,1,0:T(8,128)}) %all-reduce.23.cloned.1.call-update) | async-done | bytes 294928 | tf_op jit(solution)/shard_map/psum | solution.py:79
  1137.8 70.3 %custom-call.32 = f32[2,4,96,96]{3,2,1,0:T(8,128)S(1)} custom-call(f32[2,4,96,96]{3,2,1,0:T(8,128)S(1)} %fusion.46), custom_call_target="Cholesky" | custom-call | tf_op jit(solution)/shard_map/jit(cholesky)/cholesky | solution.py:80
  1208.5 59.0 %custom-call.33 = f32[2,4,1,96,96]{3,4,2,1,0:T(8,128)S(1)} custom-call(f32[2,4,1,96,96]{4,3,2,1,0:T(8,128)S(1)} %select_bitcast_fusion.1), custom_call_target="InvertDiagBlocksLowerTriangular" | custom-call | tf_op jit(solution)/shard_map/triangular_solve/custom-call.0 | solution.py:41
  1277.9 37.5 %all-reduce.25.cloned.1.call-done = f32[2,4,96,96]{2,3,1,0:T(8,128)} async-done(((f32[2,4,96,96]{2,3,1,0:T(8,128)}), f32[2,4,96,96]{2,3,1,0:T(8,128)}) %all-reduce.25.cloned.1.call-update) | async-done | bytes 294928 | tf_op jit(solution)/shard_map/psum | solution.py:79
  1317.5 70.3 %custom-call.34 = f32[2,4,96,96]{3,2,1,0:T(8,128)S(1)} custom-call(f32[2,4,96,96]{3,2,1,0:T(8,128)S(1)} %fusion.43), custom_call_target="Cholesky" | custom-call | tf_op jit(solution)/shard_map/jit(cholesky)/cholesky | solution.py:80
  1388.2 59.0 %custom-call.35 = f32[2,4,1,96,96]{3,4,2,1,0:T(8,128)S(1)} custom-call(f32[2,4,1,96,96]{4,3,2,1,0:T(8,128)S(1)} %select_bitcast_fusion), custom_call_target="InvertDiagBlocksLowerTriangular" | custom-call | tf_op jit(solution)/shard_map/triangular_solve/custom-call.0 | solution.py:41
  1456.8 5.2 collective-permute-done.17
  1463.7 34.8 %all-reduce.27.cloned.1.call-done = (f32[2,4,96,96]{3,2,1,0:T(8,128)}, f32[2,4,96,96]{3,2,1,0:T(8,128)}) async-done(((f32[2,4,96,96]{3,2,1,0:T(8,128)}, f32[2,4,96,96]{3,2,1,0:T(8,128)}), (f32[2,4,96,96]{3,2,1,0:T(8,128)}, f32[2,4,96,96]{3,2,1,0:T(8,128)})) %all-reduce.27.cloned.1.call-update) | async-done | bytes 589840 | tf_op jit(solution)/shard_map/psum | solution.py:84
  1508.5 44.4 %while.13 = (s32[]{:T(128)}, f32[2,192]{1,0:T(2,128)S(1)}, s32[]{:T(128)}, f32[2,192,192]{2,1,0:T(8,128)S(1)}, s32[]{:T(128)}) while((s32[]{:T(128)}, f32[2,192]{1,0:T(2,128)S(1)}, s32[]{:T(128)}, f32[2,192,192]{2,1,0:T(8,128)S(1)}, s32[]{:T(128)}) %tuple.45), condition=%wide.region_13.16_spmd, body=%wide.region_12.15_spmd.sunk | while | flops 885123 | bytes 311919 | solution.py:99
  1519.9 4.3 collective-permute-start
  1526.0 5.1 collective-permute-start
  1532.8 5.1 collective-permute-start
  1539.7 5.1 collective-permute-start
  1546.5 5.1 collective-permute-start
  (191 shorter events, 143.1 us)
Async XLA Ops:
  6.5 50.4 %all-reduce.11.cloned.1.call-start = ((), (), s32[]{:S(2)}) async-start(), calls=%async_computation | async-start | bytes 786432 | tf_op jit(solution)/shard_map/psum | solution.py:79
  7.7 5.9 collective-permute-start.1
  9.1 4.5 collective-permute-start.2
  16.2 220.4 %all-reduce.13.cloned.1.call-start = ((), (), s32[]{:S(2)}) async-start(), calls=%async_computation.1 | async-start | bytes 786432 | tf_op jit(solution)/shard_map/psum | solution.py:79
  190.4 4.4 collective-permute-start.3
  191.7 4.4 collective-permute-start.4
  198.6 217.8 %all-reduce.15.cloned.1.call-start = ((), (), s32[]{:S(2)}) async-start(), calls=%async_computation.2 | async-start | bytes 786432 | tf_op jit(solution)/shard_map/psum | solution.py:79
  370.1 4.4 collective-permute-start.5
  371.4 4.4 collective-permute-start.6
  378.3 217.8 %all-reduce.17.cloned.1.call-start = ((), (), s32[]{:S(2)}) async-start(), calls=%async_computation.3 | async-start | bytes 786432 | tf_op jit(solution)/shard_map/psum | solution.py:79
  549.9 4.4 collective-permute-start.7
  551.2 4.4 collective-permute-start.8
  558.0 218.1 %all-reduce.19.cloned.1.call-start = ((), (), s32[]{:S(2)}) async-start(), calls=%async_computation.4 | async-start | bytes 786432 | tf_op jit(solution)/shard_map/psum | solution.py:79
  737.3 218.6 %all-reduce.21.cloned.1.call-start = ((), (), s32[]{:S(2)}) async-start(), calls=%async_computation.5 | async-start | bytes 786432 | tf_op jit(solution)/shard_map/psum | solution.py:79
  909.6 4.4 collective-permute-start.11
  910.9 4.4 collective-permute-start.12
  917.8 217.8 %all-reduce.23.cloned.1.call-start = ((), (), s32[]{:S(2)}) async-start(), calls=%async_computation.6 | async-start | bytes 786432 | tf_op jit(solution)/shard_map/psum | solution.py:79
  1090.7 4.4 collective-permute-start.14
  1097.5 217.8 %all-reduce.25.cloned.1.call-start = ((), (), s32[]{:S(2)}) async-start(), calls=%async_computation.7 | async-start | bytes 786432 | tf_op jit(solution)/shard_map/psum | solution.py:79
  1269.1 4.4 collective-permute-start.15
  1270.4 4.4 collective-permute-start.16
  1277.3 221.3 %all-reduce.27.cloned.1.call-start = ((), (), s32[]{:S(2)}) async-start(), calls=%async_computation.8 | async-start | bytes 1572864 | tf_op jit(solution)/shard_map/psum | solution.py:84
  1448.8 5.9 collective-permute-start.18
  1450.1 4.6 collective-permute-start.19
  1453.3 8.7 collective-permute-start.17
  1508.9 4.7 collective-permute-start
  1514.0 5.5 collective-permute-start
  1519.9 5.6 collective-permute-start
  1526.0 6.4 collective-permute-start
  1532.8 6.4 collective-permute-start
  1539.7 6.4 collective-permute-start
  1546.5 6.4 collective-permute-start
  (5 other events, 23.5 us)
Sparse Core Ops, SparseCore 0:
  16.3 40.5 all-reduce.10
  198.7 37.8 all-reduce.12
  378.4 37.8 all-reduce.14
  558.2 37.8 all-reduce.16
  737.4 38.7 all-reduce.18
  917.9 37.8 all-reduce.20
  1097.7 37.8 all-reduce.22
  1277.4 37.8 all-reduce.24
  1463.7 34.7 all-reduce.26
where the time goes:
time: 1570 us; the launch traced here: 1560 us
  other arithmetic  1050 us (67%)
  waiting for transfers between devices  365 us (23%)
  starting transfers between devices  73.6 us (5%)
  matrix products  49.3 us (3%)
    another operation x25, other arithmetic, local(): basis = solve_lower(jnp.linalg.cholesky(gram), image)  564 us
    another operation x17, other arithmetic, solve_lower(): lax.linalg.triangular_solve(lower, values, left_side=True, lower=True)  473 us
    psum x8, waiting for transfers between devices, local(): gram = lax.psum(inner(image, image), 'alt')  305 us
    psum x1, waiting for transfers between devices, local(): lax.psum((inner(basis, himage), inner(ahead, basis)), 'alt')  34.8 us
    ppermute x8, starting transfers between devices, shifted(): lax.ppermute(value, axis, [(source, source + steps) for source in range(f...  33.6 us
  transfers between devices with their start and end apart: 35, of which 24 were waited for; matrix products, arithmetic and copies ran while one was open for 0% of the time, Pallas kernels for 0%

commit v1 on v0

v1 whole, which is shorter than its diff:
```python
import functools

import jax
import jax.numpy as jnp
from jax import lax
from jax.experimental import pallas as pl
from jax.experimental.pallas import tpu as pltpu
from jax.sharding import PartitionSpec as P

ITERS = 8

phase_step = 0.15
relief = 0.1
HIGHEST = lax.Precision.HIGHEST
VMEM_LIMIT = 48 * 2**20


def mm(left, right):
    return lax.dot_general(
        left, right, (((1,), (0,)), ((), ())), precision=HIGHEST, preferred_element_type=jnp.float32
    )


def mmt(left, right):
    return lax.dot_general(
        left, right, (((1,), (1,)), ((), ())), precision=HIGHEST, preferred_element_type=jnp.float32
    )


def kernel_call(body, out_shape, args, specs, scratch=(), flops=0):
    nbytes = sum(4 * a.size for a in args) + sum(4 * o.size for o in jax.tree.leaves(out_shape))
    return pl.pallas_call(
        body,
        out_shape=out_shape,
        in_specs=specs,
        out_specs=jax.tree.map(lambda _: pl.BlockSpec(memory_space=pltpu.VMEM), out_shape),
        scratch_shapes=scratch,
        cost_estimate=pl.CostEstimate(flops=flops, bytes_accessed=nbytes, transcendentals=0),
        compiler_params=pltpu.CompilerParams(vmem_limit_bytes=VMEM_LIMIT),
    )(*args)


VM = pl.BlockSpec(memory_space=pltpu.VMEM)
SM = pl.BlockSpec(memory_space=pltpu.SMEM)


def shape(*dims):
    return jax.ShapeDtypeStruct(dims, jnp.float32)


def row_of(value, at):
    return jnp.broadcast_to(value[at : at + 1, :], value.shape)


def lane_of(value, at):
    return jnp.broadcast_to(value[:, at : at + 1], value.shape)


def inverse_factors(grams):
    blocks = len(grams[0])
    lanes = lax.broadcasted_iota(jnp.int32, (8, 128), 1)
    subs = lax.broadcasted_iota(jnp.int32, (8, 128), 0)
    works = [list(gram) for gram in grams]
    results = [[None] * blocks for _ in grams]
    for k in range(blocks):
        first = 8 * k
        panels = [
            [[lane_of(work[v], first + c) for v in range(k, blocks)] for c in range(8)]
            for work in works
        ]
        pivots = [jnp.ones((8, 128), jnp.float32) for _ in works]
        for c in range(8):
            for i, work in enumerate(works):
                panel = panels[i]
                pivot = row_of(panel[c][0], c)
                inv = pltpu.reciprocal(pivot, approx=True)
                inv = inv * (2.0 - pivot * inv)
                pivots[i] = jnp.where(subs == c, pivot, pivots[i])
                factor = [column * inv for column in panel[c]]
                factor[0] = jnp.where(subs > c, factor[0], 0.0)
                line = row_of(work[k], c) + jnp.where(lanes == first + c, 1.0, 0.0)
                for d in range(c + 1, 8):
                    weight = row_of(panel[d][0], c)
                    panel[d][0] = panel[d][0] - (panel[c][0] * weight) * inv
                    for v in range(1, blocks - k):
                        panel[d][v] = panel[d][v] - factor[v] * weight
                for v in range(blocks - k):
                    work[k + v] = work[k + v] - factor[v] * line
        for i, work in enumerate(works):
            unit = jnp.where(lanes == subs + first, 1.0, 0.0)
            results[i][k] = jnp.where(lanes < subs + first, work[k], unit) * lax.rsqrt(pivots[i])
    return results


def edge_weights(width):
    lanes = lax.broadcasted_iota(jnp.int32, (1, width), 1)
    return jnp.where(lanes == 0, 0.0, 0.5), jnp.where(lanes == width - 1, 0.0, 0.5)


def apply_rows(value, coef, from_low, from_high):
    width = value.shape[1]
    return (
        coef * value
        + from_low * pltpu.roll(value, 1, 1)
        + from_high * pltpu.roll(value, width - 1, 1)
    )


def iterate_body(n_alt, chunk, seg_count, modes, width, scale_ref, *refs):
    blocks = refs[:n_alt]
    out_refs = refs[n_alt : n_alt + chunk]
    coef_ref, image_ref, gram_ref, inv_ref = refs[n_alt + chunk :]
    place = lax.axis_index("alt")
    flat = place * chunk
    freq = flat // seg_count
    first = flat - freq * seg_count
    total = n_alt * width
    for k, block in enumerate(blocks):
        source = lax.rem(place + n_alt - k, n_alt)
        span = pl.ds(pl.multiple_of(source * width, width), width)
        start = block[0:modes, :] * (1.0 / float(total) ** 0.5)
        for i in range(chunk):
            out_refs[i][:, span] = start
            change = block[pl.ds(modes + 1 + first + i, 1), :]
            coef_ref[i : i + 1, span] = scale_ref[freq] * (
                block[modes : modes + 1, :] * (1.0 + relief * change)
            )
    from_low, from_high = edge_weights(total)
    down = 2.0**-11
    gram_ref[...] = jnp.zeros_like(gram_ref)

    def step(_, carry):
        for i in range(chunk):
            coef = coef_ref[i : i + 1, :]
            for at in range(0, modes, 8):
                image_ref[i, at : at + 8, :] = apply_rows(
                    out_refs[i][at : at + 8, :], coef, from_low, from_high
                )
            image = image_ref[i]
            gram_ref[i, :, 0:modes] = mmt(image, image) * down
        grams = [[gram_ref[i, at : at + 8, :] for at in range(0, modes, 8)] for i in range(chunk)]
        results = inverse_factors(grams)
        for i in range(chunk):
            for at in range(0, modes, 8):
                inv_ref[i, at : at + 8, :] = results[i][at // 8] * down**0.5
        for i in range(chunk):
            inv = inv_ref[i, :, 0:modes]
            for at in range(0, total, 256):
                out_refs[i][:, at : at + 256] = mm(inv, image_ref[i, :, at : at + 256])
        return carry

    lax.fori_loop(0, ITERS, step, 0)


def unit_of(modes):
    rows = lax.broadcasted_iota(jnp.int32, (modes, modes), 0)
    return jnp.where(rows == lax.broadcasted_iota(jnp.int32, (modes, modes), 1), 1.0, 0.0)


def complex_mm(left, right):
    return (
        mm(left[0], right[0]) - mm(left[1], right[1]),
        mm(left[0], right[1]) + mm(left[1], right[0]),
    )


def advance_body(modes, total, coef_ref, first_ref, second_ref, inner_ref, rest_ref, image_ref):
    from_low, from_high = edge_weights(total)
    unit = unit_of(modes)
    turns = []
    for i, ref in enumerate((first_ref, second_ref)):
        for at in range(0, modes, 8):
            image_ref[at : at + 8, :] = apply_rows(
                ref[at : at + 8, :], coef_ref[i : i + 1, :], from_low, from_high
            )
        phase = phase_step * mmt(ref[...], image_ref[...])
        square = mm(phase, phase)
        turns.append(
            (unit - 0.5 * square + mm(square, square) / 24.0, phase - mm(phase, square) / 6.0)
        )
    corr = mmt(second_ref[...], first_ref[...])
    inner = (mm(corr, turns[0][0]), mm(corr, turns[0][1]))
    rest = complex_mm(turns[1], inner)
    for part in range(2):
        inner_ref[part] = inner[part]
        rest_ref[part] = rest[part]


def product_body(next_ref, second_ref, rest_ref, out_ref):
    corr = mmt(next_ref[...], second_ref[...])
    for part in range(2):
        out_ref[part] = mm(corr, rest_ref[part])


def chain_place(halves):
    return lax.axis_index("range") * halves + lax.rem(lax.axis_index("alt"), halves)


def padded(ref, missing):
    return (ref[0] + jnp.where(missing, unit_of(ref.shape[1]), 0.0), ref[1])


def join_body(halves, back_new, back_old, new_ref, old_ref, out_ref):
    at = chain_place(halves)
    new = padded(new_ref, at < back_new) if back_new else (new_ref[0], new_ref[1])
    real, imag = complex_mm(new, padded(old_ref, at < back_old))
    out_ref[0] = real
    out_ref[1] = imag


def turn_vector(matrix, vector):
    rows = lax.broadcasted_iota(jnp.int32, vector.shape, 0)
    swapped = jnp.where(
        rows == 0, -row_of(vector, 1), jnp.where(rows == 1, row_of(vector, 0), 0.0)
    )
    return mmt(vector, matrix[0]) + mmt(swapped, matrix[1])


def source_rows(source_ref, halves):
    return source_ref[lax.axis_index("alt") // halves]


def early_body(halves, span_ref, source_ref, out_ref):
    out_ref[...] = turn_vector((span_ref[0], span_ref[1]), source_rows(source_ref, halves))


def field_body(halves, back, n_alt, width, scale, *refs):
    span_ref, early_ref, came_ref, inner_ref, first_ref, second_ref, out_ref = refs
    at = chain_place(halves)
    came = turn_vector((span_ref[0], span_ref[1]), came_ref[...])
    amp = jnp.where(at < back, early_ref[...], came)
    amps = (amp, turn_vector((inner_ref[0], inner_ref[1]), amp))
    for i, ref in enumerate((first_ref, second_ref)):
        for k in range(n_alt):
            part = mm(amps[i], ref[:, k * width : (k + 1) * width])
            out_ref[k, i] = scale * part[0:2, :]


def local(freq_scale, base_profile, perturb, start_block, source):
    freqs = freq_scale.shape[0]
    seg_count = perturb.shape[0]
    modes, width = start_block.shape
    n_alt = lax.axis_size("alt")
    n_range = lax.axis_size("range")
    total = width * n_alt
    chunk = freqs * seg_count // n_alt
    halves = seg_count // chunk
    length = n_range * halves
    assert chunk == 2 and halves * chunk == seg_count and halves * freqs == n_alt

    def along_chain(value, steps):
        pairs = []
        for freq in range(freqs):
            for at in range(max(0, -steps), min(length, length - steps)):
                ends = []
                for d in (at, at + steps):
                    ends.append(d // halves * n_alt + freq * halves + d % halves)
                pairs.append(tuple(ends))
        return lax.ppermute(value, ("range", "alt"), pairs)

    lines = [start_block, base_profile[None, :], perturb]
    filler = -(modes + 1 + seg_count) % 8
    mine = jnp.concatenate(lines + [jnp.zeros((filler, width), jnp.float32)], axis=0)
    blocks = [mine]
    for k in range(1, n_alt):
        blocks.append(lax.ppermute(mine, "alt", [(i, (i + k) % n_alt) for i in range(n_alt)]))
    flops = 2 * modes * modes * total
    first, second, coef = kernel_call(
        functools.partial(iterate_body, n_alt, chunk, seg_count, modes, width),
        [shape(modes, total)] * chunk + [shape(chunk, total)],
        [freq_scale] + blocks,
        [SM] + [VM] * n_alt,
        [pltpu.VMEM((chunk, modes, total), jnp.float32)]
        + [pltpu.VMEM((chunk, modes, 128), jnp.float32)] * 2,
        flops=2 * ITERS * chunk * flops,
    )
    following = along_chain(first, -1)
    inner, rest = kernel_call(
        functools.partial(advance_body, modes, total),
        [shape(2, modes, modes)] * 2,
        [coef, first, second],
        [VM] * 3,
        [pltpu.VMEM((modes, total), jnp.float32)],
        flops=8 * flops,
    )
    product = kernel_call(
        product_body, shape(2, modes, modes), [following, second, rest], [VM] * 3, flops=flops
    )
    reach = 2
    span = kernel_call(
        functools.partial(join_body, halves, 1, 2),
        shape(2, modes, modes),
        [along_chain(product, 1), along_chain(product, 2)],
        [VM] * 2,
        flops=flops,
    )
    while 2 * reach < length:
        span = kernel_call(
            functools.partial(join_body, halves, 0, reach),
            shape(2, modes, modes),
            [span, along_chain(span, reach)],
            [VM] * 2,
            flops=flops,
        )
        reach *= 2
    rows = jnp.concatenate([source, jnp.zeros((freqs, 6, modes), jnp.float32)], axis=1)
    early = kernel_call(
        functools.partial(early_body, halves), shape(8, modes), [span, rows], [VM] * 2
    )
    parts = kernel_call(
        functools.partial(
            field_body, halves, reach, n_alt, width, (float(total) / float(modes)) ** 0.5
        ),
        shape(n_alt, chunk, 2, width),
        [span, early, along_chain(early, reach), inner, first, second],
        [VM] * 6,
    )
    field = lax.all_to_all(parts, "alt", 0, 0)
    return field.reshape(freqs, seg_count, 2, width)


def solution(mesh):
    in_specs = (P("freq"), P("alt"), P("range", "alt"), P(None, "alt"), P("freq", None, None))
    out_specs = P("freq", "range", None, "alt")
    return jax.shard_map(local, mesh=mesh, in_specs=in_specs, out_specs=out_specs, check_vma=False)
```

time: 1570 us -> 107 us (0.07)
  other arithmetic: 1050 us -> 0.98 us
  waiting for transfers between devices: 365 us -> 11.5 us
  Pallas kernels: 0 us -> 53.9 us
  matrix products: 49.3 us -> 0 us
  starting transfers between devices: 73.6 us -> 32.4 us
    another operation x42 -> x0, other arithmetic: 1040 us -> none  [the longest x25 564 us: local(): basis = solve_lower(jnp.linalg.cholesky(gram), image)]
    psum x9 -> x0, waiting for transfers between devices: 340 us -> none  [the longest x8 305 us: local(): gram = lax.psum(inner(image, image), 'alt')]
    pallas_call x0 -> x8, Pallas kernels: none -> 53.9 us  [kernel_call(): pl.pallas_call(body, out_shape=out_shape, in_specs=specs, out_specs=jax.t...]
    ppermute x26 -> x9, starting transfers between devices: 71 us -> 32.4 us  [the longest x6 28 us: along_chain(): return lax.ppermute(value, ('range', 'alt'), pairs)]
    dot_general x30 -> x0, matrix products: 37.9 us -> none  [the longest x10 23.5 us: inner(): jnp.einsum('...mz,...nz->...mn', left, right, precision=lax.Precision.HIG...]
  transfers between devices with their start and end apart: 35 -> 9, of which waited for: 24 -> 7; matrix products, arithmetic and copies ran while one was open for 0% -> 0% of each run, Pallas kernels for 0% -> 3%
where the time goes in v1:
time: 107 us
  Pallas kernels  53.9 us (50%)
  starting transfers between devices  32.4 us (30%)
  waiting for transfers between devices  11.5 us (11%)
  blocking collectives  6.42 us (6%)
  local copies, waits for them, and re-layouts  1.38 us (1%)
    pallas_call x8, Pallas kernels, kernel_call(): pl.pallas_call(body, out_shape=out_shape, in_specs=specs, out_specs=jax.t...  53.9 us
    ppermute x6, starting transfers between devices, along_chain(): return lax.ppermute(value, ('range', 'alt'), pairs)  28 us
    ppermute x6, waiting for transfers between devices, along_chain(): return lax.ppermute(value, ('range', 'alt'), pairs)  7.87 us
    all_to_all x1, blocking collectives, local(): field = lax.all_to_all(parts, 'alt', 0, 0)  6.42 us
    ppermute x3, starting transfers between devices, local(): lax.ppermute(mine, 'alt', [(i, (i + k) % n_alt) for i in range(n_alt)])  4.46 us
    ppermute x3, waiting for transfers between devices, local(): lax.ppermute(mine, 'alt', [(i, (i + k) % n_alt) for i in range(n_alt)])  3.6 us
  transfers between devices with their start and end apart: 9, of which 7 were waited for; matrix products, arithmetic and copies ran while one was open for 0% of the time, Pallas kernels for 3%

profile of v1, /device:TPU:0, one launch (start us, length us, event | category | flops | bytes accessed | tf_op | source)
XLA Modules:
  0.0 106.8 jit_solution(3824221816021335134)
XLA Ops:
  0.0 0.1 pad.4.clone
  0.1 0.6 copy-done.1
  0.7 0.1 copy-done.3
  0.8 1.0 maximum_maximum_fusion.refs_0_
  1.8 0.5 collective-permute-start
  2.3 2.6 %collective-permute-start.1 = (f32[104,256]{1,0:T(8,128)S(1)}, f32[104,256]{1,0:T(8,128)S(1)}, u32[]{:S(2)}, u32[]{:S(2)}) collective-permute-start(f32[104,256]{1,0:T(8,128)S(1)} %maximum_maximum_fusion.refs_0_), channel_id=1, source_target_pairs={{0,2},{1,3},{2,0},{3,1},{4,6},{5,7},{6,4},{7,5},{8,10},{9,11},{10,... | collective-permute-start | bytes 319496 | tf_op jit(solution)/shard_map/ppermute | solution.py:266
  4.8 1.4 %collective-permute-start.2 = (f32[104,256]{1,0:T(8,128)S(1)}, f32[104,256]{1,0:T(8,128)S(1)}, u32[]{:S(2)}, u32[]{:S(2)}) collective-permute-start(f32[104,256]{1,0:T(8,128)S(1)} %maximum_maximum_fusion.refs_0_), channel_id=1, source_target_pairs={{0,3},{1,0},{2,1},{3,2},{4,7},{5,4},{6,5},{7,6},{8,11},{9,8},{10,9... | collective-permute-start | bytes 319496 | tf_op jit(solution)/shard_map/ppermute | solution.py:266
  6.2 0.6 collective-permute-done.refs_1_
  6.8 1.3 %collective-permute-done.1.refs_2_ = f32[104,256]{1,0:T(8,128)S(1)} collective-permute-done((f32[104,256]{1,0:T(8,128)S(1)}, f32[104,256]{1,0:T(8,128)S(1)}, u32[]{:S(2)}, u32[]{:S(2)}) %collective-permute-start.1) | collective-permute-done | bytes 106528 | tf_op jit(solution)/shard_map/ppermute | solution.py:266
  8.1 1.7 %collective-permute-done.2.refs_3_ = f32[104,256]{1,0:T(8,128)S(1)} collective-permute-done((f32[104,256]{1,0:T(8,128)S(1)}, f32[104,256]{1,0:T(8,128)S(1)}, u32[]{:S(2)}, u32[]{:S(2)}) %collective-permute-start.2) | collective-permute-done | bytes 106528 | tf_op jit(solution)/shard_map/ppermute | solution.py:266
  9.8 47.7 %shard_map.55 = (f32[96,1024]{1,0:T(8,128)S(1)}, f32[96,1024]{1,0:T(8,128)S(1)}, f32[2,1024]{1,0:T(2,128)S(1)}) custom-call(f32[2]{0:T(128)S(1)} %copy-done, f32[104,256]{1,0:T(8,128)S(1)} %maximum_maximum_fusion.refs_0_, f32[104,256]{1,0:T(8,128)S(1)} %collective-permute-done.refs_1_, f32[104,256]{1,0:T(8,128)S(1)} %collective-permute-done.1.refs_2_, ...), custom_call_target="tpu_custom_call" | custom-call | flops 603979776 | bytes 1220616 | tf_op jit(solution)/shard_map/pallas_call | solution.py:32
  57.5 1.3 %collective-permute-start.3 = (f32[96,1024]{1,0:T(8,128)S(1)}, f32[96,1024]{1,0:T(8,128)S(1)}, u32[]{:S(2)}, u32[]{:S(2)}) collective-permute-start(f32[96,1024]{1,0:T(8,128)S(1)} %get-tuple-element.10.first_ref.refs_4_), channel_id=1, source_target_pairs={{1,0},{4,1},{5,4},{8,5},{9,8},{12,9},{13,12},{16,13},{17,16},{20,1... | collective-permute-start | bytes 1179656 | tf_op jit(solution)/shard_map/ppermute | solution.py:259
  58.8 3.1 %shard_map.56 = (f32[2,96,96]{2,1,0:T(8,128)S(1)}, f32[2,96,96]{2,1,0:T(8,128)S(1)}) custom-call(f32[2,1024]{1,0:T(2,128)S(1)} %get-tuple-element.12.coef_ref, f32[96,1024]{1,0:T(8,128)S(1)} %get-tuple-element.10.first_ref.refs_4_, f32[96,1024]{1,0:T(8,128)S(1)} %get-tuple-element.11.second_ref.refs_5_), custom_call_target="tpu_custom_call" | custom-call | flops 150994944 | bytes 942080 | tf_op jit(solution)/shard_map/pallas_call | solution.py:32
  61.9 0.0 collective-permute-done.3.next_ref
  61.9 0.8 shard_map.57
  62.7 6.6 %collective-permute-start.4 = (f32[2,96,96]{2,1,0:T(8,128)S(1)}, f32[2,96,96]{2,1,0:T(8,128)S(1)}, u32[]{:S(2)}, u32[]{:S(2)}) collective-permute-start(f32[2,96,96]{2,1,0:T(8,128)S(1)} %shard_map.57), channel_id=1, source_target_pairs={{0,1},{1,4},{4,5},{5,8},{8,9},{9,12},{12,13},{13,16},{16,17},{17,2... | collective-permute-start | bytes 221192 | tf_op jit(solution)/shard_map/ppermute | solution.py:259
  69.3 5.1 %collective-permute-start.5 = (f32[2,96,96]{2,1,0:T(8,128)S(1)}, f32[2,96,96]{2,1,0:T(8,128)S(1)}, u32[]{:S(2)}, u32[]{:S(2)}) collective-permute-start(f32[2,96,96]{2,1,0:T(8,128)S(1)} %shard_map.57), channel_id=1, source_target_pairs={{0,4},{1,5},{4,8},{5,9},{8,12},{9,13},{12,16},{13,17},{16,20},{17,... | collective-permute-start | bytes 221192 | tf_op jit(solution)/shard_map/ppermute | solution.py:259
  74.5 2.2 %collective-permute-done.5.old_ref = f32[2,96,96]{2,1,0:T(8,128)S(1)} collective-permute-done((f32[2,96,96]{2,1,0:T(8,128)S(1)}, f32[2,96,96]{2,1,0:T(8,128)S(1)}, u32[]{:S(2)}, u32[]{:S(2)}) %collective-permute-start.5) | collective-permute-done | bytes 73760 | tf_op jit(solution)/shard_map/ppermute | solution.py:259
  76.7 0.3 shard_map.58.new_ref
  77.0 0.0 copy-start.2
  77.0 4.4 %collective-permute-start.6 = (f32[2,96,96]{2,1,0:T(8,128)S(1)}, f32[2,96,96]{2,1,0:T(8,128)S(1)}, u32[]{:S(2)}, u32[]{:S(2)}) collective-permute-start(f32[2,96,96]{2,1,0:T(8,128)S(1)} %shard_map.58.new_ref), channel_id=1, source_target_pairs={{0,4},{1,5},{4,8},{5,9},{8,12},{9,13},{12,16},{13,17},{16,20},{17,... | collective-permute-start | bytes 221192 | tf_op jit(solution)/shard_map/ppermute | solution.py:259
  81.4 2.2 %collective-permute-done.6.old_ref = f32[2,96,96]{2,1,0:T(8,128)S(1)} collective-permute-done((f32[2,96,96]{2,1,0:T(8,128)S(1)}, f32[2,96,96]{2,1,0:T(8,128)S(1)}, u32[]{:S(2)}, u32[]{:S(2)}) %collective-permute-start.6) | collective-permute-done | bytes 73760 | tf_op jit(solution)/shard_map/ppermute | solution.py:259
  83.6 0.3 shard_map.59.new_ref
  83.9 5.3 %collective-permute-start.7 = (f32[2,96,96]{2,1,0:T(8,128)S(1)}, f32[2,96,96]{2,1,0:T(8,128)S(1)}, u32[]{:S(2)}, u32[]{:S(2)}) collective-permute-start(f32[2,96,96]{2,1,0:T(8,128)S(1)} %shard_map.59.new_ref), channel_id=1, source_target_pairs={{0,8},{1,9},{4,12},{5,13},{8,16},{9,17},{12,20},{13,21},{16,24},{1... | collective-permute-start | bytes 221192 | tf_op jit(solution)/shard_map/ppermute | solution.py:259
  89.2 2.2 %collective-permute-done.7.old_ref = f32[2,96,96]{2,1,0:T(8,128)S(1)} collective-permute-done((f32[2,96,96]{2,1,0:T(8,128)S(1)}, f32[2,96,96]{2,1,0:T(8,128)S(1)}, u32[]{:S(2)}, u32[]{:S(2)}) %collective-permute-start.7) | collective-permute-done | bytes 73760 | tf_op jit(solution)/shard_map/ppermute | solution.py:259
  91.4 0.3 shard_map.60.span_ref.refs_0_
  91.7 0.2 shard_map.61.refs_1_
  92.0 5.3 %collective-permute-start.8 = (f32[8,96]{1,0:T(8,128)S(1)}, f32[8,96]{1,0:T(8,128)S(1)}, u32[]{:S(2)}, u32[]{:S(2)}) collective-permute-start(f32[8,96]{1,0:T(8,128)S(1)} %shard_map.61.refs_1_), channel_id=1, source_target_pairs={{0,16},{1,17},{4,20},{5,21},{8,24},{9,25},{12,28},{13,29},{2,18},{... | collective-permute-start | bytes 9224 | tf_op jit(solution)/shard_map/ppermute | solution.py:259
  97.3 1.3 %collective-permute-done.8.refs_2_ = f32[8,96]{1,0:T(8,128)S(1)} collective-permute-done((f32[8,96]{1,0:T(8,128)S(1)}, f32[8,96]{1,0:T(8,128)S(1)}, u32[]{:S(2)}, u32[]{:S(2)}) %collective-permute-start.8) | collective-permute-done | bytes 3104 | tf_op jit(solution)/shard_map/ppermute | solution.py:259
  98.6 1.1 %shard_map.62 = f32[4,2,2,256]{3,2,1,0:T(2,128)S(1)} custom-call(f32[2,96,96]{2,1,0:T(8,128)S(1)} %shard_map.60.span_ref.refs_0_, f32[8,96]{1,0:T(8,128)S(1)} %shard_map.61.refs_1_, f32[8,96]{1,0:T(8,128)S(1)} %collective-permute-done.8.refs_2_, f32[2,96,96]{2,1,0:T(8,128)S(1)} %get-tuple-element.14.refs_3_, ...), custom_call_target="tpu_custom_call" | custom-call | bytes 956416 | tf_op jit(solution)/shard_map/pallas_call | solution.py:32
  99.7 6.4 %all_to_all.5 = f32[4,2,2,256]{3,2,1,0:T(2,128)S(1)} all-to-all(f32[4,2,2,256]{3,2,1,0:T(2,128)S(1)} %shard_map.62), channel_id=1, replica_groups=mesh['range'=8,'alt'=4,'freq'=1] {'alt'}, dimensions={0} | all-to-all | bytes 32768 | tf_op jit(solution)/shard_map/all_to_all | solution.py:318
  106.2 0.6 copy.7
  (8 shorter events, 0.0 us)
Async XLA Ops:
  0.0 0.7 copy-start.1
  0.1 0.7 copy-start.3
  0.8 9.1 %copy-start = (f32[2]{0:T(128)S(1)}, f32[2]{0:T(128)}, u32[]{:S(2)}) copy-start(f32[2]{0:T(128)} %scale_ref.1) | copy-start | bytes 28
  1.8 5.0 %collective-permute-start = (f32[104,256]{1,0:T(8,128)S(1)}, f32[104,256]{1,0:T(8,128)S(1)}, u32[]{:S(2)}, u32[]{:S(2)}) collective-permute-start(f32[104,256]{1,0:T(8,128)S(1)} %maximum_maximum_fusion.refs_0_), channel_id=1, source_target_pairs={{0,1},{1,2},{2,3},{3,0},{4,5},{5,6},{6,7},{7,4},{8,9},{9,10},{10,1... | collective-permute-start | bytes 319496 | tf_op jit(solution)/shard_map/ppermute | solution.py:266
  2.3 5.9 %collective-permute-start.1 = (f32[104,256]{1,0:T(8,128)S(1)}, f32[104,256]{1,0:T(8,128)S(1)}, u32[]{:S(2)}, u32[]{:S(2)}) collective-permute-start(f32[104,256]{1,0:T(8,128)S(1)} %maximum_maximum_fusion.refs_0_), channel_id=1, source_target_pairs={{0,2},{1,3},{2,0},{3,1},{4,6},{5,7},{6,4},{7,5},{8,10},{9,11},{10,... | collective-permute-start | bytes 319496 | tf_op jit(solution)/shard_map/ppermute | solution.py:266
  4.8 5.0 %collective-permute-start.2 = (f32[104,256]{1,0:T(8,128)S(1)}, f32[104,256]{1,0:T(8,128)S(1)}, u32[]{:S(2)}, u32[]{:S(2)}) collective-permute-start(f32[104,256]{1,0:T(8,128)S(1)} %maximum_maximum_fusion.refs_0_), channel_id=1, source_target_pairs={{0,3},{1,0},{2,1},{3,2},{4,7},{5,4},{6,5},{7,6},{8,11},{9,8},{10,9... | collective-permute-start | bytes 319496 | tf_op jit(solution)/shard_map/ppermute | solution.py:266
  57.5 4.4 %collective-permute-start.3 = (f32[96,1024]{1,0:T(8,128)S(1)}, f32[96,1024]{1,0:T(8,128)S(1)}, u32[]{:S(2)}, u32[]{:S(2)}) collective-permute-start(f32[96,1024]{1,0:T(8,128)S(1)} %get-tuple-element.10.first_ref.refs_4_), channel_id=1, source_target_pairs={{1,0},{4,1},{5,4},{8,5},{9,8},{12,9},{13,12},{16,13},{17,16},{20,1... | collective-permute-start | bytes 1179656 | tf_op jit(solution)/shard_map/ppermute | solution.py:259
  62.7 11.7 %collective-permute-start.4 = (f32[2,96,96]{2,1,0:T(8,128)S(1)}, f32[2,96,96]{2,1,0:T(8,128)S(1)}, u32[]{:S(2)}, u32[]{:S(2)}) collective-permute-start(f32[2,96,96]{2,1,0:T(8,128)S(1)} %shard_map.57), channel_id=1, source_target_pairs={{0,1},{1,4},{4,5},{5,8},{8,9},{9,12},{12,13},{13,16},{16,17},{17,2... | collective-permute-start | bytes 221192 | tf_op jit(solution)/shard_map/ppermute | solution.py:259
  69.3 7.4 %collective-permute-start.5 = (f32[2,96,96]{2,1,0:T(8,128)S(1)}, f32[2,96,96]{2,1,0:T(8,128)S(1)}, u32[]{:S(2)}, u32[]{:S(2)}) collective-permute-start(f32[2,96,96]{2,1,0:T(8,128)S(1)} %shard_map.57), channel_id=1, source_target_pairs={{0,4},{1,5},{4,8},{5,9},{8,12},{9,13},{12,16},{13,17},{16,20},{17,... | collective-permute-start | bytes 221192 | tf_op jit(solution)/shard_map/ppermute | solution.py:259
  77.0 12.2 %copy-start.2 = (f32[2,2,96]{2,1,0:T(2,128)S(1)}, f32[2,2,96]{2,1,0:T(2,128)}, u32[]{:S(2)}) copy-start(f32[2,2,96]{2,1,0:T(2,128)} %param.9) | copy-start | bytes 4612
  77.0 6.6 %collective-permute-start.6 = (f32[2,96,96]{2,1,0:T(8,128)S(1)}, f32[2,96,96]{2,1,0:T(8,128)S(1)}, u32[]{:S(2)}, u32[]{:S(2)}) collective-permute-start(f32[2,96,96]{2,1,0:T(8,128)S(1)} %shard_map.58.new_ref), channel_id=1, source_target_pairs={{0,4},{1,5},{4,8},{5,9},{8,12},{9,13},{12,16},{13,17},{16,20},{17,... | collective-permute-start | bytes 221192 | tf_op jit(solution)/shard_map/ppermute | solution.py:259
  83.9 7.5 %collective-permute-start.7 = (f32[2,96,96]{2,1,0:T(8,128)S(1)}, f32[2,96,96]{2,1,0:T(8,128)S(1)}, u32[]{:S(2)}, u32[]{:S(2)}) collective-permute-start(f32[2,96,96]{2,1,0:T(8,128)S(1)} %shard_map.59.new_ref), channel_id=1, source_target_pairs={{0,8},{1,9},{4,12},{5,13},{8,16},{9,17},{12,20},{13,21},{16,24},{1... | collective-permute-start | bytes 221192 | tf_op jit(solution)/shard_map/ppermute | solution.py:259
  92.0 6.6 %collective-permute-start.8 = (f32[8,96]{1,0:T(8,128)S(1)}, f32[8,96]{1,0:T(8,128)S(1)}, u32[]{:S(2)}, u32[]{:S(2)}) collective-permute-start(f32[8,96]{1,0:T(8,128)S(1)} %shard_map.61.refs_1_), channel_id=1, source_target_pairs={{0,16},{1,17},{4,20},{5,21},{8,24},{9,25},{12,28},{13,29},{2,18},{... | collective-permute-start | bytes 9224 | tf_op jit(solution)/shard_map/ppermute | solution.py:259

commit v2 on v1

--- a/solution.py
+++ b/solution.py
@@ -13,6 +13,7 @@
 relief = 0.1
 HIGHEST = lax.Precision.HIGHEST
 VMEM_LIMIT = 48 * 2**20
+HALF = 48
 
 
 def mm(left, right):
@@ -24,6 +25,18 @@
 def mmt(left, right):
     return lax.dot_general(
         left, right, (((1,), (1,)), ((), ())), precision=HIGHEST, preferred_element_type=jnp.float32
+    )
+
+
+def short_mm(left, right):
+    return lax.dot_general(
+        left, right, (((1,), (0,)), ((), ())), preferred_element_type=jnp.float32
+    )
+
+
+def short_mmt(left, right):
+    return lax.dot_general(
+        left, right, (((1,), (1,)), ((), ())), preferred_element_type=jnp.float32
     )
 
 
@@ -52,44 +65,78 @@
     return jnp.broadcast_to(value[at : at + 1, :], value.shape)
 
 
-def lane_of(value, at):
-    return jnp.broadcast_to(value[:, at : at + 1], value.shape)
-
-
-def inverse_factors(grams):
-    blocks = len(grams[0])
+def pack_pair(one, two):
+    left = lax.broadcasted_iota(jnp.int32, one.shape, 1) < 64
+    return [
+        jnp.where(left, one, pltpu.roll(two, 64, 1)),
+        jnp.where(left, pltpu.roll(one, 128 - HALF, 1), pltpu.roll(two, 64 - HALF, 1)),
+    ]
+
+
+def unpack_pair(low, high):
+    early = lax.broadcasted_iota(jnp.int32, low.shape, 1) < HALF
+    return (
+        jnp.where(early, low, pltpu.roll(high, HALF, 1)),
+        jnp.where(early, pltpu.roll(low, 64, 1), pltpu.roll(high, 64 + HALF, 1)),
+    )
+
+
+def inverse_factors(one, two):
+    count = len(one)
     lanes = lax.broadcasted_iota(jnp.int32, (8, 128), 1)
     subs = lax.broadcasted_iota(jnp.int32, (8, 128), 0)
-    works = [list(gram) for gram in grams]
-    results = [[None] * blocks for _ in grams]
-    for k in range(blocks):
-        first = 8 * k
-        panels = [
-            [[lane_of(work[v], first + c) for v in range(k, blocks)] for c in range(8)]
-            for work in works
+    base = jnp.where(lanes < 64, 0, 64)
+    column = lanes - base
+    work = [pack_pair(a, b) for a, b in zip(one, two)]
+    results = []
+
+    def place(k):
+        side = 8 * k // HALF
+        return side, 8 * k - side * HALF
+
+    def spread(v, k):
+        side, first = place(k)
+        return [
+            jnp.take_along_axis(work[v][side], base + (first + c), axis=1) for c in range(8)
         ]
-        pivots = [jnp.ones((8, 128), jnp.float32) for _ in works]
+
+    panel = spread(0, 0)
+    for k in range(count):
+        side, first = place(k)
+        below = [spread(v, k) for v in range(k + 1, count)]
+        ahead = spread(k + 1, k + 1) if k + 1 < count else None
+        weights = [[None] * 8 for _ in range(8)]
+        inverses, lines = [], []
+        scales = jnp.ones((8, 128), jnp.float32)
         for c in range(8):
-            for i, work in enumerate(works):
-                panel = panels[i]
-                pivot = row_of(panel[c][0], c)
-                inv = pltpu.reciprocal(pivot, approx=True)
-                inv = inv * (2.0 - pivot * inv)
-                pivots[i] = jnp.where(subs == c, pivot, pivots[i])
-                factor = [column * inv for column in panel[c]]
-                factor[0] = jnp.where(subs > c, factor[0], 0.0)
-                line = row_of(work[k], c) + jnp.where(lanes == first + c, 1.0, 0.0)
+            inv = 1.0 / row_of(panel[c], c)
+            inverses.append(inv)
+            scales = jnp.where(subs == c, inv, scales)
+            for d in range(c + 1, 8):
+                weights[c][d] = row_of(panel[d], c)
+                panel[d] = panel[d] - (panel[c] * weights[c][d]) * inv
+            factor = jnp.where(subs > c, panel[c] * inv, 0.0)
+            line = [row_of(part, c) for part in work[k]]
+            line[side] = line[side] + jnp.where(column == first + c, 1.0, 0.0)
+            lines.append(line)
+            work[k] = [part - factor * along for part, along in zip(work[k], line)]
+        for v in range(k + 1, count):
+            panel = below[v - k - 1]
+            for c in range(8):
+                factor = panel[c] * inverses[c]
                 for d in range(c + 1, 8):
-                    weight = row_of(panel[d][0], c)
-                    panel[d][0] = panel[d][0] - (panel[c][0] * weight) * inv
-                    for v in range(1, blocks - k):
-                        panel[d][v] = panel[d][v] - factor[v] * weight
-                for v in range(blocks - k):
-                    work[k + v] = work[k + v] - factor[v] * line
-        for i, work in enumerate(works):
-            unit = jnp.where(lanes == subs + first, 1.0, 0.0)
-            results[i][k] = jnp.where(lanes < subs + first, work[k], unit) * lax.rsqrt(pivots[i])
-    return results
+                    panel[d] = panel[d] - factor * weights[c][d]
+                if v == k + 1:
+                    for d in range(8):
+                        ahead[d] = ahead[d] - factor * row_of(panel[c], d)
+                work[v] = [part - factor * along for part, along in zip(work[v], lines[c])]
+        panel = ahead
+        root = lax.sqrt(scales)
+        unit = jnp.where(column == subs + first, 1.0, 0.0)
+        own = jnp.where(column < subs + first, work[k][side], unit) * root
+        other = work[k][0] * root if side else jnp.zeros((8, 128), jnp.float32)
+        results.append(unpack_pair(other, own) if side else unpack_pair(own, other))
+    return [pair[0] for pair in results], [pair[1] for pair in results]
 
 
 def edge_weights(width):
@@ -109,7 +156,7 @@
 def iterate_body(n_alt, chunk, seg_count, modes, width, scale_ref, *refs):
     blocks = refs[:n_alt]
     out_refs = refs[n_alt : n_alt + chunk]
-    coef_ref, image_ref, gram_ref, inv_ref = refs[n_alt + chunk :]
+    coef_ref, split_ref, image_ref, gram_ref, inv_ref = refs[n_alt + chunk :]
     place = lax.axis_index("alt")
     flat = place * chunk
     freq = flat // seg_count
@@ -129,27 +176,47 @@
     down = 2.0**-11
     gram_ref[...] = jnp.zeros_like(gram_ref)
 
+    def factorise():
+        grams = [[gram_ref[i, at : at + 8, :] for at in range(0, modes, 8)] for i in range(chunk)]
+        results = inverse_factors(*grams)
+        for i in range(chunk):
+            for at in range(0, modes, 8):
+                inv_ref[i, at : at + 8, :] = results[i][at // 8] * down**0.5
+
     def step(_, carry):
         for i in range(chunk):
             coef = coef_ref[i : i + 1, :]
-            for at in range(0, modes, 8):
-                image_ref[i, at : at + 8, :] = apply_rows(
-                    out_refs[i][at : at + 8, :], coef, from_low, from_high
+            for at in range(0, modes, 16):
+                image = apply_rows(out_refs[i][at : at + 16, :], coef, from_low, from_high)
+                for part in range(3):
+                    piece = image.astype(jnp.bfloat16)
+                    split_ref[i, part, at : at + 16, :] = piece
+                    image = image - piece.astype(jnp.float32)
+            high, low = split_ref[i, 0], split_ref[i, 1]
+            gram = short_mmt(high, high) + short_mmt(high, low) + short_mmt(low, high)
+            gram_ref[i, :, 0:modes] = gram * down
+        factorise()
+        for i in range(chunk):
+            inv = inv_ref[i, :, 0:modes].astype(jnp.bfloat16)
+            for at in range(0, total, 256):
+                out_refs[i][:, at : at + 256] = sum(
+                    short_mm(inv, split_ref[i, part, :, at : at + 256]) for part in range(3)
                 )
-            image = image_ref[i]
-            gram_ref[i, :, 0:modes] = mmt(image, image) * down
-        grams = [[gram_ref[i, at : at + 8, :] for at in range(0, modes, 8)] for i in range(chunk)]
-        results = inverse_factors(grams)
-        for i in range(chunk):
-            for at in range(0, modes, 8):
-                inv_ref[i, at : at + 8, :] = results[i][at // 8] * down**0.5
-        for i in range(chunk):
-            inv = inv_ref[i, :, 0:modes]
-            for at in range(0, total, 256):
-                out_refs[i][:, at : at + 256] = mm(inv, image_ref[i, :, at : at + 256])
         return carry
 
-    lax.fori_loop(0, ITERS, step, 0)
+    lax.fori_loop(0, ITERS - 1, step, 0)
+    for i in range(chunk):
+        for at in range(0, modes, 8):
+            image_ref[i, at : at + 8, :] = apply_rows(
+                out_refs[i][at : at + 8, :], coef_ref[i : i + 1, :], from_low, from_high
+            )
+        image = image_ref[i]
+        gram_ref[i, :, 0:modes] = mmt(image, image) * down
+    factorise()
+    for i in range(chunk):
+        inv = inv_ref[i, :, 0:modes]
+        for at in range(0, total, 256):
+            out_refs[i][:, at : at + 256] = mm(inv, image_ref[i, :, at : at + 256])
 
 
 def unit_of(modes):
@@ -246,7 +313,7 @@
     chunk = freqs * seg_count // n_alt
     halves = seg_count // chunk
     length = n_range * halves
-    assert chunk == 2 and halves * chunk == seg_count and halves * freqs == n_alt
+    assert modes == 2 * HALF and chunk == 2 and halves * chunk == seg_count and halves * freqs == n_alt
 
     def along_chain(value, steps):
         pairs = []
@@ -270,7 +337,8 @@
         [shape(modes, total)] * chunk + [shape(chunk, total)],
         [freq_scale] + blocks,
         [SM] + [VM] * n_alt,
-        [pltpu.VMEM((chunk, modes, total), jnp.float32)]
+        [pltpu.VMEM((chunk, 3, modes, total), jnp.bfloat16)]
+        + [pltpu.VMEM((chunk, modes, total), jnp.float32)]
         + [pltpu.VMEM((chunk, modes, 128), jnp.float32)] * 2,
         flops=2 * ITERS * chunk * flops,
     )

time: 107 us -> 88.1 us (0.82)
  Pallas kernels: 53.9 us -> 35 us
    pallas_call x8, Pallas kernels: 53.9 us -> 35 us  [kernel_call(): pl.pallas_call(body, out_shape=out_shape, in_specs=specs, out_specs=jax.t...]
  transfers between devices with their start and end apart: 9 -> 9, of which waited for: 7 -> 7; matrix products, arithmetic and copies ran while one was open for 0% -> 0% of each run, Pallas kernels for 3% -> 4%
where the time goes in v2:
time: 88.1 us; the launch traced here: 87.8 us
  Pallas kernels  35 us (40%)
  starting transfers between devices  32.5 us (37%)
  waiting for transfers between devices  11.5 us (13%)
  blocking collectives  6.39 us (7%)
  local copies, waits for them, and re-layouts  1.38 us (2%)
  other arithmetic  0.98 us (1%)
    pallas_call x8, Pallas kernels, kernel_call(): pl.pallas_call(body, out_shape=out_shape, in_specs=specs, out_specs=jax.t...  35 us
    ppermute x6, starting transfers between devices, along_chain(): return lax.ppermute(value, ('range', 'alt'), pairs)  28 us
    ppermute x6, waiting for transfers between devices, along_chain(): return lax.ppermute(value, ('range', 'alt'), pairs)  7.87 us
    all_to_all x1, blocking collectives, local(): field = lax.all_to_all(parts, 'alt', 0, 0)  6.39 us
    ppermute x3, starting transfers between devices, local(): lax.ppermute(mine, 'alt', [(i, (i + k) % n_alt) for i in range(n_alt)])  4.46 us
    ppermute x3, waiting for transfers between devices, local(): lax.ppermute(mine, 'alt', [(i, (i + k) % n_alt) for i in range(n_alt)])  3.6 us
  transfers between devices with their start and end apart: 9, of which 7 were waited for; matrix products, arithmetic and copies ran while one was open for 0% of the time, Pallas kernels for 4%

profile of v2, /device:TPU:0, one launch (start us, length us, event | category | flops | bytes accessed | tf_op | source)
XLA Modules:
  0.0 87.8 jit_solution(8327065926844746118)
XLA Ops:
  0.0 0.1 pad.4.clone
  0.1 0.6 copy-done.1
  0.7 0.1 copy-done.3
  0.8 1.0 %maximum_maximum_fusion.refs_0_ = f32[104,256]{1,0:T(8,128)S(1)} fusion(f32[4,256]{1,0:T(4,128)S(1)} %copy-done.1, f32[1,256]{1,0:T(1,128)S(1)} %bitcast.3, f32[96,256]{1,0:T(8,128)} %param.8, f32[104]{0:T(128)S(1)} %pad.4.clone), kind=kLoop, calls=%fused_computation | loop fusion | flops 79872 | bytes 210336 | tf_op jit(solution)/shard_map/concatenate | solution.py:330
  1.8 0.5 collective-permute-start
  2.3 2.6 %collective-permute-start.1 = (f32[104,256]{1,0:T(8,128)S(1)}, f32[104,256]{1,0:T(8,128)S(1)}, u32[]{:S(2)}, u32[]{:S(2)}) collective-permute-start(f32[104,256]{1,0:T(8,128)S(1)} %maximum_maximum_fusion.refs_0_), channel_id=1, source_target_pairs={{0,2},{1,3},{2,0},{3,1},{4,6},{5,7},{6,4},{7,5},{8,10},{9,11},{10,... | collective-permute-start | bytes 319496 | tf_op jit(solution)/shard_map/ppermute | solution.py:333
  4.8 1.4 %collective-permute-start.2 = (f32[104,256]{1,0:T(8,128)S(1)}, f32[104,256]{1,0:T(8,128)S(1)}, u32[]{:S(2)}, u32[]{:S(2)}) collective-permute-start(f32[104,256]{1,0:T(8,128)S(1)} %maximum_maximum_fusion.refs_0_), channel_id=1, source_target_pairs={{0,3},{1,0},{2,1},{3,2},{4,7},{5,4},{6,5},{7,6},{8,11},{9,8},{10,9... | collective-permute-start | bytes 319496 | tf_op jit(solution)/shard_map/ppermute | solution.py:333
  6.2 0.6 collective-permute-done.refs_1_
  6.8 1.3 %collective-permute-done.1.refs_2_ = f32[104,256]{1,0:T(8,128)S(1)} collective-permute-done((f32[104,256]{1,0:T(8,128)S(1)}, f32[104,256]{1,0:T(8,128)S(1)}, u32[]{:S(2)}, u32[]{:S(2)}) %collective-permute-start.1) | collective-permute-done | bytes 106528 | tf_op jit(solution)/shard_map/ppermute | solution.py:333
  8.1 1.7 %collective-permute-done.2.refs_3_ = f32[104,256]{1,0:T(8,128)S(1)} collective-permute-done((f32[104,256]{1,0:T(8,128)S(1)}, f32[104,256]{1,0:T(8,128)S(1)}, u32[]{:S(2)}, u32[]{:S(2)}) %collective-permute-start.2) | collective-permute-done | bytes 106528 | tf_op jit(solution)/shard_map/ppermute | solution.py:333
  9.8 28.7 %shard_map.55 = (f32[96,1024]{1,0:T(8,128)S(1)}, f32[96,1024]{1,0:T(8,128)S(1)}, f32[2,1024]{1,0:T(2,128)S(1)}) custom-call(f32[2]{0:T(128)S(1)} %copy-done, f32[104,256]{1,0:T(8,128)S(1)} %maximum_maximum_fusion.refs_0_, f32[104,256]{1,0:T(8,128)S(1)} %collective-permute-done.refs_1_, f32[104,256]{1,0:T(8,128)S(1)} %collective-permute-done.1.refs_2_, ...), custom_call_target="tpu_custom_call" | custom-call | flops 603979776 | bytes 1220616 | tf_op jit(solution)/shard_map/pallas_call | solution.py:45
  38.5 1.3 %collective-permute-start.3 = (f32[96,1024]{1,0:T(8,128)S(1)}, f32[96,1024]{1,0:T(8,128)S(1)}, u32[]{:S(2)}, u32[]{:S(2)}) collective-permute-start(f32[96,1024]{1,0:T(8,128)S(1)} %get-tuple-element.10.first_ref.refs_4_), channel_id=1, source_target_pairs={{1,0},{4,1},{5,4},{8,5},{9,8},{12,9},{13,12},{16,13},{17,16},{20,1... | collective-permute-start | bytes 1179656 | tf_op jit(solution)/shard_map/ppermute | solution.py:326
  39.8 3.1 %shard_map.56 = (f32[2,96,96]{2,1,0:T(8,128)S(1)}, f32[2,96,96]{2,1,0:T(8,128)S(1)}) custom-call(f32[2,1024]{1,0:T(2,128)S(1)} %get-tuple-element.12.coef_ref, f32[96,1024]{1,0:T(8,128)S(1)} %get-tuple-element.10.first_ref.refs_4_, f32[96,1024]{1,0:T(8,128)S(1)} %get-tuple-element.11.second_ref.refs_5_), custom_call_target="tpu_custom_call" | custom-call | flops 150994944 | bytes 942080 | tf_op jit(solution)/shard_map/pallas_call | solution.py:45
  43.0 0.0 collective-permute-done.3.next_ref
  43.0 0.8 shard_map.57
  43.8 6.6 %collective-permute-start.4 = (f32[2,96,96]{2,1,0:T(8,128)S(1)}, f32[2,96,96]{2,1,0:T(8,128)S(1)}, u32[]{:S(2)}, u32[]{:S(2)}) collective-permute-start(f32[2,96,96]{2,1,0:T(8,128)S(1)} %shard_map.57), channel_id=1, source_target_pairs={{0,1},{1,4},{4,5},{5,8},{8,9},{9,12},{12,13},{13,16},{16,17},{17,2... | collective-permute-start | bytes 221192 | tf_op jit(solution)/shard_map/ppermute | solution.py:326
  50.3 5.1 %collective-permute-start.5 = (f32[2,96,96]{2,1,0:T(8,128)S(1)}, f32[2,96,96]{2,1,0:T(8,128)S(1)}, u32[]{:S(2)}, u32[]{:S(2)}) collective-permute-start(f32[2,96,96]{2,1,0:T(8,128)S(1)} %shard_map.57), channel_id=1, source_target_pairs={{0,4},{1,5},{4,8},{5,9},{8,12},{9,13},{12,16},{13,17},{16,20},{17,... | collective-permute-start | bytes 221192 | tf_op jit(solution)/shard_map/ppermute | solution.py:326
  55.5 2.2 %collective-permute-done.5.old_ref = f32[2,96,96]{2,1,0:T(8,128)S(1)} collective-permute-done((f32[2,96,96]{2,1,0:T(8,128)S(1)}, f32[2,96,96]{2,1,0:T(8,128)S(1)}, u32[]{:S(2)}, u32[]{:S(2)}) %collective-permute-start.5) | collective-permute-done | bytes 73760 | tf_op jit(solution)/shard_map/ppermute | solution.py:326
  57.7 0.3 shard_map.58.new_ref
  58.0 0.0 copy-start.2
  58.0 4.4 %collective-permute-start.6 = (f32[2,96,96]{2,1,0:T(8,128)S(1)}, f32[2,96,96]{2,1,0:T(8,128)S(1)}, u32[]{:S(2)}, u32[]{:S(2)}) collective-permute-start(f32[2,96,96]{2,1,0:T(8,128)S(1)} %shard_map.58.new_ref), channel_id=1, source_target_pairs={{0,4},{1,5},{4,8},{5,9},{8,12},{9,13},{12,16},{13,17},{16,20},{17,... | collective-permute-start | bytes 221192 | tf_op jit(solution)/shard_map/ppermute | solution.py:326
  62.4 2.2 %collective-permute-done.6.old_ref = f32[2,96,96]{2,1,0:T(8,128)S(1)} collective-permute-done((f32[2,96,96]{2,1,0:T(8,128)S(1)}, f32[2,96,96]{2,1,0:T(8,128)S(1)}, u32[]{:S(2)}, u32[]{:S(2)}) %collective-permute-start.6) | collective-permute-done | bytes 73760 | tf_op jit(solution)/shard_map/ppermute | solution.py:326
  64.6 0.3 shard_map.59.new_ref
  65.0 5.3 %collective-permute-start.7 = (f32[2,96,96]{2,1,0:T(8,128)S(1)}, f32[2,96,96]{2,1,0:T(8,128)S(1)}, u32[]{:S(2)}, u32[]{:S(2)}) collective-permute-start(f32[2,96,96]{2,1,0:T(8,128)S(1)} %shard_map.59.new_ref), channel_id=1, source_target_pairs={{0,8},{1,9},{4,12},{5,13},{8,16},{9,17},{12,20},{13,21},{16,24},{1... | collective-permute-start | bytes 221192 | tf_op jit(solution)/shard_map/ppermute | solution.py:326
  70.3 2.2 %collective-permute-done.7.old_ref = f32[2,96,96]{2,1,0:T(8,128)S(1)} collective-permute-done((f32[2,96,96]{2,1,0:T(8,128)S(1)}, f32[2,96,96]{2,1,0:T(8,128)S(1)}, u32[]{:S(2)}, u32[]{:S(2)}) %collective-permute-start.7) | collective-permute-done | bytes 73760 | tf_op jit(solution)/shard_map/ppermute | solution.py:326
  72.4 0.3 shard_map.60.span_ref.refs_0_
  72.8 0.2 shard_map.61.refs_1_
  73.0 5.4 %collective-permute-start.8 = (f32[8,96]{1,0:T(8,128)S(1)}, f32[8,96]{1,0:T(8,128)S(1)}, u32[]{:S(2)}, u32[]{:S(2)}) collective-permute-start(f32[8,96]{1,0:T(8,128)S(1)} %shard_map.61.refs_1_), channel_id=1, source_target_pairs={{0,16},{1,17},{4,20},{5,21},{8,24},{9,25},{12,28},{13,29},{2,18},{... | collective-permute-start | bytes 9224 | tf_op jit(solution)/shard_map/ppermute | solution.py:326
  78.4 1.3 %collective-permute-done.8.refs_2_ = f32[8,96]{1,0:T(8,128)S(1)} collective-permute-done((f32[8,96]{1,0:T(8,128)S(1)}, f32[8,96]{1,0:T(8,128)S(1)}, u32[]{:S(2)}, u32[]{:S(2)}) %collective-permute-start.8) | collective-permute-done | bytes 3104 | tf_op jit(solution)/shard_map/ppermute | solution.py:326
  79.7 1.1 %shard_map.62 = f32[4,2,2,256]{3,2,1,0:T(2,128)S(1)} custom-call(f32[2,96,96]{2,1,0:T(8,128)S(1)} %shard_map.60.span_ref.refs_0_, f32[8,96]{1,0:T(8,128)S(1)} %shard_map.61.refs_1_, f32[8,96]{1,0:T(8,128)S(1)} %collective-permute-done.8.refs_2_, f32[2,96,96]{2,1,0:T(8,128)S(1)} %get-tuple-element.14.refs_3_, ...), custom_call_target="tpu_custom_call" | custom-call | bytes 956416 | tf_op jit(solution)/shard_map/pallas_call | solution.py:45
  80.8 6.4 %all_to_all.5 = f32[4,2,2,256]{3,2,1,0:T(2,128)S(1)} all-to-all(f32[4,2,2,256]{3,2,1,0:T(2,128)S(1)} %shard_map.62), channel_id=1, replica_groups=mesh['range'=8,'alt'=4,'freq'=1] {'alt'}, dimensions={0} | all-to-all | bytes 32768 | tf_op jit(solution)/shard_map/all_to_all | solution.py:386
  87.2 0.6 copy.7
  (8 shorter events, 0.0 us)
Async XLA Ops:
  0.0 0.7 copy-start.1
  0.1 0.7 copy-start.3
  0.8 9.1 %copy-start = (f32[2]{0:T(128)S(1)}, f32[2]{0:T(128)}, u32[]{:S(2)}) copy-start(f32[2]{0:T(128)} %scale_ref.1) | copy-start | bytes 28
  1.8 5.0 %collective-permute-start = (f32[104,256]{1,0:T(8,128)S(1)}, f32[104,256]{1,0:T(8,128)S(1)}, u32[]{:S(2)}, u32[]{:S(2)}) collective-permute-start(f32[104,256]{1,0:T(8,128)S(1)} %maximum_maximum_fusion.refs_0_), channel_id=1, source_target_pairs={{0,1},{1,2},{2,3},{3,0},{4,5},{5,6},{6,7},{7,4},{8,9},{9,10},{10,1... | collective-permute-start | bytes 319496 | tf_op jit(solution)/shard_map/ppermute | solution.py:333
  2.3 5.9 %collective-permute-start.1 = (f32[104,256]{1,0:T(8,128)S(1)}, f32[104,256]{1,0:T(8,128)S(1)}, u32[]{:S(2)}, u32[]{:S(2)}) collective-permute-start(f32[104,256]{1,0:T(8,128)S(1)} %maximum_maximum_fusion.refs_0_), channel_id=1, source_target_pairs={{0,2},{1,3},{2,0},{3,1},{4,6},{5,7},{6,4},{7,5},{8,10},{9,11},{10,... | collective-permute-start | bytes 319496 | tf_op jit(solution)/shard_map/ppermute | solution.py:333
  4.8 5.0 %collective-permute-start.2 = (f32[104,256]{1,0:T(8,128)S(1)}, f32[104,256]{1,0:T(8,128)S(1)}, u32[]{:S(2)}, u32[]{:S(2)}) collective-permute-start(f32[104,256]{1,0:T(8,128)S(1)} %maximum_maximum_fusion.refs_0_), channel_id=1, source_target_pairs={{0,3},{1,0},{2,1},{3,2},{4,7},{5,4},{6,5},{7,6},{8,11},{9,8},{10,9... | collective-permute-start | bytes 319496 | tf_op jit(solution)/shard_map/ppermute | solution.py:333
  38.5 4.4 %collective-permute-start.3 = (f32[96,1024]{1,0:T(8,128)S(1)}, f32[96,1024]{1,0:T(8,128)S(1)}, u32[]{:S(2)}, u32[]{:S(2)}) collective-permute-start(f32[96,1024]{1,0:T(8,128)S(1)} %get-tuple-element.10.first_ref.refs_4_), channel_id=1, source_target_pairs={{1,0},{4,1},{5,4},{8,5},{9,8},{12,9},{13,12},{16,13},{17,16},{20,1... | collective-permute-start | bytes 1179656 | tf_op jit(solution)/shard_map/ppermute | solution.py:326
  43.8 11.7 %collective-permute-start.4 = (f32[2,96,96]{2,1,0:T(8,128)S(1)}, f32[2,96,96]{2,1,0:T(8,128)S(1)}, u32[]{:S(2)}, u32[]{:S(2)}) collective-permute-start(f32[2,96,96]{2,1,0:T(8,128)S(1)} %shard_map.57), channel_id=1, source_target_pairs={{0,1},{1,4},{4,5},{5,8},{8,9},{9,12},{12,13},{13,16},{16,17},{17,2... | collective-permute-start | bytes 221192 | tf_op jit(solution)/shard_map/ppermute | solution.py:326
  50.3 7.4 %collective-permute-start.5 = (f32[2,96,96]{2,1,0:T(8,128)S(1)}, f32[2,96,96]{2,1,0:T(8,128)S(1)}, u32[]{:S(2)}, u32[]{:S(2)}) collective-permute-start(f32[2,96,96]{2,1,0:T(8,128)S(1)} %shard_map.57), channel_id=1, source_target_pairs={{0,4},{1,5},{4,8},{5,9},{8,12},{9,13},{12,16},{13,17},{16,20},{17,... | collective-permute-start | bytes 221192 | tf_op jit(solution)/shard_map/ppermute | solution.py:326
  58.0 12.2 %copy-start.2 = (f32[2,2,96]{2,1,0:T(2,128)S(1)}, f32[2,2,96]{2,1,0:T(2,128)}, u32[]{:S(2)}) copy-start(f32[2,2,96]{2,1,0:T(2,128)} %param.9) | copy-start | bytes 4612
  58.0 6.6 %collective-permute-start.6 = (f32[2,96,96]{2,1,0:T(8,128)S(1)}, f32[2,96,96]{2,1,0:T(8,128)S(1)}, u32[]{:S(2)}, u32[]{:S(2)}) collective-permute-start(f32[2,96,96]{2,1,0:T(8,128)S(1)} %shard_map.58.new_ref), channel_id=1, source_target_pairs={{0,4},{1,5},{4,8},{5,9},{8,12},{9,13},{12,16},{13,17},{16,20},{17,... | collective-permute-start | bytes 221192 | tf_op jit(solution)/shard_map/ppermute | solution.py:326
  65.0 7.5 %collective-permute-start.7 = (f32[2,96,96]{2,1,0:T(8,128)S(1)}, f32[2,96,96]{2,1,0:T(8,128)S(1)}, u32[]{:S(2)}, u32[]{:S(2)}) collective-permute-start(f32[2,96,96]{2,1,0:T(8,128)S(1)} %shard_map.59.new_ref), channel_id=1, source_target_pairs={{0,8},{1,9},{4,12},{5,13},{8,16},{9,17},{12,20},{13,21},{16,24},{1... | collective-permute-start | bytes 221192 | tf_op jit(solution)/shard_map/ppermute | solution.py:326
  73.0 6.7 %collective-permute-start.8 = (f32[8,96]{1,0:T(8,128)S(1)}, f32[8,96]{1,0:T(8,128)S(1)}, u32[]{:S(2)}, u32[]{:S(2)}) collective-permute-start(f32[8,96]{1,0:T(8,128)S(1)} %shard_map.61.refs_1_), channel_id=1, source_target_pairs={{0,16},{1,17},{4,20},{5,21},{8,24},{9,25},{12,28},{13,29},{2,18},{... | collective-permute-start | bytes 9224 | tf_op jit(solution)/shard_map/ppermute | solution.py:326

commit v3 on v2

--- a/solution.py
+++ b/solution.py
@@ -103,34 +103,54 @@
     panel = spread(0, 0)
     for k in range(count):
         side, first = place(k)
-        below = [spread(v, k) for v in range(k + 1, count)]
+        near = spread(k + 1, k) if k + 1 < count else None
         ahead = spread(k + 1, k + 1) if k + 1 < count else None
         weights = [[None] * 8 for _ in range(8)]
         inverses, lines = [], []
         scales = jnp.ones((8, 128), jnp.float32)
-        for c in range(8):
-            inv = 1.0 / row_of(panel[c], c)
-            inverses.append(inv)
-            scales = jnp.where(subs == c, inv, scales)
-            for d in range(c + 1, 8):
+        for c in range(0, 8, 2):
+            corner, cross, late = (
+                row_of(panel[c], c),
+                row_of(panel[c + 1], c),
+                row_of(panel[c + 1], c + 1),
+            )
+            inv = 1.0 / corner
+            second = corner * (1.0 / (corner * late - cross * cross))
+            ratio = cross * inv
+            weights[c][c + 1] = cross
+            factor = panel[c] * inv
+            rest = panel[c + 1] - factor * cross
+            for d in range(c + 2, 8):
                 weights[c][d] = row_of(panel[d], c)
-                panel[d] = panel[d] - (panel[c] * weights[c][d]) * inv
-            factor = jnp.where(subs > c, panel[c] * inv, 0.0)
-            line = [row_of(part, c) for part in work[k]]
-            line[side] = line[side] + jnp.where(column == first + c, 1.0, 0.0)
-            lines.append(line)
-            work[k] = [part - factor * along for part, along in zip(work[k], line)]
-        for v in range(k + 1, count):
-            panel = below[v - k - 1]
+                weights[c + 1][d] = row_of(panel[d], c + 1) - ratio * weights[c][d]
+                panel[d] = (panel[d] - factor * weights[c][d]) - (
+                    rest * weights[c + 1][d]
+                ) * second
+            pair = (jnp.where(subs > c, factor, 0.0), jnp.where(subs > c + 1, rest * second, 0.0))
+            for e in range(2):
+                inverses.append((inv, second)[e])
+                scales = jnp.where(subs == c + e, inverses[-1], scales)
+                line = [row_of(part, c + e) for part in work[k]]
+                line[side] = line[side] + jnp.where(column == first + c + e, 1.0, 0.0)
+                lines.append(line)
+                work[k] = [part - pair[e] * along for part, along in zip(work[k], line)]
+        if near is not None:
             for c in range(8):
-                factor = panel[c] * inverses[c]
+                factor = near[c] * inverses[c]
                 for d in range(c + 1, 8):
-                    panel[d] = panel[d] - factor * weights[c][d]
-                if v == k + 1:
-                    for d in range(8):
-                        ahead[d] = ahead[d] - factor * row_of(panel[c], d)
+                    near[d] = near[d] - factor * weights[c][d]
+                for d in range(8):
+                    ahead[d] = ahead[d] - factor * row_of(near[c], d)
+                work[k + 1] = [
+                    part - factor * along for part, along in zip(work[k + 1], lines[c])
+                ]
+        panel = ahead
+        scaled = [[part * inv for part in line] for line, inv in zip(lines, inverses)]
+        for v in range(k + 2, count):
+            there, at = place(v)
+            for c in range(8):
+                factor = jnp.take_along_axis(scaled[c][there], base + subs + at, axis=1)
                 work[v] = [part - factor * along for part, along in zip(work[v], lines[c])]
-        panel = ahead
         root = lax.sqrt(scales)
         unit = jnp.where(column == subs + first, 1.0, 0.0)
         own = jnp.where(column < subs + first, work[k][side], unit) * root
@@ -154,23 +174,23 @@
 
 
 def iterate_body(n_alt, chunk, seg_count, modes, width, scale_ref, *refs):
-    blocks = refs[:n_alt]
-    out_refs = refs[n_alt : n_alt + chunk]
-    coef_ref, split_ref, image_ref, gram_ref, inv_ref = refs[n_alt + chunk :]
+    starts, profiles = refs[:n_alt], refs[n_alt : 2 * n_alt]
+    out_refs = refs[2 * n_alt : 2 * n_alt + chunk]
+    coef_ref, split_ref, image_ref, gram_ref, inv_ref = refs[2 * n_alt + chunk :]
     place = lax.axis_index("alt")
     flat = place * chunk
     freq = flat // seg_count
     first = flat - freq * seg_count
     total = n_alt * width
-    for k, block in enumerate(blocks):
+    for k in range(n_alt):
         source = lax.rem(place + n_alt - k, n_alt)
         span = pl.ds(pl.multiple_of(source * width, width), width)
-        start = block[0:modes, :] * (1.0 / float(total) ** 0.5)
+        start = starts[k][...] * (1.0 / float(total) ** 0.5)
         for i in range(chunk):
             out_refs[i][:, span] = start
-            change = block[pl.ds(modes + 1 + first + i, 1), :]
+            change = profiles[k][pl.ds(1 + first + i, 1), :]
             coef_ref[i : i + 1, span] = scale_ref[freq] * (
-                block[modes : modes + 1, :] * (1.0 + relief * change)
+                profiles[k][0:1, :] * (1.0 + relief * change)
             )
     from_low, from_high = edge_weights(total)
     down = 2.0**-11
@@ -253,26 +273,29 @@
         rest_ref[part] = rest[part]
 
 
-def product_body(next_ref, second_ref, rest_ref, out_ref):
-    corr = mmt(next_ref[...], second_ref[...])
-    for part in range(2):
-        out_ref[part] = mm(corr, rest_ref[part])
-
-
 def chain_place(halves):
     return lax.axis_index("range") * halves + lax.rem(lax.axis_index("alt"), halves)
 
 
-def padded(ref, missing):
+def with_start(halves, back, ref):
+    missing = chain_place(halves) < back
     return (ref[0] + jnp.where(missing, unit_of(ref.shape[1]), 0.0), ref[1])
 
 
-def join_body(halves, back_new, back_old, new_ref, old_ref, out_ref):
-    at = chain_place(halves)
-    new = padded(new_ref, at < back_new) if back_new else (new_ref[0], new_ref[1])
-    real, imag = complex_mm(new, padded(old_ref, at < back_old))
-    out_ref[0] = real
-    out_ref[1] = imag
+def product_body(halves, first_ref, before_ref, rest_ref, out_ref):
+    corr = mmt(first_ref[...], before_ref[...])
+    missing = chain_place(halves) < 1
+    out_ref[0] = mm(corr, rest_ref[0]) + jnp.where(missing, unit_of(out_ref.shape[1]), 0.0)
+    out_ref[1] = mm(corr, rest_ref[1])
+
+
+def join_body(halves, back, new_ref, old_ref, *refs):
+    out_ref = refs[1] if len(refs) > 1 else refs[0]
+    joined = complex_mm((new_ref[0], new_ref[1]), with_start(halves, back, old_ref))
+    out_ref[0], out_ref[1] = joined
+    if len(refs) > 1:
+        source = refs[0][lax.axis_index("alt") // halves]
+        refs[2][...] = turn_vector(joined, source)
 
 
 def turn_vector(matrix, vector):
@@ -283,24 +306,28 @@
     return mmt(vector, matrix[0]) + mmt(swapped, matrix[1])
 
 
-def source_rows(source_ref, halves):
-    return source_ref[lax.axis_index("alt") // halves]
-
-
-def early_body(halves, span_ref, source_ref, out_ref):
-    out_ref[...] = turn_vector((span_ref[0], span_ref[1]), source_rows(source_ref, halves))
-
-
 def field_body(halves, back, n_alt, width, scale, *refs):
-    span_ref, early_ref, came_ref, inner_ref, first_ref, second_ref, out_ref = refs
-    at = chain_place(halves)
+    span_ref, early_ref, came_ref, inner_ref, first_ref, second_ref = refs[:6]
+    place = lax.axis_index("alt")
     came = turn_vector((span_ref[0], span_ref[1]), came_ref[...])
-    amp = jnp.where(at < back, early_ref[...], came)
+    amp = jnp.where(chain_place(halves) < back, early_ref[...], came)
     amps = (amp, turn_vector((inner_ref[0], inner_ref[1]), amp))
-    for i, ref in enumerate((first_ref, second_ref)):
-        for k in range(n_alt):
-            part = mm(amps[i], ref[:, k * width : (k + 1) * width])
-            out_ref[k, i] = scale * part[0:2, :]
+    for k, out_ref in enumerate(refs[6:]):
+        target = lax.rem(place + k, n_alt)
+        span = pl.ds(pl.multiple_of(target * width, width), width)
+        for i, ref in enumerate((first_ref, second_ref)):
+            out_ref[i] = scale * mm(amps[i], ref[:, span])[0:2, :]
+
+
+def settle_body(halves, n_alt, *refs):
+    place = lax.axis_index("alt")
+    out_ref = refs[n_alt]
+    for k, part_ref in enumerate(refs[:n_alt]):
+        source = lax.rem(place + n_alt - k, n_alt)
+        chunk = part_ref.shape[0]
+        freq, half = source // halves, lax.rem(source, halves)
+        for i in range(chunk):
+            out_ref[freq, half * chunk + i] = part_ref[i]
 
 
 def local(freq_scale, base_profile, perturb, start_block, source):
@@ -325,24 +352,25 @@
                 pairs.append(tuple(ends))
         return lax.ppermute(value, ("range", "alt"), pairs)
 
-    lines = [start_block, base_profile[None, :], perturb]
-    filler = -(modes + 1 + seg_count) % 8
-    mine = jnp.concatenate(lines + [jnp.zeros((filler, width), jnp.float32)], axis=0)
-    blocks = [mine]
-    for k in range(1, n_alt):
-        blocks.append(lax.ppermute(mine, "alt", [(i, (i + k) % n_alt) for i in range(n_alt)]))
+    def around(value, k):
+        return lax.ppermute(value, "alt", [(i, (i + k) % n_alt) for i in range(n_alt)])
+
+    filler = jnp.zeros((-(1 + seg_count) % 8, width), jnp.float32)
+    profile = jnp.concatenate([base_profile[None, :], perturb, filler], axis=0)
+    starts = [start_block] + [around(start_block, k) for k in range(1, n_alt)]
+    profiles = [profile] + [around(profile, k) for k in range(1, n_alt)]
     flops = 2 * modes * modes * total
     first, second, coef = kernel_call(
         functools.partial(iterate_body, n_alt, chunk, seg_count, modes, width),
         [shape(modes, total)] * chunk + [shape(chunk, total)],
-        [freq_scale] + blocks,
-        [SM] + [VM] * n_alt,
+        [freq_scale] + starts + profiles,
+        [SM] + [VM] * (2 * n_alt),
         [pltpu.VMEM((chunk, 3, modes, total), jnp.bfloat16)]
         + [pltpu.VMEM((chunk, modes, total), jnp.float32)]
         + [pltpu.VMEM((chunk, modes, 128), jnp.float32)] * 2,
         flops=2 * ITERS * chunk * flops,
     )
-    following = along_chain(first, -1)
+    before = along_chain(second, 1)
     inner, rest = kernel_call(
         functools.partial(advance_body, modes, total),
         [shape(2, modes, modes)] * 2,
@@ -351,40 +379,43 @@
         [pltpu.VMEM((modes, total), jnp.float32)],
         flops=8 * flops,
     )
-    product = kernel_call(
-        product_body, shape(2, modes, modes), [following, second, rest], [VM] * 3, flops=flops
-    )
-    reach = 2
     span = kernel_call(
-        functools.partial(join_body, halves, 1, 2),
+        functools.partial(product_body, halves),
         shape(2, modes, modes),
-        [along_chain(product, 1), along_chain(product, 2)],
-        [VM] * 2,
+        [first, before, along_chain(rest, 1)],
+        [VM] * 3,
         flops=flops,
     )
+    rows = jnp.concatenate([source, jnp.zeros((freqs, 6, modes), jnp.float32)], axis=1)
+    reach = 1
     while 2 * reach < length:
-        span = kernel_call(
-            functools.partial(join_body, halves, 0, reach),
-            shape(2, modes, modes),
-            [span, along_chain(span, reach)],
-            [VM] * 2,
+        last = 4 * reach >= length
+        out = [shape(2, modes, modes)] + [shape(8, modes)] * last
+        results = kernel_call(
+            functools.partial(join_body, halves, reach),
+            out,
+            [span, along_chain(span, reach)] + [rows] * last,
+            [VM] * (2 + last),
             flops=flops,
         )
+        span = results[0]
         reach *= 2
-    rows = jnp.concatenate([source, jnp.zeros((freqs, 6, modes), jnp.float32)], axis=1)
-    early = kernel_call(
-        functools.partial(early_body, halves), shape(8, modes), [span, rows], [VM] * 2
-    )
+    early = results[1]
     parts = kernel_call(
         functools.partial(
             field_body, halves, reach, n_alt, width, (float(total) / float(modes)) ** 0.5
         ),
-        shape(n_alt, chunk, 2, width),
+        [shape(chunk, 2, width)] * n_alt,
         [span, early, along_chain(early, reach), inner, first, second],
         [VM] * 6,
     )
-    field = lax.all_to_all(parts, "alt", 0, 0)
-    return field.reshape(freqs, seg_count, 2, width)
+    parts = [parts[0]] + [around(parts[k], k) for k in range(1, n_alt)]
+    return kernel_call(
+        functools.partial(settle_body, halves, n_alt),
+        shape(freqs, seg_count, 2, width),
+        parts,
+        [VM] * n_alt,
+    )
 
 
 def solution(mesh):

time: 88.1 us -> 84.9 us (0.964)
  blocking collectives: 6.39 us -> 0 us
  starting transfers between devices: 32.5 us -> 36.1 us
  Pallas kernels: 35 us -> 32.5 us
  waiting for transfers between devices: 11.5 us -> 13.3 us
  other arithmetic: 0.98 us -> 0.07 us
    all_to_all x1 -> x0, blocking collectives: 6.39 us -> none  [local(): field = lax.all_to_all(parts, 'alt', 0, 0)]
    pallas_call x8, Pallas kernels: 35 us -> 32.5 us  [kernel_call(): pl.pallas_call(body, out_shape=out_shape, in_specs=specs, out_specs=jax.t...]
    ppermute x3 -> x9, starting transfers between devices: 4.46 us -> 6.81 us  [around(): lax.ppermute(value, 'alt', [(i, (i + k) % n_alt) for i in range(n_alt)])]
    ppermute x3 -> x9, waiting for transfers between devices: 3.6 us -> 5.7 us  [around(): lax.ppermute(value, 'alt', [(i, (i + k) % n_alt) for i in range(n_alt)])]
    ppermute x6, starting transfers between devices: 28 us -> 29.3 us  [along_chain(): return lax.ppermute(value, ('range', 'alt'), pairs)]
    concatenate x1, other arithmetic: 0.98 us -> 0.07 us  [local(): profile = jnp.concatenate([base_profile[None, :], perturb, filler], axis=0)]
  transfers between devices with their start and end apart: 9 -> 15, of which waited for: 7 -> 10; matrix products, arithmetic and copies ran while one was open for 0% -> 0% of each run, Pallas kernels for 4% -> 4%
where the time goes in v3:
time: 84.9 us; the launch traced here: 83.8 us
  starting transfers between devices  36.1 us (43%)
  Pallas kernels  32.5 us (38%)
  waiting for transfers between devices  13.3 us (16%)
  local copies, waits for them, and re-layouts  1.66 us (2%)
    pallas_call x8, Pallas kernels, kernel_call(): pl.pallas_call(body, out_shape=out_shape, in_specs=specs, out_specs=jax.t...  32.5 us
    ppermute x6, starting transfers between devices, along_chain(): return lax.ppermute(value, ('range', 'alt'), pairs)  29.3 us
    ppermute x6, waiting for transfers between devices, along_chain(): return lax.ppermute(value, ('range', 'alt'), pairs)  7.65 us
    ppermute x9, starting transfers between devices, around(): lax.ppermute(value, 'alt', [(i, (i + k) % n_alt) for i in range(n_alt)])  6.81 us
    ppermute x9, waiting for transfers between devices, around(): lax.ppermute(value, 'alt', [(i, (i + k) % n_alt) for i in range(n_alt)])  5.7 us
  transfers between devices with their start and end apart: 15, of which 10 were waited for; matrix products, arithmetic and copies ran while one was open for 0% of the time, Pallas kernels for 4%

profile of v3, /device:TPU:0, one launch (start us, length us, event | category | flops | bytes accessed | tf_op | source)
XLA Modules:
  0.0 83.8 jit_solution(3465459593426216661)
XLA Ops:
  0.0 0.5 collective-permute-start
  0.5 2.5 %collective-permute-start.1 = (f32[96,256]{1,0:T(8,128)}, f32[96,256]{1,0:T(8,128)S(1)}, u32[]{:S(2)}, u32[]{:S(2)}) collective-permute-start(f32[96,256]{1,0:T(8,128)} %refs_0_.1), channel_id=1, source_target_pairs={{0,2},{1,3},{2,0},{3,1},{4,6},{5,7},{6,4},{7,5},{8,10},{9,11},{10,... | collective-permute-start | bytes 294920 | tf_op jit(solution)/shard_map/ppermute | solution.py:356
  3.0 1.4 %collective-permute-start.2 = (f32[96,256]{1,0:T(8,128)}, f32[96,256]{1,0:T(8,128)S(1)}, u32[]{:S(2)}, u32[]{:S(2)}) collective-permute-start(f32[96,256]{1,0:T(8,128)} %refs_0_.1), channel_id=1, source_target_pairs={{0,3},{1,0},{2,1},{3,2},{4,7},{5,4},{6,5},{7,6},{8,11},{9,8},{10,9... | collective-permute-start | bytes 294920 | tf_op jit(solution)/shard_map/ppermute | solution.py:356
  4.5 0.7 copy-done.4
  5.2 0.4 collective-permute-start.4
  5.6 2.7 %collective-permute-done.3.refs_5_ = f32[8,256]{1,0:T(8,128)S(1)} collective-permute-done((f32[8,256]{1,0:T(8,128)S(1)}, f32[8,256]{1,0:T(8,128)S(1)}, u32[]{:S(2)}, u32[]{:S(2)}) %collective-permute-start.3) | collective-permute-done | bytes 8224 | tf_op jit(solution)/shard_map/ppermute | solution.py:356
  8.3 0.7 collective-permute-done.4.refs_6_
  9.0 0.7 collective-permute-done.5.refs_7_
  9.7 0.9 %copy-done = f32[96,256]{1,0:T(8,128)S(1)} copy-done((f32[96,256]{1,0:T(8,128)S(1)}, f32[96,256]{1,0:T(8,128)}, u32[]{:S(2)}) %copy-start) | copy-done | bytes 98328
  10.6 25.4 %shard_map.55 = (f32[96,1024]{1,0:T(8,128)S(1)}, f32[96,1024]{1,0:T(8,128)S(1)}, f32[2,1024]{1,0:T(2,128)S(1)}) custom-call(f32[2]{0:T(128)S(1)} %copy-done.1, f32[96,256]{1,0:T(8,128)S(1)} %copy-done, f32[96,256]{1,0:T(8,128)S(1)} %collective-permute-done.refs_1_, f32[96,256]{1,0:T(8,128)S(1)} %collective-permute-done.1.refs_2_, ...), custom_call_target="tpu_custom_call" | custom-call | flops 603979776 | bytes 1220616 | tf_op jit(solution)/shard_map/pallas_call | solution.py:45
  36.0 3.6 %collective-permute-start.6 = (f32[96,1024]{1,0:T(8,128)S(1)}, f32[96,1024]{1,0:T(8,128)S(1)}, u32[]{:S(2)}, u32[]{:S(2)}) collective-permute-start(f32[96,1024]{1,0:T(8,128)S(1)} %get-tuple-element.17.second_ref.refs_5_), channel_id=1, source_target_pairs={{0,1},{1,4},{4,5},{5,8},{8,9},{9,12},{12,13},{13,16},{16,17},{17,2... | collective-permute-start | bytes 1179656 | tf_op jit(solution)/shard_map/ppermute | solution.py:353
  39.6 3.1 %shard_map.56 = (f32[2,96,96]{2,1,0:T(8,128)S(1)}, f32[2,96,96]{2,1,0:T(8,128)S(1)}) custom-call(f32[2,1024]{1,0:T(2,128)S(1)} %get-tuple-element.18.coef_ref, f32[96,1024]{1,0:T(8,128)S(1)} %get-tuple-element.16.first_ref.refs_4_, f32[96,1024]{1,0:T(8,128)S(1)} %get-tuple-element.17.second_ref.refs_5_), custom_call_target="tpu_custom_call" | custom-call | flops 150994944 | bytes 942080 | tf_op jit(solution)/shard_map/pallas_call | solution.py:45
  42.8 2.0 %collective-permute-start.7 = (f32[2,96,96]{2,1,0:T(8,128)S(1)}, f32[2,96,96]{2,1,0:T(8,128)S(1)}, u32[]{:S(2)}, u32[]{:S(2)}) collective-permute-start(f32[2,96,96]{2,1,0:T(8,128)S(1)} %get-tuple-element.19), channel_id=1, source_target_pairs={{0,1},{1,4},{4,5},{5,8},{8,9},{9,12},{12,13},{13,16},{16,17},{17,2... | collective-permute-start | bytes 221192 | tf_op jit(solution)/shard_map/ppermute | solution.py:353
  44.7 0.9 %collective-permute-done.7.rest_ref = f32[2,96,96]{2,1,0:T(8,128)S(1)} collective-permute-done((f32[2,96,96]{2,1,0:T(8,128)S(1)}, f32[2,96,96]{2,1,0:T(8,128)S(1)}, u32[]{:S(2)}, u32[]{:S(2)}) %collective-permute-start.7) | collective-permute-done | bytes 73760 | tf_op jit(solution)/shard_map/ppermute | solution.py:353
  45.7 0.8 shard_map.57.new_ref
  46.5 4.2 %collective-permute-start.8 = (f32[2,96,96]{2,1,0:T(8,128)S(1)}, f32[2,96,96]{2,1,0:T(8,128)S(1)}, u32[]{:S(2)}, u32[]{:S(2)}) collective-permute-start(f32[2,96,96]{2,1,0:T(8,128)S(1)} %shard_map.57.new_ref), channel_id=1, source_target_pairs={{0,1},{1,4},{4,5},{5,8},{8,9},{9,12},{12,13},{13,16},{16,17},{17,2... | collective-permute-start | bytes 221192 | tf_op jit(solution)/shard_map/ppermute | solution.py:353
  50.7 0.9 %collective-permute-done.8.old_ref = f32[2,96,96]{2,1,0:T(8,128)S(1)} collective-permute-done((f32[2,96,96]{2,1,0:T(8,128)S(1)}, f32[2,96,96]{2,1,0:T(8,128)S(1)}, u32[]{:S(2)}, u32[]{:S(2)}) %collective-permute-start.8) | collective-permute-done | bytes 73760 | tf_op jit(solution)/shard_map/ppermute | solution.py:353
  51.6 0.3 shard_map.58.new_ref
  51.9 7.3 %collective-permute-start.9 = (f32[2,96,96]{2,1,0:T(8,128)S(1)}, f32[2,96,96]{2,1,0:T(8,128)S(1)}, u32[]{:S(2)}, u32[]{:S(2)}) collective-permute-start(f32[2,96,96]{2,1,0:T(8,128)S(1)} %shard_map.58.new_ref), channel_id=1, source_target_pairs={{0,4},{1,5},{4,8},{5,9},{8,12},{9,13},{12,16},{13,17},{16,20},{17,... | collective-permute-start | bytes 221192 | tf_op jit(solution)/shard_map/ppermute | solution.py:353
  59.2 2.3 %collective-permute-done.9.old_ref = f32[2,96,96]{2,1,0:T(8,128)S(1)} collective-permute-done((f32[2,96,96]{2,1,0:T(8,128)S(1)}, f32[2,96,96]{2,1,0:T(8,128)S(1)}, u32[]{:S(2)}, u32[]{:S(2)}) %collective-permute-start.9) | collective-permute-done | bytes 73760 | tf_op jit(solution)/shard_map/ppermute | solution.py:353
  61.5 0.3 shard_map.59.new_ref
  61.9 6.9 %collective-permute-start.10 = (f32[2,96,96]{2,1,0:T(8,128)S(1)}, f32[2,96,96]{2,1,0:T(8,128)S(1)}, u32[]{:S(2)}, u32[]{:S(2)}) collective-permute-start(f32[2,96,96]{2,1,0:T(8,128)S(1)} %shard_map.59.new_ref), channel_id=1, source_target_pairs={{0,8},{1,9},{4,12},{5,13},{8,16},{9,17},{12,20},{13,21},{16,24},{1... | collective-permute-start | bytes 221192 | tf_op jit(solution)/shard_map/ppermute | solution.py:353
  68.8 2.2 %collective-permute-done.10.old_ref = f32[2,96,96]{2,1,0:T(8,128)S(1)} collective-permute-done((f32[2,96,96]{2,1,0:T(8,128)S(1)}, f32[2,96,96]{2,1,0:T(8,128)S(1)}, u32[]{:S(2)}, u32[]{:S(2)}) %collective-permute-start.10) | collective-permute-done | bytes 73760 | tf_op jit(solution)/shard_map/ppermute | solution.py:353
  71.0 0.7 shard_map.60
  71.7 5.3 %collective-permute-start.11 = (f32[8,96]{1,0:T(8,128)S(1)}, f32[8,96]{1,0:T(8,128)S(1)}, u32[]{:S(2)}, u32[]{:S(2)}) collective-permute-start(f32[8,96]{1,0:T(8,128)S(1)} %get-tuple-element.21.refs_1_), channel_id=1, source_target_pairs={{0,16},{1,17},{4,20},{5,21},{8,24},{9,25},{12,28},{13,29},{2,18},{... | collective-permute-start | bytes 9224 | tf_op jit(solution)/shard_map/ppermute | solution.py:353
  77.0 1.3 %collective-permute-done.11.refs_2_ = f32[8,96]{1,0:T(8,128)S(1)} collective-permute-done((f32[8,96]{1,0:T(8,128)S(1)}, f32[8,96]{1,0:T(8,128)S(1)}, u32[]{:S(2)}, u32[]{:S(2)}) %collective-permute-start.11) | collective-permute-done | bytes 3104 | tf_op jit(solution)/shard_map/ppermute | solution.py:353
  78.4 1.2 %shard_map.61 = (f32[2,2,256]{2,1,0:T(2,128)S(1)}, f32[2,2,256]{2,1,0:T(2,128)S(1)}, f32[2,2,256]{2,1,0:T(2,128)S(1)}, f32[2,2,256]{2,1,0:T(2,128)S(1)}) custom-call(f32[2,96,96]{2,1,0:T(8,128)S(1)} %get-tuple-element.20.refs_0_, f32[8,96]{1,0:T(8,128)S(1)} %get-tuple-element.21.refs_1_, f32[8,96]{1,0:T(8,128)S(1)} %collective-permute-done.11.refs_2_, ...), custom_call_target="tpu_custom_call" | custom-call | bytes 956416 | tf_op jit(solution)/shard_map/pallas_call | solution.py:45
  79.6 0.6 collective-permute-start.13
  80.2 1.4 %collective-permute-start.14 = (f32[2,2,256]{2,1,0:T(2,128)S(1)}, f32[2,2,256]{2,1,0:T(2,128)S(1)}, u32[]{:S(2)}, u32[]{:S(2)}) collective-permute-start(f32[2,2,256]{2,1,0:T(2,128)S(1)} %get-tuple-element.26), channel_id=1, source_target_pairs={{0,3},{1,0},{2,1},{3,2},{4,7},{5,4},{6,5},{7,6},{8,11},{9,8},{10,9... | collective-permute-start | bytes 12296 | tf_op jit(solution)/shard_map/ppermute | solution.py:356
  81.6 1.0 %collective-permute-done.12.refs_1_ = f32[2,2,256]{2,1,0:T(2,128)S(1)} collective-permute-done((f32[2,2,256]{2,1,0:T(2,128)S(1)}, f32[2,2,256]{2,1,0:T(2,128)S(1)}, u32[]{:S(2)}, u32[]{:S(2)}) %collective-permute-start.12) | collective-permute-done | bytes 4128 | tf_op jit(solution)/shard_map/ppermute | solution.py:356
  82.6 0.6 collective-permute-done.13.refs_2_
  83.2 0.6 shard_map.62
  (20 shorter events, 0.2 us)
Async XLA Ops:
  0.0 4.5 %copy-start.2 = (f32[4,256]{1,0:T(4,128)S(1)}, f32[4,256]{1,0:T(4,128)}, u32[]{:S(2)}) copy-start(f32[4,256]{1,0:T(4,128)} %param.7) | copy-start | bytes 12292
  0.0 9.7 %collective-permute-start = (f32[96,256]{1,0:T(8,128)}, f32[96,256]{1,0:T(8,128)S(1)}, u32[]{:S(2)}, u32[]{:S(2)}) collective-permute-start(f32[96,256]{1,0:T(8,128)} %refs_0_.1), channel_id=1, source_target_pairs={{0,1},{1,2},{2,3},{3,0},{4,5},{5,6},{6,7},{7,4},{8,9},{9,10},{10,1... | collective-permute-start | bytes 294920 | tf_op jit(solution)/shard_map/ppermute | solution.py:356
  0.5 9.2 %collective-permute-start.1 = (f32[96,256]{1,0:T(8,128)}, f32[96,256]{1,0:T(8,128)S(1)}, u32[]{:S(2)}, u32[]{:S(2)}) collective-permute-start(f32[96,256]{1,0:T(8,128)} %refs_0_.1), channel_id=1, source_target_pairs={{0,2},{1,3},{2,0},{3,1},{4,6},{5,7},{6,4},{7,5},{8,10},{9,11},{10,... | collective-permute-start | bytes 294920 | tf_op jit(solution)/shard_map/ppermute | solution.py:356
  3.0 6.7 %collective-permute-start.2 = (f32[96,256]{1,0:T(8,128)}, f32[96,256]{1,0:T(8,128)S(1)}, u32[]{:S(2)}, u32[]{:S(2)}) collective-permute-start(f32[96,256]{1,0:T(8,128)} %refs_0_.1), channel_id=1, source_target_pairs={{0,3},{1,0},{2,1},{3,2},{4,7},{5,4},{6,5},{7,6},{8,11},{9,8},{10,9... | collective-permute-start | bytes 294920 | tf_op jit(solution)/shard_map/ppermute | solution.py:356
  4.5 0.7 copy-start.4
  5.2 4.5 %copy-start.1 = (f32[2]{0:T(128)S(1)}, f32[2]{0:T(128)}, u32[]{:S(2)}) copy-start(f32[2]{0:T(128)} %scale_ref.1) | copy-start | bytes 28
  5.2 3.1 %collective-permute-start.3 = (f32[8,256]{1,0:T(8,128)S(1)}, f32[8,256]{1,0:T(8,128)S(1)}, u32[]{:S(2)}, u32[]{:S(2)}) collective-permute-start(f32[8,256]{1,0:T(8,128)S(1)} %maximum_maximum_fusion.refs_4_), channel_id=1, source_target_pairs={{0,1},{1,2},{2,3},{3,0},{4,5},{5,6},{6,7},{7,4},{8,9},{9,10},{10,1... | collective-permute-start | bytes 24584 | tf_op jit(solution)/shard_map/ppermute | solution.py:356
  5.2 3.7 %collective-permute-start.4 = (f32[8,256]{1,0:T(8,128)S(1)}, f32[8,256]{1,0:T(8,128)S(1)}, u32[]{:S(2)}, u32[]{:S(2)}) collective-permute-start(f32[8,256]{1,0:T(8,128)S(1)} %maximum_maximum_fusion.refs_4_), channel_id=1, source_target_pairs={{0,2},{1,3},{2,0},{3,1},{4,6},{5,7},{6,4},{7,5},{8,10},{9,11},{10,... | collective-permute-start | bytes 24584 | tf_op jit(solution)/shard_map/ppermute | solution.py:356
  8.3 1.4 %collective-permute-start.5 = (f32[8,256]{1,0:T(8,128)S(1)}, f32[8,256]{1,0:T(8,128)S(1)}, u32[]{:S(2)}, u32[]{:S(2)}) collective-permute-start(f32[8,256]{1,0:T(8,128)S(1)} %maximum_maximum_fusion.refs_4_), channel_id=1, source_target_pairs={{0,3},{1,0},{2,1},{3,2},{4,7},{5,4},{6,5},{7,6},{8,11},{9,8},{10,9... | collective-permute-start | bytes 24584 | tf_op jit(solution)/shard_map/ppermute | solution.py:356
  9.7 0.9 %copy-start = (f32[96,256]{1,0:T(8,128)S(1)}, f32[96,256]{1,0:T(8,128)}, u32[]{:S(2)}) copy-start(f32[96,256]{1,0:T(8,128)} %refs_0_.1) | copy-start | bytes 294916
  36.0 9.7 %collective-permute-start.6 = (f32[96,1024]{1,0:T(8,128)S(1)}, f32[96,1024]{1,0:T(8,128)S(1)}, u32[]{:S(2)}, u32[]{:S(2)}) collective-permute-start(f32[96,1024]{1,0:T(8,128)S(1)} %get-tuple-element.17.second_ref.refs_5_), channel_id=1, source_target_pairs={{0,1},{1,4},{4,5},{5,8},{8,9},{9,12},{12,13},{13,16},{16,17},{17,2... | collective-permute-start | bytes 1179656 | tf_op jit(solution)/shard_map/ppermute | solution.py:353
  42.8 2.9 %collective-permute-start.7 = (f32[2,96,96]{2,1,0:T(8,128)S(1)}, f32[2,96,96]{2,1,0:T(8,128)S(1)}, u32[]{:S(2)}, u32[]{:S(2)}) collective-permute-start(f32[2,96,96]{2,1,0:T(8,128)S(1)} %get-tuple-element.19), channel_id=1, source_target_pairs={{0,1},{1,4},{4,5},{5,8},{8,9},{9,12},{12,13},{13,16},{16,17},{17,2... | collective-permute-start | bytes 221192 | tf_op jit(solution)/shard_map/ppermute | solution.py:353
  46.5 5.1 %collective-permute-start.8 = (f32[2,96,96]{2,1,0:T(8,128)S(1)}, f32[2,96,96]{2,1,0:T(8,128)S(1)}, u32[]{:S(2)}, u32[]{:S(2)}) collective-permute-start(f32[2,96,96]{2,1,0:T(8,128)S(1)} %shard_map.57.new_ref), channel_id=1, source_target_pairs={{0,1},{1,4},{4,5},{5,8},{8,9},{9,12},{12,13},{13,16},{16,17},{17,2... | collective-permute-start | bytes 221192 | tf_op jit(solution)/shard_map/ppermute | solution.py:353
  51.9 16.9 %copy-start.3 = (f32[2,2,96]{2,1,0:T(2,128)S(1)}, f32[2,2,96]{2,1,0:T(2,128)}, u32[]{:S(2)}) copy-start(f32[2,2,96]{2,1,0:T(2,128)} %param.9) | copy-start | bytes 4612
  51.9 9.6 %collective-permute-start.9 = (f32[2,96,96]{2,1,0:T(8,128)S(1)}, f32[2,96,96]{2,1,0:T(8,128)S(1)}, u32[]{:S(2)}, u32[]{:S(2)}) collective-permute-start(f32[2,96,96]{2,1,0:T(8,128)S(1)} %shard_map.58.new_ref), channel_id=1, source_target_pairs={{0,4},{1,5},{4,8},{5,9},{8,12},{9,13},{12,16},{13,17},{16,20},{17,... | collective-permute-start | bytes 221192 | tf_op jit(solution)/shard_map/ppermute | solution.py:353
  61.9 9.1 %collective-permute-start.10 = (f32[2,96,96]{2,1,0:T(8,128)S(1)}, f32[2,96,96]{2,1,0:T(8,128)S(1)}, u32[]{:S(2)}, u32[]{:S(2)}) collective-permute-start(f32[2,96,96]{2,1,0:T(8,128)S(1)} %shard_map.59.new_ref), channel_id=1, source_target_pairs={{0,8},{1,9},{4,12},{5,13},{8,16},{9,17},{12,20},{13,21},{16,24},{1... | collective-permute-start | bytes 221192 | tf_op jit(solution)/shard_map/ppermute | solution.py:353
  71.7 6.7 %collective-permute-start.11 = (f32[8,96]{1,0:T(8,128)S(1)}, f32[8,96]{1,0:T(8,128)S(1)}, u32[]{:S(2)}, u32[]{:S(2)}) collective-permute-start(f32[8,96]{1,0:T(8,128)S(1)} %get-tuple-element.21.refs_1_), channel_id=1, source_target_pairs={{0,16},{1,17},{4,20},{5,21},{8,24},{9,25},{12,28},{13,29},{2,18},{... | collective-permute-start | bytes 9224 | tf_op jit(solution)/shard_map/ppermute | solution.py:353
  79.6 3.0 %collective-permute-start.12 = (f32[2,2,256]{2,1,0:T(2,128)S(1)}, f32[2,2,256]{2,1,0:T(2,128)S(1)}, u32[]{:S(2)}, u32[]{:S(2)}) collective-permute-start(f32[2,2,256]{2,1,0:T(2,128)S(1)} %get-tuple-element.24), channel_id=1, source_target_pairs={{0,1},{1,2},{2,3},{3,0},{4,5},{5,6},{6,7},{7,4},{8,9},{9,10},{10,1... | collective-permute-start | bytes 12296 | tf_op jit(solution)/shard_map/ppermute | solution.py:356
  79.6 3.7 %collective-permute-start.13 = (f32[2,2,256]{2,1,0:T(2,128)S(1)}, f32[2,2,256]{2,1,0:T(2,128)S(1)}, u32[]{:S(2)}, u32[]{:S(2)}) collective-permute-start(f32[2,2,256]{2,1,0:T(2,128)S(1)} %get-tuple-element.25), channel_id=1, source_target_pairs={{0,2},{1,3},{2,0},{3,1},{4,6},{5,7},{6,4},{7,5},{8,10},{9,11},{10,... | collective-permute-start | bytes 12296 | tf_op jit(solution)/shard_map/ppermute | solution.py:356
  80.2 3.1 %collective-permute-start.14 = (f32[2,2,256]{2,1,0:T(2,128)S(1)}, f32[2,2,256]{2,1,0:T(2,128)S(1)}, u32[]{:S(2)}, u32[]{:S(2)}) collective-permute-start(f32[2,2,256]{2,1,0:T(2,128)S(1)} %get-tuple-element.26), channel_id=1, source_target_pairs={{0,3},{1,0},{2,1},{3,2},{4,7},{5,4},{6,5},{7,6},{8,11},{9,8},{10,9... | collective-permute-start | bytes 12296 | tf_op jit(solution)/shard_map/ppermute | solution.py:356

commit v4 on v3

--- a/solution.py
+++ b/solution.py
@@ -174,23 +174,22 @@
 
 
 def iterate_body(n_alt, chunk, seg_count, modes, width, scale_ref, *refs):
-    starts, profiles = refs[:n_alt], refs[n_alt : 2 * n_alt]
-    out_refs = refs[2 * n_alt : 2 * n_alt + chunk]
-    coef_ref, split_ref, image_ref, gram_ref, inv_ref = refs[2 * n_alt + chunk :]
+    blocks, out_refs = refs[:n_alt], refs[n_alt : n_alt + chunk]
+    coef_ref, split_ref, image_ref, gram_ref, inv_ref = refs[n_alt + chunk :]
     place = lax.axis_index("alt")
     flat = place * chunk
     freq = flat // seg_count
     first = flat - freq * seg_count
     total = n_alt * width
-    for k in range(n_alt):
+    for k, block in enumerate(blocks):
         source = lax.rem(place + n_alt - k, n_alt)
         span = pl.ds(pl.multiple_of(source * width, width), width)
-        start = starts[k][...] * (1.0 / float(total) ** 0.5)
+        start = block[0:modes, :] * (1.0 / float(total) ** 0.5)
         for i in range(chunk):
             out_refs[i][:, span] = start
-            change = profiles[k][pl.ds(1 + first + i, 1), :]
+            change = block[pl.ds(modes + 1 + first + i, 1), :]
             coef_ref[i : i + 1, span] = scale_ref[freq] * (
-                profiles[k][0:1, :] * (1.0 + relief * change)
+                block[modes : modes + 1, :] * (1.0 + relief * change)
             )
     from_low, from_high = edge_weights(total)
     down = 2.0**-11
@@ -277,25 +276,22 @@
     return lax.axis_index("range") * halves + lax.rem(lax.axis_index("alt"), halves)
 
 
-def with_start(halves, back, ref):
-    missing = chain_place(halves) < back
-    return (ref[0] + jnp.where(missing, unit_of(ref.shape[1]), 0.0), ref[1])
-
-
-def product_body(halves, first_ref, before_ref, rest_ref, out_ref):
-    corr = mmt(first_ref[...], before_ref[...])
-    missing = chain_place(halves) < 1
-    out_ref[0] = mm(corr, rest_ref[0]) + jnp.where(missing, unit_of(out_ref.shape[1]), 0.0)
-    out_ref[1] = mm(corr, rest_ref[1])
-
-
-def join_body(halves, back, new_ref, old_ref, *refs):
-    out_ref = refs[1] if len(refs) > 1 else refs[0]
-    joined = complex_mm((new_ref[0], new_ref[1]), with_start(halves, back, old_ref))
-    out_ref[0], out_ref[1] = joined
-    if len(refs) > 1:
-        source = refs[0][lax.axis_index("alt") // halves]
-        refs[2][...] = turn_vector(joined, source)
+def product_body(next_ref, second_ref, rest_ref, out_ref):
+    corr = mmt(next_ref[...], second_ref[...])
+    for part in range(2):
+        out_ref[part] = mm(corr, rest_ref[part])
+
+
+def join_body(halves, backs, *refs):
+    at = chain_place(halves)
+    spans = []
+    for back, ref in zip(backs, refs):
+        missing = jnp.where(at < back, unit_of(ref.shape[1]), 0.0)
+        spans.append((ref[0] + missing, ref[1]) if back else (ref[0], ref[1]))
+    while len(spans) > 1:
+        pairs = [complex_mm(*spans[i : i + 2]) for i in range(0, len(spans) - 1, 2)]
+        spans = pairs + spans[len(pairs) * 2 :]
+    refs[-1][0], refs[-1][1] = spans[0]
 
 
 def turn_vector(matrix, vector):
@@ -306,13 +302,16 @@
     return mmt(vector, matrix[0]) + mmt(swapped, matrix[1])
 
 
-def field_body(halves, back, n_alt, width, scale, *refs):
-    span_ref, early_ref, came_ref, inner_ref, first_ref, second_ref = refs[:6]
+def field_body(halves, backs, n_alt, width, scale, source_ref, *refs):
+    count = len(backs)
+    inner_ref, first_ref, second_ref = refs[count : count + 3]
     place = lax.axis_index("alt")
-    came = turn_vector((span_ref[0], span_ref[1]), came_ref[...])
-    amp = jnp.where(chain_place(halves) < back, early_ref[...], came)
+    amp = source_ref[place // halves]
+    for back, ref in reversed(list(zip(backs, refs))):
+        moved = turn_vector((ref[0], ref[1]), amp)
+        amp = jnp.where(chain_place(halves) < back, amp, moved)
     amps = (amp, turn_vector((inner_ref[0], inner_ref[1]), amp))
-    for k, out_ref in enumerate(refs[6:]):
+    for k, out_ref in enumerate(refs[count + 3 :]):
         target = lax.rem(place + k, n_alt)
         span = pl.ds(pl.multiple_of(target * width, width), width)
         for i, ref in enumerate((first_ref, second_ref)):
@@ -355,22 +354,22 @@
     def around(value, k):
         return lax.ppermute(value, "alt", [(i, (i + k) % n_alt) for i in range(n_alt)])
 
-    filler = jnp.zeros((-(1 + seg_count) % 8, width), jnp.float32)
-    profile = jnp.concatenate([base_profile[None, :], perturb, filler], axis=0)
-    starts = [start_block] + [around(start_block, k) for k in range(1, n_alt)]
-    profiles = [profile] + [around(profile, k) for k in range(1, n_alt)]
+    lines = [start_block, base_profile[None, :], perturb]
+    filler = jnp.zeros((-(modes + 1 + seg_count) % 8, width), jnp.float32)
+    mine = jnp.concatenate(lines + [filler], axis=0)
+    blocks = [mine] + [around(mine, k) for k in range(1, n_alt)]
     flops = 2 * modes * modes * total
     first, second, coef = kernel_call(
         functools.partial(iterate_body, n_alt, chunk, seg_count, modes, width),
         [shape(modes, total)] * chunk + [shape(chunk, total)],
-        [freq_scale] + starts + profiles,
-        [SM] + [VM] * (2 * n_alt),
+        [freq_scale] + blocks,
+        [SM] + [VM] * n_alt,
         [pltpu.VMEM((chunk, 3, modes, total), jnp.bfloat16)]
         + [pltpu.VMEM((chunk, modes, total), jnp.float32)]
         + [pltpu.VMEM((chunk, modes, 128), jnp.float32)] * 2,
         flops=2 * ITERS * chunk * flops,
     )
-    before = along_chain(second, 1)
+    following = along_chain(first, -1)
     inner, rest = kernel_call(
         functools.partial(advance_body, modes, total),
         [shape(2, modes, modes)] * 2,
@@ -379,35 +378,35 @@
         [pltpu.VMEM((modes, total), jnp.float32)],
         flops=8 * flops,
     )
-    span = kernel_call(
-        functools.partial(product_body, halves),
-        shape(2, modes, modes),
-        [first, before, along_chain(rest, 1)],
-        [VM] * 3,
-        flops=flops,
-    )
-    rows = jnp.concatenate([source, jnp.zeros((freqs, 6, modes), jnp.float32)], axis=1)
-    reach = 1
-    while 2 * reach < length:
-        last = 4 * reach >= length
-        out = [shape(2, modes, modes)] + [shape(8, modes)] * last
-        results = kernel_call(
-            functools.partial(join_body, halves, reach),
-            out,
-            [span, along_chain(span, reach)] + [rows] * last,
-            [VM] * (2 + last),
+    product = kernel_call(
+        product_body, shape(2, modes, modes), [following, second, rest], [VM] * 3, flops=flops
+    )
+
+    def join(spans, backs):
+        return kernel_call(
+            functools.partial(join_body, halves, backs),
+            shape(2, modes, modes),
+            spans,
+            [VM] * len(spans),
             flops=flops,
         )
-        span = results[0]
-        reach *= 2
-    early = results[1]
+
+    reach = min(4, length)
+    backs = range(1, reach + 1)
+    span = join([along_chain(product, back) for back in backs], backs)
+    while length > 4 * reach:
+        backs = range(0, 4 * reach, reach)
+        span = join([span] + [along_chain(span, back) for back in backs[1:]], backs)
+        reach *= 4
+    rows = jnp.concatenate([source, jnp.zeros((freqs, 6, modes), jnp.float32)], axis=1)
+    backs = range(0, length, reach)
     parts = kernel_call(
         functools.partial(
-            field_body, halves, reach, n_alt, width, (float(total) / float(modes)) ** 0.5
+            field_body, halves, backs, n_alt, width, (float(total) / float(modes)) ** 0.5
         ),
         [shape(chunk, 2, width)] * n_alt,
-        [span, early, along_chain(early, reach), inner, first, second],
-        [VM] * 6,
+        [rows, span] + [along_chain(span, back) for back in backs[1:]] + [inner, first, second],
+        [VM] * (4 + len(backs)),
     )
     parts = [parts[0]] + [around(parts[k], k) for k in range(1, n_alt)]
     return kernel_call(

time: 84.9 us -> 80.9 us (0.953)
  the two profiles are of different devices: /device:TPU:0 before, /device:TPU:27 now
where the time goes in v4:
time: 80.9 us; the launch traced here: 80.6 us
  Pallas kernels  33.1 us (41%)
  waiting for transfers between devices  28.1 us (35%)
  starting transfers between devices  17.4 us (22%)
  other arithmetic  0.98 us (1%)
    pallas_call x6, Pallas kernels, kernel_call(): pl.pallas_call(body, out_shape=out_shape, in_specs=specs, out_specs=jax.t...  33.1 us
    ppermute x8, waiting for transfers between devices, along_chain(): return lax.ppermute(value, ('range', 'alt'), pairs)  19.6 us
    ppermute x8, starting transfers between devices, along_chain(): return lax.ppermute(value, ('range', 'alt'), pairs)  12.2 us
    ppermute x6, waiting for transfers between devices, around(): lax.ppermute(value, 'alt', [(i, (i + k) % n_alt) for i in range(n_alt)])  8.54 us
    ppermute x6, starting transfers between devices, around(): lax.ppermute(value, 'alt', [(i, (i + k) % n_alt) for i in range(n_alt)])  5.19 us
  transfers between devices with their start and end apart: 14, of which 12 were waited for; matrix products, arithmetic and copies ran while one was open for 0% of the time, Pallas kernels for 4%

profile of v4, /device:TPU:27, one launch (start us, length us, event | category | flops | bytes accessed | tf_op | source)
XLA Modules:
  0.0 80.6 jit_solution(12810452065901777155)
XLA Ops:
  0.1 0.6 copy-done.1
  0.8 1.0 %maximum_maximum_fusion.refs_0_ = f32[104,256]{1,0:T(8,128)S(1)} fusion(f32[4,256]{1,0:T(4,128)S(1)} %copy-done.1, f32[1,256]{1,0:T(1,128)S(1)} %bitcast.1, f32[96,256]{1,0:T(8,128)} %param.8, f32[104]{0:T(128)S(1)} %pad.4.clone), kind=kLoop, calls=%fused_computation | loop fusion | flops 79872 | bytes 210336 | tf_op jit(solution)/shard_map/concatenate | solution.py:359
  1.8 0.9 %collective-permute-start = (f32[104,256]{1,0:T(8,128)S(1)}, f32[104,256]{1,0:T(8,128)S(1)}, u32[]{:S(2)}, u32[]{:S(2)}) collective-permute-start(f32[104,256]{1,0:T(8,128)S(1)} %maximum_maximum_fusion.refs_0_), channel_id=1, source_target_pairs={{0,1},{1,2},{2,3},{3,0},{4,5},{5,6},{6,7},{7,4},{8,9},{9,10},{10,1... | collective-permute-start | bytes 319496 | tf_op jit(solution)/shard_map/ppermute | solution.py:355
  2.6 1.2 %collective-permute-start.1 = (f32[104,256]{1,0:T(8,128)S(1)}, f32[104,256]{1,0:T(8,128)S(1)}, u32[]{:S(2)}, u32[]{:S(2)}) collective-permute-start(f32[104,256]{1,0:T(8,128)S(1)} %maximum_maximum_fusion.refs_0_), channel_id=1, source_target_pairs={{0,2},{1,3},{2,0},{3,1},{4,6},{5,7},{6,4},{7,5},{8,10},{9,11},{10,... | collective-permute-start | bytes 319496 | tf_op jit(solution)/shard_map/ppermute | solution.py:355
  3.8 1.0 %collective-permute-done.refs_1_ = f32[104,256]{1,0:T(8,128)S(1)} collective-permute-done((f32[104,256]{1,0:T(8,128)S(1)}, f32[104,256]{1,0:T(8,128)S(1)}, u32[]{:S(2)}, u32[]{:S(2)}) %collective-permute-start) | collective-permute-done | bytes 106528 | tf_op jit(solution)/shard_map/ppermute | solution.py:355
  4.8 3.9 %collective-permute-done.1.refs_2_ = f32[104,256]{1,0:T(8,128)S(1)} collective-permute-done((f32[104,256]{1,0:T(8,128)S(1)}, f32[104,256]{1,0:T(8,128)S(1)}, u32[]{:S(2)}, u32[]{:S(2)}) %collective-permute-start.1) | collective-permute-done | bytes 106528 | tf_op jit(solution)/shard_map/ppermute | solution.py:355
  8.7 0.6 collective-permute-done.2.refs_3_
  9.3 25.3 %shard_map.55 = (f32[96,1024]{1,0:T(8,128)S(1)}, f32[96,1024]{1,0:T(8,128)S(1)}, f32[2,1024]{1,0:T(2,128)S(1)}) custom-call(f32[2]{0:T(128)S(1)} %copy-done, f32[104,256]{1,0:T(8,128)S(1)} %maximum_maximum_fusion.refs_0_, f32[104,256]{1,0:T(8,128)S(1)} %collective-permute-done.refs_1_, f32[104,256]{1,0:T(8,128)S(1)} %collective-permute-done.1.refs_2_, ...), custom_call_target="tpu_custom_call" | custom-call | flops 603979776 | bytes 1220616 | tf_op jit(solution)/shard_map/pallas_call | solution.py:45
  34.7 1.9 %collective-permute-start.3 = (f32[96,1024]{1,0:T(8,128)S(1)}, f32[96,1024]{1,0:T(8,128)S(1)}, u32[]{:S(2)}, u32[]{:S(2)}) collective-permute-start(f32[96,1024]{1,0:T(8,128)S(1)} %get-tuple-element.14.first_ref.refs_5_), channel_id=1, source_target_pairs={{1,0},{4,1},{5,4},{8,5},{9,8},{12,9},{13,12},{16,13},{17,16},{20,1... | collective-permute-start | bytes 1179656 | tf_op jit(solution)/shard_map/ppermute | solution.py:352
  36.6 3.1 %shard_map.56 = (f32[2,96,96]{2,1,0:T(8,128)S(1)}, f32[2,96,96]{2,1,0:T(8,128)S(1)}) custom-call(f32[2,1024]{1,0:T(2,128)S(1)} %get-tuple-element.16.coef_ref, f32[96,1024]{1,0:T(8,128)S(1)} %get-tuple-element.14.first_ref.refs_5_, f32[96,1024]{1,0:T(8,128)S(1)} %get-tuple-element.15.second_ref.refs_6_), custom_call_target="tpu_custom_call" | custom-call | flops 150994944 | bytes 942080 | tf_op jit(solution)/shard_map/pallas_call | solution.py:45
  39.8 4.0 %collective-permute-done.3.next_ref = f32[96,1024]{1,0:T(8,128)S(1)} collective-permute-done((f32[96,1024]{1,0:T(8,128)S(1)}, f32[96,1024]{1,0:T(8,128)S(1)}, u32[]{:S(2)}, u32[]{:S(2)}) %collective-permute-start.3) | collective-permute-done | bytes 393248 | tf_op jit(solution)/shard_map/ppermute | solution.py:352
  43.8 0.8 shard_map.57
  44.6 1.9 %collective-permute-start.4 = (f32[2,96,96]{2,1,0:T(8,128)S(1)}, f32[2,96,96]{2,1,0:T(8,128)S(1)}, u32[]{:S(2)}, u32[]{:S(2)}) collective-permute-start(f32[2,96,96]{2,1,0:T(8,128)S(1)} %shard_map.57), channel_id=1, source_target_pairs={{0,1},{1,4},{4,5},{5,8},{8,9},{9,12},{12,13},{13,16},{16,17},{17,2... | collective-permute-start | bytes 221192 | tf_op jit(solution)/shard_map/ppermute | solution.py:352
  46.5 1.9 %collective-permute-start.5 = (f32[2,96,96]{2,1,0:T(8,128)S(1)}, f32[2,96,96]{2,1,0:T(8,128)S(1)}, u32[]{:S(2)}, u32[]{:S(2)}) collective-permute-start(f32[2,96,96]{2,1,0:T(8,128)S(1)} %shard_map.57), channel_id=1, source_target_pairs={{0,4},{1,5},{4,8},{5,9},{8,12},{9,13},{12,16},{13,17},{16,20},{17,... | collective-permute-start | bytes 221192 | tf_op jit(solution)/shard_map/ppermute | solution.py:352
  48.5 1.3 %collective-permute-start.6 = (f32[2,96,96]{2,1,0:T(8,128)S(1)}, f32[2,96,96]{2,1,0:T(8,128)S(1)}, u32[]{:S(2)}, u32[]{:S(2)}) collective-permute-start(f32[2,96,96]{2,1,0:T(8,128)S(1)} %shard_map.57), channel_id=1, source_target_pairs={{0,5},{1,8},{4,9},{5,12},{8,13},{9,16},{12,17},{13,20},{16,21},{17... | collective-permute-start | bytes 221192 | tf_op jit(solution)/shard_map/ppermute | solution.py:352
  49.8 1.3 %collective-permute-start.7 = (f32[2,96,96]{2,1,0:T(8,128)S(1)}, f32[2,96,96]{2,1,0:T(8,128)S(1)}, u32[]{:S(2)}, u32[]{:S(2)}) collective-permute-start(f32[2,96,96]{2,1,0:T(8,128)S(1)} %shard_map.57), channel_id=1, source_target_pairs={{0,8},{1,9},{4,12},{5,13},{8,16},{9,17},{12,20},{13,21},{16,24},{1... | collective-permute-start | bytes 221192 | tf_op jit(solution)/shard_map/ppermute | solution.py:352
  51.1 2.1 %collective-permute-done.5.refs_1_ = f32[2,96,96]{2,1,0:T(8,128)S(1)} collective-permute-done((f32[2,96,96]{2,1,0:T(8,128)S(1)}, f32[2,96,96]{2,1,0:T(8,128)S(1)}, u32[]{:S(2)}, u32[]{:S(2)}) %collective-permute-start.5) | collective-permute-done | bytes 73760 | tf_op jit(solution)/shard_map/ppermute | solution.py:352
  53.2 3.1 %collective-permute-done.6.refs_2_ = f32[2,96,96]{2,1,0:T(8,128)S(1)} collective-permute-done((f32[2,96,96]{2,1,0:T(8,128)S(1)}, f32[2,96,96]{2,1,0:T(8,128)S(1)}, u32[]{:S(2)}, u32[]{:S(2)}) %collective-permute-start.6) | collective-permute-done | bytes 73760 | tf_op jit(solution)/shard_map/ppermute | solution.py:352
  56.3 0.7 collective-permute-done.7.refs_3_
  57.0 0.8 shard_map.58.refs_0_
  57.8 1.3 %collective-permute-start.10 = (f32[2,96,96]{2,1,0:T(8,128)S(1)}, f32[2,96,96]{2,1,0:T(8,128)S(1)}, u32[]{:S(2)}, u32[]{:S(2)}) collective-permute-start(f32[2,96,96]{2,1,0:T(8,128)S(1)} %shard_map.58.refs_0_), channel_id=1, source_target_pairs={{0,24},{1,25},{4,28},{5,29},{2,26},{3,27},{6,30},{7,31}} | collective-permute-start | bytes 221192 | tf_op jit(solution)/shard_map/ppermute | solution.py:352
  59.1 1.3 %collective-permute-start.8 = (f32[2,96,96]{2,1,0:T(8,128)S(1)}, f32[2,96,96]{2,1,0:T(8,128)S(1)}, u32[]{:S(2)}, u32[]{:S(2)}) collective-permute-start(f32[2,96,96]{2,1,0:T(8,128)S(1)} %shard_map.58.refs_0_), channel_id=1, source_target_pairs={{0,8},{1,9},{4,12},{5,13},{8,16},{9,17},{12,20},{13,21},{16,24},{1... | collective-permute-start | bytes 221192 | tf_op jit(solution)/shard_map/ppermute | solution.py:352
  60.4 1.3 %collective-permute-start.9 = (f32[2,96,96]{2,1,0:T(8,128)S(1)}, f32[2,96,96]{2,1,0:T(8,128)S(1)}, u32[]{:S(2)}, u32[]{:S(2)}) collective-permute-start(f32[2,96,96]{2,1,0:T(8,128)S(1)} %shard_map.58.refs_0_), channel_id=1, source_target_pairs={{0,16},{1,17},{4,20},{5,21},{8,24},{9,25},{12,28},{13,29},{2,18},{... | collective-permute-start | bytes 221192 | tf_op jit(solution)/shard_map/ppermute | solution.py:352
  61.7 3.3 %collective-permute-done.10.refs_3_ = f32[2,96,96]{2,1,0:T(8,128)S(1)} collective-permute-done((f32[2,96,96]{2,1,0:T(8,128)S(1)}, f32[2,96,96]{2,1,0:T(8,128)S(1)}, u32[]{:S(2)}, u32[]{:S(2)}) %collective-permute-start.10) | collective-permute-done | bytes 73760 | tf_op jit(solution)/shard_map/ppermute | solution.py:352
  65.0 3.5 %collective-permute-done.8.refs_1_ = f32[2,96,96]{2,1,0:T(8,128)S(1)} collective-permute-done((f32[2,96,96]{2,1,0:T(8,128)S(1)}, f32[2,96,96]{2,1,0:T(8,128)S(1)}, u32[]{:S(2)}, u32[]{:S(2)}) %collective-permute-start.8) | collective-permute-done | bytes 73760 | tf_op jit(solution)/shard_map/ppermute | solution.py:352
  68.6 2.8 %collective-permute-done.9.refs_2_ = f32[2,96,96]{2,1,0:T(8,128)S(1)} collective-permute-done((f32[2,96,96]{2,1,0:T(8,128)S(1)}, f32[2,96,96]{2,1,0:T(8,128)S(1)}, u32[]{:S(2)}, u32[]{:S(2)}) %collective-permute-start.9) | collective-permute-done | bytes 73760 | tf_op jit(solution)/shard_map/ppermute | solution.py:352
  71.3 2.5 %shard_map.59 = (f32[2,2,256]{2,1,0:T(2,128)S(1)}, f32[2,2,256]{2,1,0:T(2,128)S(1)}, f32[2,2,256]{2,1,0:T(2,128)S(1)}, f32[2,2,256]{2,1,0:T(2,128)S(1)}) custom-call(f32[2,8,96]{2,1,0:T(8,128)S(1)} %concatenate.6.source_ref, f32[2,96,96]{2,1,0:T(8,128)S(1)} %shard_map.58.refs_0_, f32[2,96,96]{2,1,0:T(8,128)S(1)} %collective-permute-done.8.refs_1_, ...), custom_call_target="tpu_custom_call" | custom-call | bytes 1177600 | tf_op jit(solution)/shard_map/pallas_call | solution.py:45
  73.8 1.9 %collective-permute-start.11 = (f32[2,2,256]{2,1,0:T(2,128)S(1)}, f32[2,2,256]{2,1,0:T(2,128)S(1)}, u32[]{:S(2)}, u32[]{:S(2)}) collective-permute-start(f32[2,2,256]{2,1,0:T(2,128)S(1)} %get-tuple-element.20), channel_id=1, source_target_pairs={{0,1},{1,2},{2,3},{3,0},{4,5},{5,6},{6,7},{7,4},{8,9},{9,10},{10,1... | collective-permute-start | bytes 12296 | tf_op jit(solution)/shard_map/ppermute | solution.py:355
  75.7 1.2 %collective-permute-start.12 = (f32[2,2,256]{2,1,0:T(2,128)S(1)}, f32[2,2,256]{2,1,0:T(2,128)S(1)}, u32[]{:S(2)}, u32[]{:S(2)}) collective-permute-start(f32[2,2,256]{2,1,0:T(2,128)S(1)} %get-tuple-element.21), channel_id=1, source_target_pairs={{0,2},{1,3},{2,0},{3,1},{4,6},{5,7},{6,4},{7,5},{8,10},{9,11},{10,... | collective-permute-start | bytes 12296 | tf_op jit(solution)/shard_map/ppermute | solution.py:355
  77.0 1.3 %collective-permute-done.12.refs_2_ = f32[2,2,256]{2,1,0:T(2,128)S(1)} collective-permute-done((f32[2,2,256]{2,1,0:T(2,128)S(1)}, f32[2,2,256]{2,1,0:T(2,128)S(1)}, u32[]{:S(2)}, u32[]{:S(2)}) %collective-permute-start.12) | collective-permute-done | bytes 4128 | tf_op jit(solution)/shard_map/ppermute | solution.py:355
  78.2 1.7 %collective-permute-done.13.refs_3_ = f32[2,2,256]{2,1,0:T(2,128)S(1)} collective-permute-done((f32[2,2,256]{2,1,0:T(2,128)S(1)}, f32[2,2,256]{2,1,0:T(2,128)S(1)}, u32[]{:S(2)}, u32[]{:S(2)}) %collective-permute-start.13) | collective-permute-done | bytes 4128 | tf_op jit(solution)/shard_map/ppermute | solution.py:355
  80.0 0.6 shard_map.60
  (14 shorter events, 0.2 us)
Async XLA Ops:
  0.0 0.7 copy-start.1
  0.1 0.7 copy-start.3
  0.8 8.6 %copy-start = (f32[2]{0:T(128)S(1)}, f32[2]{0:T(128)}, u32[]{:S(2)}) copy-start(f32[2]{0:T(128)} %scale_ref.1) | copy-start | bytes 28
  1.8 3.0 %collective-permute-start = (f32[104,256]{1,0:T(8,128)S(1)}, f32[104,256]{1,0:T(8,128)S(1)}, u32[]{:S(2)}, u32[]{:S(2)}) collective-permute-start(f32[104,256]{1,0:T(8,128)S(1)} %maximum_maximum_fusion.refs_0_), channel_id=1, source_target_pairs={{0,1},{1,2},{2,3},{3,0},{4,5},{5,6},{6,7},{7,4},{8,9},{9,10},{10,1... | collective-permute-start | bytes 319496 | tf_op jit(solution)/shard_map/ppermute | solution.py:355
  2.6 6.1 %collective-permute-start.1 = (f32[104,256]{1,0:T(8,128)S(1)}, f32[104,256]{1,0:T(8,128)S(1)}, u32[]{:S(2)}, u32[]{:S(2)}) collective-permute-start(f32[104,256]{1,0:T(8,128)S(1)} %maximum_maximum_fusion.refs_0_), channel_id=1, source_target_pairs={{0,2},{1,3},{2,0},{3,1},{4,6},{5,7},{6,4},{7,5},{8,10},{9,11},{10,... | collective-permute-start | bytes 319496 | tf_op jit(solution)/shard_map/ppermute | solution.py:355
  3.8 5.5 %collective-permute-start.2 = (f32[104,256]{1,0:T(8,128)S(1)}, f32[104,256]{1,0:T(8,128)S(1)}, u32[]{:S(2)}, u32[]{:S(2)}) collective-permute-start(f32[104,256]{1,0:T(8,128)S(1)} %maximum_maximum_fusion.refs_0_), channel_id=1, source_target_pairs={{0,3},{1,0},{2,1},{3,2},{4,7},{5,4},{6,5},{7,6},{8,11},{9,8},{10,9... | collective-permute-start | bytes 319496 | tf_op jit(solution)/shard_map/ppermute | solution.py:355
  34.7 9.1 %collective-permute-start.3 = (f32[96,1024]{1,0:T(8,128)S(1)}, f32[96,1024]{1,0:T(8,128)S(1)}, u32[]{:S(2)}, u32[]{:S(2)}) collective-permute-start(f32[96,1024]{1,0:T(8,128)S(1)} %get-tuple-element.14.first_ref.refs_5_), channel_id=1, source_target_pairs={{1,0},{4,1},{5,4},{8,5},{9,8},{12,9},{13,12},{16,13},{17,16},{20,1... | collective-permute-start | bytes 1179656 | tf_op jit(solution)/shard_map/ppermute | solution.py:352
  44.6 17.1 %copy-start.2 = (f32[2,2,96]{2,1,0:T(2,128)S(1)}, f32[2,2,96]{2,1,0:T(2,128)}, u32[]{:S(2)}) copy-start(f32[2,2,96]{2,1,0:T(2,128)} %param.9) | copy-start | bytes 4612
  44.6 6.5 %collective-permute-start.4 = (f32[2,96,96]{2,1,0:T(8,128)S(1)}, f32[2,96,96]{2,1,0:T(8,128)S(1)}, u32[]{:S(2)}, u32[]{:S(2)}) collective-permute-start(f32[2,96,96]{2,1,0:T(8,128)S(1)} %shard_map.57), channel_id=1, source_target_pairs={{0,1},{1,4},{4,5},{5,8},{8,9},{9,12},{12,13},{13,16},{16,17},{17,2... | collective-permute-start | bytes 221192 | tf_op jit(solution)/shard_map/ppermute | solution.py:352
  46.5 6.7 %collective-permute-start.5 = (f32[2,96,96]{2,1,0:T(8,128)S(1)}, f32[2,96,96]{2,1,0:T(8,128)S(1)}, u32[]{:S(2)}, u32[]{:S(2)}) collective-permute-start(f32[2,96,96]{2,1,0:T(8,128)S(1)} %shard_map.57), channel_id=1, source_target_pairs={{0,4},{1,5},{4,8},{5,9},{8,12},{9,13},{12,16},{13,17},{16,20},{17,... | collective-permute-start | bytes 221192 | tf_op jit(solution)/shard_map/ppermute | solution.py:352
  48.5 7.8 %collective-permute-start.6 = (f32[2,96,96]{2,1,0:T(8,128)S(1)}, f32[2,96,96]{2,1,0:T(8,128)S(1)}, u32[]{:S(2)}, u32[]{:S(2)}) collective-permute-start(f32[2,96,96]{2,1,0:T(8,128)S(1)} %shard_map.57), channel_id=1, source_target_pairs={{0,5},{1,8},{4,9},{5,12},{8,13},{9,16},{12,17},{13,20},{16,21},{17... | collective-permute-start | bytes 221192 | tf_op jit(solution)/shard_map/ppermute | solution.py:352
  49.8 7.2 %collective-permute-start.7 = (f32[2,96,96]{2,1,0:T(8,128)S(1)}, f32[2,96,96]{2,1,0:T(8,128)S(1)}, u32[]{:S(2)}, u32[]{:S(2)}) collective-permute-start(f32[2,96,96]{2,1,0:T(8,128)S(1)} %shard_map.57), channel_id=1, source_target_pairs={{0,8},{1,9},{4,12},{5,13},{8,16},{9,17},{12,20},{13,21},{16,24},{1... | collective-permute-start | bytes 221192 | tf_op jit(solution)/shard_map/ppermute | solution.py:352
  57.8 7.3 %collective-permute-start.10 = (f32[2,96,96]{2,1,0:T(8,128)S(1)}, f32[2,96,96]{2,1,0:T(8,128)S(1)}, u32[]{:S(2)}, u32[]{:S(2)}) collective-permute-start(f32[2,96,96]{2,1,0:T(8,128)S(1)} %shard_map.58.refs_0_), channel_id=1, source_target_pairs={{0,24},{1,25},{4,28},{5,29},{2,26},{3,27},{6,30},{7,31}} | collective-permute-start | bytes 221192 | tf_op jit(solution)/shard_map/ppermute | solution.py:352
  59.1 9.5 %collective-permute-start.8 = (f32[2,96,96]{2,1,0:T(8,128)S(1)}, f32[2,96,96]{2,1,0:T(8,128)S(1)}, u32[]{:S(2)}, u32[]{:S(2)}) collective-permute-start(f32[2,96,96]{2,1,0:T(8,128)S(1)} %shard_map.58.refs_0_), channel_id=1, source_target_pairs={{0,8},{1,9},{4,12},{5,13},{8,16},{9,17},{12,20},{13,21},{16,24},{1... | collective-permute-start | bytes 221192 | tf_op jit(solution)/shard_map/ppermute | solution.py:352
  60.4 11.0 %collective-permute-start.9 = (f32[2,96,96]{2,1,0:T(8,128)S(1)}, f32[2,96,96]{2,1,0:T(8,128)S(1)}, u32[]{:S(2)}, u32[]{:S(2)}) collective-permute-start(f32[2,96,96]{2,1,0:T(8,128)S(1)} %shard_map.58.refs_0_), channel_id=1, source_target_pairs={{0,16},{1,17},{4,20},{5,21},{8,24},{9,25},{12,28},{13,29},{2,18},{... | collective-permute-start | bytes 221192 | tf_op jit(solution)/shard_map/ppermute | solution.py:352
  73.8 3.1 %collective-permute-start.11 = (f32[2,2,256]{2,1,0:T(2,128)S(1)}, f32[2,2,256]{2,1,0:T(2,128)S(1)}, u32[]{:S(2)}, u32[]{:S(2)}) collective-permute-start(f32[2,2,256]{2,1,0:T(2,128)S(1)} %get-tuple-element.20), channel_id=1, source_target_pairs={{0,1},{1,2},{2,3},{3,0},{4,5},{5,6},{6,7},{7,4},{8,9},{9,10},{10,1... | collective-permute-start | bytes 12296 | tf_op jit(solution)/shard_map/ppermute | solution.py:355
  75.7 2.5 %collective-permute-start.12 = (f32[2,2,256]{2,1,0:T(2,128)S(1)}, f32[2,2,256]{2,1,0:T(2,128)S(1)}, u32[]{:S(2)}, u32[]{:S(2)}) collective-permute-start(f32[2,2,256]{2,1,0:T(2,128)S(1)} %get-tuple-element.21), channel_id=1, source_target_pairs={{0,2},{1,3},{2,0},{3,1},{4,6},{5,7},{6,4},{7,5},{8,10},{9,11},{10,... | collective-permute-start | bytes 12296 | tf_op jit(solution)/shard_map/ppermute | solution.py:355
  76.9 3.0 %collective-permute-start.13 = (f32[2,2,256]{2,1,0:T(2,128)S(1)}, f32[2,2,256]{2,1,0:T(2,128)S(1)}, u32[]{:S(2)}, u32[]{:S(2)}) collective-permute-start(f32[2,2,256]{2,1,0:T(2,128)S(1)} %get-tuple-element.22), channel_id=1, source_target_pairs={{0,3},{1,0},{2,1},{3,2},{4,7},{5,4},{6,5},{7,6},{8,11},{9,8},{10,9... | collective-permute-start | bytes 12296 | tf_op jit(solution)/shard_map/ppermute | solution.py:355

commit v5 on v4

--- a/solution.py
+++ b/solution.py
@@ -282,16 +282,43 @@
         out_ref[part] = mm(corr, rest_ref[part])
 
 
-def join_body(halves, backs, *refs):
-    at = chain_place(halves)
+def group_body(halves, group, *refs):
+    at = lax.rem(chain_place(halves), group)
+    sorted_ref, out_ref = refs[group:]
+    for k, ref in enumerate(refs[:group]):
+        sorted_ref[lax.rem(at + group - k, group)] = ref[...]
+    spans = [(sorted_ref[j, 0], sorted_ref[j, 1]) for j in reversed(range(group))]
+    out_ref[0], out_ref[1] = fold(spans)
+
+
+def fold(spans):
+    while len(spans) > 1:
+        pairs = [complex_mm(*spans[i : i + 2]) for i in range(0, len(spans) - 1, 2)]
+        spans = pairs + spans[len(pairs) * 2 :]
+    return spans[0]
+
+
+def inside_body(halves, group, sorted_ref, inner_ref, out_ref):
+    at = lax.rem(chain_place(halves), group)
+    unit = unit_of(inner_ref.shape[1])
+    spans = []
+    for j in reversed(range(group - 1)):
+        real = jnp.where(j < at, sorted_ref[j, 0], unit)
+        spans.append((real, jnp.where(j < at, sorted_ref[j, 1], 0.0)))
+    reached = fold(spans)
+    following = complex_mm((inner_ref[0], inner_ref[1]), reached)
+    for part in range(2):
+        out_ref[0, part] = reached[part]
+        out_ref[1, part] = following[part]
+
+
+def join_body(halves, group, backs, *refs):
+    at = chain_place(halves) // group
     spans = []
     for back, ref in zip(backs, refs):
         missing = jnp.where(at < back, unit_of(ref.shape[1]), 0.0)
         spans.append((ref[0] + missing, ref[1]) if back else (ref[0], ref[1]))
-    while len(spans) > 1:
-        pairs = [complex_mm(*spans[i : i + 2]) for i in range(0, len(spans) - 1, 2)]
-        spans = pairs + spans[len(pairs) * 2 :]
-    refs[-1][0], refs[-1][1] = spans[0]
+    refs[-1][0], refs[-1][1] = fold(spans)
 
 
 def turn_vector(matrix, vector):
@@ -302,15 +329,15 @@
     return mmt(vector, matrix[0]) + mmt(swapped, matrix[1])
 
 
-def field_body(halves, backs, n_alt, width, scale, source_ref, *refs):
+def field_body(halves, group, backs, n_alt, width, scale, source_ref, *refs):
     count = len(backs)
-    inner_ref, first_ref, second_ref = refs[count : count + 3]
+    inside_ref, first_ref, second_ref = refs[count : count + 3]
     place = lax.axis_index("alt")
     amp = source_ref[place // halves]
     for back, ref in reversed(list(zip(backs, refs))):
         moved = turn_vector((ref[0], ref[1]), amp)
-        amp = jnp.where(chain_place(halves) < back, amp, moved)
-    amps = (amp, turn_vector((inner_ref[0], inner_ref[1]), amp))
+        amp = jnp.where(chain_place(halves) // group < back, amp, moved)
+    amps = [turn_vector((inside_ref[i, 0], inside_ref[i, 1]), amp) for i in range(2)]
     for k, out_ref in enumerate(refs[count + 3 :]):
         target = lax.rem(place + k, n_alt)
         span = pl.ds(pl.multiple_of(target * width, width), width)
@@ -341,14 +368,14 @@
     length = n_range * halves
     assert modes == 2 * HALF and chunk == 2 and halves * chunk == seg_count and halves * freqs == n_alt
 
+    def device(freq, at):
+        return at // halves * n_alt + freq * halves + at % halves
+
     def along_chain(value, steps):
         pairs = []
         for freq in range(freqs):
             for at in range(max(0, -steps), min(length, length - steps)):
-                ends = []
-                for d in (at, at + steps):
-                    ends.append(d // halves * n_alt + freq * halves + d % halves)
-                pairs.append(tuple(ends))
+                pairs.append((device(freq, at), device(freq, at + steps)))
         return lax.ppermute(value, ("range", "alt"), pairs)
 
     def around(value, k):
@@ -382,31 +409,64 @@
         product_body, shape(2, modes, modes), [following, second, rest], [VM] * 3, flops=flops
     )
 
+    group = 4
+    groups = length // group
+    assert groups * group == length
+
+    def turned(k):
+        pairs = []
+        for freq in range(freqs):
+            for at in range(length):
+                goal = at // group * group + (at + k) % group
+                pairs.append((device(freq, at), device(freq, goal)))
+        return lax.ppermute(product, ("range", "alt"), pairs)
+
+    ordered, span = kernel_call(
+        functools.partial(group_body, halves, group),
+        [shape(group, 2, modes, modes), shape(2, modes, modes)],
+        [product] + [turned(k) for k in range(1, group)],
+        [VM] * group,
+        flops=flops,
+    )
+
     def join(spans, backs):
         return kernel_call(
-            functools.partial(join_body, halves, backs),
+            functools.partial(join_body, halves, group, backs),
             shape(2, modes, modes),
             spans,
             [VM] * len(spans),
             flops=flops,
         )
 
-    reach = min(4, length)
-    backs = range(1, reach + 1)
-    span = join([along_chain(product, back) for back in backs], backs)
-    while length > 4 * reach:
-        backs = range(0, 4 * reach, reach)
-        span = join([span] + [along_chain(span, back) for back in backs[1:]], backs)
-        reach *= 4
+    def from_back(backs):
+        return [along_chain(span, group * back) if back else span for back in backs]
+
+    backs = range(1, groups)
+    if groups > 4:
+        backs = range(1, 5)
+        span = join(from_back(backs), backs)
+        reach = 4
+        while groups > 4 * reach:
+            backs = range(0, 4 * reach, reach)
+            span = join(from_back(backs), backs)
+            reach *= 4
+        backs = range(0, groups, reach)
+    came = from_back(backs)
+    inside = kernel_call(
+        functools.partial(inside_body, halves, group),
+        shape(2, 2, modes, modes),
+        [ordered, inner],
+        [VM] * 2,
+        flops=flops,
+    )
     rows = jnp.concatenate([source, jnp.zeros((freqs, 6, modes), jnp.float32)], axis=1)
-    backs = range(0, length, reach)
     parts = kernel_call(
         functools.partial(
-            field_body, halves, backs, n_alt, width, (float(total) / float(modes)) ** 0.5
+            field_body, halves, group, backs, n_alt, width, (float(total) / float(modes)) ** 0.5
         ),
         [shape(chunk, 2, width)] * n_alt,
-        [rows, span] + [along_chain(span, back) for back in backs[1:]] + [inner, first, second],
-        [VM] * (4 + len(backs)),
+        [rows] + came + [inside, first, second],
+        [VM] * (4 + len(came)),
     )
     parts = [parts[0]] + [around(parts[k], k) for k in range(1, n_alt)]
     return kernel_call(

time: 80.9 us -> 72.9 us (0.901)
  the two profiles are of different devices: /device:TPU:27 before, /device:TPU:0 now
where the time goes in v5:
time: 72.9 us; the launch traced here: 72 us
  Pallas kernels  33.7 us (46%)
  starting transfers between devices  25.2 us (35%)
  waiting for transfers between devices  11.2 us (15%)
  other arithmetic  0.98 us (1%)
  local copies, waits for them, and re-layouts  0.77 us (1%)
    pallas_call x7, Pallas kernels, kernel_call(): pl.pallas_call(body, out_shape=out_shape, in_specs=specs, out_specs=jax.t...  33.7 us
    ppermute x4, starting transfers between devices, along_chain(): return lax.ppermute(value, ('range', 'alt'), pairs)  9.8 us
    ppermute x3, starting transfers between devices, turned(): return lax.ppermute(product, ('range', 'alt'), pairs)  7.93 us
    ppermute x6, starting transfers between devices, around(): lax.ppermute(value, 'alt', [(i, (i + k) % n_alt) for i in range(n_alt)])  7.42 us
    ppermute x6, waiting for transfers between devices, around(): lax.ppermute(value, 'alt', [(i, (i + k) % n_alt) for i in range(n_alt)])  4.93 us
    ppermute x3, waiting for transfers between devices, turned(): return lax.ppermute(product, ('range', 'alt'), pairs)  3.6 us
    ppermute x4, waiting for transfers between devices, along_chain(): return lax.ppermute(value, ('range', 'alt'), pairs)  2.7 us
  transfers between devices with their start and end apart: 13, of which 10 were waited for; matrix products, arithmetic and copies ran while one was open for 0% of the time, Pallas kernels for 6%

profile of v5, /device:TPU:0, one launch (start us, length us, event | category | flops | bytes accessed | tf_op | source)
XLA Modules:
  0.0 72.0 jit_solution(16895787577359211109)
XLA Ops:
  0.0 0.1 pad.4.clone
  0.1 0.6 copy-done.1
  0.7 0.1 copy-done.3
  0.8 1.0 %maximum_maximum_fusion.refs_0_ = f32[104,256]{1,0:T(8,128)S(1)} fusion(f32[4,256]{1,0:T(4,128)S(1)} %copy-done.1, f32[1,256]{1,0:T(1,128)S(1)} %bitcast.1, f32[96,256]{1,0:T(8,128)} %param.8, f32[104]{0:T(128)S(1)} %pad.4.clone), kind=kLoop, calls=%fused_computation | loop fusion | flops 79872 | bytes 210336 | tf_op jit(solution)/shard_map/concatenate | solution.py:386
  1.8 0.5 collective-permute-start
  2.3 2.6 %collective-permute-start.1 = (f32[104,256]{1,0:T(8,128)S(1)}, f32[104,256]{1,0:T(8,128)S(1)}, u32[]{:S(2)}, u32[]{:S(2)}) collective-permute-start(f32[104,256]{1,0:T(8,128)S(1)} %maximum_maximum_fusion.refs_0_), channel_id=1, source_target_pairs={{0,2},{1,3},{2,0},{3,1},{4,6},{5,7},{6,4},{7,5},{8,10},{9,11},{10,... | collective-permute-start | bytes 319496 | tf_op jit(solution)/shard_map/ppermute | solution.py:382
  4.8 1.4 %collective-permute-start.2 = (f32[104,256]{1,0:T(8,128)S(1)}, f32[104,256]{1,0:T(8,128)S(1)}, u32[]{:S(2)}, u32[]{:S(2)}) collective-permute-start(f32[104,256]{1,0:T(8,128)S(1)} %maximum_maximum_fusion.refs_0_), channel_id=1, source_target_pairs={{0,3},{1,0},{2,1},{3,2},{4,7},{5,4},{6,5},{7,6},{8,11},{9,8},{10,9... | collective-permute-start | bytes 319496 | tf_op jit(solution)/shard_map/ppermute | solution.py:382
  6.2 0.6 collective-permute-done.refs_1_
  6.8 1.3 %collective-permute-done.1.refs_2_ = f32[104,256]{1,0:T(8,128)S(1)} collective-permute-done((f32[104,256]{1,0:T(8,128)S(1)}, f32[104,256]{1,0:T(8,128)S(1)}, u32[]{:S(2)}, u32[]{:S(2)}) %collective-permute-start.1) | collective-permute-done | bytes 106528 | tf_op jit(solution)/shard_map/ppermute | solution.py:382
  8.1 1.7 %collective-permute-done.2.refs_3_ = f32[104,256]{1,0:T(8,128)S(1)} collective-permute-done((f32[104,256]{1,0:T(8,128)S(1)}, f32[104,256]{1,0:T(8,128)S(1)}, u32[]{:S(2)}, u32[]{:S(2)}) %collective-permute-start.2) | collective-permute-done | bytes 106528 | tf_op jit(solution)/shard_map/ppermute | solution.py:382
  9.8 25.3 %shard_map.55 = (f32[96,1024]{1,0:T(8,128)S(1)}, f32[96,1024]{1,0:T(8,128)S(1)}, f32[2,1024]{1,0:T(2,128)S(1)}) custom-call(f32[2]{0:T(128)S(1)} %copy-done, f32[104,256]{1,0:T(8,128)S(1)} %maximum_maximum_fusion.refs_0_, f32[104,256]{1,0:T(8,128)S(1)} %collective-permute-done.refs_1_, f32[104,256]{1,0:T(8,128)S(1)} %collective-permute-done.1.refs_2_, ...), custom_call_target="tpu_custom_call" | custom-call | flops 603979776 | bytes 1220616 | tf_op jit(solution)/shard_map/pallas_call | solution.py:45
  35.2 1.3 %collective-permute-start.3 = (f32[96,1024]{1,0:T(8,128)S(1)}, f32[96,1024]{1,0:T(8,128)S(1)}, u32[]{:S(2)}, u32[]{:S(2)}) collective-permute-start(f32[96,1024]{1,0:T(8,128)S(1)} %get-tuple-element.16.first_ref.refs_4_), channel_id=1, source_target_pairs={{1,0},{4,1},{5,4},{8,5},{9,8},{12,9},{13,12},{16,13},{17,16},{20,1... | collective-permute-start | bytes 1179656 | tf_op jit(solution)/shard_map/ppermute | solution.py:379
  36.5 3.1 %shard_map.56 = (f32[2,96,96]{2,1,0:T(8,128)S(1)}, f32[2,96,96]{2,1,0:T(8,128)S(1)}) custom-call(f32[2,1024]{1,0:T(2,128)S(1)} %get-tuple-element.18.coef_ref, f32[96,1024]{1,0:T(8,128)S(1)} %get-tuple-element.16.first_ref.refs_4_, f32[96,1024]{1,0:T(8,128)S(1)} %get-tuple-element.17.second_ref.refs_5_), custom_call_target="tpu_custom_call" | custom-call | flops 150994944 | bytes 942080 | tf_op jit(solution)/shard_map/pallas_call | solution.py:45
  39.6 0.8 %shard_map.57.refs_0_ = f32[2,96,96]{2,1,0:T(8,128)S(1)} custom-call(f32[96,1024]{1,0:T(8,128)S(1)} %collective-permute-done.3.next_ref, f32[96,1024]{1,0:T(8,128)S(1)} %get-tuple-element.17.second_ref.refs_5_, f32[2,96,96]{2,1,0:T(8,128)S(1)} %get-tuple-element.19.rest_ref), custom_call_target="tpu_custom_call" | custom-call | flops 18874368 | bytes 933888 | tf_op jit(solution)/shard_map/pallas_call | solution.py:45
  40.4 4.7 %collective-permute-start.4 = (f32[2,96,96]{2,1,0:T(8,128)S(1)}, f32[2,96,96]{2,1,0:T(8,128)S(1)}, u32[]{:S(2)}, u32[]{:S(2)}) collective-permute-start(f32[2,96,96]{2,1,0:T(8,128)S(1)} %shard_map.57.refs_0_), channel_id=1, source_target_pairs={{0,1},{1,4},{4,5},{5,0},{8,9},{9,12},{12,13},{13,8},{16,17},{17,20... | collective-permute-start | bytes 221192 | tf_op jit(solution)/shard_map/ppermute | solution.py:422
  45.1 3.2 %collective-permute-start.5 = (f32[2,96,96]{2,1,0:T(8,128)S(1)}, f32[2,96,96]{2,1,0:T(8,128)S(1)}, u32[]{:S(2)}, u32[]{:S(2)}) collective-permute-start(f32[2,96,96]{2,1,0:T(8,128)S(1)} %shard_map.57.refs_0_), channel_id=1, source_target_pairs={{0,4},{1,5},{4,0},{5,1},{8,12},{9,13},{12,8},{13,9},{16,20},{17,21... | collective-permute-start | bytes 221192 | tf_op jit(solution)/shard_map/ppermute | solution.py:422
  48.3 2.3 %collective-permute-done.4.refs_1_ = f32[2,96,96]{2,1,0:T(8,128)S(1)} collective-permute-done((f32[2,96,96]{2,1,0:T(8,128)S(1)}, f32[2,96,96]{2,1,0:T(8,128)S(1)}, u32[]{:S(2)}, u32[]{:S(2)}) %collective-permute-start.4) | collective-permute-done | bytes 73760 | tf_op jit(solution)/shard_map/ppermute | solution.py:422
  50.7 1.3 %collective-permute-done.5.refs_2_ = f32[2,96,96]{2,1,0:T(8,128)S(1)} collective-permute-done((f32[2,96,96]{2,1,0:T(8,128)S(1)}, f32[2,96,96]{2,1,0:T(8,128)S(1)}, u32[]{:S(2)}, u32[]{:S(2)}) %collective-permute-start.5) | collective-permute-done | bytes 73760 | tf_op jit(solution)/shard_map/ppermute | solution.py:422
  51.9 0.8 %shard_map.58 = (f32[4,2,96,96]{3,2,1,0:T(8,128)S(1)}, f32[2,96,96]{2,1,0:T(8,128)S(1)}) custom-call(f32[2,96,96]{2,1,0:T(8,128)S(1)} %shard_map.57.refs_0_, f32[2,96,96]{2,1,0:T(8,128)S(1)} %collective-permute-done.4.refs_1_, f32[2,96,96]{2,1,0:T(8,128)S(1)} %collective-permute-done.5.refs_2_, f32[2,96,96]{2,1,0:T(8,128)S(1)} %collective-permute-done.6.refs_3_), custom_call_target="tpu_custom_call" | custom-call | flops 18874368 | bytes 663552 | tf_op jit(solution)/shard_map/pallas_call | solution.py:45
  52.8 3.5 %collective-permute-start.7 = (f32[2,96,96]{2,1,0:T(8,128)S(1)}, f32[2,96,96]{2,1,0:T(8,128)S(1)}, u32[]{:S(2)}, u32[]{:S(2)}) collective-permute-start(f32[2,96,96]{2,1,0:T(8,128)S(1)} %get-tuple-element.20), channel_id=1, source_target_pairs={{0,8},{1,9},{4,12},{5,13},{8,16},{9,17},{12,20},{13,21},{16,24},{1... | collective-permute-start | bytes 221192 | tf_op jit(solution)/shard_map/ppermute | solution.py:379
  56.2 3.7 %collective-permute-start.8 = (f32[2,96,96]{2,1,0:T(8,128)S(1)}, f32[2,96,96]{2,1,0:T(8,128)S(1)}, u32[]{:S(2)}, u32[]{:S(2)}) collective-permute-start(f32[2,96,96]{2,1,0:T(8,128)S(1)} %get-tuple-element.20), channel_id=1, source_target_pairs={{0,16},{1,17},{4,20},{5,21},{8,24},{9,25},{12,28},{13,29},{2,18},{... | collective-permute-start | bytes 221192 | tf_op jit(solution)/shard_map/ppermute | solution.py:379
  60.0 1.3 %collective-permute-start.9 = (f32[2,96,96]{2,1,0:T(8,128)S(1)}, f32[2,96,96]{2,1,0:T(8,128)S(1)}, u32[]{:S(2)}, u32[]{:S(2)}) collective-permute-start(f32[2,96,96]{2,1,0:T(8,128)S(1)} %get-tuple-element.20), channel_id=1, source_target_pairs={{0,24},{1,25},{4,28},{5,29},{2,26},{3,27},{6,30},{7,31}} | collective-permute-start | bytes 221192 | tf_op jit(solution)/shard_map/ppermute | solution.py:379
  61.3 0.9 %shard_map.59.refs_3_ = f32[2,2,96,96]{3,2,1,0:T(8,128)S(1)} custom-call(f32[4,2,96,96]{3,2,1,0:T(8,128)S(1)} %get-tuple-element.21.sorted_ref, f32[2,96,96]{2,1,0:T(8,128)S(1)} %get-tuple-element.22.inner_ref), custom_call_target="tpu_custom_call" | custom-call | flops 18874368 | bytes 516096 | tf_op jit(solution)/shard_map/pallas_call | solution.py:45
  62.2 0.9 %collective-permute-done.8.refs_1_ = f32[2,96,96]{2,1,0:T(8,128)S(1)} collective-permute-done((f32[2,96,96]{2,1,0:T(8,128)S(1)}, f32[2,96,96]{2,1,0:T(8,128)S(1)}, u32[]{:S(2)}, u32[]{:S(2)}) %collective-permute-start.8) | collective-permute-done | bytes 73760 | tf_op jit(solution)/shard_map/ppermute | solution.py:379
  63.1 1.8 %collective-permute-done.9.refs_2_ = f32[2,96,96]{2,1,0:T(8,128)S(1)} collective-permute-done((f32[2,96,96]{2,1,0:T(8,128)S(1)}, f32[2,96,96]{2,1,0:T(8,128)S(1)}, u32[]{:S(2)}, u32[]{:S(2)}) %collective-permute-start.9) | collective-permute-done | bytes 73760 | tf_op jit(solution)/shard_map/ppermute | solution.py:379
  64.9 2.2 %shard_map.60 = (f32[2,2,256]{2,1,0:T(2,128)S(1)}, f32[2,2,256]{2,1,0:T(2,128)S(1)}, f32[2,2,256]{2,1,0:T(2,128)S(1)}, f32[2,2,256]{2,1,0:T(2,128)S(1)}) custom-call(f32[2,8,96]{2,1,0:T(8,128)S(1)} %concatenate.6.source_ref, f32[2,96,96]{2,1,0:T(8,128)S(1)} %collective-permute-done.7.refs_0_, f32[2,96,96]{2,1,0:T(8,128)S(1)} %collective-permute-done.8.refs_1_, ...), custom_call_target="tpu_custom_call" | custom-call | bytes 1177600 | tf_op jit(solution)/shard_map/pallas_call | solution.py:45
  67.1 1.5 %collective-permute-start.11 = (f32[2,2,256]{2,1,0:T(2,128)S(1)}, f32[2,2,256]{2,1,0:T(2,128)S(1)}, u32[]{:S(2)}, u32[]{:S(2)}) collective-permute-start(f32[2,2,256]{2,1,0:T(2,128)S(1)} %get-tuple-element.25), channel_id=1, source_target_pairs={{0,2},{1,3},{2,0},{3,1},{4,6},{5,7},{6,4},{7,5},{8,10},{9,11},{10,... | collective-permute-start | bytes 12296 | tf_op jit(solution)/shard_map/ppermute | solution.py:382
  68.6 1.4 %collective-permute-start.12 = (f32[2,2,256]{2,1,0:T(2,128)S(1)}, f32[2,2,256]{2,1,0:T(2,128)S(1)}, u32[]{:S(2)}, u32[]{:S(2)}) collective-permute-start(f32[2,2,256]{2,1,0:T(2,128)S(1)} %get-tuple-element.26), channel_id=1, source_target_pairs={{0,3},{1,0},{2,1},{3,2},{4,7},{5,4},{6,5},{7,6},{8,11},{9,8},{10,9... | collective-permute-start | bytes 12296 | tf_op jit(solution)/shard_map/ppermute | solution.py:382
  70.1 0.1 collective-permute-done.10.refs_1_
  70.1 0.6 collective-permute-done.11.refs_2_
  70.8 0.6 collective-permute-done.12.refs_3_
  71.4 0.6 shard_map.61
  (13 shorter events, 0.0 us)
Async XLA Ops:
  0.0 0.7 copy-start.1
  0.1 0.7 copy-start.3
  0.8 9.1 %copy-start = (f32[2]{0:T(128)S(1)}, f32[2]{0:T(128)}, u32[]{:S(2)}) copy-start(f32[2]{0:T(128)} %scale_ref.1) | copy-start | bytes 28
  1.8 5.0 %collective-permute-start = (f32[104,256]{1,0:T(8,128)S(1)}, f32[104,256]{1,0:T(8,128)S(1)}, u32[]{:S(2)}, u32[]{:S(2)}) collective-permute-start(f32[104,256]{1,0:T(8,128)S(1)} %maximum_maximum_fusion.refs_0_), channel_id=1, source_target_pairs={{0,1},{1,2},{2,3},{3,0},{4,5},{5,6},{6,7},{7,4},{8,9},{9,10},{10,1... | collective-permute-start | bytes 319496 | tf_op jit(solution)/shard_map/ppermute | solution.py:382
  2.3 5.9 %collective-permute-start.1 = (f32[104,256]{1,0:T(8,128)S(1)}, f32[104,256]{1,0:T(8,128)S(1)}, u32[]{:S(2)}, u32[]{:S(2)}) collective-permute-start(f32[104,256]{1,0:T(8,128)S(1)} %maximum_maximum_fusion.refs_0_), channel_id=1, source_target_pairs={{0,2},{1,3},{2,0},{3,1},{4,6},{5,7},{6,4},{7,5},{8,10},{9,11},{10,... | collective-permute-start | bytes 319496 | tf_op jit(solution)/shard_map/ppermute | solution.py:382
  4.8 5.0 %collective-permute-start.2 = (f32[104,256]{1,0:T(8,128)S(1)}, f32[104,256]{1,0:T(8,128)S(1)}, u32[]{:S(2)}, u32[]{:S(2)}) collective-permute-start(f32[104,256]{1,0:T(8,128)S(1)} %maximum_maximum_fusion.refs_0_), channel_id=1, source_target_pairs={{0,3},{1,0},{2,1},{3,2},{4,7},{5,4},{6,5},{7,6},{8,11},{9,8},{10,9... | collective-permute-start | bytes 319496 | tf_op jit(solution)/shard_map/ppermute | solution.py:382
  35.2 4.4 %collective-permute-start.3 = (f32[96,1024]{1,0:T(8,128)S(1)}, f32[96,1024]{1,0:T(8,128)S(1)}, u32[]{:S(2)}, u32[]{:S(2)}) collective-permute-start(f32[96,1024]{1,0:T(8,128)S(1)} %get-tuple-element.16.first_ref.refs_4_), channel_id=1, source_target_pairs={{1,0},{4,1},{5,4},{8,5},{9,8},{12,9},{13,12},{16,13},{17,16},{20,1... | collective-permute-start | bytes 1179656 | tf_op jit(solution)/shard_map/ppermute | solution.py:379
  40.4 10.2 %collective-permute-start.4 = (f32[2,96,96]{2,1,0:T(8,128)S(1)}, f32[2,96,96]{2,1,0:T(8,128)S(1)}, u32[]{:S(2)}, u32[]{:S(2)}) collective-permute-start(f32[2,96,96]{2,1,0:T(8,128)S(1)} %shard_map.57.refs_0_), channel_id=1, source_target_pairs={{0,1},{1,4},{4,5},{5,0},{8,9},{9,12},{12,13},{13,8},{16,17},{17,20... | collective-permute-start | bytes 221192 | tf_op jit(solution)/shard_map/ppermute | solution.py:422
  45.1 6.8 %collective-permute-start.5 = (f32[2,96,96]{2,1,0:T(8,128)S(1)}, f32[2,96,96]{2,1,0:T(8,128)S(1)}, u32[]{:S(2)}, u32[]{:S(2)}) collective-permute-start(f32[2,96,96]{2,1,0:T(8,128)S(1)} %shard_map.57.refs_0_), channel_id=1, source_target_pairs={{0,4},{1,5},{4,0},{5,1},{8,12},{9,13},{12,8},{13,9},{16,20},{17,21... | collective-permute-start | bytes 221192 | tf_op jit(solution)/shard_map/ppermute | solution.py:422
  48.3 3.6 %collective-permute-start.6 = (f32[2,96,96]{2,1,0:T(8,128)S(1)}, f32[2,96,96]{2,1,0:T(8,128)S(1)}, u32[]{:S(2)}, u32[]{:S(2)}) collective-permute-start(f32[2,96,96]{2,1,0:T(8,128)S(1)} %shard_map.57.refs_0_), channel_id=1, source_target_pairs={{0,5},{1,0},{4,1},{5,4},{8,13},{9,8},{12,9},{13,12},{16,21},{17,16... | collective-permute-start | bytes 221192 | tf_op jit(solution)/shard_map/ppermute | solution.py:422
  51.9 9.3 %copy-start.2 = (f32[2,2,96]{2,1,0:T(2,128)S(1)}, f32[2,2,96]{2,1,0:T(2,128)}, u32[]{:S(2)}) copy-start(f32[2,2,96]{2,1,0:T(2,128)} %param.9) | copy-start | bytes 4612
  52.8 9.5 %collective-permute-start.7 = (f32[2,96,96]{2,1,0:T(8,128)S(1)}, f32[2,96,96]{2,1,0:T(8,128)S(1)}, u32[]{:S(2)}, u32[]{:S(2)}) collective-permute-start(f32[2,96,96]{2,1,0:T(8,128)S(1)} %get-tuple-element.20), channel_id=1, source_target_pairs={{0,8},{1,9},{4,12},{5,13},{8,16},{9,17},{12,20},{13,21},{16,24},{1... | collective-permute-start | bytes 221192 | tf_op jit(solution)/shard_map/ppermute | solution.py:379
  56.2 6.9 %collective-permute-start.8 = (f32[2,96,96]{2,1,0:T(8,128)S(1)}, f32[2,96,96]{2,1,0:T(8,128)S(1)}, u32[]{:S(2)}, u32[]{:S(2)}) collective-permute-start(f32[2,96,96]{2,1,0:T(8,128)S(1)} %get-tuple-element.20), channel_id=1, source_target_pairs={{0,16},{1,17},{4,20},{5,21},{8,24},{9,25},{12,28},{13,29},{2,18},{... | collective-permute-start | bytes 221192 | tf_op jit(solution)/shard_map/ppermute | solution.py:379
  60.0 4.9 %collective-permute-start.9 = (f32[2,96,96]{2,1,0:T(8,128)S(1)}, f32[2,96,96]{2,1,0:T(8,128)S(1)}, u32[]{:S(2)}, u32[]{:S(2)}) collective-permute-start(f32[2,96,96]{2,1,0:T(8,128)S(1)} %get-tuple-element.20), channel_id=1, source_target_pairs={{0,24},{1,25},{4,28},{5,29},{2,26},{3,27},{6,30},{7,31}} | collective-permute-start | bytes 221192 | tf_op jit(solution)/shard_map/ppermute | solution.py:379
  67.1 3.0 %collective-permute-start.10 = (f32[2,2,256]{2,1,0:T(2,128)S(1)}, f32[2,2,256]{2,1,0:T(2,128)S(1)}, u32[]{:S(2)}, u32[]{:S(2)}) collective-permute-start(f32[2,2,256]{2,1,0:T(2,128)S(1)} %get-tuple-element.24), channel_id=1, source_target_pairs={{0,1},{1,2},{2,3},{3,0},{4,5},{5,6},{6,7},{7,4},{8,9},{9,10},{10,1... | collective-permute-start | bytes 12296 | tf_op jit(solution)/shard_map/ppermute | solution.py:382
  67.1 3.7 %collective-permute-start.11 = (f32[2,2,256]{2,1,0:T(2,128)S(1)}, f32[2,2,256]{2,1,0:T(2,128)S(1)}, u32[]{:S(2)}, u32[]{:S(2)}) collective-permute-start(f32[2,2,256]{2,1,0:T(2,128)S(1)} %get-tuple-element.25), channel_id=1, source_target_pairs={{0,2},{1,3},{2,0},{3,1},{4,6},{5,7},{6,4},{7,5},{8,10},{9,11},{10,... | collective-permute-start | bytes 12296 | tf_op jit(solution)/shard_map/ppermute | solution.py:382
  68.6 2.8 %collective-permute-start.12 = (f32[2,2,256]{2,1,0:T(2,128)S(1)}, f32[2,2,256]{2,1,0:T(2,128)S(1)}, u32[]{:S(2)}, u32[]{:S(2)}) collective-permute-start(f32[2,2,256]{2,1,0:T(2,128)S(1)} %get-tuple-element.26), channel_id=1, source_target_pairs={{0,3},{1,0},{2,1},{3,2},{4,7},{5,4},{6,5},{7,6},{8,11},{9,8},{10,9... | collective-permute-start | bytes 12296 | tf_op jit(solution)/shard_map/ppermute | solution.py:382

commit v6 on v5

--- a/solution.py
+++ b/solution.py
@@ -81,13 +81,13 @@
     )
 
 
-def inverse_factors(one, two):
-    count = len(one)
+def inverse_factors(work):
+    work = [list(pair) for pair in work]
+    count = len(work)
     lanes = lax.broadcasted_iota(jnp.int32, (8, 128), 1)
     subs = lax.broadcasted_iota(jnp.int32, (8, 128), 0)
     base = jnp.where(lanes < 64, 0, 64)
     column = lanes - base
-    work = [pack_pair(a, b) for a, b in zip(one, two)]
     results = []
 
     def place(k):
@@ -155,27 +155,29 @@
         unit = jnp.where(column == subs + first, 1.0, 0.0)
         own = jnp.where(column < subs + first, work[k][side], unit) * root
         other = work[k][0] * root if side else jnp.zeros((8, 128), jnp.float32)
-        results.append(unpack_pair(other, own) if side else unpack_pair(own, other))
-    return [pair[0] for pair in results], [pair[1] for pair in results]
-
-
-def edge_weights(width):
-    lanes = lax.broadcasted_iota(jnp.int32, (1, width), 1)
-    return jnp.where(lanes == 0, 0.0, 0.5), jnp.where(lanes == width - 1, 0.0, 0.5)
-
-
-def apply_rows(value, coef, from_low, from_high):
+        results.append((other, own) if side else (own, other))
+    return results
+
+
+def doubled_operator(value, coef):
     width = value.shape[1]
-    return (
-        coef * value
-        + from_low * pltpu.roll(value, 1, 1)
-        + from_high * pltpu.roll(value, width - 1, 1)
-    )
+    lanes = lax.broadcasted_iota(jnp.int32, (value.shape[0], 128), 1)
+    below, above = pltpu.roll(value, 1, 1), pltpu.roll(value, width - 1, 1)
+    below = jnp.concatenate(
+        [jnp.where(lanes == 0, 0.0, below[:, :128]), below[:, 128:]], axis=1
+    )
+    above = jnp.concatenate(
+        [above[:, :-128], jnp.where(lanes == 127, 0.0, above[:, -128:])], axis=1
+    )
+    return coef * value + (below + above)
+
+
+DOWN = 2.0**-13
 
 
 def iterate_body(n_alt, chunk, seg_count, modes, width, scale_ref, *refs):
-    blocks, out_refs = refs[:n_alt], refs[n_alt : n_alt + chunk]
-    coef_ref, split_ref, image_ref, gram_ref, inv_ref = refs[n_alt + chunk :]
+    blocks, image_refs = refs[:n_alt], refs[n_alt : n_alt + chunk]
+    coef_ref, basis_ref, split_ref, gram_ref, inv_ref = refs[n_alt + chunk :]
     place = lax.axis_index("alt")
     flat = place * chunk
     freq = flat // seg_count
@@ -186,56 +188,63 @@
         span = pl.ds(pl.multiple_of(source * width, width), width)
         start = block[0:modes, :] * (1.0 / float(total) ** 0.5)
         for i in range(chunk):
-            out_refs[i][:, span] = start
+            basis_ref[i, :, span] = start
             change = block[pl.ds(modes + 1 + first + i, 1), :]
-            coef_ref[i : i + 1, span] = scale_ref[freq] * (
+            coef_ref[i : i + 1, span] = (2.0 * scale_ref[freq]) * (
                 block[modes : modes + 1, :] * (1.0 + relief * change)
             )
-    from_low, from_high = edge_weights(total)
-    down = 2.0**-11
-    gram_ref[...] = jnp.zeros_like(gram_ref)
-
-    def factorise():
-        grams = [[gram_ref[i, at : at + 8, :] for at in range(0, modes, 8)] for i in range(chunk)]
-        results = inverse_factors(*grams)
-        for i in range(chunk):
-            for at in range(0, modes, 8):
-                inv_ref[i, at : at + 8, :] = results[i][at // 8] * down**0.5
+    split_ref[...] = jnp.zeros_like(split_ref)
+    left = lax.broadcasted_iota(jnp.int32, (8, 128), 1) < 64
+
+    def packed_row(i, at):
+        return at // HALF * 128 + i * 64 + at % HALF
 
     def step(_, carry):
         for i in range(chunk):
             coef = coef_ref[i : i + 1, :]
             for at in range(0, modes, 16):
-                image = apply_rows(out_refs[i][at : at + 16, :], coef, from_low, from_high)
+                image = doubled_operator(basis_ref[i, at : at + 16, :], coef)
+                row = packed_row(i, at)
                 for part in range(3):
                     piece = image.astype(jnp.bfloat16)
-                    split_ref[i, part, at : at + 16, :] = piece
+                    split_ref[part, row : row + 16, :] = piece
                     image = image - piece.astype(jnp.float32)
-            high, low = split_ref[i, 0], split_ref[i, 1]
-            gram = short_mmt(high, high) + short_mmt(high, low) + short_mmt(low, high)
-            gram_ref[i, :, 0:modes] = gram * down
-        factorise()
+        gram_ref[...] = short_mmt(split_ref[0], split_ref[0]) * DOWN
+        work = []
+        for at in range(0, modes, 8):
+            one, two = packed_row(0, at), packed_row(1, at)
+            work.append(
+                [
+                    jnp.where(
+                        left,
+                        gram_ref[one : one + 8, side : side + 128],
+                        gram_ref[two : two + 8, side : side + 128],
+                    )
+                    for side in (0, 128)
+                ]
+            )
+        rows = inverse_factors(work)
+        for at in range(0, modes, 16):
+            for half in range(2):
+                part = jnp.concatenate([rows[at // 8][half], rows[at // 8 + 1][half]], axis=0)
+                part = part * DOWN**0.5
+                here = lax.broadcasted_iota(jnp.int32, part.shape, 1) < 64
+                span = slice(half * 128, half * 128 + 128)
+                inv_ref[0, at : at + 16, span] = jnp.where(here, part, 0.0).astype(jnp.bfloat16)
+                inv_ref[1, at : at + 16, span] = jnp.where(here, 0.0, part).astype(jnp.bfloat16)
         for i in range(chunk):
-            inv = inv_ref[i, :, 0:modes].astype(jnp.bfloat16)
             for at in range(0, total, 256):
-                out_refs[i][:, at : at + 256] = sum(
-                    short_mm(inv, split_ref[i, part, :, at : at + 256]) for part in range(3)
+                basis_ref[i, :, at : at + 256] = sum(
+                    short_mm(inv_ref[i], split_ref[part, :, at : at + 256]) for part in range(3)
                 )
         return carry
 
     lax.fori_loop(0, ITERS - 1, step, 0)
     for i in range(chunk):
         for at in range(0, modes, 8):
-            image_ref[i, at : at + 8, :] = apply_rows(
-                out_refs[i][at : at + 8, :], coef_ref[i : i + 1, :], from_low, from_high
+            image_refs[i][at : at + 8, :] = doubled_operator(
+                basis_ref[i, at : at + 8, :], coef_ref[i : i + 1, :]
             )
-        image = image_ref[i]
-        gram_ref[i, :, 0:modes] = mmt(image, image) * down
-    factorise()
-    for i in range(chunk):
-        inv = inv_ref[i, :, 0:modes]
-        for at in range(0, total, 256):
-            out_refs[i][:, at : at + 256] = mm(inv, image_ref[i, :, at : at + 256])
 
 
 def unit_of(modes):
@@ -250,23 +259,39 @@
     )
 
 
-def advance_body(modes, total, coef_ref, first_ref, second_ref, inner_ref, rest_ref, image_ref):
-    from_low, from_high = edge_weights(total)
+def finish_body(halves, modes, total, coef_ref, *refs):
+    image_refs, basis_refs = refs[0:2], refs[2:4]
+    turn_ref, inner_ref, rest_ref, gram_ref, double_ref = refs[4:]
     unit = unit_of(modes)
+    gram_ref[...] = jnp.zeros_like(gram_ref)
+    for i in range(2):
+        image = image_refs[i][...]
+        gram_ref[i, :, 0:modes] = mmt(image, image) * DOWN
+    grams = [gram_ref[i, at : at + 8, :] for at in range(0, modes, 8) for i in range(2)]
+    rows = inverse_factors([pack_pair(*grams[i : i + 2]) for i in range(0, len(grams), 2)])
+    for k, pair in enumerate(rows):
+        for i, part in enumerate(unpack_pair(*pair)):
+            gram_ref[i, 8 * k : 8 * k + 8, :] = part * DOWN**0.5
     turns = []
-    for i, ref in enumerate((first_ref, second_ref)):
+    for i in range(2):
+        inv = gram_ref[i, :, 0:modes]
+        for at in range(0, total, 256):
+            basis_refs[i][:, at : at + 256] = mm(inv, image_refs[i][:, at : at + 256])
+    for i, ref in enumerate(basis_refs):
         for at in range(0, modes, 8):
-            image_ref[at : at + 8, :] = apply_rows(
-                ref[at : at + 8, :], coef_ref[i : i + 1, :], from_low, from_high
+            double_ref[at : at + 8, :] = doubled_operator(
+                ref[at : at + 8, :], coef_ref[i : i + 1, :]
             )
-        phase = phase_step * mmt(ref[...], image_ref[...])
+        phase = (0.5 * phase_step) * mmt(ref[...], double_ref[...])
         square = mm(phase, phase)
         turns.append(
             (unit - 0.5 * square + mm(square, square) / 24.0, phase - mm(phase, square) / 6.0)
         )
-    corr = mmt(second_ref[...], first_ref[...])
+    corr = mmt(basis_refs[1][...], basis_refs[0][...])
     inner = (mm(corr, turns[0][0]), mm(corr, turns[0][1]))
-    rest = complex_mm(turns[1], inner)
+    turn = jnp.where(chain_place(halves) == 0, unit, gram_ref[0, :, 0:modes])
+    turn_ref[...] = turn
+    rest = complex_mm(turns[1], (mm(inner[0], turn), mm(inner[1], turn)))
     for part in range(2):
         inner_ref[part] = inner[part]
         rest_ref[part] = rest[part]
@@ -298,7 +323,7 @@
     return spans[0]
 
 
-def inside_body(halves, group, sorted_ref, inner_ref, out_ref):
+def inside_body(halves, group, sorted_ref, turn_ref, inner_ref, out_ref):
     at = lax.rem(chain_place(halves), group)
     unit = unit_of(inner_ref.shape[1])
     spans = []
@@ -306,6 +331,7 @@
         real = jnp.where(j < at, sorted_ref[j, 0], unit)
         spans.append((real, jnp.where(j < at, sorted_ref[j, 1], 0.0)))
     reached = fold(spans)
+    reached = (mm(turn_ref[...], reached[0]), mm(turn_ref[...], reached[1]))
     following = complex_mm((inner_ref[0], inner_ref[1]), reached)
     for part in range(2):
         out_ref[0, part] = reached[part]
@@ -386,24 +412,27 @@
     mine = jnp.concatenate(lines + [filler], axis=0)
     blocks = [mine] + [around(mine, k) for k in range(1, n_alt)]
     flops = 2 * modes * modes * total
-    first, second, coef = kernel_call(
+    image, other, coef = kernel_call(
         functools.partial(iterate_body, n_alt, chunk, seg_count, modes, width),
         [shape(modes, total)] * chunk + [shape(chunk, total)],
         [freq_scale] + blocks,
         [SM] + [VM] * n_alt,
-        [pltpu.VMEM((chunk, 3, modes, total), jnp.bfloat16)]
-        + [pltpu.VMEM((chunk, modes, total), jnp.float32)]
-        + [pltpu.VMEM((chunk, modes, 128), jnp.float32)] * 2,
+        [
+            pltpu.VMEM((chunk, modes, total), jnp.float32),
+            pltpu.VMEM((3, 256, total), jnp.bfloat16),
+            pltpu.VMEM((256, 256), jnp.float32),
+            pltpu.VMEM((chunk, modes, 256), jnp.bfloat16),
+        ],
         flops=2 * ITERS * chunk * flops,
     )
-    following = along_chain(first, -1)
-    inner, rest = kernel_call(
-        functools.partial(advance_body, modes, total),
-        [shape(2, modes, modes)] * 2,
-        [coef, first, second],
+    following = along_chain(image, -1)
+    first, second, turn, inner, rest = kernel_call(
+        functools.partial(finish_body, halves, modes, total),
+        [shape(modes, total)] * 2 + [shape(modes, modes)] + [shape(2, modes, modes)] * 2,
+        [coef, image, other],
         [VM] * 3,
-        [pltpu.VMEM((modes, total), jnp.float32)],
-        flops=8 * flops,
+        [pltpu.VMEM((2, modes, 128), jnp.float32), pltpu.VMEM((modes, total), jnp.float32)],
+        flops=16 * flops,
     )
     product = kernel_call(
         product_body, shape(2, modes, modes), [following, second, rest], [VM] * 3, flops=flops
@@ -413,18 +442,18 @@
     groups = length // group
     assert groups * group == length
 
-    def turned(k):
+    def turned(value, size, k):
         pairs = []
         for freq in range(freqs):
             for at in range(length):
-                goal = at // group * group + (at + k) % group
+                goal = at // size * size + (at + k) % size
                 pairs.append((device(freq, at), device(freq, goal)))
-        return lax.ppermute(product, ("range", "alt"), pairs)
+        return lax.ppermute(value, ("range", "alt"), pairs)
 
     ordered, span = kernel_call(
         functools.partial(group_body, halves, group),
         [shape(group, 2, modes, modes), shape(2, modes, modes)],
-        [product] + [turned(k) for k in range(1, group)],
+        [product] + [turned(product, group, k) for k in range(1, group)],
         [VM] * group,
         flops=flops,
     )
@@ -441,8 +470,10 @@
     def from_back(backs):
         return [along_chain(span, group * back) if back else span for back in backs]
 
-    backs = range(1, groups)
-    if groups > 4:
+    if groups <= 4:
+        backs = range(1, groups)
+        came = [turned(span, length, group * back) for back in backs]
+    else:
         backs = range(1, 5)
         span = join(from_back(backs), backs)
         reach = 4
@@ -451,12 +482,12 @@
             span = join(from_back(backs), backs)
             reach *= 4
         backs = range(0, groups, reach)
-    came = from_back(backs)
+        came = from_back(backs)
     inside = kernel_call(
         functools.partial(inside_body, halves, group),
         shape(2, 2, modes, modes),
-        [ordered, inner],
-        [VM] * 2,
+        [ordered, turn, inner],
+        [VM] * 3,
         flops=flops,
     )
     rows = jnp.concatenate([source, jnp.zeros((freqs, 6, modes), jnp.float32)], axis=1)

time: 72.9 us -> 69 us (0.947)
  starting transfers between devices: 25.2 us -> 18.9 us
  waiting for transfers between devices: 11.2 us -> 13.5 us
    ppermute x4 -> x1, starting transfers between devices: 9.8 us -> 1.29 us  [along_chain(): return lax.ppermute(value, ('range', 'alt'), pairs)]
    ppermute x3 -> x6, waiting for transfers between devices: 3.6 us -> 8.57 us  [turned(): return lax.ppermute(value, ('range', 'alt'), pairs)]
    ppermute x4 -> x1, waiting for transfers between devices: 2.7 us -> 0.01 us  [along_chain(): return lax.ppermute(value, ('range', 'alt'), pairs)]
    ppermute x3 -> x6, starting transfers between devices: 7.93 us -> 10.2 us  [turned(): return lax.ppermute(value, ('range', 'alt'), pairs)]
  transfers between devices with their start and end apart: 13 -> 13, of which waited for: 10 -> 11; matrix products, arithmetic and copies ran while one was open for 0% -> 0% of each run, Pallas kernels for 6% -> 12%
where the time goes in v6:
time: 69 us; the launch traced here: 68.6 us
  Pallas kernels  34.4 us (50%)
  starting transfers between devices  18.9 us (27%)
  waiting for transfers between devices  13.5 us (20%)
  other arithmetic  0.98 us (1%)
  local copies, waits for them, and re-layouts  0.77 us (1%)
    pallas_call x7, Pallas kernels, kernel_call(): pl.pallas_call(body, out_shape=out_shape, in_specs=specs, out_specs=jax.t...  34.4 us
    ppermute x6, starting transfers between devices, turned(): return lax.ppermute(value, ('range', 'alt'), pairs)  10.2 us
    ppermute x6, waiting for transfers between devices, turned(): return lax.ppermute(value, ('range', 'alt'), pairs)  8.57 us
    ppermute x6, starting transfers between devices, around(): lax.ppermute(value, 'alt', [(i, (i + k) % n_alt) for i in range(n_alt)])  7.42 us
    ppermute x6, waiting for transfers between devices, around(): lax.ppermute(value, 'alt', [(i, (i + k) % n_alt) for i in range(n_alt)])  4.93 us
  transfers between devices with their start and end apart: 13, of which 11 were waited for; matrix products, arithmetic and copies ran while one was open for 0% of the time, Pallas kernels for 12%

profile of v6, /device:TPU:0, one launch (start us, length us, event | category | flops | bytes accessed | tf_op | source)
XLA Modules:
  0.0 68.6 jit_solution(4071273068321553932)
XLA Ops:
  0.0 0.1 pad.4.clone
  0.1 0.6 copy-done.1
  0.8 1.0 %maximum_maximum_fusion.refs_0_ = f32[104,256]{1,0:T(8,128)S(1)} fusion(f32[4,256]{1,0:T(4,128)S(1)} %copy-done.1, f32[1,256]{1,0:T(1,128)S(1)} %bitcast.1, f32[96,256]{1,0:T(8,128)} %param.8, f32[104]{0:T(128)S(1)} %pad.4.clone), kind=kLoop, calls=%fused_computation | loop fusion | flops 79872 | bytes 210336 | tf_op jit(solution)/shard_map/concatenate | solution.py:412
  1.8 0.5 collective-permute-start
  2.3 2.6 %collective-permute-start.1 = (f32[104,256]{1,0:T(8,128)S(1)}, f32[104,256]{1,0:T(8,128)S(1)}, u32[]{:S(2)}, u32[]{:S(2)}) collective-permute-start(f32[104,256]{1,0:T(8,128)S(1)} %maximum_maximum_fusion.refs_0_), channel_id=1, source_target_pairs={{0,2},{1,3},{2,0},{3,1},{4,6},{5,7},{6,4},{7,5},{8,10},{9,11},{10,... | collective-permute-start | bytes 319496 | tf_op jit(solution)/shard_map/ppermute | solution.py:408
  4.8 1.4 %collective-permute-start.2 = (f32[104,256]{1,0:T(8,128)S(1)}, f32[104,256]{1,0:T(8,128)S(1)}, u32[]{:S(2)}, u32[]{:S(2)}) collective-permute-start(f32[104,256]{1,0:T(8,128)S(1)} %maximum_maximum_fusion.refs_0_), channel_id=1, source_target_pairs={{0,3},{1,0},{2,1},{3,2},{4,7},{5,4},{6,5},{7,6},{8,11},{9,8},{10,9... | collective-permute-start | bytes 319496 | tf_op jit(solution)/shard_map/ppermute | solution.py:408
  6.2 0.6 collective-permute-done.refs_1_
  6.8 1.3 %collective-permute-done.1.refs_2_ = f32[104,256]{1,0:T(8,128)S(1)} collective-permute-done((f32[104,256]{1,0:T(8,128)S(1)}, f32[104,256]{1,0:T(8,128)S(1)}, u32[]{:S(2)}, u32[]{:S(2)}) %collective-permute-start.1) | collective-permute-done | bytes 106528 | tf_op jit(solution)/shard_map/ppermute | solution.py:408
  8.1 1.7 %collective-permute-done.2.refs_3_ = f32[104,256]{1,0:T(8,128)S(1)} collective-permute-done((f32[104,256]{1,0:T(8,128)S(1)}, f32[104,256]{1,0:T(8,128)S(1)}, u32[]{:S(2)}, u32[]{:S(2)}) %collective-permute-start.2) | collective-permute-done | bytes 106528 | tf_op jit(solution)/shard_map/ppermute | solution.py:408
  9.8 21.8 %shard_map.55 = (f32[96,1024]{1,0:T(8,128)S(1)}, f32[96,1024]{1,0:T(8,128)S(1)}, f32[2,1024]{1,0:T(2,128)S(1)}) custom-call(f32[2]{0:T(128)S(1)} %copy-done, f32[104,256]{1,0:T(8,128)S(1)} %maximum_maximum_fusion.refs_0_, f32[104,256]{1,0:T(8,128)S(1)} %collective-permute-done.refs_1_, f32[104,256]{1,0:T(8,128)S(1)} %collective-permute-done.1.refs_2_, ...), custom_call_target="tpu_custom_call" | custom-call | flops 603979776 | bytes 1220616 | tf_op jit(solution)/shard_map/pallas_call | solution.py:45
  31.6 1.3 %collective-permute-start.3 = (f32[96,1024]{1,0:T(8,128)S(1)}, f32[96,1024]{1,0:T(8,128)S(1)}, u32[]{:S(2)}, u32[]{:S(2)}) collective-permute-start(f32[96,1024]{1,0:T(8,128)S(1)} %get-tuple-element.19.refs_0_), channel_id=1, source_target_pairs={{1,0},{4,1},{5,4},{8,5},{9,8},{12,9},{13,12},{16,13},{17,16},{20,1... | collective-permute-start | bytes 1179656 | tf_op jit(solution)/shard_map/ppermute | solution.py:405
  32.9 7.0 %shard_map.56 = (f32[96,1024]{1,0:T(8,128)S(1)}, f32[96,1024]{1,0:T(8,128)S(1)}, f32[96,96]{1,0:T(8,128)S(1)}, f32[2,96,96]{2,1,0:T(8,128)S(1)}, f32[2,96,96]{2,1,0:T(8,128)S(1)}) custom-call(f32[2,1024]{1,0:T(2,128)S(1)} %get-tuple-element.20.coef_ref, f32[96,1024]{1,0:T(8,128)S(1)} %get-tuple-element.19.refs_0_, f32[96,1024]{1,0:T(8,128)S(1)} %get-tuple-element.21.refs_1_), custom_call_target="tpu_custom_call" | custom-call | flops 301989888 | bytes 1765376 | tf_op jit(solution)/shard_map/pallas_call | solution.py:45
  40.0 0.8 %shard_map.57.refs_0_ = f32[2,96,96]{2,1,0:T(8,128)S(1)} custom-call(f32[96,1024]{1,0:T(8,128)S(1)} %collective-permute-done.3.next_ref, f32[96,1024]{1,0:T(8,128)S(1)} %get-tuple-element.22.second_ref.refs_5_, f32[2,96,96]{2,1,0:T(8,128)S(1)} %get-tuple-element.23.rest_ref), custom_call_target="tpu_custom_call" | custom-call | flops 18874368 | bytes 933888 | tf_op jit(solution)/shard_map/pallas_call | solution.py:45
  40.8 1.2 %collective-permute-start.4 = (f32[2,96,96]{2,1,0:T(8,128)S(1)}, f32[2,96,96]{2,1,0:T(8,128)S(1)}, u32[]{:S(2)}, u32[]{:S(2)}) collective-permute-start(f32[2,96,96]{2,1,0:T(8,128)S(1)} %shard_map.57.refs_0_), channel_id=1, source_target_pairs={{0,1},{1,4},{4,5},{5,0},{8,9},{9,12},{12,13},{13,8},{16,17},{17,20... | collective-permute-start | bytes 221192 | tf_op jit(solution)/shard_map/ppermute | solution.py:451
  42.0 2.8 %collective-permute-start.5 = (f32[2,96,96]{2,1,0:T(8,128)S(1)}, f32[2,96,96]{2,1,0:T(8,128)S(1)}, u32[]{:S(2)}, u32[]{:S(2)}) collective-permute-start(f32[2,96,96]{2,1,0:T(8,128)S(1)} %shard_map.57.refs_0_), channel_id=1, source_target_pairs={{0,4},{1,5},{4,0},{5,1},{8,12},{9,13},{12,8},{13,9},{16,20},{17,21... | collective-permute-start | bytes 221192 | tf_op jit(solution)/shard_map/ppermute | solution.py:451
  44.8 2.3 %collective-permute-done.4.refs_1_ = f32[2,96,96]{2,1,0:T(8,128)S(1)} collective-permute-done((f32[2,96,96]{2,1,0:T(8,128)S(1)}, f32[2,96,96]{2,1,0:T(8,128)S(1)}, u32[]{:S(2)}, u32[]{:S(2)}) %collective-permute-start.4) | collective-permute-done | bytes 73760 | tf_op jit(solution)/shard_map/ppermute | solution.py:451
  47.1 1.3 %collective-permute-done.5.refs_2_ = f32[2,96,96]{2,1,0:T(8,128)S(1)} collective-permute-done((f32[2,96,96]{2,1,0:T(8,128)S(1)}, f32[2,96,96]{2,1,0:T(8,128)S(1)}, u32[]{:S(2)}, u32[]{:S(2)}) %collective-permute-start.5) | collective-permute-done | bytes 73760 | tf_op jit(solution)/shard_map/ppermute | solution.py:451
  48.4 0.8 %shard_map.58 = (f32[4,2,96,96]{3,2,1,0:T(8,128)S(1)}, f32[2,96,96]{2,1,0:T(8,128)S(1)}) custom-call(f32[2,96,96]{2,1,0:T(8,128)S(1)} %shard_map.57.refs_0_, f32[2,96,96]{2,1,0:T(8,128)S(1)} %collective-permute-done.4.refs_1_, f32[2,96,96]{2,1,0:T(8,128)S(1)} %collective-permute-done.5.refs_2_, f32[2,96,96]{2,1,0:T(8,128)S(1)} %collective-permute-done.6.refs_3_), custom_call_target="tpu_custom_call" | custom-call | flops 18874368 | bytes 663552 | tf_op jit(solution)/shard_map/pallas_call | solution.py:45
  49.2 2.2 %collective-permute-start.7 = (f32[2,96,96]{2,1,0:T(8,128)S(1)}, f32[2,96,96]{2,1,0:T(8,128)S(1)}, u32[]{:S(2)}, u32[]{:S(2)}) collective-permute-start(f32[2,96,96]{2,1,0:T(8,128)S(1)} %get-tuple-element.24), channel_id=1, source_target_pairs={{0,8},{1,9},{4,12},{5,13},{8,16},{9,17},{12,20},{13,21},{16,24},{1... | collective-permute-start | bytes 221192 | tf_op jit(solution)/shard_map/ppermute | solution.py:451
  51.4 2.6 %collective-permute-start.8 = (f32[2,96,96]{2,1,0:T(8,128)S(1)}, f32[2,96,96]{2,1,0:T(8,128)S(1)}, u32[]{:S(2)}, u32[]{:S(2)}) collective-permute-start(f32[2,96,96]{2,1,0:T(8,128)S(1)} %get-tuple-element.24), channel_id=1, source_target_pairs={{0,16},{1,17},{4,20},{5,21},{8,24},{9,25},{12,28},{13,29},{16,0},{... | collective-permute-start | bytes 221192 | tf_op jit(solution)/shard_map/ppermute | solution.py:451
  54.0 1.3 %collective-permute-start.9 = (f32[2,96,96]{2,1,0:T(8,128)S(1)}, f32[2,96,96]{2,1,0:T(8,128)S(1)}, u32[]{:S(2)}, u32[]{:S(2)}) collective-permute-start(f32[2,96,96]{2,1,0:T(8,128)S(1)} %get-tuple-element.24), channel_id=1, source_target_pairs={{0,24},{1,25},{4,28},{5,29},{8,0},{9,1},{12,4},{13,5},{16,8},{17,9... | collective-permute-start | bytes 221192 | tf_op jit(solution)/shard_map/ppermute | solution.py:451
  55.4 1.1 %shard_map.59.refs_3_ = f32[2,2,96,96]{3,2,1,0:T(8,128)S(1)} custom-call(f32[4,2,96,96]{3,2,1,0:T(8,128)S(1)} %get-tuple-element.25.sorted_ref, f32[96,96]{1,0:T(8,128)S(1)} %get-tuple-element.26.turn_ref, f32[2,96,96]{2,1,0:T(8,128)S(1)} %get-tuple-element.27.inner_ref), custom_call_target="tpu_custom_call" | custom-call | flops 18874368 | bytes 552960 | tf_op jit(solution)/shard_map/pallas_call | solution.py:45
  56.5 0.1 collective-permute-done.7.refs_0_
  56.6 4.8 %collective-permute-done.8.refs_1_ = f32[2,96,96]{2,1,0:T(8,128)S(1)} collective-permute-done((f32[2,96,96]{2,1,0:T(8,128)S(1)}, f32[2,96,96]{2,1,0:T(8,128)S(1)}, u32[]{:S(2)}, u32[]{:S(2)}) %collective-permute-start.8) | collective-permute-done | bytes 73760 | tf_op jit(solution)/shard_map/ppermute | solution.py:451
  61.4 0.1 collective-permute-done.9.refs_2_
  61.5 2.2 %shard_map.60 = (f32[2,2,256]{2,1,0:T(2,128)S(1)}, f32[2,2,256]{2,1,0:T(2,128)S(1)}, f32[2,2,256]{2,1,0:T(2,128)S(1)}, f32[2,2,256]{2,1,0:T(2,128)S(1)}) custom-call(f32[2,8,96]{2,1,0:T(8,128)S(1)} %concatenate.6.source_ref, f32[2,96,96]{2,1,0:T(8,128)S(1)} %collective-permute-done.7.refs_0_, f32[2,96,96]{2,1,0:T(8,128)S(1)} %collective-permute-done.8.refs_1_, ...), custom_call_target="tpu_custom_call" | custom-call | bytes 1177600 | tf_op jit(solution)/shard_map/pallas_call | solution.py:45
  63.7 1.5 %collective-permute-start.11 = (f32[2,2,256]{2,1,0:T(2,128)S(1)}, f32[2,2,256]{2,1,0:T(2,128)S(1)}, u32[]{:S(2)}, u32[]{:S(2)}) collective-permute-start(f32[2,2,256]{2,1,0:T(2,128)S(1)} %get-tuple-element.31), channel_id=1, source_target_pairs={{0,2},{1,3},{2,0},{3,1},{4,6},{5,7},{6,4},{7,5},{8,10},{9,11},{10,... | collective-permute-start | bytes 12296 | tf_op jit(solution)/shard_map/ppermute | solution.py:408
  65.2 1.4 %collective-permute-start.12 = (f32[2,2,256]{2,1,0:T(2,128)S(1)}, f32[2,2,256]{2,1,0:T(2,128)S(1)}, u32[]{:S(2)}, u32[]{:S(2)}) collective-permute-start(f32[2,2,256]{2,1,0:T(2,128)S(1)} %get-tuple-element.32), channel_id=1, source_target_pairs={{0,3},{1,0},{2,1},{3,2},{4,7},{5,4},{6,5},{7,6},{8,11},{9,8},{10,9... | collective-permute-start | bytes 12296 | tf_op jit(solution)/shard_map/ppermute | solution.py:408
  66.6 0.1 collective-permute-done.10.refs_1_
  66.7 0.6 collective-permute-done.11.refs_2_
  67.3 0.6 collective-permute-done.12.refs_3_
  67.9 0.6 shard_map.61
  (13 shorter events, 0.1 us)
Async XLA Ops:
  0.0 0.7 %copy-start.1 = (f32[4,256]{1,0:T(4,128)S(1)}, f32[4,256]{1,0:T(4,128)}, u32[]{:S(2)}) copy-start(f32[4,256]{1,0:T(4,128)} %param.7) | copy-start | bytes 12292
  0.1 0.7 copy-start.3
  0.8 9.1 %copy-start = (f32[2]{0:T(128)S(1)}, f32[2]{0:T(128)}, u32[]{:S(2)}) copy-start(f32[2]{0:T(128)} %scale_ref.1) | copy-start | bytes 28
  1.8 5.0 %collective-permute-start = (f32[104,256]{1,0:T(8,128)S(1)}, f32[104,256]{1,0:T(8,128)S(1)}, u32[]{:S(2)}, u32[]{:S(2)}) collective-permute-start(f32[104,256]{1,0:T(8,128)S(1)} %maximum_maximum_fusion.refs_0_), channel_id=1, source_target_pairs={{0,1},{1,2},{2,3},{3,0},{4,5},{5,6},{6,7},{7,4},{8,9},{9,10},{10,1... | collective-permute-start | bytes 319496 | tf_op jit(solution)/shard_map/ppermute | solution.py:408
  2.3 5.9 %collective-permute-start.1 = (f32[104,256]{1,0:T(8,128)S(1)}, f32[104,256]{1,0:T(8,128)S(1)}, u32[]{:S(2)}, u32[]{:S(2)}) collective-permute-start(f32[104,256]{1,0:T(8,128)S(1)} %maximum_maximum_fusion.refs_0_), channel_id=1, source_target_pairs={{0,2},{1,3},{2,0},{3,1},{4,6},{5,7},{6,4},{7,5},{8,10},{9,11},{10,... | collective-permute-start | bytes 319496 | tf_op jit(solution)/shard_map/ppermute | solution.py:408
  4.8 5.0 %collective-permute-start.2 = (f32[104,256]{1,0:T(8,128)S(1)}, f32[104,256]{1,0:T(8,128)S(1)}, u32[]{:S(2)}, u32[]{:S(2)}) collective-permute-start(f32[104,256]{1,0:T(8,128)S(1)} %maximum_maximum_fusion.refs_0_), channel_id=1, source_target_pairs={{0,3},{1,0},{2,1},{3,2},{4,7},{5,4},{6,5},{7,6},{8,11},{9,8},{10,9... | collective-permute-start | bytes 319496 | tf_op jit(solution)/shard_map/ppermute | solution.py:408
  31.6 8.4 %collective-permute-start.3 = (f32[96,1024]{1,0:T(8,128)S(1)}, f32[96,1024]{1,0:T(8,128)S(1)}, u32[]{:S(2)}, u32[]{:S(2)}) collective-permute-start(f32[96,1024]{1,0:T(8,128)S(1)} %get-tuple-element.19.refs_0_), channel_id=1, source_target_pairs={{1,0},{4,1},{5,4},{8,5},{9,8},{12,9},{13,12},{16,13},{17,16},{20,1... | collective-permute-start | bytes 1179656 | tf_op jit(solution)/shard_map/ppermute | solution.py:405
  40.8 6.3 %collective-permute-start.4 = (f32[2,96,96]{2,1,0:T(8,128)S(1)}, f32[2,96,96]{2,1,0:T(8,128)S(1)}, u32[]{:S(2)}, u32[]{:S(2)}) collective-permute-start(f32[2,96,96]{2,1,0:T(8,128)S(1)} %shard_map.57.refs_0_), channel_id=1, source_target_pairs={{0,1},{1,4},{4,5},{5,0},{8,9},{9,12},{12,13},{13,8},{16,17},{17,20... | collective-permute-start | bytes 221192 | tf_op jit(solution)/shard_map/ppermute | solution.py:451
  42.0 6.4 %collective-permute-start.5 = (f32[2,96,96]{2,1,0:T(8,128)S(1)}, f32[2,96,96]{2,1,0:T(8,128)S(1)}, u32[]{:S(2)}, u32[]{:S(2)}) collective-permute-start(f32[2,96,96]{2,1,0:T(8,128)S(1)} %shard_map.57.refs_0_), channel_id=1, source_target_pairs={{0,4},{1,5},{4,0},{5,1},{8,12},{9,13},{12,8},{13,9},{16,20},{17,21... | collective-permute-start | bytes 221192 | tf_op jit(solution)/shard_map/ppermute | solution.py:451
  44.8 3.6 %collective-permute-start.6 = (f32[2,96,96]{2,1,0:T(8,128)S(1)}, f32[2,96,96]{2,1,0:T(8,128)S(1)}, u32[]{:S(2)}, u32[]{:S(2)}) collective-permute-start(f32[2,96,96]{2,1,0:T(8,128)S(1)} %shard_map.57.refs_0_), channel_id=1, source_target_pairs={{0,5},{1,0},{4,1},{5,4},{8,13},{9,8},{12,9},{13,12},{16,21},{17,16... | collective-permute-start | bytes 221192 | tf_op jit(solution)/shard_map/ppermute | solution.py:451
  48.4 7.0 %copy-start.2 = (f32[2,2,96]{2,1,0:T(2,128)S(1)}, f32[2,2,96]{2,1,0:T(2,128)}, u32[]{:S(2)}) copy-start(f32[2,2,96]{2,1,0:T(2,128)} %param.9) | copy-start | bytes 4612
  49.2 7.4 %collective-permute-start.7 = (f32[2,96,96]{2,1,0:T(8,128)S(1)}, f32[2,96,96]{2,1,0:T(8,128)S(1)}, u32[]{:S(2)}, u32[]{:S(2)}) collective-permute-start(f32[2,96,96]{2,1,0:T(8,128)S(1)} %get-tuple-element.24), channel_id=1, source_target_pairs={{0,8},{1,9},{4,12},{5,13},{8,16},{9,17},{12,20},{13,21},{16,24},{1... | collective-permute-start | bytes 221192 | tf_op jit(solution)/shard_map/ppermute | solution.py:451
  51.4 10.0 %collective-permute-start.8 = (f32[2,96,96]{2,1,0:T(8,128)S(1)}, f32[2,96,96]{2,1,0:T(8,128)S(1)}, u32[]{:S(2)}, u32[]{:S(2)}) collective-permute-start(f32[2,96,96]{2,1,0:T(8,128)S(1)} %get-tuple-element.24), channel_id=1, source_target_pairs={{0,16},{1,17},{4,20},{5,21},{8,24},{9,25},{12,28},{13,29},{16,0},{... | collective-permute-start | bytes 221192 | tf_op jit(solution)/shard_map/ppermute | solution.py:451
  54.0 7.5 %collective-permute-start.9 = (f32[2,96,96]{2,1,0:T(8,128)S(1)}, f32[2,96,96]{2,1,0:T(8,128)S(1)}, u32[]{:S(2)}, u32[]{:S(2)}) collective-permute-start(f32[2,96,96]{2,1,0:T(8,128)S(1)} %get-tuple-element.24), channel_id=1, source_target_pairs={{0,24},{1,25},{4,28},{5,29},{8,0},{9,1},{12,4},{13,5},{16,8},{17,9... | collective-permute-start | bytes 221192 | tf_op jit(solution)/shard_map/ppermute | solution.py:451
  63.7 3.0 %collective-permute-start.10 = (f32[2,2,256]{2,1,0:T(2,128)S(1)}, f32[2,2,256]{2,1,0:T(2,128)S(1)}, u32[]{:S(2)}, u32[]{:S(2)}) collective-permute-start(f32[2,2,256]{2,1,0:T(2,128)S(1)} %get-tuple-element.30), channel_id=1, source_target_pairs={{0,1},{1,2},{2,3},{3,0},{4,5},{5,6},{6,7},{7,4},{8,9},{9,10},{10,1... | collective-permute-start | bytes 12296 | tf_op jit(solution)/shard_map/ppermute | solution.py:408
  63.7 3.7 %collective-permute-start.11 = (f32[2,2,256]{2,1,0:T(2,128)S(1)}, f32[2,2,256]{2,1,0:T(2,128)S(1)}, u32[]{:S(2)}, u32[]{:S(2)}) collective-permute-start(f32[2,2,256]{2,1,0:T(2,128)S(1)} %get-tuple-element.31), channel_id=1, source_target_pairs={{0,2},{1,3},{2,0},{3,1},{4,6},{5,7},{6,4},{7,5},{8,10},{9,11},{10,... | collective-permute-start | bytes 12296 | tf_op jit(solution)/shard_map/ppermute | solution.py:408
  65.2 2.8 %collective-permute-start.12 = (f32[2,2,256]{2,1,0:T(2,128)S(1)}, f32[2,2,256]{2,1,0:T(2,128)S(1)}, u32[]{:S(2)}, u32[]{:S(2)}) collective-permute-start(f32[2,2,256]{2,1,0:T(2,128)S(1)} %get-tuple-element.32), channel_id=1, source_target_pairs={{0,3},{1,0},{2,1},{3,2},{4,7},{5,4},{6,5},{7,6},{8,11},{9,8},{10,9... | collective-permute-start | bytes 12296 | tf_op jit(solution)/shard_map/ppermute | solution.py:408

commit v7 on v6

--- a/solution.py
+++ b/solution.py
@@ -175,6 +175,15 @@
 DOWN = 2.0**-13
 
 
+def pack_body(modes, seg_count, start_ref, base_ref, perturb_ref, out_ref):
+    out_ref[0:modes, :] = start_ref[...]
+    out_ref[modes : modes + 1, :] = base_ref[...]
+    out_ref[modes + 1 : modes + 1 + seg_count, :] = perturb_ref[...]
+    rest = out_ref.shape[0] - (modes + 1 + seg_count)
+    if rest:
+        out_ref[modes + 1 + seg_count :, :] = jnp.zeros((rest, out_ref.shape[1]), jnp.float32)
+
+
 def iterate_body(n_alt, chunk, seg_count, modes, width, scale_ref, *refs):
     blocks, image_refs = refs[:n_alt], refs[n_alt : n_alt + chunk]
     coef_ref, basis_ref, split_ref, gram_ref, inv_ref = refs[n_alt + chunk :]
@@ -184,7 +193,7 @@
     first = flat - freq * seg_count
     total = n_alt * width
     for k, block in enumerate(blocks):
-        source = lax.rem(place + n_alt - k, n_alt)
+        source = place ^ k
         span = pl.ds(pl.multiple_of(source * width, width), width)
         start = block[0:modes, :] * (1.0 / float(total) ** 0.5)
         for i in range(chunk):
@@ -291,7 +300,8 @@
     inner = (mm(corr, turns[0][0]), mm(corr, turns[0][1]))
     turn = jnp.where(chain_place(halves) == 0, unit, gram_ref[0, :, 0:modes])
     turn_ref[...] = turn
-    rest = complex_mm(turns[1], (mm(inner[0], turn), mm(inner[1], turn)))
+    late = (mm(turns[1][0], corr), mm(turns[1][1], corr))
+    rest = complex_mm(late, (mm(turns[0][0], turn), mm(turns[0][1], turn)))
     for part in range(2):
         inner_ref[part] = inner[part]
         rest_ref[part] = rest[part]
@@ -392,7 +402,7 @@
     chunk = freqs * seg_count // n_alt
     halves = seg_count // chunk
     length = n_range * halves
-    assert modes == 2 * HALF and chunk == 2 and halves * chunk == seg_count and halves * freqs == n_alt
+    assert n_alt & (n_alt - 1) == 0 and modes == 2 * HALF and chunk == 2 and halves * chunk == seg_count and halves * freqs == n_alt
 
     def device(freq, at):
         return at // halves * n_alt + freq * halves + at % halves
@@ -407,10 +417,19 @@
     def around(value, k):
         return lax.ppermute(value, "alt", [(i, (i + k) % n_alt) for i in range(n_alt)])
 
-    lines = [start_block, base_profile[None, :], perturb]
-    filler = jnp.zeros((-(modes + 1 + seg_count) % 8, width), jnp.float32)
-    mine = jnp.concatenate(lines + [filler], axis=0)
-    blocks = [mine] + [around(mine, k) for k in range(1, n_alt)]
+    mine = kernel_call(
+        functools.partial(pack_body, modes, seg_count),
+        shape(-(-(modes + 1 + seg_count) // 8) * 8, width),
+        [start_block, base_profile[None, :], perturb],
+        [VM] * 3,
+    )
+    found, bit = {0: mine}, n_alt
+    while bit > 1:
+        bit //= 2
+        pairs = [(i, i ^ bit) for i in range(n_alt)]
+        for key in list(found):
+            found[key ^ bit] = lax.ppermute(found[key], "alt", pairs)
+    blocks = [found[k] for k in range(n_alt)]
     flops = 2 * modes * modes * total
     image, other, coef = kernel_call(
         functools.partial(iterate_body, n_alt, chunk, seg_count, modes, width),

time: 69 us -> 68.5 us (level)
  local copies, waits for them, and re-layouts: 0.77 us -> 2.27 us
  starting transfers between devices: 18.9 us -> 17.4 us
  other arithmetic: 0.98 us -> 0 us
    ppermute x6 -> x3, starting transfers between devices: 7.42 us -> 2.97 us  [around(): lax.ppermute(value, 'alt', [(i, (i + k) % n_alt) for i in range(n_alt)])]
    ppermute x0 -> x3, waiting for transfers between devices: none -> 4.28 us  [local(): found[key ^ bit] = lax.ppermute(found[key], 'alt', pairs)]
    ppermute x6 -> x3, waiting for transfers between devices: 4.93 us -> 1.33 us  [around(): lax.ppermute(value, 'alt', [(i, (i + k) % n_alt) for i in range(n_alt)])]
    ppermute x0 -> x3, starting transfers between devices: none -> 3.01 us  [local(): found[key ^ bit] = lax.ppermute(found[key], 'alt', pairs)]
    unnamed x8 -> x10, local copies, waits for them, and re-layouts: 0.69 us -> 2.26 us
    concatenate x1 -> x0, other arithmetic: 0.98 us -> none  [local(): mine = jnp.concatenate(lines + [filler], axis=0)]
    pallas_call x7 -> x8, Pallas kernels: 34.4 us -> 34.5 us  [kernel_call(): pl.pallas_call(body, out_shape=out_shape, in_specs=specs, out_specs=jax.t...]
where the time goes in v7:
time: 68.5 us; the launch traced here: 68 us
  Pallas kernels  34.5 us (50%)
  starting transfers between devices  17.4 us (25%)
  waiting for transfers between devices  13.8 us (20%)
  local copies, waits for them, and re-layouts  2.27 us (3%)
    pallas_call x8, Pallas kernels, kernel_call(): pl.pallas_call(body, out_shape=out_shape, in_specs=specs, out_specs=jax.t...  34.5 us
    ppermute x6, starting transfers between devices, turned(): return lax.ppermute(value, ('range', 'alt'), pairs)  10.1 us
    ppermute x6, waiting for transfers between devices, turned(): return lax.ppermute(value, ('range', 'alt'), pairs)  8.22 us
    ppermute x3, waiting for transfers between devices, local(): found[key ^ bit] = lax.ppermute(found[key], 'alt', pairs)  4.28 us
    ppermute x3, starting transfers between devices, local(): found[key ^ bit] = lax.ppermute(found[key], 'alt', pairs)  3.01 us
    ppermute x3, starting transfers between devices, around(): lax.ppermute(value, 'alt', [(i, (i + k) % n_alt) for i in range(n_alt)])  2.97 us
    unnamed x10, local copies, waits for them, and re-layouts  2.26 us
  transfers between devices with their start and end apart: 13, of which 11 were waited for; matrix products, arithmetic and copies ran while one was open for 0% of the time, Pallas kernels for 12%

profile of v7, /device:TPU:0, one launch (start us, length us, event | category | flops | bytes accessed | tf_op | source)
XLA Modules:
  0.0 68.0 jit_solution(16016208148195991995)
XLA Ops:
  0.0 0.7 copy-done.2
  0.7 0.9 %copy-done = f32[96,256]{1,0:T(8,128)S(1)} copy-done((f32[96,256]{1,0:T(8,128)S(1)}, f32[96,256]{1,0:T(8,128)}, u32[]{:S(2)}) %copy-start) | copy-done | bytes 98328
  1.6 0.7 %copy-done.1 = f32[4,256]{1,0:T(4,128)S(1)} copy-done((f32[4,256]{1,0:T(4,128)S(1)}, f32[4,256]{1,0:T(4,128)}, u32[]{:S(2)}) %copy-start.1) | copy-done | bytes 4120
  2.3 3.0 %collective-permute-start.1 = (f32[104,256]{1,0:T(8,128)S(1)}, f32[104,256]{1,0:T(8,128)S(1)}, u32[]{:S(2)}, u32[]{:S(2)}) collective-permute-start(f32[104,256]{1,0:T(8,128)S(1)} %shard_map.55.refs_0_), channel_id=1, source_target_pairs={{0,2},{1,3},{2,0},{3,1},{4,6},{5,7},{6,4},{7,5},{8,10},{9,11},{10,... | collective-permute-start | bytes 319496 | tf_op jit(solution)/shard_map/ppermute | solution.py:431
  5.3 3.0 %collective-permute-done.1.refs_2_ = f32[104,256]{1,0:T(8,128)S(1)} collective-permute-done((f32[104,256]{1,0:T(8,128)S(1)}, f32[104,256]{1,0:T(8,128)S(1)}, u32[]{:S(2)}, u32[]{:S(2)}) %collective-permute-start.1) | collective-permute-done | bytes 106528 | tf_op jit(solution)/shard_map/ppermute | solution.py:431
  8.2 0.0 collective-permute-start.2
  8.3 1.3 %collective-permute-done.2.refs_3_ = f32[104,256]{1,0:T(8,128)S(1)} collective-permute-done((f32[104,256]{1,0:T(8,128)S(1)}, f32[104,256]{1,0:T(8,128)S(1)}, u32[]{:S(2)}, u32[]{:S(2)}) %collective-permute-start.2) | collective-permute-done | bytes 106528 | tf_op jit(solution)/shard_map/ppermute | solution.py:431
  9.6 21.8 %shard_map.56 = (f32[96,1024]{1,0:T(8,128)S(1)}, f32[96,1024]{1,0:T(8,128)S(1)}, f32[2,1024]{1,0:T(2,128)S(1)}) custom-call(f32[2]{0:T(128)S(1)} %copy-done.3, f32[104,256]{1,0:T(8,128)S(1)} %shard_map.55.refs_0_, f32[104,256]{1,0:T(8,128)S(1)} %collective-permute-done.refs_1_, f32[104,256]{1,0:T(8,128)S(1)} %collective-permute-done.1.refs_2_, ...), custom_call_target="tpu_custom_call" | custom-call | flops 603979776 | bytes 1220616 | tf_op jit(solution)/shard_map/pallas_call | solution.py:45
  31.3 1.3 %collective-permute-start.3 = (f32[96,1024]{1,0:T(8,128)S(1)}, f32[96,1024]{1,0:T(8,128)S(1)}, u32[]{:S(2)}, u32[]{:S(2)}) collective-permute-start(f32[96,1024]{1,0:T(8,128)S(1)} %get-tuple-element.19.refs_0_), channel_id=1, source_target_pairs={{1,0},{4,1},{5,4},{8,5},{9,8},{12,9},{13,12},{16,13},{17,16},{20,1... | collective-permute-start | bytes 1179656 | tf_op jit(solution)/shard_map/ppermute | solution.py:415
  32.6 7.2 %shard_map.57 = (f32[96,1024]{1,0:T(8,128)S(1)}, f32[96,1024]{1,0:T(8,128)S(1)}, f32[96,96]{1,0:T(8,128)S(1)}, f32[2,96,96]{2,1,0:T(8,128)S(1)}, f32[2,96,96]{2,1,0:T(8,128)S(1)}) custom-call(f32[2,1024]{1,0:T(2,128)S(1)} %get-tuple-element.20.coef_ref, f32[96,1024]{1,0:T(8,128)S(1)} %get-tuple-element.19.refs_0_, f32[96,1024]{1,0:T(8,128)S(1)} %get-tuple-element.21.refs_1_), custom_call_target="tpu_custom_call" | custom-call | flops 301989888 | bytes 1765376 | tf_op jit(solution)/shard_map/pallas_call | solution.py:45
  39.8 0.8 %shard_map.58.refs_0_ = f32[2,96,96]{2,1,0:T(8,128)S(1)} custom-call(f32[96,1024]{1,0:T(8,128)S(1)} %collective-permute-done.3.next_ref, f32[96,1024]{1,0:T(8,128)S(1)} %get-tuple-element.22.second_ref.refs_5_, f32[2,96,96]{2,1,0:T(8,128)S(1)} %get-tuple-element.23.rest_ref), custom_call_target="tpu_custom_call" | custom-call | flops 18874368 | bytes 933888 | tf_op jit(solution)/shard_map/pallas_call | solution.py:45
  40.6 1.2 %collective-permute-start.4 = (f32[2,96,96]{2,1,0:T(8,128)S(1)}, f32[2,96,96]{2,1,0:T(8,128)S(1)}, u32[]{:S(2)}, u32[]{:S(2)}) collective-permute-start(f32[2,96,96]{2,1,0:T(8,128)S(1)} %shard_map.58.refs_0_), channel_id=1, source_target_pairs={{0,1},{1,4},{4,5},{5,0},{8,9},{9,12},{12,13},{13,8},{16,17},{17,20... | collective-permute-start | bytes 221192 | tf_op jit(solution)/shard_map/ppermute | solution.py:470
  41.8 2.3 %collective-permute-start.5 = (f32[2,96,96]{2,1,0:T(8,128)S(1)}, f32[2,96,96]{2,1,0:T(8,128)S(1)}, u32[]{:S(2)}, u32[]{:S(2)}) collective-permute-start(f32[2,96,96]{2,1,0:T(8,128)S(1)} %shard_map.58.refs_0_), channel_id=1, source_target_pairs={{0,4},{1,5},{4,0},{5,1},{8,12},{9,13},{12,8},{13,9},{16,20},{17,21... | collective-permute-start | bytes 221192 | tf_op jit(solution)/shard_map/ppermute | solution.py:470
  44.1 0.4 collective-permute-start.6
  44.5 1.9 %collective-permute-done.4.refs_1_ = f32[2,96,96]{2,1,0:T(8,128)S(1)} collective-permute-done((f32[2,96,96]{2,1,0:T(8,128)S(1)}, f32[2,96,96]{2,1,0:T(8,128)S(1)}, u32[]{:S(2)}, u32[]{:S(2)}) %collective-permute-start.4) | collective-permute-done | bytes 73760 | tf_op jit(solution)/shard_map/ppermute | solution.py:470
  46.4 1.3 %collective-permute-done.5.refs_2_ = f32[2,96,96]{2,1,0:T(8,128)S(1)} collective-permute-done((f32[2,96,96]{2,1,0:T(8,128)S(1)}, f32[2,96,96]{2,1,0:T(8,128)S(1)}, u32[]{:S(2)}, u32[]{:S(2)}) %collective-permute-start.5) | collective-permute-done | bytes 73760 | tf_op jit(solution)/shard_map/ppermute | solution.py:470
  47.7 0.1 collective-permute-done.6.refs_3_
  47.8 0.8 %shard_map.59 = (f32[4,2,96,96]{3,2,1,0:T(8,128)S(1)}, f32[2,96,96]{2,1,0:T(8,128)S(1)}) custom-call(f32[2,96,96]{2,1,0:T(8,128)S(1)} %shard_map.58.refs_0_, f32[2,96,96]{2,1,0:T(8,128)S(1)} %collective-permute-done.4.refs_1_, f32[2,96,96]{2,1,0:T(8,128)S(1)} %collective-permute-done.5.refs_2_, f32[2,96,96]{2,1,0:T(8,128)S(1)} %collective-permute-done.6.refs_3_), custom_call_target="tpu_custom_call" | custom-call | flops 18874368 | bytes 663552 | tf_op jit(solution)/shard_map/pallas_call | solution.py:45
  48.6 2.2 %collective-permute-start.7 = (f32[2,96,96]{2,1,0:T(8,128)S(1)}, f32[2,96,96]{2,1,0:T(8,128)S(1)}, u32[]{:S(2)}, u32[]{:S(2)}) collective-permute-start(f32[2,96,96]{2,1,0:T(8,128)S(1)} %get-tuple-element.24), channel_id=1, source_target_pairs={{0,8},{1,9},{4,12},{5,13},{8,16},{9,17},{12,20},{13,21},{16,24},{1... | collective-permute-start | bytes 221192 | tf_op jit(solution)/shard_map/ppermute | solution.py:470
  50.8 2.6 %collective-permute-start.8 = (f32[2,96,96]{2,1,0:T(8,128)S(1)}, f32[2,96,96]{2,1,0:T(8,128)S(1)}, u32[]{:S(2)}, u32[]{:S(2)}) collective-permute-start(f32[2,96,96]{2,1,0:T(8,128)S(1)} %get-tuple-element.24), channel_id=1, source_target_pairs={{0,16},{1,17},{4,20},{5,21},{8,24},{9,25},{12,28},{13,29},{16,0},{... | collective-permute-start | bytes 221192 | tf_op jit(solution)/shard_map/ppermute | solution.py:470
  53.4 1.3 %collective-permute-start.9 = (f32[2,96,96]{2,1,0:T(8,128)S(1)}, f32[2,96,96]{2,1,0:T(8,128)S(1)}, u32[]{:S(2)}, u32[]{:S(2)}) collective-permute-start(f32[2,96,96]{2,1,0:T(8,128)S(1)} %get-tuple-element.24), channel_id=1, source_target_pairs={{0,24},{1,25},{4,28},{5,29},{8,0},{9,1},{12,4},{13,5},{16,8},{17,9... | collective-permute-start | bytes 221192 | tf_op jit(solution)/shard_map/ppermute | solution.py:470
  54.8 1.1 %shard_map.60.refs_3_ = f32[2,2,96,96]{3,2,1,0:T(8,128)S(1)} custom-call(f32[4,2,96,96]{3,2,1,0:T(8,128)S(1)} %get-tuple-element.25.sorted_ref, f32[96,96]{1,0:T(8,128)S(1)} %get-tuple-element.26.turn_ref, f32[2,96,96]{2,1,0:T(8,128)S(1)} %get-tuple-element.27.inner_ref), custom_call_target="tpu_custom_call" | custom-call | flops 18874368 | bytes 552960 | tf_op jit(solution)/shard_map/pallas_call | solution.py:45
  55.9 0.1 collective-permute-done.7.refs_0_
  56.0 4.8 %collective-permute-done.8.refs_1_ = f32[2,96,96]{2,1,0:T(8,128)S(1)} collective-permute-done((f32[2,96,96]{2,1,0:T(8,128)S(1)}, f32[2,96,96]{2,1,0:T(8,128)S(1)}, u32[]{:S(2)}, u32[]{:S(2)}) %collective-permute-start.8) | collective-permute-done | bytes 73760 | tf_op jit(solution)/shard_map/ppermute | solution.py:470
  60.8 0.1 collective-permute-done.9.refs_2_
  60.9 2.2 %shard_map.61 = (f32[2,2,256]{2,1,0:T(2,128)S(1)}, f32[2,2,256]{2,1,0:T(2,128)S(1)}, f32[2,2,256]{2,1,0:T(2,128)S(1)}, f32[2,2,256]{2,1,0:T(2,128)S(1)}) custom-call(f32[2,8,96]{2,1,0:T(8,128)S(1)} %concatenate.3.source_ref, f32[2,96,96]{2,1,0:T(8,128)S(1)} %collective-permute-done.7.refs_0_, f32[2,96,96]{2,1,0:T(8,128)S(1)} %collective-permute-done.8.refs_1_, ...), custom_call_target="tpu_custom_call" | custom-call | bytes 1177600 | tf_op jit(solution)/shard_map/pallas_call | solution.py:45
  63.1 1.5 %collective-permute-start.11 = (f32[2,2,256]{2,1,0:T(2,128)S(1)}, f32[2,2,256]{2,1,0:T(2,128)S(1)}, u32[]{:S(2)}, u32[]{:S(2)}) collective-permute-start(f32[2,2,256]{2,1,0:T(2,128)S(1)} %get-tuple-element.31), channel_id=1, source_target_pairs={{0,2},{1,3},{2,0},{3,1},{4,6},{5,7},{6,4},{7,5},{8,10},{9,11},{10,... | collective-permute-start | bytes 12296 | tf_op jit(solution)/shard_map/ppermute | solution.py:418
  64.6 1.4 %collective-permute-start.12 = (f32[2,2,256]{2,1,0:T(2,128)S(1)}, f32[2,2,256]{2,1,0:T(2,128)S(1)}, u32[]{:S(2)}, u32[]{:S(2)}) collective-permute-start(f32[2,2,256]{2,1,0:T(2,128)S(1)} %get-tuple-element.32), channel_id=1, source_target_pairs={{0,3},{1,0},{2,1},{3,2},{4,7},{5,4},{6,5},{7,6},{8,11},{9,8},{10,9... | collective-permute-start | bytes 12296 | tf_op jit(solution)/shard_map/ppermute | solution.py:418
  66.1 0.1 collective-permute-done.10.refs_1_
  66.1 0.6 collective-permute-done.11.refs_2_
  66.7 0.7 collective-permute-done.12.refs_3_
  67.4 0.6 shard_map.62
  (13 shorter events, 0.0 us)
Async XLA Ops:
  0.0 0.7 copy-start.2
  0.7 0.9 %copy-start = (f32[96,256]{1,0:T(8,128)S(1)}, f32[96,256]{1,0:T(8,128)}, u32[]{:S(2)}) copy-start(f32[96,256]{1,0:T(8,128)} %start_ref.1) | copy-start | bytes 294916
  1.6 0.7 %copy-start.1 = (f32[4,256]{1,0:T(4,128)S(1)}, f32[4,256]{1,0:T(4,128)}, u32[]{:S(2)}) copy-start(f32[4,256]{1,0:T(4,128)} %perturb_ref.1) | copy-start | bytes 12292
  2.3 7.3 %copy-start.3 = (f32[2]{0:T(128)S(1)}, f32[2]{0:T(128)}, u32[]{:S(2)}) copy-start(f32[2]{0:T(128)} %scale_ref.1) | copy-start | bytes 28
  2.3 6.0 %collective-permute-start.1 = (f32[104,256]{1,0:T(8,128)S(1)}, f32[104,256]{1,0:T(8,128)S(1)}, u32[]{:S(2)}, u32[]{:S(2)}) collective-permute-start(f32[104,256]{1,0:T(8,128)S(1)} %shard_map.55.refs_0_), channel_id=1, source_target_pairs={{0,2},{1,3},{2,0},{3,1},{4,6},{5,7},{6,4},{7,5},{8,10},{9,11},{10,... | collective-permute-start | bytes 319496 | tf_op jit(solution)/shard_map/ppermute | solution.py:431
  5.3 3.0 %collective-permute-start = (f32[104,256]{1,0:T(8,128)S(1)}, f32[104,256]{1,0:T(8,128)S(1)}, u32[]{:S(2)}, u32[]{:S(2)}) collective-permute-start(f32[104,256]{1,0:T(8,128)S(1)} %shard_map.55.refs_0_), channel_id=1, source_target_pairs={{0,1},{1,0},{2,3},{3,2},{4,5},{5,4},{6,7},{7,6},{8,9},{9,8},{10,11... | collective-permute-start | bytes 319496 | tf_op jit(solution)/shard_map/ppermute | solution.py:431
  8.2 1.3 %collective-permute-start.2 = (f32[104,256]{1,0:T(8,128)S(1)}, f32[104,256]{1,0:T(8,128)S(1)}, u32[]{:S(2)}, u32[]{:S(2)}) collective-permute-start(f32[104,256]{1,0:T(8,128)S(1)} %collective-permute-done.1.refs_2_), channel_id=1, source_target_pairs={{0,1},{1,0},{2,3},{3,2},{4,5},{5,4},{6,7},{7,6},{8,9},{9,8},{10,11... | collective-permute-start | bytes 319496 | tf_op jit(solution)/shard_map/ppermute | solution.py:431
  31.3 8.5 %collective-permute-start.3 = (f32[96,1024]{1,0:T(8,128)S(1)}, f32[96,1024]{1,0:T(8,128)S(1)}, u32[]{:S(2)}, u32[]{:S(2)}) collective-permute-start(f32[96,1024]{1,0:T(8,128)S(1)} %get-tuple-element.19.refs_0_), channel_id=1, source_target_pairs={{1,0},{4,1},{5,4},{8,5},{9,8},{12,9},{13,12},{16,13},{17,16},{20,1... | collective-permute-start | bytes 1179656 | tf_op jit(solution)/shard_map/ppermute | solution.py:415
  40.6 5.8 %collective-permute-start.4 = (f32[2,96,96]{2,1,0:T(8,128)S(1)}, f32[2,96,96]{2,1,0:T(8,128)S(1)}, u32[]{:S(2)}, u32[]{:S(2)}) collective-permute-start(f32[2,96,96]{2,1,0:T(8,128)S(1)} %shard_map.58.refs_0_), channel_id=1, source_target_pairs={{0,1},{1,4},{4,5},{5,0},{8,9},{9,12},{12,13},{13,8},{16,17},{17,20... | collective-permute-start | bytes 221192 | tf_op jit(solution)/shard_map/ppermute | solution.py:470
  41.8 5.9 %collective-permute-start.5 = (f32[2,96,96]{2,1,0:T(8,128)S(1)}, f32[2,96,96]{2,1,0:T(8,128)S(1)}, u32[]{:S(2)}, u32[]{:S(2)}) collective-permute-start(f32[2,96,96]{2,1,0:T(8,128)S(1)} %shard_map.58.refs_0_), channel_id=1, source_target_pairs={{0,4},{1,5},{4,0},{5,1},{8,12},{9,13},{12,8},{13,9},{16,20},{17,21... | collective-permute-start | bytes 221192 | tf_op jit(solution)/shard_map/ppermute | solution.py:470
  44.1 3.7 %collective-permute-start.6 = (f32[2,96,96]{2,1,0:T(8,128)S(1)}, f32[2,96,96]{2,1,0:T(8,128)S(1)}, u32[]{:S(2)}, u32[]{:S(2)}) collective-permute-start(f32[2,96,96]{2,1,0:T(8,128)S(1)} %shard_map.58.refs_0_), channel_id=1, source_target_pairs={{0,5},{1,0},{4,1},{5,4},{8,13},{9,8},{12,9},{13,12},{16,21},{17,16... | collective-permute-start | bytes 221192 | tf_op jit(solution)/shard_map/ppermute | solution.py:470
  47.8 7.0 %copy-start.4 = (f32[2,2,96]{2,1,0:T(2,128)S(1)}, f32[2,2,96]{2,1,0:T(2,128)}, u32[]{:S(2)}) copy-start(f32[2,2,96]{2,1,0:T(2,128)} %param.9) | copy-start | bytes 4612
  48.6 7.4 %collective-permute-start.7 = (f32[2,96,96]{2,1,0:T(8,128)S(1)}, f32[2,96,96]{2,1,0:T(8,128)S(1)}, u32[]{:S(2)}, u32[]{:S(2)}) collective-permute-start(f32[2,96,96]{2,1,0:T(8,128)S(1)} %get-tuple-element.24), channel_id=1, source_target_pairs={{0,8},{1,9},{4,12},{5,13},{8,16},{9,17},{12,20},{13,21},{16,24},{1... | collective-permute-start | bytes 221192 | tf_op jit(solution)/shard_map/ppermute | solution.py:470
  50.8 10.0 %collective-permute-start.8 = (f32[2,96,96]{2,1,0:T(8,128)S(1)}, f32[2,96,96]{2,1,0:T(8,128)S(1)}, u32[]{:S(2)}, u32[]{:S(2)}) collective-permute-start(f32[2,96,96]{2,1,0:T(8,128)S(1)} %get-tuple-element.24), channel_id=1, source_target_pairs={{0,16},{1,17},{4,20},{5,21},{8,24},{9,25},{12,28},{13,29},{16,0},{... | collective-permute-start | bytes 221192 | tf_op jit(solution)/shard_map/ppermute | solution.py:470
  53.4 7.5 %collective-permute-start.9 = (f32[2,96,96]{2,1,0:T(8,128)S(1)}, f32[2,96,96]{2,1,0:T(8,128)S(1)}, u32[]{:S(2)}, u32[]{:S(2)}) collective-permute-start(f32[2,96,96]{2,1,0:T(8,128)S(1)} %get-tuple-element.24), channel_id=1, source_target_pairs={{0,24},{1,25},{4,28},{5,29},{8,0},{9,1},{12,4},{13,5},{16,8},{17,9... | collective-permute-start | bytes 221192 | tf_op jit(solution)/shard_map/ppermute | solution.py:470
  63.1 3.0 %collective-permute-start.10 = (f32[2,2,256]{2,1,0:T(2,128)S(1)}, f32[2,2,256]{2,1,0:T(2,128)S(1)}, u32[]{:S(2)}, u32[]{:S(2)}) collective-permute-start(f32[2,2,256]{2,1,0:T(2,128)S(1)} %get-tuple-element.30), channel_id=1, source_target_pairs={{0,1},{1,2},{2,3},{3,0},{4,5},{5,6},{6,7},{7,4},{8,9},{9,10},{10,1... | collective-permute-start | bytes 12296 | tf_op jit(solution)/shard_map/ppermute | solution.py:418
  63.1 3.7 %collective-permute-start.11 = (f32[2,2,256]{2,1,0:T(2,128)S(1)}, f32[2,2,256]{2,1,0:T(2,128)S(1)}, u32[]{:S(2)}, u32[]{:S(2)}) collective-permute-start(f32[2,2,256]{2,1,0:T(2,128)S(1)} %get-tuple-element.31), channel_id=1, source_target_pairs={{0,2},{1,3},{2,0},{3,1},{4,6},{5,7},{6,4},{7,5},{8,10},{9,11},{10,... | collective-permute-start | bytes 12296 | tf_op jit(solution)/shard_map/ppermute | solution.py:418
  64.6 2.8 %collective-permute-start.12 = (f32[2,2,256]{2,1,0:T(2,128)S(1)}, f32[2,2,256]{2,1,0:T(2,128)S(1)}, u32[]{:S(2)}, u32[]{:S(2)}) collective-permute-start(f32[2,2,256]{2,1,0:T(2,128)S(1)} %get-tuple-element.32), channel_id=1, source_target_pairs={{0,3},{1,0},{2,1},{3,2},{4,7},{5,4},{6,5},{7,6},{8,11},{9,8},{10,9... | collective-permute-start | bytes 12296 | tf_op jit(solution)/shard_map/ppermute | solution.py:418

commit v8 on v7

--- a/solution.py
+++ b/solution.py
@@ -175,13 +175,28 @@
 DOWN = 2.0**-13
 
 
-def pack_body(modes, seg_count, start_ref, base_ref, perturb_ref, out_ref):
-    out_ref[0:modes, :] = start_ref[...]
-    out_ref[modes : modes + 1, :] = base_ref[...]
-    out_ref[modes + 1 : modes + 1 + seg_count, :] = perturb_ref[...]
-    rest = out_ref.shape[0] - (modes + 1 + seg_count)
+def pack_body(modes, start_ref, base_ref, perturb_ref, out_ref, base_buf, perturb_buf, sems):
+    copies = [
+        pltpu.make_async_copy(source, target, sems.at[i])
+        for i, (source, target) in enumerate(
+            (
+                (start_ref, out_ref.at[0:modes]),
+                (base_ref, base_buf),
+                (perturb_ref, perturb_buf),
+            )
+        )
+    ]
+    for copy in copies:
+        copy.start()
+    copies[1].wait()
+    copies[2].wait()
+    seg_count = perturb_ref.shape[0]
+    rest = out_ref.shape[0] - modes - 1 - seg_count
+    lines = [base_buf[...], perturb_buf[...]]
     if rest:
-        out_ref[modes + 1 + seg_count :, :] = jnp.zeros((rest, out_ref.shape[1]), jnp.float32)
+        lines.append(jnp.zeros((rest, out_ref.shape[1]), jnp.float32))
+    out_ref[modes:, :] = jnp.concatenate(lines, axis=0)
+    copies[0].wait()
 
 
 def iterate_body(n_alt, chunk, seg_count, modes, width, scale_ref, *refs):
@@ -357,24 +372,39 @@
     refs[-1][0], refs[-1][1] = fold(spans)
 
 
-def turn_vector(matrix, vector):
-    rows = lax.broadcasted_iota(jnp.int32, vector.shape, 0)
-    swapped = jnp.where(
-        rows == 0, -row_of(vector, 1), jnp.where(rows == 1, row_of(vector, 0), 0.0)
-    )
-    return mmt(vector, matrix[0]) + mmt(swapped, matrix[1])
-
-
-def field_body(halves, group, backs, n_alt, width, scale, source_ref, *refs):
-    count = len(backs)
-    inside_ref, first_ref, second_ref = refs[count : count + 3]
+def group_span(halves, group, back, ref):
+    there = chain_place(halves) // group >= back
+    return jnp.where(there, ref[0], unit_of(ref.shape[1])), jnp.where(there, ref[1], 0.0)
+
+
+def merge_body(halves, group, back, last, inside_ref, span_ref, out_ref):
+    span = group_span(halves, group, back, span_ref)
+    for i in range(2):
+        merged = complex_mm((inside_ref[i, 0], inside_ref[i, 1]), span)
+        for part in range(2):
+            out_ref[i, part] = merged[part].T if last else merged[part]
+
+
+def field_body(halves, group, back, n_alt, width, scale, source_ref, *refs):
+    span_ref, inside_ref, first_ref, second_ref = refs[:4]
     place = lax.axis_index("alt")
-    amp = source_ref[place // halves]
-    for back, ref in reversed(list(zip(backs, refs))):
-        moved = turn_vector((ref[0], ref[1]), amp)
-        amp = jnp.where(chain_place(halves) // group < back, amp, moved)
-    amps = [turn_vector((inside_ref[i, 0], inside_ref[i, 1]), amp) for i in range(2)]
-    for k, out_ref in enumerate(refs[count + 3 :]):
+    source = source_ref[place // halves]
+    real, imag = source[0:1, :], source[1:2, :]
+    left, right = group_span(halves, group, back, span_ref)
+    came = (
+        jnp.sum(left * real - right * imag, axis=1, keepdims=True),
+        jnp.sum(left * imag + right * real, axis=1, keepdims=True),
+    )
+    rows = lax.broadcasted_iota(jnp.int32, source.shape, 0)
+    amps = []
+    for i in range(2):
+        left, right = inside_ref[i, 0], inside_ref[i, 1]
+        amp = (
+            jnp.sum(left * came[0] - right * came[1], axis=0, keepdims=True),
+            jnp.sum(left * came[1] + right * came[0], axis=0, keepdims=True),
+        )
+        amps.append(jnp.where(rows == 0, amp[0], jnp.where(rows == 1, amp[1], 0.0)))
+    for k, out_ref in enumerate(refs[4:]):
         target = lax.rem(place + k, n_alt)
         span = pl.ds(pl.multiple_of(target * width, width), width)
         for i, ref in enumerate((first_ref, second_ref)):
@@ -402,7 +432,8 @@
     chunk = freqs * seg_count // n_alt
     halves = seg_count // chunk
     length = n_range * halves
-    assert n_alt & (n_alt - 1) == 0 and modes == 2 * HALF and chunk == 2 and halves * chunk == seg_count and halves * freqs == n_alt
+    assert n_alt & (n_alt - 1) == 0 and modes == 2 * HALF
+    assert chunk == 2 and halves * chunk == seg_count and halves * freqs == n_alt
 
     def device(freq, at):
         return at // halves * n_alt + freq * halves + at % halves
@@ -418,10 +449,15 @@
         return lax.ppermute(value, "alt", [(i, (i + k) % n_alt) for i in range(n_alt)])
 
     mine = kernel_call(
-        functools.partial(pack_body, modes, seg_count),
+        functools.partial(pack_body, modes),
         shape(-(-(modes + 1 + seg_count) // 8) * 8, width),
         [start_block, base_profile[None, :], perturb],
-        [VM] * 3,
+        [pl.BlockSpec(memory_space=pl.ANY)] * 3,
+        [
+            pltpu.VMEM((1, width), jnp.float32),
+            pltpu.VMEM((seg_count, width), jnp.float32),
+            pltpu.SemaphoreType.DMA((3,)),
+        ],
     )
     found, bit = {0: mine}, n_alt
     while bit > 1:
@@ -459,7 +495,7 @@
 
     group = 4
     groups = length // group
-    assert groups * group == length
+    assert groups * group == length and groups > 2
 
     def turned(value, size, k):
         pairs = []
@@ -510,13 +546,27 @@
         flops=flops,
     )
     rows = jnp.concatenate([source, jnp.zeros((freqs, 6, modes), jnp.float32)], axis=1)
+    for at, back in enumerate(backs[:-1]):
+        inside = kernel_call(
+            functools.partial(merge_body, halves, group, back, at == len(backs) - 2),
+            shape(2, 2, modes, modes),
+            [inside, came[at]],
+            [VM] * 2,
+            flops=flops,
+        )
     parts = kernel_call(
         functools.partial(
-            field_body, halves, group, backs, n_alt, width, (float(total) / float(modes)) ** 0.5
+            field_body,
+            halves,
+            group,
+            backs[-1],
+            n_alt,
+            width,
+            (float(total) / float(modes)) ** 0.5,
         ),
         [shape(chunk, 2, width)] * n_alt,
-        [rows] + came + [inside, first, second],
-        [VM] * (4 + len(came)),
+        [rows, came[-1], inside, first, second],
+        [VM] * 5,
     )
     parts = [parts[0]] + [around(parts[k], k) for k in range(1, n_alt)]
     return kernel_call(

time: 68.5 us -> 67.4 us (0.984)
    pallas_call x8 -> x10, Pallas kernels: 34.5 us -> 34.1 us  [kernel_call(): pl.pallas_call(body, out_shape=out_shape, in_specs=specs, out_specs=jax.t...]
  transfers between devices with their start and end apart: 13 -> 13, of which waited for: 11 -> 10; matrix products, arithmetic and copies ran while one was open for 0% -> 0% of each run, Pallas kernels for 12% -> 14%
where the time goes in v8:
time: 67.4 us; the launch traced here: 67.1 us
  Pallas kernels  34.1 us (51%)
  starting transfers between devices  17.4 us (26%)
  waiting for transfers between devices  13.3 us (20%)
  local copies, waits for them, and re-layouts  2.27 us (3%)
    pallas_call x10, Pallas kernels, kernel_call(): pl.pallas_call(body, out_shape=out_shape, in_specs=specs, out_specs=jax.t...  34.1 us
    ppermute x6, starting transfers between devices, turned(): return lax.ppermute(value, ('range', 'alt'), pairs)  10.1 us
    ppermute x6, waiting for transfers between devices, turned(): return lax.ppermute(value, ('range', 'alt'), pairs)  7.66 us
    ppermute x3, waiting for transfers between devices, local(): found[key ^ bit] = lax.ppermute(found[key], 'alt', pairs)  4.28 us
    ppermute x3, starting transfers between devices, local(): found[key ^ bit] = lax.ppermute(found[key], 'alt', pairs)  3.01 us
    ppermute x3, starting transfers between devices, around(): lax.ppermute(value, 'alt', [(i, (i + k) % n_alt) for i in range(n_alt)])  2.97 us
    unnamed x10, local copies, waits for them, and re-layouts  2.26 us
  transfers between devices with their start and end apart: 13, of which 10 were waited for; matrix products, arithmetic and copies ran while one was open for 0% of the time, Pallas kernels for 14%

profile of v8, /device:TPU:0, one launch (start us, length us, event | category | flops | bytes accessed | tf_op | source)
XLA Modules:
  0.0 67.1 jit_solution(4899418225688228534)
XLA Ops:
  0.0 0.7 %copy-done.2 = f32[256]{0:T(256)S(1)} copy-done((f32[256]{0:T(256)S(1)}, f32[256]{0:T(256)}, u32[]{:S(2)}) %copy-start.2) | copy-done | bytes 1048
  0.7 0.9 %copy-done = f32[96,256]{1,0:T(8,128)S(1)} copy-done((f32[96,256]{1,0:T(8,128)S(1)}, f32[96,256]{1,0:T(8,128)}, u32[]{:S(2)}) %copy-start) | copy-done | bytes 98328
  1.6 0.7 %copy-done.1 = f32[4,256]{1,0:T(4,128)S(1)} copy-done((f32[4,256]{1,0:T(4,128)S(1)}, f32[4,256]{1,0:T(4,128)}, u32[]{:S(2)}) %copy-start.1) | copy-done | bytes 4120
  2.3 0.1 shard_map.55.refs_0_
  2.4 3.0 %collective-permute-start.1 = (f32[104,256]{1,0:T(8,128)S(1)}, f32[104,256]{1,0:T(8,128)S(1)}, u32[]{:S(2)}, u32[]{:S(2)}) collective-permute-start(f32[104,256]{1,0:T(8,128)S(1)} %shard_map.55.refs_0_), channel_id=1, source_target_pairs={{0,2},{1,3},{2,0},{3,1},{4,6},{5,7},{6,4},{7,5},{8,10},{9,11},{10,... | collective-permute-start | bytes 319496 | tf_op jit(solution)/shard_map/ppermute | solution.py:467
  5.4 3.0 %collective-permute-done.1.refs_2_ = f32[104,256]{1,0:T(8,128)S(1)} collective-permute-done((f32[104,256]{1,0:T(8,128)S(1)}, f32[104,256]{1,0:T(8,128)S(1)}, u32[]{:S(2)}, u32[]{:S(2)}) %collective-permute-start.1) | collective-permute-done | bytes 106528 | tf_op jit(solution)/shard_map/ppermute | solution.py:467
  8.4 1.3 %collective-permute-done.2.refs_3_ = f32[104,256]{1,0:T(8,128)S(1)} collective-permute-done((f32[104,256]{1,0:T(8,128)S(1)}, f32[104,256]{1,0:T(8,128)S(1)}, u32[]{:S(2)}, u32[]{:S(2)}) %collective-permute-start.2) | collective-permute-done | bytes 106528 | tf_op jit(solution)/shard_map/ppermute | solution.py:467
  9.7 21.8 %shard_map.56 = (f32[96,1024]{1,0:T(8,128)S(1)}, f32[96,1024]{1,0:T(8,128)S(1)}, f32[2,1024]{1,0:T(2,128)S(1)}) custom-call(f32[2]{0:T(128)S(1)} %copy-done.3, f32[104,256]{1,0:T(8,128)S(1)} %shard_map.55.refs_0_, f32[104,256]{1,0:T(8,128)S(1)} %collective-permute-done.refs_1_, f32[104,256]{1,0:T(8,128)S(1)} %collective-permute-done.1.refs_2_, ...), custom_call_target="tpu_custom_call" | custom-call | flops 603979776 | bytes 1220616 | tf_op jit(solution)/shard_map/pallas_call | solution.py:45
  31.5 1.3 %collective-permute-start.3 = (f32[96,1024]{1,0:T(8,128)S(1)}, f32[96,1024]{1,0:T(8,128)S(1)}, u32[]{:S(2)}, u32[]{:S(2)}) collective-permute-start(f32[96,1024]{1,0:T(8,128)S(1)} %get-tuple-element.19.refs_0_), channel_id=1, source_target_pairs={{1,0},{4,1},{5,4},{8,5},{9,8},{12,9},{13,12},{16,13},{17,16},{20,1... | collective-permute-start | bytes 1179656 | tf_op jit(solution)/shard_map/ppermute | solution.py:446
  32.8 7.2 %shard_map.57 = (f32[96,1024]{1,0:T(8,128)S(1)}, f32[96,1024]{1,0:T(8,128)S(1)}, f32[96,96]{1,0:T(8,128)S(1)}, f32[2,96,96]{2,1,0:T(8,128)S(1)}, f32[2,96,96]{2,1,0:T(8,128)S(1)}) custom-call(f32[2,1024]{1,0:T(2,128)S(1)} %get-tuple-element.20.coef_ref, f32[96,1024]{1,0:T(8,128)S(1)} %get-tuple-element.19.refs_0_, f32[96,1024]{1,0:T(8,128)S(1)} %get-tuple-element.21.refs_1_), custom_call_target="tpu_custom_call" | custom-call | flops 301989888 | bytes 1765376 | tf_op jit(solution)/shard_map/pallas_call | solution.py:45
  40.0 0.8 %shard_map.58.refs_0_ = f32[2,96,96]{2,1,0:T(8,128)S(1)} custom-call(f32[96,1024]{1,0:T(8,128)S(1)} %collective-permute-done.3.next_ref, f32[96,1024]{1,0:T(8,128)S(1)} %get-tuple-element.22.second_ref.refs_3_, f32[2,96,96]{2,1,0:T(8,128)S(1)} %get-tuple-element.23.rest_ref), custom_call_target="tpu_custom_call" | custom-call | flops 18874368 | bytes 933888 | tf_op jit(solution)/shard_map/pallas_call | solution.py:45
  40.8 1.2 %collective-permute-start.4 = (f32[2,96,96]{2,1,0:T(8,128)S(1)}, f32[2,96,96]{2,1,0:T(8,128)S(1)}, u32[]{:S(2)}, u32[]{:S(2)}) collective-permute-start(f32[2,96,96]{2,1,0:T(8,128)S(1)} %shard_map.58.refs_0_), channel_id=1, source_target_pairs={{0,1},{1,4},{4,5},{5,0},{8,9},{9,12},{12,13},{13,8},{16,17},{17,20... | collective-permute-start | bytes 221192 | tf_op jit(solution)/shard_map/ppermute | solution.py:506
  42.0 2.3 %collective-permute-start.5 = (f32[2,96,96]{2,1,0:T(8,128)S(1)}, f32[2,96,96]{2,1,0:T(8,128)S(1)}, u32[]{:S(2)}, u32[]{:S(2)}) collective-permute-start(f32[2,96,96]{2,1,0:T(8,128)S(1)} %shard_map.58.refs_0_), channel_id=1, source_target_pairs={{0,4},{1,5},{4,0},{5,1},{8,12},{9,13},{12,8},{13,9},{16,20},{17,21... | collective-permute-start | bytes 221192 | tf_op jit(solution)/shard_map/ppermute | solution.py:506
  44.3 0.4 collective-permute-start.6
  44.7 1.9 %collective-permute-done.4.refs_1_ = f32[2,96,96]{2,1,0:T(8,128)S(1)} collective-permute-done((f32[2,96,96]{2,1,0:T(8,128)S(1)}, f32[2,96,96]{2,1,0:T(8,128)S(1)}, u32[]{:S(2)}, u32[]{:S(2)}) %collective-permute-start.4) | collective-permute-done | bytes 73760 | tf_op jit(solution)/shard_map/ppermute | solution.py:506
  46.6 1.3 %collective-permute-done.5.refs_2_ = f32[2,96,96]{2,1,0:T(8,128)S(1)} collective-permute-done((f32[2,96,96]{2,1,0:T(8,128)S(1)}, f32[2,96,96]{2,1,0:T(8,128)S(1)}, u32[]{:S(2)}, u32[]{:S(2)}) %collective-permute-start.5) | collective-permute-done | bytes 73760 | tf_op jit(solution)/shard_map/ppermute | solution.py:506
  47.9 0.1 collective-permute-done.6.refs_3_
  48.0 0.8 %shard_map.59 = (f32[4,2,96,96]{3,2,1,0:T(8,128)S(1)}, f32[2,96,96]{2,1,0:T(8,128)S(1)}) custom-call(f32[2,96,96]{2,1,0:T(8,128)S(1)} %shard_map.58.refs_0_, f32[2,96,96]{2,1,0:T(8,128)S(1)} %collective-permute-done.4.refs_1_, f32[2,96,96]{2,1,0:T(8,128)S(1)} %collective-permute-done.5.refs_2_, f32[2,96,96]{2,1,0:T(8,128)S(1)} %collective-permute-done.6.refs_3_), custom_call_target="tpu_custom_call" | custom-call | flops 18874368 | bytes 663552 | tf_op jit(solution)/shard_map/pallas_call | solution.py:45
  48.8 2.2 %collective-permute-start.8 = (f32[2,96,96]{2,1,0:T(8,128)S(1)}, f32[2,96,96]{2,1,0:T(8,128)S(1)}, u32[]{:S(2)}, u32[]{:S(2)}) collective-permute-start(f32[2,96,96]{2,1,0:T(8,128)S(1)} %get-tuple-element.24), channel_id=1, source_target_pairs={{0,8},{1,9},{4,12},{5,13},{8,16},{9,17},{12,20},{13,21},{16,24},{1... | collective-permute-start | bytes 221192 | tf_op jit(solution)/shard_map/ppermute | solution.py:506
  51.0 2.6 %collective-permute-start.9 = (f32[2,96,96]{2,1,0:T(8,128)S(1)}, f32[2,96,96]{2,1,0:T(8,128)S(1)}, u32[]{:S(2)}, u32[]{:S(2)}) collective-permute-start(f32[2,96,96]{2,1,0:T(8,128)S(1)} %get-tuple-element.24), channel_id=1, source_target_pairs={{0,16},{1,17},{4,20},{5,21},{8,24},{9,25},{12,28},{13,29},{16,0},{... | collective-permute-start | bytes 221192 | tf_op jit(solution)/shard_map/ppermute | solution.py:506
  53.6 1.3 %collective-permute-start.7 = (f32[2,96,96]{2,1,0:T(8,128)S(1)}, f32[2,96,96]{2,1,0:T(8,128)S(1)}, u32[]{:S(2)}, u32[]{:S(2)}) collective-permute-start(f32[2,96,96]{2,1,0:T(8,128)S(1)} %get-tuple-element.24), channel_id=1, source_target_pairs={{0,24},{1,25},{4,28},{5,29},{8,0},{9,1},{12,4},{13,5},{16,8},{17,9... | collective-permute-start | bytes 221192 | tf_op jit(solution)/shard_map/ppermute | solution.py:506
  55.0 1.1 %shard_map.60.inside_ref = f32[2,2,96,96]{3,2,1,0:T(8,128)S(1)} custom-call(f32[4,2,96,96]{3,2,1,0:T(8,128)S(1)} %get-tuple-element.25.sorted_ref, f32[96,96]{1,0:T(8,128)S(1)} %get-tuple-element.26.turn_ref, f32[2,96,96]{2,1,0:T(8,128)S(1)} %get-tuple-element.27.inner_ref), custom_call_target="tpu_custom_call" | custom-call | flops 18874368 | bytes 552960 | tf_op jit(solution)/shard_map/pallas_call | solution.py:45
  56.2 0.5 shard_map.61.inside_ref
  56.7 4.3 %collective-permute-done.9.span_ref = f32[2,96,96]{2,1,0:T(8,128)S(1)} collective-permute-done((f32[2,96,96]{2,1,0:T(8,128)S(1)}, f32[2,96,96]{2,1,0:T(8,128)S(1)}, u32[]{:S(2)}, u32[]{:S(2)}) %collective-permute-start.9) | collective-permute-done | bytes 73760 | tf_op jit(solution)/shard_map/ppermute | solution.py:506
  61.0 0.6 shard_map.62.refs_1_
  61.6 0.6 shard_map.63
  62.2 1.5 %collective-permute-start.11 = (f32[2,2,256]{2,1,0:T(2,128)S(1)}, f32[2,2,256]{2,1,0:T(2,128)S(1)}, u32[]{:S(2)}, u32[]{:S(2)}) collective-permute-start(f32[2,2,256]{2,1,0:T(2,128)S(1)} %get-tuple-element.31), channel_id=1, source_target_pairs={{0,2},{1,3},{2,0},{3,1},{4,6},{5,7},{6,4},{7,5},{8,10},{9,11},{10,... | collective-permute-start | bytes 12296 | tf_op jit(solution)/shard_map/ppermute | solution.py:449
  63.7 1.4 %collective-permute-start.12 = (f32[2,2,256]{2,1,0:T(2,128)S(1)}, f32[2,2,256]{2,1,0:T(2,128)S(1)}, u32[]{:S(2)}, u32[]{:S(2)}) collective-permute-start(f32[2,2,256]{2,1,0:T(2,128)S(1)} %get-tuple-element.32), channel_id=1, source_target_pairs={{0,3},{1,0},{2,1},{3,2},{4,7},{5,4},{6,5},{7,6},{8,11},{9,8},{10,9... | collective-permute-start | bytes 12296 | tf_op jit(solution)/shard_map/ppermute | solution.py:449
  65.1 0.1 collective-permute-done.10.refs_1_
  65.2 0.6 collective-permute-done.11.refs_2_
  65.8 0.6 collective-permute-done.12.refs_3_
  66.5 0.6 shard_map.64
  (15 shorter events, 0.2 us)
Async XLA Ops:
  0.0 0.7 %copy-start.2 = (f32[256]{0:T(256)S(1)}, f32[256]{0:T(256)}, u32[]{:S(2)}) copy-start(f32[256]{0:T(256)} %param.6) | copy-start | bytes 3076
  0.7 0.9 %copy-start = (f32[96,256]{1,0:T(8,128)S(1)}, f32[96,256]{1,0:T(8,128)}, u32[]{:S(2)}) copy-start(f32[96,256]{1,0:T(8,128)} %start_ref.1) | copy-start | bytes 294916
  1.6 0.7 %copy-start.1 = (f32[4,256]{1,0:T(4,128)S(1)}, f32[4,256]{1,0:T(4,128)}, u32[]{:S(2)}) copy-start(f32[4,256]{1,0:T(4,128)} %perturb_ref.1) | copy-start | bytes 12292
  2.3 7.4 %copy-start.3 = (f32[2]{0:T(128)S(1)}, f32[2]{0:T(128)}, u32[]{:S(2)}) copy-start(f32[2]{0:T(128)} %scale_ref.1) | copy-start | bytes 28
  2.4 6.0 %collective-permute-start.1 = (f32[104,256]{1,0:T(8,128)S(1)}, f32[104,256]{1,0:T(8,128)S(1)}, u32[]{:S(2)}, u32[]{:S(2)}) collective-permute-start(f32[104,256]{1,0:T(8,128)S(1)} %shard_map.55.refs_0_), channel_id=1, source_target_pairs={{0,2},{1,3},{2,0},{3,1},{4,6},{5,7},{6,4},{7,5},{8,10},{9,11},{10,... | collective-permute-start | bytes 319496 | tf_op jit(solution)/shard_map/ppermute | solution.py:467
  5.4 3.0 %collective-permute-start = (f32[104,256]{1,0:T(8,128)S(1)}, f32[104,256]{1,0:T(8,128)S(1)}, u32[]{:S(2)}, u32[]{:S(2)}) collective-permute-start(f32[104,256]{1,0:T(8,128)S(1)} %shard_map.55.refs_0_), channel_id=1, source_target_pairs={{0,1},{1,0},{2,3},{3,2},{4,5},{5,4},{6,7},{7,6},{8,9},{9,8},{10,11... | collective-permute-start | bytes 319496 | tf_op jit(solution)/shard_map/ppermute | solution.py:467
  8.4 1.3 %collective-permute-start.2 = (f32[104,256]{1,0:T(8,128)S(1)}, f32[104,256]{1,0:T(8,128)S(1)}, u32[]{:S(2)}, u32[]{:S(2)}) collective-permute-start(f32[104,256]{1,0:T(8,128)S(1)} %collective-permute-done.1.refs_2_), channel_id=1, source_target_pairs={{0,1},{1,0},{2,3},{3,2},{4,5},{5,4},{6,7},{7,6},{8,9},{9,8},{10,11... | collective-permute-start | bytes 319496 | tf_op jit(solution)/shard_map/ppermute | solution.py:467
  31.5 8.5 %collective-permute-start.3 = (f32[96,1024]{1,0:T(8,128)S(1)}, f32[96,1024]{1,0:T(8,128)S(1)}, u32[]{:S(2)}, u32[]{:S(2)}) collective-permute-start(f32[96,1024]{1,0:T(8,128)S(1)} %get-tuple-element.19.refs_0_), channel_id=1, source_target_pairs={{1,0},{4,1},{5,4},{8,5},{9,8},{12,9},{13,12},{16,13},{17,16},{20,1... | collective-permute-start | bytes 1179656 | tf_op jit(solution)/shard_map/ppermute | solution.py:446
  40.8 5.8 %collective-permute-start.4 = (f32[2,96,96]{2,1,0:T(8,128)S(1)}, f32[2,96,96]{2,1,0:T(8,128)S(1)}, u32[]{:S(2)}, u32[]{:S(2)}) collective-permute-start(f32[2,96,96]{2,1,0:T(8,128)S(1)} %shard_map.58.refs_0_), channel_id=1, source_target_pairs={{0,1},{1,4},{4,5},{5,0},{8,9},{9,12},{12,13},{13,8},{16,17},{17,20... | collective-permute-start | bytes 221192 | tf_op jit(solution)/shard_map/ppermute | solution.py:506
  42.0 5.9 %collective-permute-start.5 = (f32[2,96,96]{2,1,0:T(8,128)S(1)}, f32[2,96,96]{2,1,0:T(8,128)S(1)}, u32[]{:S(2)}, u32[]{:S(2)}) collective-permute-start(f32[2,96,96]{2,1,0:T(8,128)S(1)} %shard_map.58.refs_0_), channel_id=1, source_target_pairs={{0,4},{1,5},{4,0},{5,1},{8,12},{9,13},{12,8},{13,9},{16,20},{17,21... | collective-permute-start | bytes 221192 | tf_op jit(solution)/shard_map/ppermute | solution.py:506
  44.3 3.7 %collective-permute-start.6 = (f32[2,96,96]{2,1,0:T(8,128)S(1)}, f32[2,96,96]{2,1,0:T(8,128)S(1)}, u32[]{:S(2)}, u32[]{:S(2)}) collective-permute-start(f32[2,96,96]{2,1,0:T(8,128)S(1)} %shard_map.58.refs_0_), channel_id=1, source_target_pairs={{0,5},{1,0},{4,1},{5,4},{8,13},{9,8},{12,9},{13,12},{16,21},{17,16... | collective-permute-start | bytes 221192 | tf_op jit(solution)/shard_map/ppermute | solution.py:506
  48.0 7.0 %copy-start.4 = (f32[2,2,96]{2,1,0:T(2,128)S(1)}, f32[2,2,96]{2,1,0:T(2,128)}, u32[]{:S(2)}) copy-start(f32[2,2,96]{2,1,0:T(2,128)} %param.9) | copy-start | bytes 4612
  48.8 7.4 %collective-permute-start.8 = (f32[2,96,96]{2,1,0:T(8,128)S(1)}, f32[2,96,96]{2,1,0:T(8,128)S(1)}, u32[]{:S(2)}, u32[]{:S(2)}) collective-permute-start(f32[2,96,96]{2,1,0:T(8,128)S(1)} %get-tuple-element.24), channel_id=1, source_target_pairs={{0,8},{1,9},{4,12},{5,13},{8,16},{9,17},{12,20},{13,21},{16,24},{1... | collective-permute-start | bytes 221192 | tf_op jit(solution)/shard_map/ppermute | solution.py:506
  51.0 10.0 %collective-permute-start.9 = (f32[2,96,96]{2,1,0:T(8,128)S(1)}, f32[2,96,96]{2,1,0:T(8,128)S(1)}, u32[]{:S(2)}, u32[]{:S(2)}) collective-permute-start(f32[2,96,96]{2,1,0:T(8,128)S(1)} %get-tuple-element.24), channel_id=1, source_target_pairs={{0,16},{1,17},{4,20},{5,21},{8,24},{9,25},{12,28},{13,29},{16,0},{... | collective-permute-start | bytes 221192 | tf_op jit(solution)/shard_map/ppermute | solution.py:506
  53.6 8.0 %collective-permute-start.7 = (f32[2,96,96]{2,1,0:T(8,128)S(1)}, f32[2,96,96]{2,1,0:T(8,128)S(1)}, u32[]{:S(2)}, u32[]{:S(2)}) collective-permute-start(f32[2,96,96]{2,1,0:T(8,128)S(1)} %get-tuple-element.24), channel_id=1, source_target_pairs={{0,24},{1,25},{4,28},{5,29},{8,0},{9,1},{12,4},{13,5},{16,8},{17,9... | collective-permute-start | bytes 221192 | tf_op jit(solution)/shard_map/ppermute | solution.py:506
  62.2 3.0 %collective-permute-start.10 = (f32[2,2,256]{2,1,0:T(2,128)S(1)}, f32[2,2,256]{2,1,0:T(2,128)S(1)}, u32[]{:S(2)}, u32[]{:S(2)}) collective-permute-start(f32[2,2,256]{2,1,0:T(2,128)S(1)} %get-tuple-element.30), channel_id=1, source_target_pairs={{0,1},{1,2},{2,3},{3,0},{4,5},{5,6},{6,7},{7,4},{8,9},{9,10},{10,1... | collective-permute-start | bytes 12296 | tf_op jit(solution)/shard_map/ppermute | solution.py:449
  62.2 3.6 %collective-permute-start.11 = (f32[2,2,256]{2,1,0:T(2,128)S(1)}, f32[2,2,256]{2,1,0:T(2,128)S(1)}, u32[]{:S(2)}, u32[]{:S(2)}) collective-permute-start(f32[2,2,256]{2,1,0:T(2,128)S(1)} %get-tuple-element.31), channel_id=1, source_target_pairs={{0,2},{1,3},{2,0},{3,1},{4,6},{5,7},{6,4},{7,5},{8,10},{9,11},{10,... | collective-permute-start | bytes 12296 | tf_op jit(solution)/shard_map/ppermute | solution.py:449
  63.7 2.7 %collective-permute-start.12 = (f32[2,2,256]{2,1,0:T(2,128)S(1)}, f32[2,2,256]{2,1,0:T(2,128)S(1)}, u32[]{:S(2)}, u32[]{:S(2)}) collective-permute-start(f32[2,2,256]{2,1,0:T(2,128)S(1)} %get-tuple-element.32), channel_id=1, source_target_pairs={{0,3},{1,0},{2,1},{3,2},{4,7},{5,4},{6,5},{7,6},{8,11},{9,8},{10,9... | collective-permute-start | bytes 12296 | tf_op jit(solution)/shard_map/ppermute | solution.py:449

commit v9 on v8

--- a/solution.py
+++ b/solution.py
@@ -332,13 +332,17 @@
         out_ref[part] = mm(corr, rest_ref[part])
 
 
-def group_body(halves, group, *refs):
-    at = lax.rem(chain_place(halves), group)
-    sorted_ref, out_ref = refs[group:]
-    for k, ref in enumerate(refs[:group]):
-        sorted_ref[lax.rem(at + group - k, group)] = ref[...]
-    spans = [(sorted_ref[j, 0], sorted_ref[j, 1]) for j in reversed(range(group))]
-    out_ref[0], out_ref[1] = fold(spans)
+def later_half(halves, bit):
+    return lax.rem(chain_place(halves) // bit, 2) == 1
+
+
+def pair_body(halves, bit, own_ref, other_ref, out_ref):
+    later = later_half(halves, bit)
+    own, other = (own_ref[0], own_ref[1]), (other_ref[0], other_ref[1])
+    pairs = list(zip(own, other))
+    out_ref[0], out_ref[1] = complex_mm(
+        [jnp.where(later, a, b) for a, b in pairs], [jnp.where(later, b, a) for a, b in pairs]
+    )
 
 
 def fold(spans):
@@ -348,13 +352,13 @@
     return spans[0]
 
 
-def inside_body(halves, group, sorted_ref, turn_ref, inner_ref, out_ref):
-    at = lax.rem(chain_place(halves), group)
+def inside_body(halves, bits, *refs):
+    turn_ref, inner_ref, out_ref = refs[len(bits) :]
     unit = unit_of(inner_ref.shape[1])
     spans = []
-    for j in reversed(range(group - 1)):
-        real = jnp.where(j < at, sorted_ref[j, 0], unit)
-        spans.append((real, jnp.where(j < at, sorted_ref[j, 1], 0.0)))
+    for bit, ref in zip(bits, refs):
+        later = later_half(halves, bit)
+        spans.append((jnp.where(later, ref[0], unit), jnp.where(later, ref[1], 0.0)))
     reached = fold(spans)
     reached = (mm(turn_ref[...], reached[0]), mm(turn_ref[...], reached[1]))
     following = complex_mm((inner_ref[0], inner_ref[1]), reached)
@@ -452,7 +456,7 @@
         functools.partial(pack_body, modes),
         shape(-(-(modes + 1 + seg_count) // 8) * 8, width),
         [start_block, base_profile[None, :], perturb],
-        [pl.BlockSpec(memory_space=pl.ANY)] * 3,
+        [pl.BlockSpec(memory_space=pltpu.HBM)] * 3,
         [
             pltpu.VMEM((1, width), jnp.float32),
             pltpu.VMEM((seg_count, width), jnp.float32),
@@ -505,13 +509,21 @@
                 pairs.append((device(freq, at), device(freq, goal)))
         return lax.ppermute(value, ("range", "alt"), pairs)
 
-    ordered, span = kernel_call(
-        functools.partial(group_body, halves, group),
-        [shape(group, 2, modes, modes), shape(2, modes, modes)],
-        [product] + [turned(product, group, k) for k in range(1, group)],
-        [VM] * group,
-        flops=flops,
-    )
+    span, beside, bits = product, [], (1, 2)
+    for bit in bits:
+        pairs = [
+            (device(freq, at), device(freq, at ^ bit))
+            for freq in range(freqs)
+            for at in range(length)
+        ]
+        beside.append(lax.ppermute(span, ("range", "alt"), pairs))
+        span = kernel_call(
+            functools.partial(pair_body, halves, bit),
+            shape(2, modes, modes),
+            [span, beside[-1]],
+            [VM] * 2,
+            flops=flops,
+        )
 
     def join(spans, backs):
         return kernel_call(
@@ -539,10 +551,10 @@
         backs = range(0, groups, reach)
         came = from_back(backs)
     inside = kernel_call(
-        functools.partial(inside_body, halves, group),
+        functools.partial(inside_body, halves, bits),
         shape(2, 2, modes, modes),
-        [ordered, turn, inner],
-        [VM] * 3,
+        beside + [turn, inner],
+        [VM] * 4,
         flops=flops,
     )
     rows = jnp.concatenate([source, jnp.zeros((freqs, 6, modes), jnp.float32)], axis=1)

time: 67.4 us -> 66.7 us (0.990)
  starting transfers between devices: 17.4 us -> 15.9 us
  waiting for transfers between devices: 13.3 us -> 14.6 us
    ppermute x0 -> x2, waiting for transfers between devices: none -> 4.25 us  [local(): beside.append(lax.ppermute(span, ('range', 'alt'), pairs))]
    ppermute x6 -> x3, waiting for transfers between devices: 7.66 us -> 3.54 us  [turned(): return lax.ppermute(value, ('range', 'alt'), pairs)]
    ppermute x6 -> x3, starting transfers between devices: 10.1 us -> 6.06 us  [turned(): return lax.ppermute(value, ('range', 'alt'), pairs)]
    ppermute x0 -> x2, starting transfers between devices: none -> 3.58 us  [local(): beside.append(lax.ppermute(span, ('range', 'alt'), pairs))]
    ppermute x3, waiting for transfers between devices: 1.33 us -> 2.52 us  [around(): lax.ppermute(value, 'alt', [(i, (i + k) % n_alt) for i in range(n_alt)])]
    ppermute x3, starting transfers between devices: 2.97 us -> 2.01 us  [around(): lax.ppermute(value, 'alt', [(i, (i + k) % n_alt) for i in range(n_alt)])]
    pallas_call x10 -> x11, Pallas kernels: 34.1 us -> 33.6 us  [kernel_call(): pl.pallas_call(body, out_shape=out_shape, in_specs=specs, out_specs=jax.t...]
  transfers between devices with their start and end apart: 13 -> 12, of which waited for: 10 -> 8; matrix products, arithmetic and copies ran while one was open for 0% -> 0% of each run, Pallas kernels for 14% -> 14%
where the time goes in v9:
time: 66.7 us; the launch traced here: 66.5 us
  Pallas kernels  33.6 us (50%)
  starting transfers between devices  15.9 us (24%)
  waiting for transfers between devices  14.6 us (22%)
  local copies, waits for them, and re-layouts  2.27 us (3%)
    pallas_call x11, Pallas kernels, kernel_call(): pl.pallas_call(body, out_shape=out_shape, in_specs=specs, out_specs=jax.t...  33.6 us
    ppermute x3, starting transfers between devices, turned(): return lax.ppermute(value, ('range', 'alt'), pairs)  6.06 us
    ppermute x3, waiting for transfers between devices, local(): found[key ^ bit] = lax.ppermute(found[key], 'alt', pairs)  4.28 us
    ppermute x2, waiting for transfers between devices, local(): beside.append(lax.ppermute(span, ('range', 'alt'), pairs))  4.25 us
    ppermute x2, starting transfers between devices, local(): beside.append(lax.ppermute(span, ('range', 'alt'), pairs))  3.58 us
    ppermute x3, waiting for transfers between devices, turned(): return lax.ppermute(value, ('range', 'alt'), pairs)  3.54 us
    ppermute x3, starting transfers between devices, local(): found[key ^ bit] = lax.ppermute(found[key], 'alt', pairs)  3.01 us
    ppermute x3, waiting for transfers between devices, around(): lax.ppermute(value, 'alt', [(i, (i + k) % n_alt) for i in range(n_alt)])  2.52 us
  transfers between devices with their start and end apart: 12, of which 8 were waited for; matrix products, arithmetic and copies ran while one was open for 0% of the time, Pallas kernels for 14%

profile of v9, /device:TPU:0, one launch (start us, length us, event | category | flops | bytes accessed | tf_op | source)
XLA Modules:
  0.0 66.5 jit_solution(16004621634827383380)
XLA Ops:
  0.0 0.7 %copy-done.2 = f32[256]{0:T(256)S(1)} copy-done((f32[256]{0:T(256)S(1)}, f32[256]{0:T(256)}, u32[]{:S(2)}) %copy-start.2) | copy-done | bytes 1048
  0.7 0.9 %copy-done = f32[96,256]{1,0:T(8,128)S(1)} copy-done((f32[96,256]{1,0:T(8,128)S(1)}, f32[96,256]{1,0:T(8,128)}, u32[]{:S(2)}) %copy-start) | copy-done | bytes 98328
  1.6 0.7 %copy-done.1 = f32[4,256]{1,0:T(4,128)S(1)} copy-done((f32[4,256]{1,0:T(4,128)S(1)}, f32[4,256]{1,0:T(4,128)}, u32[]{:S(2)}) %copy-start.1) | copy-done | bytes 4120
  2.3 0.1 shard_map.55.refs_0_
  2.4 3.0 %collective-permute-start.1 = (f32[104,256]{1,0:T(8,128)S(1)}, f32[104,256]{1,0:T(8,128)S(1)}, u32[]{:S(2)}, u32[]{:S(2)}) collective-permute-start(f32[104,256]{1,0:T(8,128)S(1)} %shard_map.55.refs_0_), channel_id=1, source_target_pairs={{0,2},{1,3},{2,0},{3,1},{4,6},{5,7},{6,4},{7,5},{8,10},{9,11},{10,... | collective-permute-start | bytes 319496 | tf_op jit(solution)/shard_map/ppermute | solution.py:471
  5.4 3.0 %collective-permute-done.1.refs_2_ = f32[104,256]{1,0:T(8,128)S(1)} collective-permute-done((f32[104,256]{1,0:T(8,128)S(1)}, f32[104,256]{1,0:T(8,128)S(1)}, u32[]{:S(2)}, u32[]{:S(2)}) %collective-permute-start.1) | collective-permute-done | bytes 106528 | tf_op jit(solution)/shard_map/ppermute | solution.py:471
  8.4 1.3 %collective-permute-done.2.refs_3_ = f32[104,256]{1,0:T(8,128)S(1)} collective-permute-done((f32[104,256]{1,0:T(8,128)S(1)}, f32[104,256]{1,0:T(8,128)S(1)}, u32[]{:S(2)}, u32[]{:S(2)}) %collective-permute-start.2) | collective-permute-done | bytes 106528 | tf_op jit(solution)/shard_map/ppermute | solution.py:471
  9.7 21.8 %shard_map.56 = (f32[96,1024]{1,0:T(8,128)S(1)}, f32[96,1024]{1,0:T(8,128)S(1)}, f32[2,1024]{1,0:T(2,128)S(1)}) custom-call(f32[2]{0:T(128)S(1)} %copy-done.3, f32[104,256]{1,0:T(8,128)S(1)} %shard_map.55.refs_0_, f32[104,256]{1,0:T(8,128)S(1)} %collective-permute-done.refs_1_, f32[104,256]{1,0:T(8,128)S(1)} %collective-permute-done.1.refs_2_, ...), custom_call_target="tpu_custom_call" | custom-call | flops 603979776 | bytes 1220616 | tf_op jit(solution)/shard_map/pallas_call | solution.py:45
  31.5 1.3 %collective-permute-start.3 = (f32[96,1024]{1,0:T(8,128)S(1)}, f32[96,1024]{1,0:T(8,128)S(1)}, u32[]{:S(2)}, u32[]{:S(2)}) collective-permute-start(f32[96,1024]{1,0:T(8,128)S(1)} %get-tuple-element.17.refs_0_), channel_id=1, source_target_pairs={{1,0},{4,1},{5,4},{8,5},{9,8},{12,9},{13,12},{16,13},{17,16},{20,1... | collective-permute-start | bytes 1179656 | tf_op jit(solution)/shard_map/ppermute | solution.py:450
  32.8 7.2 %shard_map.57 = (f32[96,1024]{1,0:T(8,128)S(1)}, f32[96,1024]{1,0:T(8,128)S(1)}, f32[96,96]{1,0:T(8,128)S(1)}, f32[2,96,96]{2,1,0:T(8,128)S(1)}, f32[2,96,96]{2,1,0:T(8,128)S(1)}) custom-call(f32[2,1024]{1,0:T(2,128)S(1)} %get-tuple-element.18.coef_ref, f32[96,1024]{1,0:T(8,128)S(1)} %get-tuple-element.17.refs_0_, f32[96,1024]{1,0:T(8,128)S(1)} %get-tuple-element.19.refs_1_), custom_call_target="tpu_custom_call" | custom-call | flops 301989888 | bytes 1765376 | tf_op jit(solution)/shard_map/pallas_call | solution.py:45
  40.0 0.8 %shard_map.58.own_ref = f32[2,96,96]{2,1,0:T(8,128)S(1)} custom-call(f32[96,1024]{1,0:T(8,128)S(1)} %collective-permute-done.3.next_ref, f32[96,1024]{1,0:T(8,128)S(1)} %get-tuple-element.20.second_ref.refs_3_, f32[2,96,96]{2,1,0:T(8,128)S(1)} %get-tuple-element.21.rest_ref), custom_call_target="tpu_custom_call" | custom-call | flops 18874368 | bytes 933888 | tf_op jit(solution)/shard_map/pallas_call | solution.py:45
  40.8 1.2 %collective-permute-start.4 = (f32[2,96,96]{2,1,0:T(8,128)S(1)}, f32[2,96,96]{2,1,0:T(8,128)S(1)}, u32[]{:S(2)}, u32[]{:S(2)}) collective-permute-start(f32[2,96,96]{2,1,0:T(8,128)S(1)} %shard_map.58.own_ref), channel_id=1, source_target_pairs={{0,1},{1,0},{4,5},{5,4},{8,9},{9,8},{12,13},{13,12},{16,17},{17,16... | collective-permute-start | bytes 221192 | tf_op jit(solution)/shard_map/ppermute | solution.py:519
  42.0 0.9 %collective-permute-done.4.other_ref.refs_0_ = f32[2,96,96]{2,1,0:T(8,128)S(1)} collective-permute-done((f32[2,96,96]{2,1,0:T(8,128)S(1)}, f32[2,96,96]{2,1,0:T(8,128)S(1)}, u32[]{:S(2)}, u32[]{:S(2)}) %collective-permute-start.4) | collective-permute-done | bytes 73760 | tf_op jit(solution)/shard_map/ppermute | solution.py:519
  42.9 0.3 shard_map.59.own_ref
  43.2 0.0 copy-start.4
  43.3 2.4 %collective-permute-start.5 = (f32[2,96,96]{2,1,0:T(8,128)S(1)}, f32[2,96,96]{2,1,0:T(8,128)S(1)}, u32[]{:S(2)}, u32[]{:S(2)}) collective-permute-start(f32[2,96,96]{2,1,0:T(8,128)S(1)} %shard_map.59.own_ref), channel_id=1, source_target_pairs={{0,4},{1,5},{4,0},{5,1},{8,12},{9,13},{12,8},{13,9},{16,20},{17,21... | collective-permute-start | bytes 221192 | tf_op jit(solution)/shard_map/ppermute | solution.py:519
  45.6 3.3 %collective-permute-done.5.other_ref.refs_1_ = f32[2,96,96]{2,1,0:T(8,128)S(1)} collective-permute-done((f32[2,96,96]{2,1,0:T(8,128)S(1)}, f32[2,96,96]{2,1,0:T(8,128)S(1)}, u32[]{:S(2)}, u32[]{:S(2)}) %collective-permute-start.5) | collective-permute-done | bytes 73760 | tf_op jit(solution)/shard_map/ppermute | solution.py:519
  48.9 0.3 shard_map.60
  49.3 2.1 %collective-permute-start.7 = (f32[2,96,96]{2,1,0:T(8,128)S(1)}, f32[2,96,96]{2,1,0:T(8,128)S(1)}, u32[]{:S(2)}, u32[]{:S(2)}) collective-permute-start(f32[2,96,96]{2,1,0:T(8,128)S(1)} %shard_map.60), channel_id=1, source_target_pairs={{0,8},{1,9},{4,12},{5,13},{8,16},{9,17},{12,20},{13,21},{16,24},{1... | collective-permute-start | bytes 221192 | tf_op jit(solution)/shard_map/ppermute | solution.py:510
  51.4 2.6 %collective-permute-start.8 = (f32[2,96,96]{2,1,0:T(8,128)S(1)}, f32[2,96,96]{2,1,0:T(8,128)S(1)}, u32[]{:S(2)}, u32[]{:S(2)}) collective-permute-start(f32[2,96,96]{2,1,0:T(8,128)S(1)} %shard_map.60), channel_id=1, source_target_pairs={{0,16},{1,17},{4,20},{5,21},{8,24},{9,25},{12,28},{13,29},{16,0},{... | collective-permute-start | bytes 221192 | tf_op jit(solution)/shard_map/ppermute | solution.py:510
  54.0 1.3 %collective-permute-start.6 = (f32[2,96,96]{2,1,0:T(8,128)S(1)}, f32[2,96,96]{2,1,0:T(8,128)S(1)}, u32[]{:S(2)}, u32[]{:S(2)}) collective-permute-start(f32[2,96,96]{2,1,0:T(8,128)S(1)} %shard_map.60), channel_id=1, source_target_pairs={{0,24},{1,25},{4,28},{5,29},{8,0},{9,1},{12,4},{13,5},{16,8},{17,9... | collective-permute-start | bytes 221192 | tf_op jit(solution)/shard_map/ppermute | solution.py:510
  55.3 0.9 %shard_map.61.inside_ref = f32[2,2,96,96]{3,2,1,0:T(8,128)S(1)} custom-call(f32[2,96,96]{2,1,0:T(8,128)S(1)} %collective-permute-done.4.other_ref.refs_0_, f32[2,96,96]{2,1,0:T(8,128)S(1)} %collective-permute-done.5.other_ref.refs_1_, f32[96,96]{1,0:T(8,128)S(1)} %get-tuple-element.22.refs_2_, f32[2,96,96]{2,1,0:T(8,128)S(1)} %get-tuple-element.23.refs_3_), custom_call_target="tpu_custom_call" | custom-call | flops 18874368 | bytes 405504 | tf_op jit(solution)/shard_map/pallas_call | solution.py:45
  56.2 1.0 %collective-permute-done.7.span_ref = f32[2,96,96]{2,1,0:T(8,128)S(1)} collective-permute-done((f32[2,96,96]{2,1,0:T(8,128)S(1)}, f32[2,96,96]{2,1,0:T(8,128)S(1)}, u32[]{:S(2)}, u32[]{:S(2)}) %collective-permute-start.7) | collective-permute-done | bytes 73760 | tf_op jit(solution)/shard_map/ppermute | solution.py:510
  57.2 0.5 shard_map.62.inside_ref
  57.6 2.6 %collective-permute-done.8.span_ref = f32[2,96,96]{2,1,0:T(8,128)S(1)} collective-permute-done((f32[2,96,96]{2,1,0:T(8,128)S(1)}, f32[2,96,96]{2,1,0:T(8,128)S(1)}, u32[]{:S(2)}, u32[]{:S(2)}) %collective-permute-start.8) | collective-permute-done | bytes 73760 | tf_op jit(solution)/shard_map/ppermute | solution.py:510
  60.2 0.6 shard_map.63.refs_1_
  60.8 0.6 shard_map.64
  61.4 1.5 %collective-permute-start.10 = (f32[2,2,256]{2,1,0:T(2,128)S(1)}, f32[2,2,256]{2,1,0:T(2,128)S(1)}, u32[]{:S(2)}, u32[]{:S(2)}) collective-permute-start(f32[2,2,256]{2,1,0:T(2,128)S(1)} %get-tuple-element.27), channel_id=1, source_target_pairs={{0,2},{1,3},{2,0},{3,1},{4,6},{5,7},{6,4},{7,5},{8,10},{9,11},{10,... | collective-permute-start | bytes 12296 | tf_op jit(solution)/shard_map/ppermute | solution.py:453
  62.9 0.5 collective-permute-start.9
  63.4 1.6 %collective-permute-done.10.refs_2_ = f32[2,2,256]{2,1,0:T(2,128)S(1)} collective-permute-done((f32[2,2,256]{2,1,0:T(2,128)S(1)}, f32[2,2,256]{2,1,0:T(2,128)S(1)}, u32[]{:S(2)}, u32[]{:S(2)}) %collective-permute-start.10) | collective-permute-done | bytes 4128 | tf_op jit(solution)/shard_map/ppermute | solution.py:453
  65.0 0.9 %collective-permute-done.9.refs_1_ = f32[2,2,256]{2,1,0:T(2,128)S(1)} collective-permute-done((f32[2,2,256]{2,1,0:T(2,128)S(1)}, f32[2,2,256]{2,1,0:T(2,128)S(1)}, u32[]{:S(2)}, u32[]{:S(2)}) %collective-permute-start.9) | collective-permute-done | bytes 4128 | tf_op jit(solution)/shard_map/ppermute | solution.py:453
  65.9 0.6 shard_map.65
  (14 shorter events, 0.0 us)
Async XLA Ops:
  0.0 0.7 %copy-start.2 = (f32[256]{0:T(256)S(1)}, f32[256]{0:T(256)}, u32[]{:S(2)}) copy-start(f32[256]{0:T(256)} %param.6) | copy-start | bytes 3076
  0.7 0.9 %copy-start = (f32[96,256]{1,0:T(8,128)S(1)}, f32[96,256]{1,0:T(8,128)}, u32[]{:S(2)}) copy-start(f32[96,256]{1,0:T(8,128)} %start_ref.1) | copy-start | bytes 294916
  1.6 0.7 %copy-start.1 = (f32[4,256]{1,0:T(4,128)S(1)}, f32[4,256]{1,0:T(4,128)}, u32[]{:S(2)}) copy-start(f32[4,256]{1,0:T(4,128)} %perturb_ref.1) | copy-start | bytes 12292
  2.3 7.4 %copy-start.3 = (f32[2]{0:T(128)S(1)}, f32[2]{0:T(128)}, u32[]{:S(2)}) copy-start(f32[2]{0:T(128)} %scale_ref.1) | copy-start | bytes 28
  2.4 6.0 %collective-permute-start.1 = (f32[104,256]{1,0:T(8,128)S(1)}, f32[104,256]{1,0:T(8,128)S(1)}, u32[]{:S(2)}, u32[]{:S(2)}) collective-permute-start(f32[104,256]{1,0:T(8,128)S(1)} %shard_map.55.refs_0_), channel_id=1, source_target_pairs={{0,2},{1,3},{2,0},{3,1},{4,6},{5,7},{6,4},{7,5},{8,10},{9,11},{10,... | collective-permute-start | bytes 319496 | tf_op jit(solution)/shard_map/ppermute | solution.py:471
  5.4 3.0 %collective-permute-start = (f32[104,256]{1,0:T(8,128)S(1)}, f32[104,256]{1,0:T(8,128)S(1)}, u32[]{:S(2)}, u32[]{:S(2)}) collective-permute-start(f32[104,256]{1,0:T(8,128)S(1)} %shard_map.55.refs_0_), channel_id=1, source_target_pairs={{0,1},{1,0},{2,3},{3,2},{4,5},{5,4},{6,7},{7,6},{8,9},{9,8},{10,11... | collective-permute-start | bytes 319496 | tf_op jit(solution)/shard_map/ppermute | solution.py:471
  8.4 1.3 %collective-permute-start.2 = (f32[104,256]{1,0:T(8,128)S(1)}, f32[104,256]{1,0:T(8,128)S(1)}, u32[]{:S(2)}, u32[]{:S(2)}) collective-permute-start(f32[104,256]{1,0:T(8,128)S(1)} %collective-permute-done.1.refs_2_), channel_id=1, source_target_pairs={{0,1},{1,0},{2,3},{3,2},{4,5},{5,4},{6,7},{7,6},{8,9},{9,8},{10,11... | collective-permute-start | bytes 319496 | tf_op jit(solution)/shard_map/ppermute | solution.py:471
  31.5 8.5 %collective-permute-start.3 = (f32[96,1024]{1,0:T(8,128)S(1)}, f32[96,1024]{1,0:T(8,128)S(1)}, u32[]{:S(2)}, u32[]{:S(2)}) collective-permute-start(f32[96,1024]{1,0:T(8,128)S(1)} %get-tuple-element.17.refs_0_), channel_id=1, source_target_pairs={{1,0},{4,1},{5,4},{8,5},{9,8},{12,9},{13,12},{16,13},{17,16},{20,1... | collective-permute-start | bytes 1179656 | tf_op jit(solution)/shard_map/ppermute | solution.py:450
  40.8 2.1 %collective-permute-start.4 = (f32[2,96,96]{2,1,0:T(8,128)S(1)}, f32[2,96,96]{2,1,0:T(8,128)S(1)}, u32[]{:S(2)}, u32[]{:S(2)}) collective-permute-start(f32[2,96,96]{2,1,0:T(8,128)S(1)} %shard_map.58.own_ref), channel_id=1, source_target_pairs={{0,1},{1,0},{4,5},{5,4},{8,9},{9,8},{12,13},{13,12},{16,17},{17,16... | collective-permute-start | bytes 221192 | tf_op jit(solution)/shard_map/ppermute | solution.py:519
  43.2 12.1 %copy-start.4 = (f32[2,2,96]{2,1,0:T(2,128)S(1)}, f32[2,2,96]{2,1,0:T(2,128)}, u32[]{:S(2)}) copy-start(f32[2,2,96]{2,1,0:T(2,128)} %param.9) | copy-start | bytes 4612
  43.3 5.7 %collective-permute-start.5 = (f32[2,96,96]{2,1,0:T(8,128)S(1)}, f32[2,96,96]{2,1,0:T(8,128)S(1)}, u32[]{:S(2)}, u32[]{:S(2)}) collective-permute-start(f32[2,96,96]{2,1,0:T(8,128)S(1)} %shard_map.59.own_ref), channel_id=1, source_target_pairs={{0,4},{1,5},{4,0},{5,1},{8,12},{9,13},{12,8},{13,9},{16,20},{17,21... | collective-permute-start | bytes 221192 | tf_op jit(solution)/shard_map/ppermute | solution.py:519
  49.3 7.9 %collective-permute-start.7 = (f32[2,96,96]{2,1,0:T(8,128)S(1)}, f32[2,96,96]{2,1,0:T(8,128)S(1)}, u32[]{:S(2)}, u32[]{:S(2)}) collective-permute-start(f32[2,96,96]{2,1,0:T(8,128)S(1)} %shard_map.60), channel_id=1, source_target_pairs={{0,8},{1,9},{4,12},{5,13},{8,16},{9,17},{12,20},{13,21},{16,24},{1... | collective-permute-start | bytes 221192 | tf_op jit(solution)/shard_map/ppermute | solution.py:510
  51.4 8.8 %collective-permute-start.8 = (f32[2,96,96]{2,1,0:T(8,128)S(1)}, f32[2,96,96]{2,1,0:T(8,128)S(1)}, u32[]{:S(2)}, u32[]{:S(2)}) collective-permute-start(f32[2,96,96]{2,1,0:T(8,128)S(1)} %shard_map.60), channel_id=1, source_target_pairs={{0,16},{1,17},{4,20},{5,21},{8,24},{9,25},{12,28},{13,29},{16,0},{... | collective-permute-start | bytes 221192 | tf_op jit(solution)/shard_map/ppermute | solution.py:510
  54.0 6.8 %collective-permute-start.6 = (f32[2,96,96]{2,1,0:T(8,128)S(1)}, f32[2,96,96]{2,1,0:T(8,128)S(1)}, u32[]{:S(2)}, u32[]{:S(2)}) collective-permute-start(f32[2,96,96]{2,1,0:T(8,128)S(1)} %shard_map.60), channel_id=1, source_target_pairs={{0,24},{1,25},{4,28},{5,29},{8,0},{9,1},{12,4},{13,5},{16,8},{17,9... | collective-permute-start | bytes 221192 | tf_op jit(solution)/shard_map/ppermute | solution.py:510
  61.4 3.6 %collective-permute-start.10 = (f32[2,2,256]{2,1,0:T(2,128)S(1)}, f32[2,2,256]{2,1,0:T(2,128)S(1)}, u32[]{:S(2)}, u32[]{:S(2)}) collective-permute-start(f32[2,2,256]{2,1,0:T(2,128)S(1)} %get-tuple-element.27), channel_id=1, source_target_pairs={{0,2},{1,3},{2,0},{3,1},{4,6},{5,7},{6,4},{7,5},{8,10},{9,11},{10,... | collective-permute-start | bytes 12296 | tf_op jit(solution)/shard_map/ppermute | solution.py:453
  62.9 2.1 %collective-permute-start.11 = (f32[2,2,256]{2,1,0:T(2,128)S(1)}, f32[2,2,256]{2,1,0:T(2,128)S(1)}, u32[]{:S(2)}, u32[]{:S(2)}) collective-permute-start(f32[2,2,256]{2,1,0:T(2,128)S(1)} %get-tuple-element.28), channel_id=1, source_target_pairs={{0,3},{1,0},{2,1},{3,2},{4,7},{5,4},{6,5},{7,6},{8,11},{9,8},{10,9... | collective-permute-start | bytes 12296 | tf_op jit(solution)/shard_map/ppermute | solution.py:453
  62.9 3.0 %collective-permute-start.9 = (f32[2,2,256]{2,1,0:T(2,128)S(1)}, f32[2,2,256]{2,1,0:T(2,128)S(1)}, u32[]{:S(2)}, u32[]{:S(2)}) collective-permute-start(f32[2,2,256]{2,1,0:T(2,128)S(1)} %get-tuple-element.26), channel_id=1, source_target_pairs={{0,1},{1,2},{2,3},{3,0},{4,5},{5,6},{6,7},{7,4},{8,9},{9,10},{10,1... | collective-permute-start | bytes 12296 | tf_op jit(solution)/shard_map/ppermute | solution.py:453

commit v10 on v9

--- a/solution.py
+++ b/solution.py
@@ -13,6 +13,7 @@
 relief = 0.1
 HIGHEST = lax.Precision.HIGHEST
 VMEM_LIMIT = 48 * 2**20
+PACK_LIMIT = 62 * 2**20
 HALF = 48
 
 
@@ -40,7 +41,7 @@
     )
 
 
-def kernel_call(body, out_shape, args, specs, scratch=(), flops=0):
+def kernel_call(body, out_shape, args, specs, scratch=(), flops=0, limit=VMEM_LIMIT):
     nbytes = sum(4 * a.size for a in args) + sum(4 * o.size for o in jax.tree.leaves(out_shape))
     return pl.pallas_call(
         body,
@@ -49,7 +50,7 @@
         out_specs=jax.tree.map(lambda _: pl.BlockSpec(memory_space=pltpu.VMEM), out_shape),
         scratch_shapes=scratch,
         cost_estimate=pl.CostEstimate(flops=flops, bytes_accessed=nbytes, transcendentals=0),
-        compiler_params=pltpu.CompilerParams(vmem_limit_bytes=VMEM_LIMIT),
+        compiler_params=pltpu.CompilerParams(vmem_limit_bytes=limit),
     )(*args)
 
 
@@ -462,6 +463,7 @@
             pltpu.VMEM((seg_count, width), jnp.float32),
             pltpu.SemaphoreType.DMA((3,)),
         ],
+        limit=PACK_LIMIT,
     )
     found, bit = {0: mine}, n_alt
     while bit > 1:

time: 66.7 us -> 66.9 us (level)
  local copies, waits for them, and re-layouts: 2.27 us -> 0.91 us
  Pallas kernels: 33.6 us -> 34.9 us
    unnamed x10 -> x6, local copies, waits for them, and re-layouts: 2.27 us -> 0.91 us
    pallas_call x11, Pallas kernels: 33.6 us -> 34.9 us  [kernel_call(): pl.pallas_call(body, out_shape=out_shape, in_specs=specs, out_specs=jax.t...]
where the time goes in v10:
time: 66.9 us; the launch traced here: 66.7 us
  Pallas kernels  34.9 us (52%)
  starting transfers between devices  16 us (24%)
  waiting for transfers between devices  14.8 us (22%)
  local copies, waits for them, and re-layouts  0.91 us (1%)
    pallas_call x11, Pallas kernels, kernel_call(): pl.pallas_call(body, out_shape=out_shape, in_specs=specs, out_specs=jax.t...  34.9 us
    ppermute x3, starting transfers between devices, turned(): return lax.ppermute(value, ('range', 'alt'), pairs)  6.01 us
    ppermute x3, waiting for transfers between devices, local(): found[key ^ bit] = lax.ppermute(found[key], 'alt', pairs)  4.49 us
    ppermute x2, waiting for transfers between devices, local(): beside.append(lax.ppermute(span, ('range', 'alt'), pairs))  4.25 us
    ppermute x2, starting transfers between devices, local(): beside.append(lax.ppermute(span, ('range', 'alt'), pairs))  3.62 us
    ppermute x3, waiting for transfers between devices, turned(): return lax.ppermute(value, ('range', 'alt'), pairs)  3.53 us
    ppermute x3, starting transfers between devices, local(): found[key ^ bit] = lax.ppermute(found[key], 'alt', pairs)  3.01 us
    ppermute x3, waiting for transfers between devices, around(): lax.ppermute(value, 'alt', [(i, (i + k) % n_alt) for i in range(n_alt)])  2.52 us
  transfers between devices with their start and end apart: 12, of which 8 were waited for; matrix products, arithmetic and copies ran while one was open for 0% of the time, Pallas kernels for 14%

profile of v10, /device:TPU:0, one launch (start us, length us, event | category | flops | bytes accessed | tf_op | source)
XLA Modules:
  0.0 66.7 jit_solution(10766971331160066203)
XLA Ops:
  0.0 1.6 %shard_map.55.refs_0_ = f32[104,256]{1,0:T(8,128)} custom-call(f32[96,256]{1,0:T(8,128)} %start_ref.1, f32[1,256]{1,0:T(1,128)} %bitcast.1, f32[4,256]{1,0:T(4,128)} %perturb_ref.1), custom_call_target="tpu_custom_call" | custom-call | bytes 209920 | tf_op jit(solution)/shard_map/pallas_call | solution.py:46
  1.6 3.0 %collective-permute-start.1 = (f32[104,256]{1,0:T(8,128)}, f32[104,256]{1,0:T(8,128)S(1)}, u32[]{:S(2)}, u32[]{:S(2)}) collective-permute-start(f32[104,256]{1,0:T(8,128)} %shard_map.55.refs_0_), channel_id=1, source_target_pairs={{0,2},{1,3},{2,0},{3,1},{4,6},{5,7},{6,4},{7,5},{8,10},{9,11},{10,... | collective-permute-start | bytes 319496 | tf_op jit(solution)/shard_map/ppermute | solution.py:473
  4.6 0.0 collective-permute-start
  4.6 3.2 %collective-permute-done.1.refs_2_ = f32[104,256]{1,0:T(8,128)S(1)} collective-permute-done((f32[104,256]{1,0:T(8,128)}, f32[104,256]{1,0:T(8,128)S(1)}, u32[]{:S(2)}, u32[]{:S(2)}) %collective-permute-start.1) | collective-permute-done | bytes 106528 | tf_op jit(solution)/shard_map/ppermute | solution.py:473
  7.8 1.3 %collective-permute-done.2.refs_3_ = f32[104,256]{1,0:T(8,128)S(1)} collective-permute-done((f32[104,256]{1,0:T(8,128)S(1)}, f32[104,256]{1,0:T(8,128)S(1)}, u32[]{:S(2)}, u32[]{:S(2)}) %collective-permute-start.2) | collective-permute-done | bytes 106528 | tf_op jit(solution)/shard_map/ppermute | solution.py:473
  9.1 0.9 %copy-done = f32[104,256]{1,0:T(8,128)S(1)} copy-done((f32[104,256]{1,0:T(8,128)S(1)}, f32[104,256]{1,0:T(8,128)}, u32[]{:S(2)}) %copy-start) | copy-done | bytes 106520
  10.0 21.8 %shard_map.56 = (f32[96,1024]{1,0:T(8,128)S(1)}, f32[96,1024]{1,0:T(8,128)S(1)}, f32[2,1024]{1,0:T(2,128)S(1)}) custom-call(f32[2]{0:T(128)S(1)} %copy-done.1, f32[104,256]{1,0:T(8,128)S(1)} %copy-done, f32[104,256]{1,0:T(8,128)S(1)} %collective-permute-done.refs_1_, f32[104,256]{1,0:T(8,128)S(1)} %collective-permute-done.1.refs_2_, ...), custom_call_target="tpu_custom_call" | custom-call | flops 603979776 | bytes 1220616 | tf_op jit(solution)/shard_map/pallas_call | solution.py:46
  31.8 1.3 %collective-permute-start.3 = (f32[96,1024]{1,0:T(8,128)S(1)}, f32[96,1024]{1,0:T(8,128)S(1)}, u32[]{:S(2)}, u32[]{:S(2)}) collective-permute-start(f32[96,1024]{1,0:T(8,128)S(1)} %get-tuple-element.17.refs_0_), channel_id=1, source_target_pairs={{1,0},{4,1},{5,4},{8,5},{9,8},{12,9},{13,12},{16,13},{17,16},{20,1... | collective-permute-start | bytes 1179656 | tf_op jit(solution)/shard_map/ppermute | solution.py:451
  33.1 7.1 %shard_map.57 = (f32[96,1024]{1,0:T(8,128)S(1)}, f32[96,1024]{1,0:T(8,128)S(1)}, f32[96,96]{1,0:T(8,128)S(1)}, f32[2,96,96]{2,1,0:T(8,128)S(1)}, f32[2,96,96]{2,1,0:T(8,128)S(1)}) custom-call(f32[2,1024]{1,0:T(2,128)S(1)} %get-tuple-element.18.coef_ref, f32[96,1024]{1,0:T(8,128)S(1)} %get-tuple-element.17.refs_0_, f32[96,1024]{1,0:T(8,128)S(1)} %get-tuple-element.19.refs_1_), custom_call_target="tpu_custom_call" | custom-call | flops 301989888 | bytes 1765376 | tf_op jit(solution)/shard_map/pallas_call | solution.py:46
  40.2 0.0 collective-permute-done.3.next_ref
  40.2 0.8 %shard_map.58.own_ref = f32[2,96,96]{2,1,0:T(8,128)S(1)} custom-call(f32[96,1024]{1,0:T(8,128)S(1)} %collective-permute-done.3.next_ref, f32[96,1024]{1,0:T(8,128)S(1)} %get-tuple-element.20.second_ref.refs_3_, f32[2,96,96]{2,1,0:T(8,128)S(1)} %get-tuple-element.21.rest_ref), custom_call_target="tpu_custom_call" | custom-call | flops 18874368 | bytes 933888 | tf_op jit(solution)/shard_map/pallas_call | solution.py:46
  41.0 1.2 %collective-permute-start.4 = (f32[2,96,96]{2,1,0:T(8,128)S(1)}, f32[2,96,96]{2,1,0:T(8,128)S(1)}, u32[]{:S(2)}, u32[]{:S(2)}) collective-permute-start(f32[2,96,96]{2,1,0:T(8,128)S(1)} %shard_map.58.own_ref), channel_id=1, source_target_pairs={{0,1},{1,0},{4,5},{5,4},{8,9},{9,8},{12,13},{13,12},{16,17},{17,16... | collective-permute-start | bytes 221192 | tf_op jit(solution)/shard_map/ppermute | solution.py:521
  42.2 0.9 %collective-permute-done.4.other_ref.refs_0_ = f32[2,96,96]{2,1,0:T(8,128)S(1)} collective-permute-done((f32[2,96,96]{2,1,0:T(8,128)S(1)}, f32[2,96,96]{2,1,0:T(8,128)S(1)}, u32[]{:S(2)}, u32[]{:S(2)}) %collective-permute-start.4) | collective-permute-done | bytes 73760 | tf_op jit(solution)/shard_map/ppermute | solution.py:521
  43.1 0.3 shard_map.59.own_ref
  43.4 0.0 copy-start.2
  43.5 2.4 %collective-permute-start.5 = (f32[2,96,96]{2,1,0:T(8,128)S(1)}, f32[2,96,96]{2,1,0:T(8,128)S(1)}, u32[]{:S(2)}, u32[]{:S(2)}) collective-permute-start(f32[2,96,96]{2,1,0:T(8,128)S(1)} %shard_map.59.own_ref), channel_id=1, source_target_pairs={{0,4},{1,5},{4,0},{5,1},{8,12},{9,13},{12,8},{13,9},{16,20},{17,21... | collective-permute-start | bytes 221192 | tf_op jit(solution)/shard_map/ppermute | solution.py:521
  45.9 3.3 %collective-permute-done.5.other_ref.refs_1_ = f32[2,96,96]{2,1,0:T(8,128)S(1)} collective-permute-done((f32[2,96,96]{2,1,0:T(8,128)S(1)}, f32[2,96,96]{2,1,0:T(8,128)S(1)}, u32[]{:S(2)}, u32[]{:S(2)}) %collective-permute-start.5) | collective-permute-done | bytes 73760 | tf_op jit(solution)/shard_map/ppermute | solution.py:521
  49.2 0.3 shard_map.60
  49.5 2.1 %collective-permute-start.7 = (f32[2,96,96]{2,1,0:T(8,128)S(1)}, f32[2,96,96]{2,1,0:T(8,128)S(1)}, u32[]{:S(2)}, u32[]{:S(2)}) collective-permute-start(f32[2,96,96]{2,1,0:T(8,128)S(1)} %shard_map.60), channel_id=1, source_target_pairs={{0,8},{1,9},{4,12},{5,13},{8,16},{9,17},{12,20},{13,21},{16,24},{1... | collective-permute-start | bytes 221192 | tf_op jit(solution)/shard_map/ppermute | solution.py:512
  51.6 2.6 %collective-permute-start.8 = (f32[2,96,96]{2,1,0:T(8,128)S(1)}, f32[2,96,96]{2,1,0:T(8,128)S(1)}, u32[]{:S(2)}, u32[]{:S(2)}) collective-permute-start(f32[2,96,96]{2,1,0:T(8,128)S(1)} %shard_map.60), channel_id=1, source_target_pairs={{0,16},{1,17},{4,20},{5,21},{8,24},{9,25},{12,28},{13,29},{16,0},{... | collective-permute-start | bytes 221192 | tf_op jit(solution)/shard_map/ppermute | solution.py:512
  54.2 1.4 %collective-permute-start.6 = (f32[2,96,96]{2,1,0:T(8,128)S(1)}, f32[2,96,96]{2,1,0:T(8,128)S(1)}, u32[]{:S(2)}, u32[]{:S(2)}) collective-permute-start(f32[2,96,96]{2,1,0:T(8,128)S(1)} %shard_map.60), channel_id=1, source_target_pairs={{0,24},{1,25},{4,28},{5,29},{8,0},{9,1},{12,4},{13,5},{16,8},{17,9... | collective-permute-start | bytes 221192 | tf_op jit(solution)/shard_map/ppermute | solution.py:512
  55.5 0.9 %shard_map.61.inside_ref = f32[2,2,96,96]{3,2,1,0:T(8,128)S(1)} custom-call(f32[2,96,96]{2,1,0:T(8,128)S(1)} %collective-permute-done.4.other_ref.refs_0_, f32[2,96,96]{2,1,0:T(8,128)S(1)} %collective-permute-done.5.other_ref.refs_1_, f32[96,96]{1,0:T(8,128)S(1)} %get-tuple-element.22.refs_2_, f32[2,96,96]{2,1,0:T(8,128)S(1)} %get-tuple-element.23.refs_3_), custom_call_target="tpu_custom_call" | custom-call | flops 18874368 | bytes 405504 | tf_op jit(solution)/shard_map/pallas_call | solution.py:46
  56.4 1.0 %collective-permute-done.7.span_ref = f32[2,96,96]{2,1,0:T(8,128)S(1)} collective-permute-done((f32[2,96,96]{2,1,0:T(8,128)S(1)}, f32[2,96,96]{2,1,0:T(8,128)S(1)}, u32[]{:S(2)}, u32[]{:S(2)}) %collective-permute-start.7) | collective-permute-done | bytes 73760 | tf_op jit(solution)/shard_map/ppermute | solution.py:512
  57.3 0.5 shard_map.62.inside_ref
  57.8 2.6 %collective-permute-done.8.span_ref = f32[2,96,96]{2,1,0:T(8,128)S(1)} collective-permute-done((f32[2,96,96]{2,1,0:T(8,128)S(1)}, f32[2,96,96]{2,1,0:T(8,128)S(1)}, u32[]{:S(2)}, u32[]{:S(2)}) %collective-permute-start.8) | collective-permute-done | bytes 73760 | tf_op jit(solution)/shard_map/ppermute | solution.py:512
  60.4 0.6 shard_map.63.refs_1_
  61.0 0.6 shard_map.64
  61.6 1.5 %collective-permute-start.10 = (f32[2,2,256]{2,1,0:T(2,128)S(1)}, f32[2,2,256]{2,1,0:T(2,128)S(1)}, u32[]{:S(2)}, u32[]{:S(2)}) collective-permute-start(f32[2,2,256]{2,1,0:T(2,128)S(1)} %get-tuple-element.27), channel_id=1, source_target_pairs={{0,2},{1,3},{2,0},{3,1},{4,6},{5,7},{6,4},{7,5},{8,10},{9,11},{10,... | collective-permute-start | bytes 12296 | tf_op jit(solution)/shard_map/ppermute | solution.py:454
  63.1 0.5 collective-permute-start.9
  63.6 1.6 %collective-permute-done.10.refs_2_ = f32[2,2,256]{2,1,0:T(2,128)S(1)} collective-permute-done((f32[2,2,256]{2,1,0:T(2,128)S(1)}, f32[2,2,256]{2,1,0:T(2,128)S(1)}, u32[]{:S(2)}, u32[]{:S(2)}) %collective-permute-start.10) | collective-permute-done | bytes 4128 | tf_op jit(solution)/shard_map/ppermute | solution.py:454
  65.2 0.9 %collective-permute-done.9.refs_1_ = f32[2,2,256]{2,1,0:T(2,128)S(1)} collective-permute-done((f32[2,2,256]{2,1,0:T(2,128)S(1)}, f32[2,2,256]{2,1,0:T(2,128)S(1)}, u32[]{:S(2)}, u32[]{:S(2)}) %collective-permute-start.9) | collective-permute-done | bytes 4128 | tf_op jit(solution)/shard_map/ppermute | solution.py:454
  66.1 0.6 shard_map.65
  (10 shorter events, 0.0 us)
Async XLA Ops:
  0.0 9.1 %copy-start.1 = (f32[2]{0:T(128)S(1)}, f32[2]{0:T(128)}, u32[]{:S(2)}) copy-start(f32[2]{0:T(128)} %scale_ref.1) | copy-start | bytes 28
  1.6 6.2 %collective-permute-start.1 = (f32[104,256]{1,0:T(8,128)}, f32[104,256]{1,0:T(8,128)S(1)}, u32[]{:S(2)}, u32[]{:S(2)}) collective-permute-start(f32[104,256]{1,0:T(8,128)} %shard_map.55.refs_0_), channel_id=1, source_target_pairs={{0,2},{1,3},{2,0},{3,1},{4,6},{5,7},{6,4},{7,5},{8,10},{9,11},{10,... | collective-permute-start | bytes 319496 | tf_op jit(solution)/shard_map/ppermute | solution.py:473
  4.6 3.2 %collective-permute-start = (f32[104,256]{1,0:T(8,128)}, f32[104,256]{1,0:T(8,128)S(1)}, u32[]{:S(2)}, u32[]{:S(2)}) collective-permute-start(f32[104,256]{1,0:T(8,128)} %shard_map.55.refs_0_), channel_id=1, source_target_pairs={{0,1},{1,0},{2,3},{3,2},{4,5},{5,4},{6,7},{7,6},{8,9},{9,8},{10,11... | collective-permute-start | bytes 319496 | tf_op jit(solution)/shard_map/ppermute | solution.py:473
  7.8 1.3 %collective-permute-start.2 = (f32[104,256]{1,0:T(8,128)S(1)}, f32[104,256]{1,0:T(8,128)S(1)}, u32[]{:S(2)}, u32[]{:S(2)}) collective-permute-start(f32[104,256]{1,0:T(8,128)S(1)} %collective-permute-done.1.refs_2_), channel_id=1, source_target_pairs={{0,1},{1,0},{2,3},{3,2},{4,5},{5,4},{6,7},{7,6},{8,9},{9,8},{10,11... | collective-permute-start | bytes 319496 | tf_op jit(solution)/shard_map/ppermute | solution.py:473
  9.1 0.9 %copy-start = (f32[104,256]{1,0:T(8,128)S(1)}, f32[104,256]{1,0:T(8,128)}, u32[]{:S(2)}) copy-start(f32[104,256]{1,0:T(8,128)} %shard_map.55.refs_0_) | copy-start | bytes 319492
  31.8 8.4 %collective-permute-start.3 = (f32[96,1024]{1,0:T(8,128)S(1)}, f32[96,1024]{1,0:T(8,128)S(1)}, u32[]{:S(2)}, u32[]{:S(2)}) collective-permute-start(f32[96,1024]{1,0:T(8,128)S(1)} %get-tuple-element.17.refs_0_), channel_id=1, source_target_pairs={{1,0},{4,1},{5,4},{8,5},{9,8},{12,9},{13,12},{16,13},{17,16},{20,1... | collective-permute-start | bytes 1179656 | tf_op jit(solution)/shard_map/ppermute | solution.py:451
  41.0 2.1 %collective-permute-start.4 = (f32[2,96,96]{2,1,0:T(8,128)S(1)}, f32[2,96,96]{2,1,0:T(8,128)S(1)}, u32[]{:S(2)}, u32[]{:S(2)}) collective-permute-start(f32[2,96,96]{2,1,0:T(8,128)S(1)} %shard_map.58.own_ref), channel_id=1, source_target_pairs={{0,1},{1,0},{4,5},{5,4},{8,9},{9,8},{12,13},{13,12},{16,17},{17,16... | collective-permute-start | bytes 221192 | tf_op jit(solution)/shard_map/ppermute | solution.py:521
  43.4 12.1 %copy-start.2 = (f32[2,2,96]{2,1,0:T(2,128)S(1)}, f32[2,2,96]{2,1,0:T(2,128)}, u32[]{:S(2)}) copy-start(f32[2,2,96]{2,1,0:T(2,128)} %param.9) | copy-start | bytes 4612
  43.5 5.7 %collective-permute-start.5 = (f32[2,96,96]{2,1,0:T(8,128)S(1)}, f32[2,96,96]{2,1,0:T(8,128)S(1)}, u32[]{:S(2)}, u32[]{:S(2)}) collective-permute-start(f32[2,96,96]{2,1,0:T(8,128)S(1)} %shard_map.59.own_ref), channel_id=1, source_target_pairs={{0,4},{1,5},{4,0},{5,1},{8,12},{9,13},{12,8},{13,9},{16,20},{17,21... | collective-permute-start | bytes 221192 | tf_op jit(solution)/shard_map/ppermute | solution.py:521
  49.5 7.8 %collective-permute-start.7 = (f32[2,96,96]{2,1,0:T(8,128)S(1)}, f32[2,96,96]{2,1,0:T(8,128)S(1)}, u32[]{:S(2)}, u32[]{:S(2)}) collective-permute-start(f32[2,96,96]{2,1,0:T(8,128)S(1)} %shard_map.60), channel_id=1, source_target_pairs={{0,8},{1,9},{4,12},{5,13},{8,16},{9,17},{12,20},{13,21},{16,24},{1... | collective-permute-start | bytes 221192 | tf_op jit(solution)/shard_map/ppermute | solution.py:512
  51.6 8.8 %collective-permute-start.8 = (f32[2,96,96]{2,1,0:T(8,128)S(1)}, f32[2,96,96]{2,1,0:T(8,128)S(1)}, u32[]{:S(2)}, u32[]{:S(2)}) collective-permute-start(f32[2,96,96]{2,1,0:T(8,128)S(1)} %shard_map.60), channel_id=1, source_target_pairs={{0,16},{1,17},{4,20},{5,21},{8,24},{9,25},{12,28},{13,29},{16,0},{... | collective-permute-start | bytes 221192 | tf_op jit(solution)/shard_map/ppermute | solution.py:512
  54.2 6.8 %collective-permute-start.6 = (f32[2,96,96]{2,1,0:T(8,128)S(1)}, f32[2,96,96]{2,1,0:T(8,128)S(1)}, u32[]{:S(2)}, u32[]{:S(2)}) collective-permute-start(f32[2,96,96]{2,1,0:T(8,128)S(1)} %shard_map.60), channel_id=1, source_target_pairs={{0,24},{1,25},{4,28},{5,29},{8,0},{9,1},{12,4},{13,5},{16,8},{17,9... | collective-permute-start | bytes 221192 | tf_op jit(solution)/shard_map/ppermute | solution.py:512
  61.6 3.6 %collective-permute-start.10 = (f32[2,2,256]{2,1,0:T(2,128)S(1)}, f32[2,2,256]{2,1,0:T(2,128)S(1)}, u32[]{:S(2)}, u32[]{:S(2)}) collective-permute-start(f32[2,2,256]{2,1,0:T(2,128)S(1)} %get-tuple-element.27), channel_id=1, source_target_pairs={{0,2},{1,3},{2,0},{3,1},{4,6},{5,7},{6,4},{7,5},{8,10},{9,11},{10,... | collective-permute-start | bytes 12296 | tf_op jit(solution)/shard_map/ppermute | solution.py:454
  63.1 2.1 %collective-permute-start.11 = (f32[2,2,256]{2,1,0:T(2,128)S(1)}, f32[2,2,256]{2,1,0:T(2,128)S(1)}, u32[]{:S(2)}, u32[]{:S(2)}) collective-permute-start(f32[2,2,256]{2,1,0:T(2,128)S(1)} %get-tuple-element.28), channel_id=1, source_target_pairs={{0,3},{1,0},{2,1},{3,2},{4,7},{5,4},{6,5},{7,6},{8,11},{9,8},{10,9... | collective-permute-start | bytes 12296 | tf_op jit(solution)/shard_map/ppermute | solution.py:454
  63.1 3.0 %collective-permute-start.9 = (f32[2,2,256]{2,1,0:T(2,128)S(1)}, f32[2,2,256]{2,1,0:T(2,128)S(1)}, u32[]{:S(2)}, u32[]{:S(2)}) collective-permute-start(f32[2,2,256]{2,1,0:T(2,128)S(1)} %get-tuple-element.26), channel_id=1, source_target_pairs={{0,1},{1,2},{2,3},{3,0},{4,5},{5,6},{6,7},{7,4},{8,9},{9,10},{10,1... | collective-permute-start | bytes 12296 | tf_op jit(solution)/shard_map/ppermute | solution.py:454

commit v11 on v9

--- a/solution.py
+++ b/solution.py
@@ -263,7 +263,7 @@
                 )
         return carry
 
-    lax.fori_loop(0, ITERS - 1, step, 0)
+    lax.fori_loop(0, ITERS - 1, step, 0, unroll=True)
     for i in range(chunk):
         for at in range(0, modes, 8):
             image_refs[i][at : at + 8, :] = doubled_operator(

time: 66.7 us -> 64.9 us (0.973)
  Pallas kernels: 33.6 us -> 31.8 us
    pallas_call x11, Pallas kernels: 33.6 us -> 31.8 us  [kernel_call(): pl.pallas_call(body, out_shape=out_shape, in_specs=specs, out_specs=jax.t...]
where the time goes in v11:
time: 64.9 us; the launch traced here: 64.7 us
  Pallas kernels  31.8 us (49%)
  starting transfers between devices  15.9 us (24%)
  waiting for transfers between devices  14.6 us (22%)
  local copies, waits for them, and re-layouts  2.27 us (3%)
    pallas_call x11, Pallas kernels, kernel_call(): pl.pallas_call(body, out_shape=out_shape, in_specs=specs, out_specs=jax.t...  31.8 us
    ppermute x3, starting transfers between devices, turned(): return lax.ppermute(value, ('range', 'alt'), pairs)  6.06 us
    ppermute x3, waiting for transfers between devices, local(): found[key ^ bit] = lax.ppermute(found[key], 'alt', pairs)  4.28 us
    ppermute x2, waiting for transfers between devices, local(): beside.append(lax.ppermute(span, ('range', 'alt'), pairs))  4.25 us
    ppermute x2, starting transfers between devices, local(): beside.append(lax.ppermute(span, ('range', 'alt'), pairs))  3.58 us
    ppermute x3, waiting for transfers between devices, turned(): return lax.ppermute(value, ('range', 'alt'), pairs)  3.54 us
    ppermute x3, starting transfers between devices, local(): found[key ^ bit] = lax.ppermute(found[key], 'alt', pairs)  3.01 us
    ppermute x3, waiting for transfers between devices, around(): lax.ppermute(value, 'alt', [(i, (i + k) % n_alt) for i in range(n_alt)])  2.52 us
  transfers between devices with their start and end apart: 12, of which 8 were waited for; matrix products, arithmetic and copies ran while one was open for 0% of the time, Pallas kernels for 14%

profile of v11, /device:TPU:0, one launch (start us, length us, event | category | flops | bytes accessed | tf_op | source)
XLA Modules:
  0.0 64.7 jit_solution(1749545153124693808)
XLA Ops:
  0.0 0.7 %copy-done.2 = f32[256]{0:T(256)S(1)} copy-done((f32[256]{0:T(256)S(1)}, f32[256]{0:T(256)}, u32[]{:S(2)}) %copy-start.2) | copy-done | bytes 1048
  0.7 0.9 %copy-done = f32[96,256]{1,0:T(8,128)S(1)} copy-done((f32[96,256]{1,0:T(8,128)S(1)}, f32[96,256]{1,0:T(8,128)}, u32[]{:S(2)}) %copy-start) | copy-done | bytes 98328
  1.6 0.7 %copy-done.1 = f32[4,256]{1,0:T(4,128)S(1)} copy-done((f32[4,256]{1,0:T(4,128)S(1)}, f32[4,256]{1,0:T(4,128)}, u32[]{:S(2)}) %copy-start.1) | copy-done | bytes 4120
  2.3 0.1 shard_map.55.refs_0_
  2.4 3.0 %collective-permute-start.1 = (f32[104,256]{1,0:T(8,128)S(1)}, f32[104,256]{1,0:T(8,128)S(1)}, u32[]{:S(2)}, u32[]{:S(2)}) collective-permute-start(f32[104,256]{1,0:T(8,128)S(1)} %shard_map.55.refs_0_), channel_id=1, source_target_pairs={{0,2},{1,3},{2,0},{3,1},{4,6},{5,7},{6,4},{7,5},{8,10},{9,11},{10,... | collective-permute-start | bytes 319496 | tf_op jit(solution)/shard_map/ppermute | solution.py:471
  5.4 3.0 %collective-permute-done.1.refs_2_ = f32[104,256]{1,0:T(8,128)S(1)} collective-permute-done((f32[104,256]{1,0:T(8,128)S(1)}, f32[104,256]{1,0:T(8,128)S(1)}, u32[]{:S(2)}, u32[]{:S(2)}) %collective-permute-start.1) | collective-permute-done | bytes 106528 | tf_op jit(solution)/shard_map/ppermute | solution.py:471
  8.4 1.3 %collective-permute-done.2.refs_3_ = f32[104,256]{1,0:T(8,128)S(1)} collective-permute-done((f32[104,256]{1,0:T(8,128)S(1)}, f32[104,256]{1,0:T(8,128)S(1)}, u32[]{:S(2)}, u32[]{:S(2)}) %collective-permute-start.2) | collective-permute-done | bytes 106528 | tf_op jit(solution)/shard_map/ppermute | solution.py:471
  9.7 20.0 %shard_map.56 = (f32[96,1024]{1,0:T(8,128)S(1)}, f32[96,1024]{1,0:T(8,128)S(1)}, f32[2,1024]{1,0:T(2,128)S(1)}) custom-call(f32[2]{0:T(128)S(1)} %copy-done.3, f32[104,256]{1,0:T(8,128)S(1)} %shard_map.55.refs_0_, f32[104,256]{1,0:T(8,128)S(1)} %collective-permute-done.refs_1_, f32[104,256]{1,0:T(8,128)S(1)} %collective-permute-done.1.refs_2_, ...), custom_call_target="tpu_custom_call" | custom-call | flops 603979776 | bytes 1220616 | tf_op jit(solution)/shard_map/pallas_call | solution.py:45
  29.7 1.3 %collective-permute-start.3 = (f32[96,1024]{1,0:T(8,128)S(1)}, f32[96,1024]{1,0:T(8,128)S(1)}, u32[]{:S(2)}, u32[]{:S(2)}) collective-permute-start(f32[96,1024]{1,0:T(8,128)S(1)} %get-tuple-element.17.refs_0_), channel_id=1, source_target_pairs={{1,0},{4,1},{5,4},{8,5},{9,8},{12,9},{13,12},{16,13},{17,16},{20,1... | collective-permute-start | bytes 1179656 | tf_op jit(solution)/shard_map/ppermute | solution.py:450
  31.0 7.2 %shard_map.57 = (f32[96,1024]{1,0:T(8,128)S(1)}, f32[96,1024]{1,0:T(8,128)S(1)}, f32[96,96]{1,0:T(8,128)S(1)}, f32[2,96,96]{2,1,0:T(8,128)S(1)}, f32[2,96,96]{2,1,0:T(8,128)S(1)}) custom-call(f32[2,1024]{1,0:T(2,128)S(1)} %get-tuple-element.18.coef_ref, f32[96,1024]{1,0:T(8,128)S(1)} %get-tuple-element.17.refs_0_, f32[96,1024]{1,0:T(8,128)S(1)} %get-tuple-element.19.refs_1_), custom_call_target="tpu_custom_call" | custom-call | flops 301989888 | bytes 1765376 | tf_op jit(solution)/shard_map/pallas_call | solution.py:45
  38.2 0.8 %shard_map.58.own_ref = f32[2,96,96]{2,1,0:T(8,128)S(1)} custom-call(f32[96,1024]{1,0:T(8,128)S(1)} %collective-permute-done.3.next_ref, f32[96,1024]{1,0:T(8,128)S(1)} %get-tuple-element.20.second_ref.refs_3_, f32[2,96,96]{2,1,0:T(8,128)S(1)} %get-tuple-element.21.rest_ref), custom_call_target="tpu_custom_call" | custom-call | flops 18874368 | bytes 933888 | tf_op jit(solution)/shard_map/pallas_call | solution.py:45
  39.0 1.2 %collective-permute-start.4 = (f32[2,96,96]{2,1,0:T(8,128)S(1)}, f32[2,96,96]{2,1,0:T(8,128)S(1)}, u32[]{:S(2)}, u32[]{:S(2)}) collective-permute-start(f32[2,96,96]{2,1,0:T(8,128)S(1)} %shard_map.58.own_ref), channel_id=1, source_target_pairs={{0,1},{1,0},{4,5},{5,4},{8,9},{9,8},{12,13},{13,12},{16,17},{17,16... | collective-permute-start | bytes 221192 | tf_op jit(solution)/shard_map/ppermute | solution.py:519
  40.2 0.9 %collective-permute-done.4.other_ref.refs_0_ = f32[2,96,96]{2,1,0:T(8,128)S(1)} collective-permute-done((f32[2,96,96]{2,1,0:T(8,128)S(1)}, f32[2,96,96]{2,1,0:T(8,128)S(1)}, u32[]{:S(2)}, u32[]{:S(2)}) %collective-permute-start.4) | collective-permute-done | bytes 73760 | tf_op jit(solution)/shard_map/ppermute | solution.py:519
  41.2 0.3 shard_map.59.own_ref
  41.5 0.0 copy-start.4
  41.5 2.4 %collective-permute-start.5 = (f32[2,96,96]{2,1,0:T(8,128)S(1)}, f32[2,96,96]{2,1,0:T(8,128)S(1)}, u32[]{:S(2)}, u32[]{:S(2)}) collective-permute-start(f32[2,96,96]{2,1,0:T(8,128)S(1)} %shard_map.59.own_ref), channel_id=1, source_target_pairs={{0,4},{1,5},{4,0},{5,1},{8,12},{9,13},{12,8},{13,9},{16,20},{17,21... | collective-permute-start | bytes 221192 | tf_op jit(solution)/shard_map/ppermute | solution.py:519
  43.9 3.3 %collective-permute-done.5.other_ref.refs_1_ = f32[2,96,96]{2,1,0:T(8,128)S(1)} collective-permute-done((f32[2,96,96]{2,1,0:T(8,128)S(1)}, f32[2,96,96]{2,1,0:T(8,128)S(1)}, u32[]{:S(2)}, u32[]{:S(2)}) %collective-permute-start.5) | collective-permute-done | bytes 73760 | tf_op jit(solution)/shard_map/ppermute | solution.py:519
  47.2 0.3 shard_map.60
  47.5 2.1 %collective-permute-start.7 = (f32[2,96,96]{2,1,0:T(8,128)S(1)}, f32[2,96,96]{2,1,0:T(8,128)S(1)}, u32[]{:S(2)}, u32[]{:S(2)}) collective-permute-start(f32[2,96,96]{2,1,0:T(8,128)S(1)} %shard_map.60), channel_id=1, source_target_pairs={{0,8},{1,9},{4,12},{5,13},{8,16},{9,17},{12,20},{13,21},{16,24},{1... | collective-permute-start | bytes 221192 | tf_op jit(solution)/shard_map/ppermute | solution.py:510
  49.6 2.6 %collective-permute-start.8 = (f32[2,96,96]{2,1,0:T(8,128)S(1)}, f32[2,96,96]{2,1,0:T(8,128)S(1)}, u32[]{:S(2)}, u32[]{:S(2)}) collective-permute-start(f32[2,96,96]{2,1,0:T(8,128)S(1)} %shard_map.60), channel_id=1, source_target_pairs={{0,16},{1,17},{4,20},{5,21},{8,24},{9,25},{12,28},{13,29},{16,0},{... | collective-permute-start | bytes 221192 | tf_op jit(solution)/shard_map/ppermute | solution.py:510
  52.2 1.3 %collective-permute-start.6 = (f32[2,96,96]{2,1,0:T(8,128)S(1)}, f32[2,96,96]{2,1,0:T(8,128)S(1)}, u32[]{:S(2)}, u32[]{:S(2)}) collective-permute-start(f32[2,96,96]{2,1,0:T(8,128)S(1)} %shard_map.60), channel_id=1, source_target_pairs={{0,24},{1,25},{4,28},{5,29},{8,0},{9,1},{12,4},{13,5},{16,8},{17,9... | collective-permute-start | bytes 221192 | tf_op jit(solution)/shard_map/ppermute | solution.py:510
  53.5 0.9 %shard_map.61.inside_ref = f32[2,2,96,96]{3,2,1,0:T(8,128)S(1)} custom-call(f32[2,96,96]{2,1,0:T(8,128)S(1)} %collective-permute-done.4.other_ref.refs_0_, f32[2,96,96]{2,1,0:T(8,128)S(1)} %collective-permute-done.5.other_ref.refs_1_, f32[96,96]{1,0:T(8,128)S(1)} %get-tuple-element.22.refs_2_, f32[2,96,96]{2,1,0:T(8,128)S(1)} %get-tuple-element.23.refs_3_), custom_call_target="tpu_custom_call" | custom-call | flops 18874368 | bytes 405504 | tf_op jit(solution)/shard_map/pallas_call | solution.py:45
  54.4 1.0 %collective-permute-done.7.span_ref = f32[2,96,96]{2,1,0:T(8,128)S(1)} collective-permute-done((f32[2,96,96]{2,1,0:T(8,128)S(1)}, f32[2,96,96]{2,1,0:T(8,128)S(1)}, u32[]{:S(2)}, u32[]{:S(2)}) %collective-permute-start.7) | collective-permute-done | bytes 73760 | tf_op jit(solution)/shard_map/ppermute | solution.py:510
  55.4 0.5 shard_map.62.inside_ref
  55.9 2.6 %collective-permute-done.8.span_ref = f32[2,96,96]{2,1,0:T(8,128)S(1)} collective-permute-done((f32[2,96,96]{2,1,0:T(8,128)S(1)}, f32[2,96,96]{2,1,0:T(8,128)S(1)}, u32[]{:S(2)}, u32[]{:S(2)}) %collective-permute-start.8) | collective-permute-done | bytes 73760 | tf_op jit(solution)/shard_map/ppermute | solution.py:510
  58.4 0.6 shard_map.63.refs_1_
  59.0 0.6 shard_map.64
  59.6 1.5 %collective-permute-start.10 = (f32[2,2,256]{2,1,0:T(2,128)S(1)}, f32[2,2,256]{2,1,0:T(2,128)S(1)}, u32[]{:S(2)}, u32[]{:S(2)}) collective-permute-start(f32[2,2,256]{2,1,0:T(2,128)S(1)} %get-tuple-element.27), channel_id=1, source_target_pairs={{0,2},{1,3},{2,0},{3,1},{4,6},{5,7},{6,4},{7,5},{8,10},{9,11},{10,... | collective-permute-start | bytes 12296 | tf_op jit(solution)/shard_map/ppermute | solution.py:453
  61.1 0.5 collective-permute-start.9
  61.6 1.6 %collective-permute-done.10.refs_2_ = f32[2,2,256]{2,1,0:T(2,128)S(1)} collective-permute-done((f32[2,2,256]{2,1,0:T(2,128)S(1)}, f32[2,2,256]{2,1,0:T(2,128)S(1)}, u32[]{:S(2)}, u32[]{:S(2)}) %collective-permute-start.10) | collective-permute-done | bytes 4128 | tf_op jit(solution)/shard_map/ppermute | solution.py:453
  63.2 0.9 %collective-permute-done.9.refs_1_ = f32[2,2,256]{2,1,0:T(2,128)S(1)} collective-permute-done((f32[2,2,256]{2,1,0:T(2,128)S(1)}, f32[2,2,256]{2,1,0:T(2,128)S(1)}, u32[]{:S(2)}, u32[]{:S(2)}) %collective-permute-start.9) | collective-permute-done | bytes 4128 | tf_op jit(solution)/shard_map/ppermute | solution.py:453
  64.1 0.6 shard_map.65
  (14 shorter events, 0.0 us)
Async XLA Ops:
  0.0 0.7 %copy-start.2 = (f32[256]{0:T(256)S(1)}, f32[256]{0:T(256)}, u32[]{:S(2)}) copy-start(f32[256]{0:T(256)} %param.6) | copy-start | bytes 3076
  0.7 0.9 %copy-start = (f32[96,256]{1,0:T(8,128)S(1)}, f32[96,256]{1,0:T(8,128)}, u32[]{:S(2)}) copy-start(f32[96,256]{1,0:T(8,128)} %start_ref.1) | copy-start | bytes 294916
  1.6 0.7 %copy-start.1 = (f32[4,256]{1,0:T(4,128)S(1)}, f32[4,256]{1,0:T(4,128)}, u32[]{:S(2)}) copy-start(f32[4,256]{1,0:T(4,128)} %perturb_ref.1) | copy-start | bytes 12292
  2.3 7.4 %copy-start.3 = (f32[2]{0:T(128)S(1)}, f32[2]{0:T(128)}, u32[]{:S(2)}) copy-start(f32[2]{0:T(128)} %scale_ref.1) | copy-start | bytes 28
  2.4 6.0 %collective-permute-start.1 = (f32[104,256]{1,0:T(8,128)S(1)}, f32[104,256]{1,0:T(8,128)S(1)}, u32[]{:S(2)}, u32[]{:S(2)}) collective-permute-start(f32[104,256]{1,0:T(8,128)S(1)} %shard_map.55.refs_0_), channel_id=1, source_target_pairs={{0,2},{1,3},{2,0},{3,1},{4,6},{5,7},{6,4},{7,5},{8,10},{9,11},{10,... | collective-permute-start | bytes 319496 | tf_op jit(solution)/shard_map/ppermute | solution.py:471
  5.4 3.0 %collective-permute-start = (f32[104,256]{1,0:T(8,128)S(1)}, f32[104,256]{1,0:T(8,128)S(1)}, u32[]{:S(2)}, u32[]{:S(2)}) collective-permute-start(f32[104,256]{1,0:T(8,128)S(1)} %shard_map.55.refs_0_), channel_id=1, source_target_pairs={{0,1},{1,0},{2,3},{3,2},{4,5},{5,4},{6,7},{7,6},{8,9},{9,8},{10,11... | collective-permute-start | bytes 319496 | tf_op jit(solution)/shard_map/ppermute | solution.py:471
  8.4 1.3 %collective-permute-start.2 = (f32[104,256]{1,0:T(8,128)S(1)}, f32[104,256]{1,0:T(8,128)S(1)}, u32[]{:S(2)}, u32[]{:S(2)}) collective-permute-start(f32[104,256]{1,0:T(8,128)S(1)} %collective-permute-done.1.refs_2_), channel_id=1, source_target_pairs={{0,1},{1,0},{2,3},{3,2},{4,5},{5,4},{6,7},{7,6},{8,9},{9,8},{10,11... | collective-permute-start | bytes 319496 | tf_op jit(solution)/shard_map/ppermute | solution.py:471
  29.7 8.5 %collective-permute-start.3 = (f32[96,1024]{1,0:T(8,128)S(1)}, f32[96,1024]{1,0:T(8,128)S(1)}, u32[]{:S(2)}, u32[]{:S(2)}) collective-permute-start(f32[96,1024]{1,0:T(8,128)S(1)} %get-tuple-element.17.refs_0_), channel_id=1, source_target_pairs={{1,0},{4,1},{5,4},{8,5},{9,8},{12,9},{13,12},{16,13},{17,16},{20,1... | collective-permute-start | bytes 1179656 | tf_op jit(solution)/shard_map/ppermute | solution.py:450
  39.0 2.2 %collective-permute-start.4 = (f32[2,96,96]{2,1,0:T(8,128)S(1)}, f32[2,96,96]{2,1,0:T(8,128)S(1)}, u32[]{:S(2)}, u32[]{:S(2)}) collective-permute-start(f32[2,96,96]{2,1,0:T(8,128)S(1)} %shard_map.58.own_ref), channel_id=1, source_target_pairs={{0,1},{1,0},{4,5},{5,4},{8,9},{9,8},{12,13},{13,12},{16,17},{17,16... | collective-permute-start | bytes 221192 | tf_op jit(solution)/shard_map/ppermute | solution.py:519
  41.5 12.1 %copy-start.4 = (f32[2,2,96]{2,1,0:T(2,128)S(1)}, f32[2,2,96]{2,1,0:T(2,128)}, u32[]{:S(2)}) copy-start(f32[2,2,96]{2,1,0:T(2,128)} %param.9) | copy-start | bytes 4612
  41.5 5.7 %collective-permute-start.5 = (f32[2,96,96]{2,1,0:T(8,128)S(1)}, f32[2,96,96]{2,1,0:T(8,128)S(1)}, u32[]{:S(2)}, u32[]{:S(2)}) collective-permute-start(f32[2,96,96]{2,1,0:T(8,128)S(1)} %shard_map.59.own_ref), channel_id=1, source_target_pairs={{0,4},{1,5},{4,0},{5,1},{8,12},{9,13},{12,8},{13,9},{16,20},{17,21... | collective-permute-start | bytes 221192 | tf_op jit(solution)/shard_map/ppermute | solution.py:519
  47.5 7.9 %collective-permute-start.7 = (f32[2,96,96]{2,1,0:T(8,128)S(1)}, f32[2,96,96]{2,1,0:T(8,128)S(1)}, u32[]{:S(2)}, u32[]{:S(2)}) collective-permute-start(f32[2,96,96]{2,1,0:T(8,128)S(1)} %shard_map.60), channel_id=1, source_target_pairs={{0,8},{1,9},{4,12},{5,13},{8,16},{9,17},{12,20},{13,21},{16,24},{1... | collective-permute-start | bytes 221192 | tf_op jit(solution)/shard_map/ppermute | solution.py:510
  49.6 8.8 %collective-permute-start.8 = (f32[2,96,96]{2,1,0:T(8,128)S(1)}, f32[2,96,96]{2,1,0:T(8,128)S(1)}, u32[]{:S(2)}, u32[]{:S(2)}) collective-permute-start(f32[2,96,96]{2,1,0:T(8,128)S(1)} %shard_map.60), channel_id=1, source_target_pairs={{0,16},{1,17},{4,20},{5,21},{8,24},{9,25},{12,28},{13,29},{16,0},{... | collective-permute-start | bytes 221192 | tf_op jit(solution)/shard_map/ppermute | solution.py:510
  52.2 6.8 %collective-permute-start.6 = (f32[2,96,96]{2,1,0:T(8,128)S(1)}, f32[2,96,96]{2,1,0:T(8,128)S(1)}, u32[]{:S(2)}, u32[]{:S(2)}) collective-permute-start(f32[2,96,96]{2,1,0:T(8,128)S(1)} %shard_map.60), channel_id=1, source_target_pairs={{0,24},{1,25},{4,28},{5,29},{8,0},{9,1},{12,4},{13,5},{16,8},{17,9... | collective-permute-start | bytes 221192 | tf_op jit(solution)/shard_map/ppermute | solution.py:510
  59.6 3.6 %collective-permute-start.10 = (f32[2,2,256]{2,1,0:T(2,128)S(1)}, f32[2,2,256]{2,1,0:T(2,128)S(1)}, u32[]{:S(2)}, u32[]{:S(2)}) collective-permute-start(f32[2,2,256]{2,1,0:T(2,128)S(1)} %get-tuple-element.27), channel_id=1, source_target_pairs={{0,2},{1,3},{2,0},{3,1},{4,6},{5,7},{6,4},{7,5},{8,10},{9,11},{10,... | collective-permute-start | bytes 12296 | tf_op jit(solution)/shard_map/ppermute | solution.py:453
  61.1 2.1 %collective-permute-start.11 = (f32[2,2,256]{2,1,0:T(2,128)S(1)}, f32[2,2,256]{2,1,0:T(2,128)S(1)}, u32[]{:S(2)}, u32[]{:S(2)}) collective-permute-start(f32[2,2,256]{2,1,0:T(2,128)S(1)} %get-tuple-element.28), channel_id=1, source_target_pairs={{0,3},{1,0},{2,1},{3,2},{4,7},{5,4},{6,5},{7,6},{8,11},{9,8},{10,9... | collective-permute-start | bytes 12296 | tf_op jit(solution)/shard_map/ppermute | solution.py:453
  61.1 3.0 %collective-permute-start.9 = (f32[2,2,256]{2,1,0:T(2,128)S(1)}, f32[2,2,256]{2,1,0:T(2,128)S(1)}, u32[]{:S(2)}, u32[]{:S(2)}) collective-permute-start(f32[2,2,256]{2,1,0:T(2,128)S(1)} %get-tuple-element.26), channel_id=1, source_target_pairs={{0,1},{1,2},{2,3},{3,0},{4,5},{5,6},{6,7},{7,4},{8,9},{9,10},{10,1... | collective-permute-start | bytes 12296 | tf_op jit(solution)/shard_map/ppermute | solution.py:453

commit v12 on v11

--- a/solution.py
+++ b/solution.py
@@ -175,30 +175,6 @@
 DOWN = 2.0**-13
 
 
-def pack_body(modes, start_ref, base_ref, perturb_ref, out_ref, base_buf, perturb_buf, sems):
-    copies = [
-        pltpu.make_async_copy(source, target, sems.at[i])
-        for i, (source, target) in enumerate(
-            (
-                (start_ref, out_ref.at[0:modes]),
-                (base_ref, base_buf),
-                (perturb_ref, perturb_buf),
-            )
-        )
-    ]
-    for copy in copies:
-        copy.start()
-    copies[1].wait()
-    copies[2].wait()
-    seg_count = perturb_ref.shape[0]
-    rest = out_ref.shape[0] - modes - 1 - seg_count
-    lines = [base_buf[...], perturb_buf[...]]
-    if rest:
-        lines.append(jnp.zeros((rest, out_ref.shape[1]), jnp.float32))
-    out_ref[modes:, :] = jnp.concatenate(lines, axis=0)
-    copies[0].wait()
-
-
 def iterate_body(n_alt, chunk, seg_count, modes, width, scale_ref, *refs):
     blocks, image_refs = refs[:n_alt], refs[n_alt : n_alt + chunk]
     coef_ref, basis_ref, split_ref, gram_ref, inv_ref = refs[n_alt + chunk :]
@@ -452,17 +428,8 @@
     def around(value, k):
         return lax.ppermute(value, "alt", [(i, (i + k) % n_alt) for i in range(n_alt)])
 
-    mine = kernel_call(
-        functools.partial(pack_body, modes),
-        shape(-(-(modes + 1 + seg_count) // 8) * 8, width),
-        [start_block, base_profile[None, :], perturb],
-        [pl.BlockSpec(memory_space=pltpu.HBM)] * 3,
-        [
-            pltpu.VMEM((1, width), jnp.float32),
-            pltpu.VMEM((seg_count, width), jnp.float32),
-            pltpu.SemaphoreType.DMA((3,)),
-        ],
-    )
+    filler = jnp.zeros((-(modes + 1 + seg_count) % 8, width), jnp.float32)
+    mine = jnp.concatenate([start_block, base_profile[None, :], perturb, filler], axis=0)
     found, bit = {0: mine}, n_alt
     while bit > 1:
         bit //= 2

time: 64.9 us -> 64.3 us (level)
  local copies, waits for them, and re-layouts: 2.27 us -> 0.77 us
  other arithmetic: 0 us -> 0.98 us
    unnamed x10 -> x8, local copies, waits for them, and re-layouts: 2.27 us -> 0.69 us
    concatenate x0 -> x1, other arithmetic: none -> 0.98 us  [local(): jnp.concatenate([start_block, base_profile[None, :], perturb, filler], ax...]
    pallas_call x11 -> x10, Pallas kernels: 31.8 us -> 31.7 us  [kernel_call(): pl.pallas_call(body, out_shape=out_shape, in_specs=specs, out_specs=jax.t...]
where the time goes in v12:
time: 64.3 us; the launch traced here: 64.1 us
  Pallas kernels  31.7 us (49%)
  starting transfers between devices  15.9 us (25%)
  waiting for transfers between devices  14.6 us (23%)
  other arithmetic  0.98 us (2%)
  local copies, waits for them, and re-layouts  0.77 us (1%)
    pallas_call x10, Pallas kernels, kernel_call(): pl.pallas_call(body, out_shape=out_shape, in_specs=specs, out_specs=jax.t...  31.7 us
    ppermute x3, starting transfers between devices, turned(): return lax.ppermute(value, ('range', 'alt'), pairs)  6.05 us
    ppermute x3, waiting for transfers between devices, local(): found[key ^ bit] = lax.ppermute(found[key], 'alt', pairs)  4.28 us
    ppermute x2, waiting for transfers between devices, local(): beside.append(lax.ppermute(span, ('range', 'alt'), pairs))  4.26 us
    ppermute x2, starting transfers between devices, local(): beside.append(lax.ppermute(span, ('range', 'alt'), pairs))  3.57 us
    ppermute x3, waiting for transfers between devices, turned(): return lax.ppermute(value, ('range', 'alt'), pairs)  3.54 us
    ppermute x3, starting transfers between devices, local(): found[key ^ bit] = lax.ppermute(found[key], 'alt', pairs)  3.01 us
    ppermute x3, waiting for transfers between devices, around(): lax.ppermute(value, 'alt', [(i, (i + k) % n_alt) for i in range(n_alt)])  2.52 us
  transfers between devices with their start and end apart: 12, of which 8 were waited for; matrix products, arithmetic and copies ran while one was open for 0% of the time, Pallas kernels for 14%

profile of v12, /device:TPU:0, one launch (start us, length us, event | category | flops | bytes accessed | tf_op | source)
XLA Modules:
  0.0 64.1 jit_solution(9948734494068032851)
XLA Ops:
  0.0 0.1 pad.4.clone
  0.1 0.6 copy-done.1
  0.7 0.1 copy-done.3
  0.8 1.0 %maximum_maximum_fusion.refs_0_ = f32[104,256]{1,0:T(8,128)S(1)} fusion(f32[4,256]{1,0:T(4,128)S(1)} %copy-done.1, f32[1,256]{1,0:T(1,128)S(1)} %bitcast.1, f32[96,256]{1,0:T(8,128)} %param.8, f32[104]{0:T(128)S(1)} %pad.4.clone), kind=kLoop, calls=%fused_computation | loop fusion | flops 79872 | bytes 210336 | tf_op jit(solution)/shard_map/concatenate | solution.py:432
  1.8 3.0 %collective-permute-start.1 = (f32[104,256]{1,0:T(8,128)S(1)}, f32[104,256]{1,0:T(8,128)S(1)}, u32[]{:S(2)}, u32[]{:S(2)}) collective-permute-start(f32[104,256]{1,0:T(8,128)S(1)} %maximum_maximum_fusion.refs_0_), channel_id=1, source_target_pairs={{0,2},{1,3},{2,0},{3,1},{4,6},{5,7},{6,4},{7,5},{8,10},{9,11},{10,... | collective-permute-start | bytes 319496 | tf_op jit(solution)/shard_map/ppermute | solution.py:438
  4.8 3.0 %collective-permute-done.1.refs_2_ = f32[104,256]{1,0:T(8,128)S(1)} collective-permute-done((f32[104,256]{1,0:T(8,128)S(1)}, f32[104,256]{1,0:T(8,128)S(1)}, u32[]{:S(2)}, u32[]{:S(2)}) %collective-permute-start.1) | collective-permute-done | bytes 106528 | tf_op jit(solution)/shard_map/ppermute | solution.py:438
  7.7 1.3 %collective-permute-done.2.refs_3_ = f32[104,256]{1,0:T(8,128)S(1)} collective-permute-done((f32[104,256]{1,0:T(8,128)S(1)}, f32[104,256]{1,0:T(8,128)S(1)}, u32[]{:S(2)}, u32[]{:S(2)}) %collective-permute-start.2) | collective-permute-done | bytes 106528 | tf_op jit(solution)/shard_map/ppermute | solution.py:438
  9.0 20.0 %shard_map.55 = (f32[96,1024]{1,0:T(8,128)S(1)}, f32[96,1024]{1,0:T(8,128)S(1)}, f32[2,1024]{1,0:T(2,128)S(1)}) custom-call(f32[2]{0:T(128)S(1)} %copy-done, f32[104,256]{1,0:T(8,128)S(1)} %maximum_maximum_fusion.refs_0_, f32[104,256]{1,0:T(8,128)S(1)} %collective-permute-done.refs_1_, f32[104,256]{1,0:T(8,128)S(1)} %collective-permute-done.1.refs_2_, ...), custom_call_target="tpu_custom_call" | custom-call | flops 603979776 | bytes 1220616 | tf_op jit(solution)/shard_map/pallas_call | solution.py:45
  29.0 1.3 %collective-permute-start.3 = (f32[96,1024]{1,0:T(8,128)S(1)}, f32[96,1024]{1,0:T(8,128)S(1)}, u32[]{:S(2)}, u32[]{:S(2)}) collective-permute-start(f32[96,1024]{1,0:T(8,128)S(1)} %get-tuple-element.17.refs_0_), channel_id=1, source_target_pairs={{1,0},{4,1},{5,4},{8,5},{9,8},{12,9},{13,12},{16,13},{17,16},{20,1... | collective-permute-start | bytes 1179656 | tf_op jit(solution)/shard_map/ppermute | solution.py:426
  30.3 7.2 %shard_map.56 = (f32[96,1024]{1,0:T(8,128)S(1)}, f32[96,1024]{1,0:T(8,128)S(1)}, f32[96,96]{1,0:T(8,128)S(1)}, f32[2,96,96]{2,1,0:T(8,128)S(1)}, f32[2,96,96]{2,1,0:T(8,128)S(1)}) custom-call(f32[2,1024]{1,0:T(2,128)S(1)} %get-tuple-element.18.coef_ref, f32[96,1024]{1,0:T(8,128)S(1)} %get-tuple-element.17.refs_0_, f32[96,1024]{1,0:T(8,128)S(1)} %get-tuple-element.19.refs_1_), custom_call_target="tpu_custom_call" | custom-call | flops 301989888 | bytes 1765376 | tf_op jit(solution)/shard_map/pallas_call | solution.py:45
  37.5 0.8 %shard_map.57.own_ref = f32[2,96,96]{2,1,0:T(8,128)S(1)} custom-call(f32[96,1024]{1,0:T(8,128)S(1)} %collective-permute-done.3.next_ref, f32[96,1024]{1,0:T(8,128)S(1)} %get-tuple-element.20.second_ref.refs_3_, f32[2,96,96]{2,1,0:T(8,128)S(1)} %get-tuple-element.21.rest_ref), custom_call_target="tpu_custom_call" | custom-call | flops 18874368 | bytes 933888 | tf_op jit(solution)/shard_map/pallas_call | solution.py:45
  38.3 1.2 %collective-permute-start.4 = (f32[2,96,96]{2,1,0:T(8,128)S(1)}, f32[2,96,96]{2,1,0:T(8,128)S(1)}, u32[]{:S(2)}, u32[]{:S(2)}) collective-permute-start(f32[2,96,96]{2,1,0:T(8,128)S(1)} %shard_map.57.own_ref), channel_id=1, source_target_pairs={{0,1},{1,0},{4,5},{5,4},{8,9},{9,8},{12,13},{13,12},{16,17},{17,16... | collective-permute-start | bytes 221192 | tf_op jit(solution)/shard_map/ppermute | solution.py:486
  39.5 0.9 %collective-permute-done.4.other_ref.refs_0_ = f32[2,96,96]{2,1,0:T(8,128)S(1)} collective-permute-done((f32[2,96,96]{2,1,0:T(8,128)S(1)}, f32[2,96,96]{2,1,0:T(8,128)S(1)}, u32[]{:S(2)}, u32[]{:S(2)}) %collective-permute-start.4) | collective-permute-done | bytes 73760 | tf_op jit(solution)/shard_map/ppermute | solution.py:486
  40.5 0.3 shard_map.58.own_ref
  40.8 0.0 copy-start.2
  40.8 2.4 %collective-permute-start.5 = (f32[2,96,96]{2,1,0:T(8,128)S(1)}, f32[2,96,96]{2,1,0:T(8,128)S(1)}, u32[]{:S(2)}, u32[]{:S(2)}) collective-permute-start(f32[2,96,96]{2,1,0:T(8,128)S(1)} %shard_map.58.own_ref), channel_id=1, source_target_pairs={{0,4},{1,5},{4,0},{5,1},{8,12},{9,13},{12,8},{13,9},{16,20},{17,21... | collective-permute-start | bytes 221192 | tf_op jit(solution)/shard_map/ppermute | solution.py:486
  43.2 3.3 %collective-permute-done.5.other_ref.refs_1_ = f32[2,96,96]{2,1,0:T(8,128)S(1)} collective-permute-done((f32[2,96,96]{2,1,0:T(8,128)S(1)}, f32[2,96,96]{2,1,0:T(8,128)S(1)}, u32[]{:S(2)}, u32[]{:S(2)}) %collective-permute-start.5) | collective-permute-done | bytes 73760 | tf_op jit(solution)/shard_map/ppermute | solution.py:486
  46.5 0.3 shard_map.59
  46.8 2.1 %collective-permute-start.7 = (f32[2,96,96]{2,1,0:T(8,128)S(1)}, f32[2,96,96]{2,1,0:T(8,128)S(1)}, u32[]{:S(2)}, u32[]{:S(2)}) collective-permute-start(f32[2,96,96]{2,1,0:T(8,128)S(1)} %shard_map.59), channel_id=1, source_target_pairs={{0,8},{1,9},{4,12},{5,13},{8,16},{9,17},{12,20},{13,21},{16,24},{1... | collective-permute-start | bytes 221192 | tf_op jit(solution)/shard_map/ppermute | solution.py:477
  48.9 2.6 %collective-permute-start.8 = (f32[2,96,96]{2,1,0:T(8,128)S(1)}, f32[2,96,96]{2,1,0:T(8,128)S(1)}, u32[]{:S(2)}, u32[]{:S(2)}) collective-permute-start(f32[2,96,96]{2,1,0:T(8,128)S(1)} %shard_map.59), channel_id=1, source_target_pairs={{0,16},{1,17},{4,20},{5,21},{8,24},{9,25},{12,28},{13,29},{16,0},{... | collective-permute-start | bytes 221192 | tf_op jit(solution)/shard_map/ppermute | solution.py:477
  51.5 1.3 %collective-permute-start.6 = (f32[2,96,96]{2,1,0:T(8,128)S(1)}, f32[2,96,96]{2,1,0:T(8,128)S(1)}, u32[]{:S(2)}, u32[]{:S(2)}) collective-permute-start(f32[2,96,96]{2,1,0:T(8,128)S(1)} %shard_map.59), channel_id=1, source_target_pairs={{0,24},{1,25},{4,28},{5,29},{8,0},{9,1},{12,4},{13,5},{16,8},{17,9... | collective-permute-start | bytes 221192 | tf_op jit(solution)/shard_map/ppermute | solution.py:477
  52.9 0.9 %shard_map.60.inside_ref = f32[2,2,96,96]{3,2,1,0:T(8,128)S(1)} custom-call(f32[2,96,96]{2,1,0:T(8,128)S(1)} %collective-permute-done.4.other_ref.refs_0_, f32[2,96,96]{2,1,0:T(8,128)S(1)} %collective-permute-done.5.other_ref.refs_1_, f32[96,96]{1,0:T(8,128)S(1)} %get-tuple-element.22.refs_2_, f32[2,96,96]{2,1,0:T(8,128)S(1)} %get-tuple-element.23.refs_3_), custom_call_target="tpu_custom_call" | custom-call | flops 18874368 | bytes 405504 | tf_op jit(solution)/shard_map/pallas_call | solution.py:45
  53.7 1.0 %collective-permute-done.7.span_ref = f32[2,96,96]{2,1,0:T(8,128)S(1)} collective-permute-done((f32[2,96,96]{2,1,0:T(8,128)S(1)}, f32[2,96,96]{2,1,0:T(8,128)S(1)}, u32[]{:S(2)}, u32[]{:S(2)}) %collective-permute-start.7) | collective-permute-done | bytes 73760 | tf_op jit(solution)/shard_map/ppermute | solution.py:477
  54.7 0.5 shard_map.61.inside_ref
  55.2 2.6 %collective-permute-done.8.span_ref = f32[2,96,96]{2,1,0:T(8,128)S(1)} collective-permute-done((f32[2,96,96]{2,1,0:T(8,128)S(1)}, f32[2,96,96]{2,1,0:T(8,128)S(1)}, u32[]{:S(2)}, u32[]{:S(2)}) %collective-permute-start.8) | collective-permute-done | bytes 73760 | tf_op jit(solution)/shard_map/ppermute | solution.py:477
  57.7 0.6 shard_map.62.refs_1_
  58.3 0.6 shard_map.63
  58.9 1.5 %collective-permute-start.10 = (f32[2,2,256]{2,1,0:T(2,128)S(1)}, f32[2,2,256]{2,1,0:T(2,128)S(1)}, u32[]{:S(2)}, u32[]{:S(2)}) collective-permute-start(f32[2,2,256]{2,1,0:T(2,128)S(1)} %get-tuple-element.27), channel_id=1, source_target_pairs={{0,2},{1,3},{2,0},{3,1},{4,6},{5,7},{6,4},{7,5},{8,10},{9,11},{10,... | collective-permute-start | bytes 12296 | tf_op jit(solution)/shard_map/ppermute | solution.py:429
  60.4 0.5 collective-permute-start.9
  60.9 1.6 %collective-permute-done.10.refs_2_ = f32[2,2,256]{2,1,0:T(2,128)S(1)} collective-permute-done((f32[2,2,256]{2,1,0:T(2,128)S(1)}, f32[2,2,256]{2,1,0:T(2,128)S(1)}, u32[]{:S(2)}, u32[]{:S(2)}) %collective-permute-start.10) | collective-permute-done | bytes 4128 | tf_op jit(solution)/shard_map/ppermute | solution.py:429
  62.5 0.9 %collective-permute-done.9.refs_1_ = f32[2,2,256]{2,1,0:T(2,128)S(1)} collective-permute-done((f32[2,2,256]{2,1,0:T(2,128)S(1)}, f32[2,2,256]{2,1,0:T(2,128)S(1)}, u32[]{:S(2)}, u32[]{:S(2)}) %collective-permute-start.9) | collective-permute-done | bytes 4128 | tf_op jit(solution)/shard_map/ppermute | solution.py:429
  63.5 0.6 shard_map.64
  (14 shorter events, 0.0 us)
Async XLA Ops:
  0.0 0.7 %copy-start.1 = (f32[4,256]{1,0:T(4,128)S(1)}, f32[4,256]{1,0:T(4,128)}, u32[]{:S(2)}) copy-start(f32[4,256]{1,0:T(4,128)} %param.7) | copy-start | bytes 12292
  0.1 0.7 %copy-start.3 = (f32[256]{0:T(256)S(1)}, f32[256]{0:T(256)}, u32[]{:S(2)}) copy-start(f32[256]{0:T(256)} %param.6) | copy-start | bytes 3076
  0.8 8.3 %copy-start = (f32[2]{0:T(128)S(1)}, f32[2]{0:T(128)}, u32[]{:S(2)}) copy-start(f32[2]{0:T(128)} %scale_ref.1) | copy-start | bytes 28
  1.8 6.0 %collective-permute-start.1 = (f32[104,256]{1,0:T(8,128)S(1)}, f32[104,256]{1,0:T(8,128)S(1)}, u32[]{:S(2)}, u32[]{:S(2)}) collective-permute-start(f32[104,256]{1,0:T(8,128)S(1)} %maximum_maximum_fusion.refs_0_), channel_id=1, source_target_pairs={{0,2},{1,3},{2,0},{3,1},{4,6},{5,7},{6,4},{7,5},{8,10},{9,11},{10,... | collective-permute-start | bytes 319496 | tf_op jit(solution)/shard_map/ppermute | solution.py:438
  4.8 3.0 %collective-permute-start = (f32[104,256]{1,0:T(8,128)S(1)}, f32[104,256]{1,0:T(8,128)S(1)}, u32[]{:S(2)}, u32[]{:S(2)}) collective-permute-start(f32[104,256]{1,0:T(8,128)S(1)} %maximum_maximum_fusion.refs_0_), channel_id=1, source_target_pairs={{0,1},{1,0},{2,3},{3,2},{4,5},{5,4},{6,7},{7,6},{8,9},{9,8},{10,11... | collective-permute-start | bytes 319496 | tf_op jit(solution)/shard_map/ppermute | solution.py:438
  7.7 1.3 %collective-permute-start.2 = (f32[104,256]{1,0:T(8,128)S(1)}, f32[104,256]{1,0:T(8,128)S(1)}, u32[]{:S(2)}, u32[]{:S(2)}) collective-permute-start(f32[104,256]{1,0:T(8,128)S(1)} %collective-permute-done.1.refs_2_), channel_id=1, source_target_pairs={{0,1},{1,0},{2,3},{3,2},{4,5},{5,4},{6,7},{7,6},{8,9},{9,8},{10,11... | collective-permute-start | bytes 319496 | tf_op jit(solution)/shard_map/ppermute | solution.py:438
  29.0 8.5 %collective-permute-start.3 = (f32[96,1024]{1,0:T(8,128)S(1)}, f32[96,1024]{1,0:T(8,128)S(1)}, u32[]{:S(2)}, u32[]{:S(2)}) collective-permute-start(f32[96,1024]{1,0:T(8,128)S(1)} %get-tuple-element.17.refs_0_), channel_id=1, source_target_pairs={{1,0},{4,1},{5,4},{8,5},{9,8},{12,9},{13,12},{16,13},{17,16},{20,1... | collective-permute-start | bytes 1179656 | tf_op jit(solution)/shard_map/ppermute | solution.py:426
  38.3 2.1 %collective-permute-start.4 = (f32[2,96,96]{2,1,0:T(8,128)S(1)}, f32[2,96,96]{2,1,0:T(8,128)S(1)}, u32[]{:S(2)}, u32[]{:S(2)}) collective-permute-start(f32[2,96,96]{2,1,0:T(8,128)S(1)} %shard_map.57.own_ref), channel_id=1, source_target_pairs={{0,1},{1,0},{4,5},{5,4},{8,9},{9,8},{12,13},{13,12},{16,17},{17,16... | collective-permute-start | bytes 221192 | tf_op jit(solution)/shard_map/ppermute | solution.py:486
  40.8 12.1 %copy-start.2 = (f32[2,2,96]{2,1,0:T(2,128)S(1)}, f32[2,2,96]{2,1,0:T(2,128)}, u32[]{:S(2)}) copy-start(f32[2,2,96]{2,1,0:T(2,128)} %param.9) | copy-start | bytes 4612
  40.8 5.7 %collective-permute-start.5 = (f32[2,96,96]{2,1,0:T(8,128)S(1)}, f32[2,96,96]{2,1,0:T(8,128)S(1)}, u32[]{:S(2)}, u32[]{:S(2)}) collective-permute-start(f32[2,96,96]{2,1,0:T(8,128)S(1)} %shard_map.58.own_ref), channel_id=1, source_target_pairs={{0,4},{1,5},{4,0},{5,1},{8,12},{9,13},{12,8},{13,9},{16,20},{17,21... | collective-permute-start | bytes 221192 | tf_op jit(solution)/shard_map/ppermute | solution.py:486
  46.8 7.9 %collective-permute-start.7 = (f32[2,96,96]{2,1,0:T(8,128)S(1)}, f32[2,96,96]{2,1,0:T(8,128)S(1)}, u32[]{:S(2)}, u32[]{:S(2)}) collective-permute-start(f32[2,96,96]{2,1,0:T(8,128)S(1)} %shard_map.59), channel_id=1, source_target_pairs={{0,8},{1,9},{4,12},{5,13},{8,16},{9,17},{12,20},{13,21},{16,24},{1... | collective-permute-start | bytes 221192 | tf_op jit(solution)/shard_map/ppermute | solution.py:477
  48.9 8.8 %collective-permute-start.8 = (f32[2,96,96]{2,1,0:T(8,128)S(1)}, f32[2,96,96]{2,1,0:T(8,128)S(1)}, u32[]{:S(2)}, u32[]{:S(2)}) collective-permute-start(f32[2,96,96]{2,1,0:T(8,128)S(1)} %shard_map.59), channel_id=1, source_target_pairs={{0,16},{1,17},{4,20},{5,21},{8,24},{9,25},{12,28},{13,29},{16,0},{... | collective-permute-start | bytes 221192 | tf_op jit(solution)/shard_map/ppermute | solution.py:477
  51.5 6.8 %collective-permute-start.6 = (f32[2,96,96]{2,1,0:T(8,128)S(1)}, f32[2,96,96]{2,1,0:T(8,128)S(1)}, u32[]{:S(2)}, u32[]{:S(2)}) collective-permute-start(f32[2,96,96]{2,1,0:T(8,128)S(1)} %shard_map.59), channel_id=1, source_target_pairs={{0,24},{1,25},{4,28},{5,29},{8,0},{9,1},{12,4},{13,5},{16,8},{17,9... | collective-permute-start | bytes 221192 | tf_op jit(solution)/shard_map/ppermute | solution.py:477
  58.9 3.6 %collective-permute-start.10 = (f32[2,2,256]{2,1,0:T(2,128)S(1)}, f32[2,2,256]{2,1,0:T(2,128)S(1)}, u32[]{:S(2)}, u32[]{:S(2)}) collective-permute-start(f32[2,2,256]{2,1,0:T(2,128)S(1)} %get-tuple-element.27), channel_id=1, source_target_pairs={{0,2},{1,3},{2,0},{3,1},{4,6},{5,7},{6,4},{7,5},{8,10},{9,11},{10,... | collective-permute-start | bytes 12296 | tf_op jit(solution)/shard_map/ppermute | solution.py:429
  60.4 2.1 %collective-permute-start.11 = (f32[2,2,256]{2,1,0:T(2,128)S(1)}, f32[2,2,256]{2,1,0:T(2,128)S(1)}, u32[]{:S(2)}, u32[]{:S(2)}) collective-permute-start(f32[2,2,256]{2,1,0:T(2,128)S(1)} %get-tuple-element.28), channel_id=1, source_target_pairs={{0,3},{1,0},{2,1},{3,2},{4,7},{5,4},{6,5},{7,6},{8,11},{9,8},{10,9... | collective-permute-start | bytes 12296 | tf_op jit(solution)/shard_map/ppermute | solution.py:429
  60.4 3.0 %collective-permute-start.9 = (f32[2,2,256]{2,1,0:T(2,128)S(1)}, f32[2,2,256]{2,1,0:T(2,128)S(1)}, u32[]{:S(2)}, u32[]{:S(2)}) collective-permute-start(f32[2,2,256]{2,1,0:T(2,128)S(1)} %get-tuple-element.26), channel_id=1, source_target_pairs={{0,1},{1,2},{2,3},{3,0},{4,5},{5,6},{6,7},{7,4},{8,9},{9,10},{10,1... | collective-permute-start | bytes 12296 | tf_op jit(solution)/shard_map/ppermute | solution.py:429

commit v13 on v12

--- a/solution.py
+++ b/solution.py
@@ -199,7 +199,7 @@
     def packed_row(i, at):
         return at // HALF * 128 + i * 64 + at % HALF
 
-    def step(_, carry):
+    def step(n):
         for i in range(chunk):
             coef = coef_ref[i : i + 1, :]
             for at in range(0, modes, 16):
@@ -207,9 +207,9 @@
                 row = packed_row(i, at)
                 for part in range(3):
                     piece = image.astype(jnp.bfloat16)
-                    split_ref[part, row : row + 16, :] = piece
+                    split_ref[3 * (n % 2) + part, row : row + 16, :] = piece
                     image = image - piece.astype(jnp.float32)
-        gram_ref[...] = short_mmt(split_ref[0], split_ref[0]) * DOWN
+        gram_ref[...] = short_mmt(split_ref[3 * (n % 2)], split_ref[3 * (n % 2)]) * DOWN
         work = []
         for at in range(0, modes, 8):
             one, two = packed_row(0, at), packed_row(1, at)
@@ -235,11 +235,12 @@
         for i in range(chunk):
             for at in range(0, total, 256):
                 basis_ref[i, :, at : at + 256] = sum(
-                    short_mm(inv_ref[i], split_ref[part, :, at : at + 256]) for part in range(3)
+                    short_mm(inv_ref[i], split_ref[3 * (n % 2) + part, :, at : at + 256])
+                    for part in range(3)
                 )
-        return carry
-
-    lax.fori_loop(0, ITERS - 1, step, 0, unroll=True)
+
+    for n in range(ITERS - 1):
+        step(n)
     for i in range(chunk):
         for at in range(0, modes, 8):
             image_refs[i][at : at + 8, :] = doubled_operator(
@@ -445,7 +446,7 @@
         [SM] + [VM] * n_alt,
         [
             pltpu.VMEM((chunk, modes, total), jnp.float32),
-            pltpu.VMEM((3, 256, total), jnp.bfloat16),
+            pltpu.VMEM((6, 256, total), jnp.bfloat16),
             pltpu.VMEM((256, 256), jnp.float32),
             pltpu.VMEM((chunk, modes, 256), jnp.bfloat16),
         ],

time: 64.3 us -> 64.3 us (level)
  no operation moved by 1% of the time
where the time goes in v13:
time: 64.3 us; the launch traced here: 64.1 us
  Pallas kernels  31.7 us (49%)
  starting transfers between devices  15.9 us (25%)
  waiting for transfers between devices  14.6 us (23%)
  other arithmetic  0.98 us (2%)
  local copies, waits for them, and re-layouts  0.77 us (1%)
    pallas_call x10, Pallas kernels, kernel_call(): pl.pallas_call(body, out_shape=out_shape, in_specs=specs, out_specs=jax.t...  31.7 us
    ppermute x3, starting transfers between devices, turned(): return lax.ppermute(value, ('range', 'alt'), pairs)  6.05 us
    ppermute x3, waiting for transfers between devices, local(): found[key ^ bit] = lax.ppermute(found[key], 'alt', pairs)  4.28 us
    ppermute x2, waiting for transfers between devices, local(): beside.append(lax.ppermute(span, ('range', 'alt'), pairs))  4.26 us
    ppermute x2, starting transfers between devices, local(): beside.append(lax.ppermute(span, ('range', 'alt'), pairs))  3.57 us
    ppermute x3, waiting for transfers between devices, turned(): return lax.ppermute(value, ('range', 'alt'), pairs)  3.54 us
    ppermute x3, starting transfers between devices, local(): found[key ^ bit] = lax.ppermute(found[key], 'alt', pairs)  3.01 us
    ppermute x3, waiting for transfers between devices, around(): lax.ppermute(value, 'alt', [(i, (i + k) % n_alt) for i in range(n_alt)])  2.52 us
  transfers between devices with their start and end apart: 12, of which 8 were waited for; matrix products, arithmetic and copies ran while one was open for 0% of the time, Pallas kernels for 14%

profile of v13, /device:TPU:0, one launch (start us, length us, event | category | flops | bytes accessed | tf_op | source)
XLA Modules:
  0.0 64.1 jit_solution(9948734494068032851)
XLA Ops:
  0.0 0.1 pad.4.clone
  0.1 0.6 copy-done.1
  0.7 0.1 copy-done.3
  0.8 1.0 %maximum_maximum_fusion.refs_0_ = f32[104,256]{1,0:T(8,128)S(1)} fusion(f32[4,256]{1,0:T(4,128)S(1)} %copy-done.1, f32[1,256]{1,0:T(1,128)S(1)} %bitcast.1, f32[96,256]{1,0:T(8,128)} %param.8, f32[104]{0:T(128)S(1)} %pad.4.clone), kind=kLoop, calls=%fused_computation | loop fusion | flops 79872 | bytes 210336 | tf_op jit(solution)/shard_map/concatenate | solution.py:433
  1.8 3.0 %collective-permute-start.1 = (f32[104,256]{1,0:T(8,128)S(1)}, f32[104,256]{1,0:T(8,128)S(1)}, u32[]{:S(2)}, u32[]{:S(2)}) collective-permute-start(f32[104,256]{1,0:T(8,128)S(1)} %maximum_maximum_fusion.refs_0_), channel_id=1, source_target_pairs={{0,2},{1,3},{2,0},{3,1},{4,6},{5,7},{6,4},{7,5},{8,10},{9,11},{10,... | collective-permute-start | bytes 319496 | tf_op jit(solution)/shard_map/ppermute | solution.py:439
  4.8 3.0 %collective-permute-done.1.refs_2_ = f32[104,256]{1,0:T(8,128)S(1)} collective-permute-done((f32[104,256]{1,0:T(8,128)S(1)}, f32[104,256]{1,0:T(8,128)S(1)}, u32[]{:S(2)}, u32[]{:S(2)}) %collective-permute-start.1) | collective-permute-done | bytes 106528 | tf_op jit(solution)/shard_map/ppermute | solution.py:439
  7.7 1.3 %collective-permute-done.2.refs_3_ = f32[104,256]{1,0:T(8,128)S(1)} collective-permute-done((f32[104,256]{1,0:T(8,128)S(1)}, f32[104,256]{1,0:T(8,128)S(1)}, u32[]{:S(2)}, u32[]{:S(2)}) %collective-permute-start.2) | collective-permute-done | bytes 106528 | tf_op jit(solution)/shard_map/ppermute | solution.py:439
  9.0 20.0 %shard_map.55 = (f32[96,1024]{1,0:T(8,128)S(1)}, f32[96,1024]{1,0:T(8,128)S(1)}, f32[2,1024]{1,0:T(2,128)S(1)}) custom-call(f32[2]{0:T(128)S(1)} %copy-done, f32[104,256]{1,0:T(8,128)S(1)} %maximum_maximum_fusion.refs_0_, f32[104,256]{1,0:T(8,128)S(1)} %collective-permute-done.refs_1_, f32[104,256]{1,0:T(8,128)S(1)} %collective-permute-done.1.refs_2_, ...), custom_call_target="tpu_custom_call" | custom-call | flops 603979776 | bytes 1220616 | tf_op jit(solution)/shard_map/pallas_call | solution.py:45
  29.0 1.3 %collective-permute-start.3 = (f32[96,1024]{1,0:T(8,128)S(1)}, f32[96,1024]{1,0:T(8,128)S(1)}, u32[]{:S(2)}, u32[]{:S(2)}) collective-permute-start(f32[96,1024]{1,0:T(8,128)S(1)} %get-tuple-element.17.refs_0_), channel_id=1, source_target_pairs={{1,0},{4,1},{5,4},{8,5},{9,8},{12,9},{13,12},{16,13},{17,16},{20,1... | collective-permute-start | bytes 1179656 | tf_op jit(solution)/shard_map/ppermute | solution.py:427
  30.3 7.2 %shard_map.56 = (f32[96,1024]{1,0:T(8,128)S(1)}, f32[96,1024]{1,0:T(8,128)S(1)}, f32[96,96]{1,0:T(8,128)S(1)}, f32[2,96,96]{2,1,0:T(8,128)S(1)}, f32[2,96,96]{2,1,0:T(8,128)S(1)}) custom-call(f32[2,1024]{1,0:T(2,128)S(1)} %get-tuple-element.18.coef_ref, f32[96,1024]{1,0:T(8,128)S(1)} %get-tuple-element.17.refs_0_, f32[96,1024]{1,0:T(8,128)S(1)} %get-tuple-element.19.refs_1_), custom_call_target="tpu_custom_call" | custom-call | flops 301989888 | bytes 1765376 | tf_op jit(solution)/shard_map/pallas_call | solution.py:45
  37.5 0.8 %shard_map.57.own_ref = f32[2,96,96]{2,1,0:T(8,128)S(1)} custom-call(f32[96,1024]{1,0:T(8,128)S(1)} %collective-permute-done.3.next_ref, f32[96,1024]{1,0:T(8,128)S(1)} %get-tuple-element.20.second_ref.refs_3_, f32[2,96,96]{2,1,0:T(8,128)S(1)} %get-tuple-element.21.rest_ref), custom_call_target="tpu_custom_call" | custom-call | flops 18874368 | bytes 933888 | tf_op jit(solution)/shard_map/pallas_call | solution.py:45
  38.3 1.2 %collective-permute-start.4 = (f32[2,96,96]{2,1,0:T(8,128)S(1)}, f32[2,96,96]{2,1,0:T(8,128)S(1)}, u32[]{:S(2)}, u32[]{:S(2)}) collective-permute-start(f32[2,96,96]{2,1,0:T(8,128)S(1)} %shard_map.57.own_ref), channel_id=1, source_target_pairs={{0,1},{1,0},{4,5},{5,4},{8,9},{9,8},{12,13},{13,12},{16,17},{17,16... | collective-permute-start | bytes 221192 | tf_op jit(solution)/shard_map/ppermute | solution.py:487
  39.5 0.9 %collective-permute-done.4.other_ref.refs_0_ = f32[2,96,96]{2,1,0:T(8,128)S(1)} collective-permute-done((f32[2,96,96]{2,1,0:T(8,128)S(1)}, f32[2,96,96]{2,1,0:T(8,128)S(1)}, u32[]{:S(2)}, u32[]{:S(2)}) %collective-permute-start.4) | collective-permute-done | bytes 73760 | tf_op jit(solution)/shard_map/ppermute | solution.py:487
  40.5 0.3 shard_map.58.own_ref
  40.8 0.0 copy-start.2
  40.8 2.4 %collective-permute-start.5 = (f32[2,96,96]{2,1,0:T(8,128)S(1)}, f32[2,96,96]{2,1,0:T(8,128)S(1)}, u32[]{:S(2)}, u32[]{:S(2)}) collective-permute-start(f32[2,96,96]{2,1,0:T(8,128)S(1)} %shard_map.58.own_ref), channel_id=1, source_target_pairs={{0,4},{1,5},{4,0},{5,1},{8,12},{9,13},{12,8},{13,9},{16,20},{17,21... | collective-permute-start | bytes 221192 | tf_op jit(solution)/shard_map/ppermute | solution.py:487
  43.2 3.3 %collective-permute-done.5.other_ref.refs_1_ = f32[2,96,96]{2,1,0:T(8,128)S(1)} collective-permute-done((f32[2,96,96]{2,1,0:T(8,128)S(1)}, f32[2,96,96]{2,1,0:T(8,128)S(1)}, u32[]{:S(2)}, u32[]{:S(2)}) %collective-permute-start.5) | collective-permute-done | bytes 73760 | tf_op jit(solution)/shard_map/ppermute | solution.py:487
  46.5 0.3 shard_map.59
  46.8 2.1 %collective-permute-start.7 = (f32[2,96,96]{2,1,0:T(8,128)S(1)}, f32[2,96,96]{2,1,0:T(8,128)S(1)}, u32[]{:S(2)}, u32[]{:S(2)}) collective-permute-start(f32[2,96,96]{2,1,0:T(8,128)S(1)} %shard_map.59), channel_id=1, source_target_pairs={{0,8},{1,9},{4,12},{5,13},{8,16},{9,17},{12,20},{13,21},{16,24},{1... | collective-permute-start | bytes 221192 | tf_op jit(solution)/shard_map/ppermute | solution.py:478
  48.9 2.6 %collective-permute-start.8 = (f32[2,96,96]{2,1,0:T(8,128)S(1)}, f32[2,96,96]{2,1,0:T(8,128)S(1)}, u32[]{:S(2)}, u32[]{:S(2)}) collective-permute-start(f32[2,96,96]{2,1,0:T(8,128)S(1)} %shard_map.59), channel_id=1, source_target_pairs={{0,16},{1,17},{4,20},{5,21},{8,24},{9,25},{12,28},{13,29},{16,0},{... | collective-permute-start | bytes 221192 | tf_op jit(solution)/shard_map/ppermute | solution.py:478
  51.5 1.3 %collective-permute-start.6 = (f32[2,96,96]{2,1,0:T(8,128)S(1)}, f32[2,96,96]{2,1,0:T(8,128)S(1)}, u32[]{:S(2)}, u32[]{:S(2)}) collective-permute-start(f32[2,96,96]{2,1,0:T(8,128)S(1)} %shard_map.59), channel_id=1, source_target_pairs={{0,24},{1,25},{4,28},{5,29},{8,0},{9,1},{12,4},{13,5},{16,8},{17,9... | collective-permute-start | bytes 221192 | tf_op jit(solution)/shard_map/ppermute | solution.py:478
  52.9 0.9 %shard_map.60.inside_ref = f32[2,2,96,96]{3,2,1,0:T(8,128)S(1)} custom-call(f32[2,96,96]{2,1,0:T(8,128)S(1)} %collective-permute-done.4.other_ref.refs_0_, f32[2,96,96]{2,1,0:T(8,128)S(1)} %collective-permute-done.5.other_ref.refs_1_, f32[96,96]{1,0:T(8,128)S(1)} %get-tuple-element.22.refs_2_, f32[2,96,96]{2,1,0:T(8,128)S(1)} %get-tuple-element.23.refs_3_), custom_call_target="tpu_custom_call" | custom-call | flops 18874368 | bytes 405504 | tf_op jit(solution)/shard_map/pallas_call | solution.py:45
  53.7 1.0 %collective-permute-done.7.span_ref = f32[2,96,96]{2,1,0:T(8,128)S(1)} collective-permute-done((f32[2,96,96]{2,1,0:T(8,128)S(1)}, f32[2,96,96]{2,1,0:T(8,128)S(1)}, u32[]{:S(2)}, u32[]{:S(2)}) %collective-permute-start.7) | collective-permute-done | bytes 73760 | tf_op jit(solution)/shard_map/ppermute | solution.py:478
  54.7 0.5 shard_map.61.inside_ref
  55.2 2.6 %collective-permute-done.8.span_ref = f32[2,96,96]{2,1,0:T(8,128)S(1)} collective-permute-done((f32[2,96,96]{2,1,0:T(8,128)S(1)}, f32[2,96,96]{2,1,0:T(8,128)S(1)}, u32[]{:S(2)}, u32[]{:S(2)}) %collective-permute-start.8) | collective-permute-done | bytes 73760 | tf_op jit(solution)/shard_map/ppermute | solution.py:478
  57.7 0.6 shard_map.62.refs_1_
  58.3 0.6 shard_map.63
  58.9 1.5 %collective-permute-start.10 = (f32[2,2,256]{2,1,0:T(2,128)S(1)}, f32[2,2,256]{2,1,0:T(2,128)S(1)}, u32[]{:S(2)}, u32[]{:S(2)}) collective-permute-start(f32[2,2,256]{2,1,0:T(2,128)S(1)} %get-tuple-element.27), channel_id=1, source_target_pairs={{0,2},{1,3},{2,0},{3,1},{4,6},{5,7},{6,4},{7,5},{8,10},{9,11},{10,... | collective-permute-start | bytes 12296 | tf_op jit(solution)/shard_map/ppermute | solution.py:430
  60.4 0.5 collective-permute-start.9
  60.9 1.6 %collective-permute-done.10.refs_2_ = f32[2,2,256]{2,1,0:T(2,128)S(1)} collective-permute-done((f32[2,2,256]{2,1,0:T(2,128)S(1)}, f32[2,2,256]{2,1,0:T(2,128)S(1)}, u32[]{:S(2)}, u32[]{:S(2)}) %collective-permute-start.10) | collective-permute-done | bytes 4128 | tf_op jit(solution)/shard_map/ppermute | solution.py:430
  62.5 0.9 %collective-permute-done.9.refs_1_ = f32[2,2,256]{2,1,0:T(2,128)S(1)} collective-permute-done((f32[2,2,256]{2,1,0:T(2,128)S(1)}, f32[2,2,256]{2,1,0:T(2,128)S(1)}, u32[]{:S(2)}, u32[]{:S(2)}) %collective-permute-start.9) | collective-permute-done | bytes 4128 | tf_op jit(solution)/shard_map/ppermute | solution.py:430
  63.5 0.6 shard_map.64
  (14 shorter events, 0.0 us)
Async XLA Ops:
  0.0 0.7 %copy-start.1 = (f32[4,256]{1,0:T(4,128)S(1)}, f32[4,256]{1,0:T(4,128)}, u32[]{:S(2)}) copy-start(f32[4,256]{1,0:T(4,128)} %param.7) | copy-start | bytes 12292
  0.1 0.7 %copy-start.3 = (f32[256]{0:T(256)S(1)}, f32[256]{0:T(256)}, u32[]{:S(2)}) copy-start(f32[256]{0:T(256)} %param.6) | copy-start | bytes 3076
  0.8 8.3 %copy-start = (f32[2]{0:T(128)S(1)}, f32[2]{0:T(128)}, u32[]{:S(2)}) copy-start(f32[2]{0:T(128)} %scale_ref.1) | copy-start | bytes 28
  1.8 6.0 %collective-permute-start.1 = (f32[104,256]{1,0:T(8,128)S(1)}, f32[104,256]{1,0:T(8,128)S(1)}, u32[]{:S(2)}, u32[]{:S(2)}) collective-permute-start(f32[104,256]{1,0:T(8,128)S(1)} %maximum_maximum_fusion.refs_0_), channel_id=1, source_target_pairs={{0,2},{1,3},{2,0},{3,1},{4,6},{5,7},{6,4},{7,5},{8,10},{9,11},{10,... | collective-permute-start | bytes 319496 | tf_op jit(solution)/shard_map/ppermute | solution.py:439
  4.8 3.0 %collective-permute-start = (f32[104,256]{1,0:T(8,128)S(1)}, f32[104,256]{1,0:T(8,128)S(1)}, u32[]{:S(2)}, u32[]{:S(2)}) collective-permute-start(f32[104,256]{1,0:T(8,128)S(1)} %maximum_maximum_fusion.refs_0_), channel_id=1, source_target_pairs={{0,1},{1,0},{2,3},{3,2},{4,5},{5,4},{6,7},{7,6},{8,9},{9,8},{10,11... | collective-permute-start | bytes 319496 | tf_op jit(solution)/shard_map/ppermute | solution.py:439
  7.7 1.3 %collective-permute-start.2 = (f32[104,256]{1,0:T(8,128)S(1)}, f32[104,256]{1,0:T(8,128)S(1)}, u32[]{:S(2)}, u32[]{:S(2)}) collective-permute-start(f32[104,256]{1,0:T(8,128)S(1)} %collective-permute-done.1.refs_2_), channel_id=1, source_target_pairs={{0,1},{1,0},{2,3},{3,2},{4,5},{5,4},{6,7},{7,6},{8,9},{9,8},{10,11... | collective-permute-start | bytes 319496 | tf_op jit(solution)/shard_map/ppermute | solution.py:439
  29.0 8.5 %collective-permute-start.3 = (f32[96,1024]{1,0:T(8,128)S(1)}, f32[96,1024]{1,0:T(8,128)S(1)}, u32[]{:S(2)}, u32[]{:S(2)}) collective-permute-start(f32[96,1024]{1,0:T(8,128)S(1)} %get-tuple-element.17.refs_0_), channel_id=1, source_target_pairs={{1,0},{4,1},{5,4},{8,5},{9,8},{12,9},{13,12},{16,13},{17,16},{20,1... | collective-permute-start | bytes 1179656 | tf_op jit(solution)/shard_map/ppermute | solution.py:427
  38.3 2.1 %collective-permute-start.4 = (f32[2,96,96]{2,1,0:T(8,128)S(1)}, f32[2,96,96]{2,1,0:T(8,128)S(1)}, u32[]{:S(2)}, u32[]{:S(2)}) collective-permute-start(f32[2,96,96]{2,1,0:T(8,128)S(1)} %shard_map.57.own_ref), channel_id=1, source_target_pairs={{0,1},{1,0},{4,5},{5,4},{8,9},{9,8},{12,13},{13,12},{16,17},{17,16... | collective-permute-start | bytes 221192 | tf_op jit(solution)/shard_map/ppermute | solution.py:487
  40.8 12.1 %copy-start.2 = (f32[2,2,96]{2,1,0:T(2,128)S(1)}, f32[2,2,96]{2,1,0:T(2,128)}, u32[]{:S(2)}) copy-start(f32[2,2,96]{2,1,0:T(2,128)} %param.9) | copy-start | bytes 4612
  40.8 5.7 %collective-permute-start.5 = (f32[2,96,96]{2,1,0:T(8,128)S(1)}, f32[2,96,96]{2,1,0:T(8,128)S(1)}, u32[]{:S(2)}, u32[]{:S(2)}) collective-permute-start(f32[2,96,96]{2,1,0:T(8,128)S(1)} %shard_map.58.own_ref), channel_id=1, source_target_pairs={{0,4},{1,5},{4,0},{5,1},{8,12},{9,13},{12,8},{13,9},{16,20},{17,21... | collective-permute-start | bytes 221192 | tf_op jit(solution)/shard_map/ppermute | solution.py:487
  46.8 7.9 %collective-permute-start.7 = (f32[2,96,96]{2,1,0:T(8,128)S(1)}, f32[2,96,96]{2,1,0:T(8,128)S(1)}, u32[]{:S(2)}, u32[]{:S(2)}) collective-permute-start(f32[2,96,96]{2,1,0:T(8,128)S(1)} %shard_map.59), channel_id=1, source_target_pairs={{0,8},{1,9},{4,12},{5,13},{8,16},{9,17},{12,20},{13,21},{16,24},{1... | collective-permute-start | bytes 221192 | tf_op jit(solution)/shard_map/ppermute | solution.py:478
  48.9 8.8 %collective-permute-start.8 = (f32[2,96,96]{2,1,0:T(8,128)S(1)}, f32[2,96,96]{2,1,0:T(8,128)S(1)}, u32[]{:S(2)}, u32[]{:S(2)}) collective-permute-start(f32[2,96,96]{2,1,0:T(8,128)S(1)} %shard_map.59), channel_id=1, source_target_pairs={{0,16},{1,17},{4,20},{5,21},{8,24},{9,25},{12,28},{13,29},{16,0},{... | collective-permute-start | bytes 221192 | tf_op jit(solution)/shard_map/ppermute | solution.py:478
  51.5 6.8 %collective-permute-start.6 = (f32[2,96,96]{2,1,0:T(8,128)S(1)}, f32[2,96,96]{2,1,0:T(8,128)S(1)}, u32[]{:S(2)}, u32[]{:S(2)}) collective-permute-start(f32[2,96,96]{2,1,0:T(8,128)S(1)} %shard_map.59), channel_id=1, source_target_pairs={{0,24},{1,25},{4,28},{5,29},{8,0},{9,1},{12,4},{13,5},{16,8},{17,9... | collective-permute-start | bytes 221192 | tf_op jit(solution)/shard_map/ppermute | solution.py:478
  58.9 3.6 %collective-permute-start.10 = (f32[2,2,256]{2,1,0:T(2,128)S(1)}, f32[2,2,256]{2,1,0:T(2,128)S(1)}, u32[]{:S(2)}, u32[]{:S(2)}) collective-permute-start(f32[2,2,256]{2,1,0:T(2,128)S(1)} %get-tuple-element.27), channel_id=1, source_target_pairs={{0,2},{1,3},{2,0},{3,1},{4,6},{5,7},{6,4},{7,5},{8,10},{9,11},{10,... | collective-permute-start | bytes 12296 | tf_op jit(solution)/shard_map/ppermute | solution.py:430
  60.4 2.1 %collective-permute-start.11 = (f32[2,2,256]{2,1,0:T(2,128)S(1)}, f32[2,2,256]{2,1,0:T(2,128)S(1)}, u32[]{:S(2)}, u32[]{:S(2)}) collective-permute-start(f32[2,2,256]{2,1,0:T(2,128)S(1)} %get-tuple-element.28), channel_id=1, source_target_pairs={{0,3},{1,0},{2,1},{3,2},{4,7},{5,4},{6,5},{7,6},{8,11},{9,8},{10,9... | collective-permute-start | bytes 12296 | tf_op jit(solution)/shard_map/ppermute | solution.py:430
  60.4 3.0 %collective-permute-start.9 = (f32[2,2,256]{2,1,0:T(2,128)S(1)}, f32[2,2,256]{2,1,0:T(2,128)S(1)}, u32[]{:S(2)}, u32[]{:S(2)}) collective-permute-start(f32[2,2,256]{2,1,0:T(2,128)S(1)} %get-tuple-element.26), channel_id=1, source_target_pairs={{0,1},{1,2},{2,3},{3,0},{4,5},{5,6},{6,7},{7,4},{8,9},{9,10},{10,1... | collective-permute-start | bytes 12296 | tf_op jit(solution)/shard_map/ppermute | solution.py:430
